TPU v7x, 256 devices: a whole 4x4x8 slice. The times are simulated.
256 devices in a mesh: grp: 2 (over core), fsdp: 16 (over y, z_lo), tp: 8 (over x, z_hi).
Axes of the slice: x: 4, y: 4, z: 8 (z_hi: 2, z_lo: 4; z = z_hi * 4 + z_lo), core: 2. Of those that a mesh axis runs over, the one named last changes fastest.
Arguments:
- frames: bfloat16 [2, 4096, 8192], P('grp', 'fsdp'), may hold values from -6 to 6
- rewards: bfloat16 [4096], P('fsdp'), may hold values from -5 to 5
- actions: int32 [2, 4096], P('grp', 'fsdp'), may hold values from 0 to 17
- fractions: int32 [2, 4096, 32], P('grp', 'fsdp'), may hold values from 0 to 63
- episode_shard: int32 [4096, 1], P('fsdp'), may hold values from 0 to 15, as said below
- table: float32 [64], replicated, may hold values from 0.02 to 0.98
- norm_gain: float32 [8192], replicated, may hold values from 0.1 to 1.9
- torso_weight: bfloat16 [8192, 4096], P(('grp', 'fsdp'), 'tp'), may hold values from -0.0625 to 0.0625
- embed_weight: bfloat16 [64, 4096], P(None, 'tp'), may hold values from -0.75 to 0.75
- value_weight: bfloat16 [18, 4096], P(None, 'tp'), may hold values from -0.59765625 to 0.59765625
Outputs:
- torso_grad: float32 [8192, 4096], P(('grp', 'fsdp'), 'tp')
- refreshed_weight: bfloat16 [8192, 4096], P(('grp', 'fsdp', 'tp'))
Inputs may be any that keep to these rules, and one draw needn't show every extreme that they name: `episode_shard`: of the rows of one index of fsdp, at most 24 belong to one learner shard, and in every such block some learner shard gets exactly 24; every learner shard gets at least one row from every block.
All inputs are finite; a program needn't handle non-finite values.
Results may differ from a plain program's by a relative error of at most 0.0075.
Values may be sent and summed in bfloat16 or wider, within the bound.
No kernel may reach another device: no remote copies, remote signals or barrier semaphores. Data moves between devices by JAX's collectives and lax.ppermute only.
A program may use at most 64 MiB of HBM per device.

v0:
```python
import jax
import jax.numpy as jnp
from jax import lax
from jax.sharding import PartitionSpec as P

ACTIONS = 18
COSINES = 64
FRACS = 64


def shards(
    frames,
    rewards,
    actions,
    fractions,
    episode_shard,
    table,
    norm_gain,
    torso_weight,
    embed_weight,
    value_weight,
):
    shard_total = lax.axis_size("fsdp")
    destination = episode_shard[:, 0]
    rows_block = destination.shape[0]
    lanes = jnp.arange(shard_total, dtype=jnp.int32)
    onehot = (destination[:, None] == lanes[None, :]).astype(jnp.int32)
    counts = lax.psum(jnp.sum(onehot.astype(jnp.float32), axis=0), "fsdp")
    row_weight = jnp.dot(
        onehot.astype(jnp.float32), float(rows_block) / counts, precision=lax.Precision.HIGHEST
    )
    rows_data = frames[0]
    action_rows = actions[0]
    fraction_rows = fractions[0]
    values = rows_data.astype(jnp.float32)
    mean_square = jnp.mean(values * values, axis=-1, keepdims=True)
    normed = (values * lax.rsqrt(mean_square + 1e-05) * norm_gain).astype(jnp.bfloat16)
    columns = normed
    preact = jnp.dot(
        columns,
        lax.all_gather(torso_weight, ("grp", "fsdp"), axis=0, tiled=True),
        preferred_element_type=jnp.float32,
    )
    choose_mask = (action_rows[:, None] == jnp.arange(ACTIONS, dtype=jnp.int32)[None, :]).astype(
        jnp.bfloat16
    )
    picked = jnp.dot(choose_mask, value_weight, preferred_element_type=jnp.float32)
    weighted = (jax.nn.silu(preact) * picked).astype(jnp.bfloat16)
    cosine = jnp.cos(
        jnp.pi * jnp.arange(COSINES, dtype=jnp.float32)[None, :] * table[:, None]
    ).astype(jnp.bfloat16)
    embedding = jax.nn.relu(
        jnp.dot(cosine, embed_weight, preferred_element_type=jnp.float32)
    ).astype(jnp.bfloat16)
    table_values = lax.dot_general(
        weighted, embedding, (((1,), (1,)), ((), ())), preferred_element_type=jnp.float32
    )
    selector = (
        fraction_rows[:, :, None] == jnp.arange(FRACS, dtype=jnp.int32)[None, None, :]
    ).astype(jnp.float32)
    partial_quant = jnp.einsum(
        "mj,mtj->mt", table_values, selector, precision=lax.Precision.HIGHEST
    )
    group_index = lax.axis_index("grp")
    own_slot = jnp.arange(2, dtype=jnp.int32)[:, None, None] == group_index
    stacked = jnp.where(
        own_slot, partial_quant[None, :, :], jnp.zeros_like(partial_quant)[None, :, :]
    )
    summed = lax.psum(stacked, ("grp", "tp"))
    target_quant = summed[0]
    online_quant = summed[1]
    learner = (group_index == 1).astype(jnp.float32)
    levels = jnp.einsum("mtj,j->mt", selector, table, precision=lax.Precision.HIGHEST)
    target_value = rewards.astype(jnp.float32)[:, None] + 0.99 * target_quant
    errors = target_value[:, None, :] - online_quant[:, :, None]
    weight = jnp.abs(levels[:, :, None] - (errors < 0).astype(jnp.float32))
    grad_quant = -(learner * row_weight)[:, None] * jnp.sum(
        weight * jnp.clip(errors, -1.0, 1.0), axis=-1
    )
    grad_table = jnp.einsum("mi,mij->mj", grad_quant, selector, precision=lax.Precision.HIGHEST)
    grad_feature = jnp.dot(
        grad_table, embedding.astype(jnp.float32), precision=lax.Precision.HIGHEST
    )
    gate_value = jax.nn.sigmoid(preact)
    grad_preact = (grad_feature * picked * gate_value * (1.0 + preact * (1.0 - gate_value))).astype(
        jnp.bfloat16
    )
    columns = normed
    torso_grad = lax.psum_scatter(
        lax.dot_general(
            columns, grad_preact, (((0,), (0,)), ((), ())), preferred_element_type=jnp.float32
        ),
        ("grp", "fsdp"),
        scatter_dimension=0,
        tiled=True,
    )
    updated = (torso_weight.astype(jnp.float32) - 0.01 * torso_grad).astype(jnp.bfloat16)
    refreshed_weight = lax.all_to_all(updated, "tp", split_axis=0, concat_axis=1, tiled=True)
    return (torso_grad, refreshed_weight)


def solution(mesh):
    placed = (
        P("grp", "fsdp", None),
        P("fsdp"),
        P("grp", "fsdp"),
        P("grp", "fsdp", None),
        P("fsdp", None),
        P(),
        P(),
        P(("grp", "fsdp"), "tp"),
        P(None, "tp"),
        P(None, "tp"),
    )
    return jax.shard_map(
        shards,
        mesh=mesh,
        in_specs=placed,
        out_specs=(P(("grp", "fsdp"), "tp"), P(("grp", "fsdp", "tp"), None)),
        check_vma=False,
    )
```

profile of v0, /device:TPU:32, one launch (start us, length us, event | category | flops | bytes accessed | tf_op | source)
XLA Modules:
  0.0 673.1 jit_solution(3532035005112224799)
XLA Ops:
  7.2 0.0 copy-start
  7.2 0.0 all-gather.2.cloned.1.call-start
  7.3 0.7 all-gather.2.cloned.1.call-update
  8.0 0.0 all-reduce.2.cloned.1.call-start
  8.0 0.8 convert_reduce_fusion
  8.8 40.2 %psum.14 = f32[16]{0:T(128)S(1)} all-reduce(f32[16]{0:T(128)S(1)} %convert_reduce_fusion), channel_id=1, replica_groups=mesh['grp'=2,'fsdp'=16,'tp'=8] {'fsdp'}, use_global_device_ids=true, to_apply=%region_2.0 | all-reduce | flops 16 | bytes 128 | tf_op jit(solution)/shard_map/psum | solution.py:28
  49.0 3.2 fusion
  52.2 0.1 fusion.25
  52.4 0.0 copy-done.5
  52.4 0.3 fusion.12
  52.7 0.3 fusion.19
  53.0 3.8 fusion.15
  56.8 24.9 %all-gather.2.cloned.1.call-done = bf16[8192,512]{1,0:T(8,128)(2,1)} async-done(((bf16[256,512]{1,0:T(8,128)(2,1)}), bf16[8192,512]{1,0:T(8,128)(2,1)}) %all-gather.2.cloned.1.call-update) | async-done | bytes 8388624 | tf_op jit(solution)/shard_map/all_gather | solution.py:41
  81.7 7.0 %fusion.10 = f32[256,512]{1,0:T(8,128)S(1)} fusion(bf16[8192,512]{1,0:T(8,128)(2,1)} %all-gather.2.cloned.1.call-done, bf16[1,256,8192]{2,1,0:T(8,128)(2,1)} %param.10, f32[8192]{0:T(1024)S(1)} %copy-done.3, f32[256]{0:T(256)S(1)} %add_rsqrt_fusion), kind=kOutput, calls=%fused_computation.17 | convolution fusion | flops 2155872256 | bytes 13140992 | tf_op jit(solution)/shard_map/dot_general | solution.py:39
  88.7 0.3 fusion.18
  89.0 0.4 select_reduce_fusion.1
  89.4 0.7 broadcast_select_fusion
  90.1 0.0 all-reduce.2.cloned.1.call-update
  90.1 0.0 reduce-scatter.2.cloned.1.call-start
  90.2 2.8 copy.17
  93.0 172.4 %all-reduce.2.cloned.1.call-done = f32[2,256,32]{1,2,0:T(8,128)} async-done(((f32[2,256,32]{1,2,0:T(8,128)}), f32[2,256,32]{1,2,0:T(8,128)}) %all-reduce.2.cloned.1.call-update) | async-done | bytes 65552 | tf_op jit(solution)/shard_map/psum | solution.py:69
  265.4 0.8 slice_bitcast_fusion
  266.1 0.8 fusion.22
  266.9 0.3 fusion.14
  267.3 0.4 select_reduce_fusion
  267.6 0.5 fusion.7
  268.2 10.4 %fusion.8 = f32[8192,512]{1,0:T(8,128)} fusion(bf16[256,512]{1,0:T(8,128)(2,1)S(1)} %fusion.7, bf16[1,256,8192]{2,1,0:T(8,128)(2,1)} %param.10, f32[8192]{0:T(1024)S(1)} %copy-done.3, f32[256]{0:T(256)S(1)} %add_rsqrt_fusion), kind=kOutput, calls=%fused_computation.16 | convolution fusion | flops 2155872256 | bytes 21267456 | tf_op jit(solution)/shard_map/dot_general | solution.py:90
  278.6 0.0 reduce-scatter.2.cloned.1.call-update
  278.6 362.9 %reduce-scatter.2.cloned.1.call-done = f32[256,512]{1,0:T(8,128)} async-done(((f32[8192,512]{1,0:T(8,128)}), f32[256,512]{1,0:T(8,128)}) %reduce-scatter.2.cloned.1.call-update) | async-done | bytes 524304 | tf_op jit(solution)/shard_map/reduce_scatter | solution.py:89
  641.5 1.1 subtract_convert_fusion
  642.6 23.2 %all_to_all.19 = bf16[8,32,512]{2,1,0:T(8,128)(2,1)S(1)} all-to-all(bf16[8,32,512]{2,1,0:T(8,128)(2,1)S(1)} %bitcast.39), channel_id=1, replica_groups=mesh['grp'=2,'fsdp'=16,'tp'=8] {'tp'}, dimensions={0} | all-to-all | bytes 524288 | tf_op jit(solution)/shard_map/all_to_all | solution.py:98
  665.8 0.7 copy.31
  (22 shorter events, 0.1 us)
Async XLA Ops:
  7.2 45.2 %copy-start = (bf16[64,512]{1,0:T(8,128)(2,1)S(1)}, bf16[64,512]{1,0:T(8,128)(2,1)}, u32[]{:S(2)}) copy-start(bf16[64,512]{1,0:T(8,128)(2,1)} %param.18) | copy-start | bytes 196612
  7.2 45.0 %copy-start.7 = (s32[256,1]{0,1:T(1,128)S(1)}, s32[256,1]{0,1:T(1,128)}, u32[]{:S(2)}) copy-start(s32[256,1]{0,1:T(1,128)} %param.14) | copy-start | bytes 3076
  7.2 45.2 %copy-start.5 = (f32[64]{0:T(128)S(1)}, f32[64]{0:T(128)}, u32[]{:S(2)}) copy-start(f32[64]{0:T(128)} %param.15) | copy-start | bytes 772
  7.2 45.5 %copy-start.4 = (bf16[18,512]{1,0:T(8,128)(2,1)S(1)}, bf16[18,512]{1,0:T(8,128)(2,1)}, u32[]{:S(2)}) copy-start(bf16[18,512]{1,0:T(8,128)(2,1)} %param.19) | copy-start | bytes 55300
  7.2 45.5 %copy-start.6 = (s32[1,256]{1,0:T(1,128)S(1)}, s32[1,256]{1,0:T(1,128)}, u32[]{:S(2)}) copy-start(s32[1,256]{1,0:T(1,128)} %param.12) | copy-start | bytes 3076
  7.2 45.8 %copy-start.2 = (s32[1,256,32]{1,2,0:T(8,128)S(1)}, s32[1,256,32]{1,2,0:T(8,128)}, u32[]{:S(2)}) copy-start(s32[1,256,32]{1,2,0:T(8,128)} %param.13) | copy-start | bytes 98308
  7.2 74.4 %all-gather.2.cloned.1.call-start = ((), (), s32[]{:S(2)}) async-start(), calls=%async_computation.2 | async-start | bytes 8650752 | tf_op jit(solution)/shard_map/all_gather | solution.py:41
  8.0 257.4 %all-reduce.2.cloned.1.call-start = ((), (), s32[]{:S(2)}) async-start(), calls=%async_computation.3 | async-start | bytes 131072 | tf_op jit(solution)/shard_map/psum | solution.py:69
  49.0 32.6 %copy-start.3 = (f32[8192]{0:T(1024)S(1)}, f32[8192]{0:T(1024)}, u32[]{:S(2)}) copy-start(f32[8192]{0:T(1024)} %param.16) | copy-start | bytes 98308
  56.8 33.4 %copy-start.8 = (bf16[256]{0:T(256)(128)(2,1)S(1)}, bf16[256]{0:T(256)(128)(2,1)}, u32[]{:S(2)}) copy-start(bf16[256]{0:T(256)(128)(2,1)} %param.11) | copy-start | bytes 1540
  90.1 551.4 %reduce-scatter.2.cloned.1.call-start = ((), (), s32[]{:S(2)}) async-start(), calls=%async_computation.4 | async-start | bytes 17301504 | tf_op jit(solution)/shard_map/reduce_scatter | solution.py:89
  278.6 362.9 %copy-start.1 = (bf16[256,512]{1,0:T(8,128)(2,1)S(1)}, bf16[256,512]{1,0:T(8,128)(2,1)}, u32[]{:S(2)}) copy-start(bf16[256,512]{1,0:T(8,128)(2,1)} %param.17) | copy-start | bytes 786436
Sparse Core Ops, SparseCore 0:
  9.9 71.6 all-gather.1
  90.2 175.1 all-reduce.1
  278.7 362.7 reduce-scatter.1
where the time goes:
time: 677 us; the launch traced here: 673 us
  waiting for transfers between devices  561 us (83%)
  blocking collectives  63.4 us (9%)
  matrix products  22.8 us (3%)
  between operations  13.9 us (2%)
  other arithmetic  7.66 us (1%)
    reduce_scatter x1, waiting for transfers between devices, shards(): lax.psum_scatter(lax.dot_general(columns, grad_preact, (((0,), (0,)), (()...  363 us
    psum x1, waiting for transfers between devices, shards(): summed = lax.psum(stacked, ('grp', 'tp'))  172 us
    psum x1, blocking collectives, shards(): counts = lax.psum(jnp.sum(onehot.astype(jnp.float32), axis=0), 'fsdp')  40.2 us
    all_gather x1, waiting for transfers between devices, shards(): lax.all_gather(torso_weight, ('grp', 'fsdp'), axis=0, tiled=True)  24.9 us
    all_to_all x1, blocking collectives, shards(): lax.all_to_all(updated, 'tp', split_axis=0, concat_axis=1, tiled=True)  23.2 us
  transfers between devices with their start and end apart: 3, of which 3 were waited for; matrix products, arithmetic and copies ran while one was open for 2% of the time, Pallas kernels for 0%

commit v1 on v0

v1 whole, which is shorter than its diff:
```python
import jax
import jax.numpy as jnp
from jax import lax
from jax.sharding import PartitionSpec as P

ACTIONS = 18
COSINES = 64
FRACS = 64
Z = 4
Y = 4

SWAP = [(0, 1), (1, 0)]


def z_from(step):
    return [(f, (f // Z) * Z + (f % Z - step) % Z) for f in range(Y * Z)]


def y_from(step):
    return [(f, (f - step * Z) % (Y * Z)) for f in range(Y * Z)]


def roll_from(array, start, axis):
    size = array.shape[axis]
    return lax.dynamic_slice_in_dim(jnp.concatenate([array, array], axis), start, size, axis)


def shards(
    frames,
    rewards,
    actions,
    fractions,
    episode_shard,
    table,
    norm_gain,
    torso_weight,
    embed_weight,
    value_weight,
):
    group = lax.axis_index("grp")
    place = lax.axis_index("fsdp")
    shard_total = lax.axis_size("fsdp")
    whole = lax.all_gather(torso_weight, ("grp", "fsdp"), axis=0, tiled=True)
    rows_block = frames.shape[1]
    width = frames.shape[2]
    half = rows_block // 2
    own_rows = group * half
    other_rows = (1 - group) * half

    def swap(array):
        kept = lax.dynamic_slice_in_dim(array, own_rows, half, 0)
        sent = lax.dynamic_slice_in_dim(array, other_rows, half, 0)
        got = lax.ppermute(sent, "grp", SWAP)
        return jnp.where(group == 0, kept, got), jnp.where(group == 0, got, kept)

    with jax.named_scope("rows_swap"):
        target_rows, online_rows = swap(frames[0])
        ints = jnp.concatenate([fractions[0].T, actions[0][None, :]], 0)
        target_ints, online_ints = swap(ints.T)
        ints_all = jnp.concatenate([target_ints, online_ints], 0).T
        fraction_rows = ints_all[:-1]
        action_rows = ints_all[-1]

    def norm(rows):
        values = rows.astype(jnp.float32)
        mean_square = jnp.mean(values * values, axis=-1, keepdims=True)
        return (values * lax.rsqrt(mean_square + 1e-05) * norm_gain).astype(jnp.bfloat16)

    normed_target = norm(target_rows)
    normed_online = norm(online_rows)
    normed = jnp.concatenate([normed_target, normed_online], 0)

    with jax.named_scope("columns_exchange"):
        block = width // (2 * shard_total)
        own_cols = lax.dynamic_slice_in_dim(normed_online, group * (width // 2), width // 2, 1)
        other_cols = lax.dynamic_slice_in_dim(
            normed_online, (1 - group) * (width // 2), width // 2, 1
        )
        pieces = jnp.stack(
            [
                own_cols.reshape(half, shard_total, block),
                other_cols.reshape(half, shard_total, block),
            ],
            2,
        )
        pieces = jnp.transpose(pieces, (1, 0, 2, 3)).reshape(shard_total, half, 2 * block)
        columns = lax.all_to_all(pieces, "fsdp", 0, 0, tiled=True)
        columns = columns.reshape(Y, Z, half, 2 * block)
        columns = roll_from(roll_from(columns, place // Z, 0), place % Z, 1)

    with jax.named_scope("counts"):
        lanes = jnp.arange(shard_total, dtype=jnp.int32)
        onehot = episode_shard[:, :1] == lanes[None, :]
        local_counts = jnp.sum(onehot.astype(jnp.float32), axis=0)
        counts = jnp.sum(
            lax.all_to_all(
                jnp.broadcast_to(local_counts[None, :], (shard_total, shard_total)),
                "fsdp",
                0,
                0,
                tiled=True,
            ),
            axis=0,
        )
        inverse = float(rows_block) / counts
        row_weight = jnp.sum(jnp.where(onehot, inverse[None, :], 0.0), axis=1)
        row_weight = lax.dynamic_slice_in_dim(row_weight, own_rows, half, 0)

    choose_mask = (action_rows[:, None] == jnp.arange(ACTIONS, dtype=jnp.int32)[None, :]).astype(
        jnp.bfloat16
    )
    picked = jnp.dot(choose_mask, value_weight, preferred_element_type=jnp.float32)
    cosine = jnp.cos(
        jnp.pi * jnp.arange(COSINES, dtype=jnp.float32)[None, :] * table[:, None]
    ).astype(jnp.bfloat16)
    embedding = jax.nn.relu(
        jnp.dot(cosine, embed_weight, preferred_element_type=jnp.float32)
    ).astype(jnp.bfloat16)
    ids = jnp.arange(FRACS, dtype=jnp.int32)
    online_fractions = fraction_rows[:, half:]
    online_select = online_fractions[:, None, :] == ids[None, :, None]
    levels = jnp.sum(jnp.where(online_select, table[None, :, None], 0.0), axis=1)
    reward_rows = lax.dynamic_slice_in_dim(rewards, own_rows, half, 0).astype(jnp.float32)

    preact = jnp.dot(normed, whole, preferred_element_type=jnp.float32)
    weighted = (jax.nn.silu(preact) * picked).astype(jnp.bfloat16)
    table_values = lax.dot_general(
        embedding, weighted, (((1,), (1,)), ((), ())), preferred_element_type=jnp.float32
    )
    partial_quant = jnp.sum(
        jnp.where(
            fraction_rows[:, None, :] == ids[None, :, None], table_values[None, :, :], 0.0
        ),
        axis=1,
    )
    with jax.named_scope("quant_sum"):
        tp_total = lax.axis_size("tp")
        quant = jnp.sum(
            lax.all_to_all(
                jnp.broadcast_to(partial_quant[None], (tp_total,) + partial_quant.shape),
                "tp",
                0,
                0,
                tiled=True,
            ),
            axis=0,
        )
    target_quant = quant[:, :half]
    online_quant = quant[:, half:]
    target_value = reward_rows[None, :] + 0.99 * target_quant
    errors = target_value[None, :, :] - online_quant[:, None, :]
    weight = jnp.abs(levels[:, None, :] - (errors < 0).astype(jnp.float32))
    grad_quant = -row_weight[None, :] * jnp.sum(weight * jnp.clip(errors, -1.0, 1.0), axis=1)
    grad_table = jnp.sum(jnp.where(online_select, grad_quant[:, None, :], 0.0), axis=0)
    grad_feature = lax.dot_general(
        grad_table,
        embedding.astype(jnp.float32),
        (((0,), (0,)), ((), ())),
        precision=lax.Precision.HIGHEST,
    )
    online_preact = preact[half:]
    gate_value = jax.nn.sigmoid(online_preact)
    grad_preact = (
        grad_feature
        * picked[half:]
        * gate_value
        * (1.0 + online_preact * (1.0 - gate_value))
    ).astype(jnp.bfloat16)

    with jax.named_scope("grad_gather"):
        quad = jnp.stack(
            [grad_preact] + [lax.ppermute(grad_preact, "fsdp", z_from(k)) for k in range(1, Z)]
        )
        below = lax.ppermute(quad, "fsdp", y_from(1))
        above = lax.ppermute(quad, "fsdp", y_from(3))
        far_low = lax.ppermute(above[: Z // 2], "fsdp", y_from(3))
        far_high = lax.ppermute(below[Z // 2 :], "fsdp", y_from(1))

    def product(cols, grads):
        return lax.dot_general(
            cols.reshape(-1, cols.shape[-1]),
            grads.reshape(-1, grads.shape[-1]),
            (((0,), (0,)), ((), ())),
            preferred_element_type=jnp.float32,
        )

    part = (
        product(columns[0], quad)
        + product(columns[1], below)
        + product(columns[3], above)
        + product(columns[2, : Z // 2], far_low)
        + product(columns[2, Z // 2 :], far_high)
    )
    torso_grad = part[:block] + lax.ppermute(part[block:], "grp", SWAP)
    updated = (torso_weight.astype(jnp.float32) - 0.01 * torso_grad).astype(jnp.bfloat16)
    refreshed_weight = lax.all_to_all(updated, "tp", split_axis=0, concat_axis=1, tiled=True)
    return (torso_grad, refreshed_weight)


def solution(mesh):
    placed = (
        P("grp", "fsdp", None),
        P("fsdp"),
        P("grp", "fsdp"),
        P("grp", "fsdp", None),
        P("fsdp", None),
        P(),
        P(),
        P(("grp", "fsdp"), "tp"),
        P(None, "tp"),
        P(None, "tp"),
    )
    return jax.shard_map(
        shards,
        mesh=mesh,
        in_specs=placed,
        out_specs=(P(("grp", "fsdp"), "tp"), P(("grp", "fsdp", "tp"), None)),
        check_vma=False,
    )
```

time: 677 us -> 218 us (0.32)
  waiting for transfers between devices: 561 us -> 111 us
  blocking collectives: 63.4 us -> 17 us
  starting transfers between devices: 0.12 us -> 33 us
  matrix products: 22.8 us -> 10.6 us
  local copies, waits for them, and re-layouts: 4.37 us -> 15.3 us
    reduce_scatter x1 -> x0, waiting for transfers between devices: 363 us -> none  [shards(): lax.psum_scatter(lax.dot_general(columns, grad_preact, (((0,), (0,)), (()...]
    psum x1 -> x0, waiting for transfers between devices: 172 us -> none  [shards(): summed = lax.psum(stacked, ('grp', 'tp'))]
    all_gather x1, waiting for transfers between devices: 24.9 us -> 74.1 us  [shards(): whole = lax.all_gather(torso_weight, ('grp', 'fsdp'), axis=0, tiled=True)]
    psum x1 -> x0, blocking collectives: 40.2 us -> none  [shards(): counts = lax.psum(jnp.sum(onehot.astype(jnp.float32), axis=0), 'fsdp')]
    ppermute x0 -> x10, waiting for transfers between devices: none -> 25 us  [the longest x1 11.4 us: shards(): above = lax.ppermute(quad, 'fsdp', y_from(3))]
    all_to_all x0 -> x3, starting transfers between devices: none -> 23.7 us  [the longest x1 8.65 us: shards(): lax.all_to_all(jnp.broadcast_to(local_counts[None, :], (shard_total, shar...]
    dot_general x6 -> x8, matrix products: 22.2 us -> 9.98 us  [the longest x1 6.33 us: shards(): preact = jnp.dot(normed, whole, preferred_element_type=jnp.float32)]
    all_to_all x0 -> x3, waiting for transfers between devices: none -> 11.2 us  [the longest x1 11.2 us: shards(): lax.all_to_all(jnp.broadcast_to(partial_quant[None], (tp_total,) + partia...]
  transfers between devices with their start and end apart: 3 -> 14, of which waited for: 3 -> 7; matrix products, arithmetic and copies ran while one was open for 2% -> 16% of each run, Pallas kernels for 0% -> 0%
where the time goes in v1:
time: 218 us; the launch traced here: 215 us
  waiting for transfers between devices  111 us (51%)
  starting transfers between devices  33 us (15%)
  blocking collectives  17 us (8%)
  local copies, waits for them, and re-layouts  15.3 us (7%)
  between operations  14.4 us (7%)
  other arithmetic  14 us (6%)
  matrix products  10.6 us (5%)
    all_gather x1, waiting for transfers between devices, shards(): whole = lax.all_gather(torso_weight, ('grp', 'fsdp'), axis=0, tiled=True)  74.1 us
    all_to_all x1, blocking collectives, shards(): lax.all_to_all(updated, 'tp', split_axis=0, concat_axis=1, tiled=True)  17 us
    ppermute x1, waiting for transfers between devices, shards(): above = lax.ppermute(quad, 'fsdp', y_from(3))  11.4 us
    all_to_all x1, waiting for transfers between devices, shards(): lax.all_to_all(jnp.broadcast_to(partial_quant[None], (tp_total,) + partia...  11.2 us
    all_to_all x1, starting transfers between devices, shards(): lax.all_to_all(jnp.broadcast_to(local_counts[None, :], (shard_total, shar...  8.65 us
    ppermute x3, waiting for transfers between devices, shards(): lax.ppermute(grad_preact, 'fsdp', z_from(k))  7.74 us
    all_to_all x1, starting transfers between devices, shards(): columns = lax.all_to_all(pieces, 'fsdp', 0, 0, tiled=True)  7.63 us
    all_to_all x1, starting transfers between devices, shards(): lax.all_to_all(jnp.broadcast_to(partial_quant[None], (tp_total,) + partia...  7.37 us
  transfers between devices with their start and end apart: 14, of which 7 were waited for; matrix products, arithmetic and copies ran while one was open for 16% of the time, Pallas kernels for 0%

profile of v1, /device:TPU:32, one launch (start us, length us, event | category | flops | bytes accessed | tf_op | source)
XLA Modules:
  0.0 215.2 jit_solution(5258170492067754753)
XLA Ops:
  7.2 0.7 all-gather.2.cloned.1.call-update
  7.9 3.1 %dynamic-slice_bitcast_fusion = bf16[128,8192]{1,0:T(8,128)(2,1)} fusion(bf16[1,256,8192]{2,1,0:T(8,128)(2,1)} %param.10, s32[]{:T(128)S(6)} %select_n.74), kind=kLoop, calls=%fused_computation.25 | loop fusion | bytes 4194308 | tf_op jit(solution)/shard_map/rows_swap/dynamic_slice | solution.py:52
  11.8 8.7 %all-to-all-start.1 = ((f32[16,1,16]{2,1,0:T(1,128)}), f32[16,1,16]{2,1,0:T(1,128)S(1)}, u32[]{:S(2)}, u32[]{:S(2)}) async-start(f32[16,1,16]{2,1,0:T(1,128)} %broadcast_in_dim.46), calls=%async_computation.1 | async-start | bytes 16384 | tf_op jit(solution)/shard_map/counts/all_to_all | solution.py:96
  20.5 3.9 %fusion.3 = (f32[128]{0:T(128)S(1)}, f32[128]{0:T(128)S(1)}) fusion(bf16[128,8192]{1,0:T(8,128)(2,1)S(1)} %collective-permute-done, bf16[1,256,8192]{2,1,0:T(8,128)(2,1)} %param.10, s32[]{:T(128)S(6)} %select_n.75, pred[]{:T(512)S(6)} %eq.32), kind=kLoop, calls=%fused_computation.7 | loop fusion | flops 8388352 | bytes 4195333 | tf_op jit(solution)/shard_map/reduce_sum | solution.py:66
  24.4 4.4 %fusion.5 = (bf16[128,8192]{1,0:T(8,128)(2,1)}, bf16[128,8192]{1,0:T(8,128)(2,1)S(1)}) fusion(f32[128]{0:T(128)S(1)} %get-tuple-element.19, f32[8192]{0:T(1024)S(1)} %copy-done.5, bf16[128,8192]{1,0:T(8,128)(2,1)} %copy-done.2, bf16[1,256,8192]{2,1,0:T(8,128)(2,1)S(1)} %copy-done.1, s32[]{:T(128)S(6)} %select_n.75, pred[]{:T(512)S(6)} %eq.32, ...), kind=kLoop, calls=%fused_computation.9 | loop fusion | flops 10485760 | bytes 8422405 | tf_op jit(solution)/shard_map/convert_element_type | solution.py:67
  28.9 1.2 constant_dynamic-slice_fusion.1
  30.0 2.3 %copy.29 = bf16[128,4096]{0,1:T(8,128)(2,1)} copy(bf16[128,4096]{1,0:T(8,128)(2,1)} %get-tuple-element.13) | data formatting | bytes 2097152 | tf_op jit(solution)/shard_map/columns_exchange/dynamic_slice | solution.py:75
  32.3 1.3 copy.30
  33.6 1.8 maximum_bitcast_fusion
  35.4 1.5 copy.31
  36.9 7.6 %all-to-all-start = ((bf16[16,128,512]{1,2,0:T(8,128)(2,1)}), bf16[16,128,512]{1,2,0:T(8,128)(2,1)}, u32[]{:S(2)}, u32[]{:S(2)}) async-start(bf16[16,128,512]{1,2,0:T(8,128)(2,1)} %bitcast.69), calls=%async_computation | async-start | bytes 4194304 | tf_op jit(solution)/shard_map/columns_exchange/all_to_all | solution.py:87
  45.1 0.7 collective-permute-done.1
  46.2 74.1 %all-gather.2.cloned.1.call-done = bf16[8192,512]{1,0:T(8,128)(2,1)} async-done(((bf16[256,512]{1,0:T(8,128)(2,1)}), bf16[8192,512]{1,0:T(8,128)(2,1)}) %all-gather.2.cloned.1.call-update) | async-done | bytes 8388624 | tf_op jit(solution)/shard_map/all_gather | solution.py:43
  120.3 6.3 %fusion.6 = f32[256,512]{1,0:T(8,128)S(1)} fusion(bf16[8192,512]{1,0:T(8,128)(2,1)} %all-gather.2.cloned.1.call-done, bf16[128,8192]{1,0:T(8,128)(2,1)S(1)} %get-tuple-element.7, bf16[128,8192]{1,0:T(8,128)(2,1)} %get-tuple-element.6), kind=kOutput, calls=%fused_computation.14 | convolution fusion | flops 2155872256 | bytes 13107200 | tf_op jit(solution)/shard_map/dot_general | solution.py:125
  126.6 0.8 copy-done.11
  128.1 0.7 broadcast_in_dim.53
  128.8 7.4 %all-to-all-start.2 = ((f32[8,32,256]{2,1,0:T(8,128)}), f32[8,32,256]{2,1,0:T(8,128)S(1)}, u32[]{:S(2)}, u32[]{:S(2)}) async-start(f32[8,32,256]{2,1,0:T(8,128)} %broadcast_in_dim.53), calls=%async_computation.2 | async-start | bytes 524288 | tf_op jit(solution)/shard_map/quant_sum/all_to_all | solution.py:139
  136.6 2.8 %copy.32 = bf16[4,4,128,512]{3,2,1,0:T(8,128)(2,1)S(1)} copy(bf16[4,4,128,512]{2,3,1,0:T(8,128)(2,1)} %bitcast.6) | data formatting | bytes 4194304 | tf_op jit(solution)/shard_map/columns_exchange/reshape | solution.py:88
  139.4 11.2 %all-to-all-done.2 = f32[8,32,256]{2,1,0:T(8,128)S(1)} async-done(((f32[8,32,256]{2,1,0:T(8,128)}), f32[8,32,256]{2,1,0:T(8,128)S(1)}, u32[]{:S(2)}, u32[]{:S(2)}) %all-to-all-start.2) | async-done | bytes 262176 | tf_op jit(solution)/shard_map/quant_sum/all_to_all | solution.py:139
  151.0 1.3 fusion.16
  152.4 2.7 %collective-permute-start.3 = (bf16[128,512]{1,0:T(8,128)(2,1)S(1)}, bf16[128,512]{1,0:T(8,128)(2,1)S(1)}, u32[]{:S(2)}, u32[]{:S(2)}) collective-permute-start(bf16[128,512]{1,0:T(8,128)(2,1)S(1)} %fusion.16), channel_id=1, source_target_pairs={{0,16},{8,24},{16,0},{24,8},{32,48},{40,56},{48,32},{56,40},{64,80... | collective-permute-start | bytes 393224 | tf_op jit(solution)/shard_map/grad_gather/ppermute | solution.py:172
  155.1 0.7 fusion.11
  155.9 7.7 %collective-permute-done.2 = bf16[128,512]{1,0:T(8,128)(2,1)S(1)} collective-permute-done((bf16[128,512]{1,0:T(8,128)(2,1)S(1)}, bf16[128,512]{1,0:T(8,128)(2,1)S(1)}, u32[]{:S(2)}, u32[]{:S(2)}) %collective-permute-start.2) | collective-permute-done | bytes 131104 | tf_op jit(solution)/shard_map/grad_gather/ppermute | solution.py:172
  163.7 2.4 %collective-permute-start.5 = (bf16[4,128,512]{2,1,0:T(8,128)(2,1)S(1)}, bf16[4,128,512]{2,1,0:T(8,128)(2,1)S(1)}, u32[]{:S(2)}, u32[]{:S(2)}) collective-permute-start(bf16[4,128,512]{2,1,0:T(8,128)(2,1)S(1)} %pad_maximum_fusion), channel_id=1, source_target_pairs={{0,96},{8,104},{16,112},{24,120},{32,0},{40,8},{48,16},{56,24},{64... | collective-permute-start | bytes 1572872 | tf_op jit(solution)/shard_map/grad_gather/ppermute | solution.py:174
  166.5 0.7 fusion.10
  167.5 11.4 %collective-permute-done.6 = bf16[4,128,512]{2,1,0:T(8,128)(2,1)S(1)} collective-permute-done((bf16[4,128,512]{2,1,0:T(8,128)(2,1)S(1)}, bf16[4,128,512]{2,1,0:T(8,128)(2,1)S(1)}, u32[]{:S(2)}, u32[]{:S(2)}) %collective-permute-start.6) | collective-permute-done | bytes 524320 | tf_op jit(solution)/shard_map/grad_gather/ppermute | solution.py:175
  179.4 2.9 %collective-permute-start.8 = (bf16[2,128,512]{2,1,0:T(8,128)(2,1)S(1)}, bf16[2,128,512]{2,1,0:T(8,128)(2,1)S(1)}, u32[]{:S(2)}, u32[]{:S(2)}) collective-permute-start(bf16[2,128,512]{2,1,0:T(8,128)(2,1)S(1)} %slice.78), channel_id=1, source_target_pairs={{0,96},{8,104},{16,112},{24,120},{32,0},{40,8},{48,16},{56,24},{64... | collective-permute-start | bytes 786440 | tf_op jit(solution)/shard_map/grad_gather/ppermute | solution.py:177
  183.2 3.3 %collective-permute-done.7 = bf16[2,128,512]{2,1,0:T(8,128)(2,1)S(1)} collective-permute-done((bf16[2,128,512]{2,1,0:T(8,128)(2,1)S(1)}, bf16[2,128,512]{2,1,0:T(8,128)(2,1)S(1)}, u32[]{:S(2)}, u32[]{:S(2)}) %collective-permute-start.7) | collective-permute-done | bytes 262176 | tf_op jit(solution)/shard_map/grad_gather/ppermute | solution.py:176
  187.8 1.9 collective-permute-done.9
  189.7 0.9 subtract_convert_fusion
  190.6 17.0 %all_to_all.35 = bf16[8,32,512]{2,1,0:T(8,128)(2,1)S(1)} all-to-all(bf16[8,32,512]{2,1,0:T(8,128)(2,1)S(1)} %bitcast.81), channel_id=1, replica_groups=mesh['grp'=2,'fsdp'=16,'tp'=8] {'tp'}, dimensions={0} | all-to-all | bytes 524288 | tf_op jit(solution)/shard_map/all_to_all | solution.py:196
  207.6 0.7 copy.36
  (74 shorter events, 6.7 us)
Async XLA Ops:
  7.2 37.5 %copy-start = (bf16[64,512]{1,0:T(8,128)(2,1)S(1)}, bf16[64,512]{1,0:T(8,128)(2,1)}, u32[]{:S(2)}) copy-start(bf16[64,512]{1,0:T(8,128)(2,1)} %param.18) | copy-start | bytes 196612
  7.2 113.1 %all-gather.2.cloned.1.call-start = ((), (), s32[]{:S(2)}) async-start(), calls=%async_computation.4 | async-start | bytes 8650752 | tf_op jit(solution)/shard_map/all_gather | solution.py:43
  7.9 3.2 %copy-start.9 = (s32[256,1]{0,1:T(1,128)S(1)}, s32[256,1]{0,1:T(1,128)}, u32[]{:S(2)}) copy-start(s32[256,1]{0,1:T(1,128)} %param.14) | copy-start | bytes 3076
  7.9 16.5 %copy-start.5 = (f32[8192]{0:T(1024)S(1)}, f32[8192]{0:T(1024)}, u32[]{:S(2)}) copy-start(f32[8192]{0:T(1024)} %param.16) | copy-start | bytes 98308
  11.1 9.4 %collective-permute-start = (bf16[128,8192]{1,0:T(8,128)(2,1)}, bf16[128,8192]{1,0:T(8,128)(2,1)S(1)}, u32[]{:S(2)}, u32[]{:S(2)}) collective-permute-start(bf16[128,8192]{1,0:T(8,128)(2,1)} %dynamic-slice_bitcast_fusion), channel_id=1, source_target_pairs={{0,128},{128,0},{1,129},{129,1},{2,130},{130,2},{3,131},{131,3},{4... | collective-permute-start | bytes 6291464 | tf_op jit(solution)/shard_map/rows_swap/ppermute | solution.py:53
  11.8 25.0 %all-to-all-start.1 = ((f32[16,1,16]{2,1,0:T(1,128)}), f32[16,1,16]{2,1,0:T(1,128)S(1)}, u32[]{:S(2)}, u32[]{:S(2)}) async-start(f32[16,1,16]{2,1,0:T(1,128)} %broadcast_in_dim.46), calls=%async_computation.1 | async-start | bytes 16384 | tf_op jit(solution)/shard_map/counts/all_to_all | solution.py:96
  20.5 4.0 %copy-start.1 = (bf16[1,256,8192]{2,1,0:T(8,128)(2,1)S(1)}, bf16[1,256,8192]{2,1,0:T(8,128)(2,1)}, u32[]{:S(2)}) copy-start(bf16[1,256,8192]{2,1,0:T(8,128)(2,1)} %param.10) | copy-start | bytes 12582916
  20.5 3.9 %copy-start.2 = (bf16[128,8192]{1,0:T(8,128)(2,1)}, bf16[128,8192]{1,0:T(8,128)(2,1)S(1)}, u32[]{:S(2)}) copy-start(bf16[128,8192]{1,0:T(8,128)(2,1)S(1)} %collective-permute-done) | copy-start | bytes 6291460
  36.9 7.7 %copy-start.4 = (s32[1,256,32]{1,2,0:T(8,128)S(1)}, s32[1,256,32]{1,2,0:T(8,128)}, u32[]{:S(2)}) copy-start(s32[1,256,32]{1,2,0:T(8,128)} %param.13) | copy-start | bytes 98308
  36.9 7.7 %copy-start.7 = (s32[1,256]{1,0:T(1,128)S(1)}, s32[1,256]{1,0:T(1,128)}, u32[]{:S(2)}) copy-start(s32[1,256]{1,0:T(1,128)} %param.12) | copy-start | bytes 3076
  36.9 7.8 %copy-start.8 = (f32[64]{0:T(128)S(1)}, f32[64]{0:T(128)}, u32[]{:S(2)}) copy-start(f32[64]{0:T(128)} %param.15) | copy-start | bytes 772
  36.9 8.1 %copy-start.10 = (bf16[256]{0:T(256)(128)(2,1)S(1)}, bf16[256]{0:T(256)(128)(2,1)}, u32[]{:S(2)}) copy-start(bf16[256]{0:T(256)(128)(2,1)} %param.11) | copy-start | bytes 1540
  36.9 9.0 %copy-start.6 = (bf16[18,512]{1,0:T(8,128)(2,1)S(1)}, bf16[18,512]{1,0:T(8,128)(2,1)}, u32[]{:S(2)}) copy-start(bf16[18,512]{1,0:T(8,128)(2,1)} %param.19) | copy-start | bytes 55300
  36.9 91.2 %all-to-all-start = ((bf16[16,128,512]{1,2,0:T(8,128)(2,1)}), bf16[16,128,512]{1,2,0:T(8,128)(2,1)}, u32[]{:S(2)}, u32[]{:S(2)}) async-start(bf16[16,128,512]{1,2,0:T(8,128)(2,1)} %bitcast.69), calls=%async_computation | async-start | bytes 4194304 | tf_op jit(solution)/shard_map/columns_exchange/all_to_all | solution.py:87
  44.6 1.3 collective-permute-start.1
  126.6 0.8 copy-start.11
  128.8 21.8 %all-to-all-start.2 = ((f32[8,32,256]{2,1,0:T(8,128)}), f32[8,32,256]{2,1,0:T(8,128)S(1)}, u32[]{:S(2)}, u32[]{:S(2)}) async-start(f32[8,32,256]{2,1,0:T(8,128)} %broadcast_in_dim.53), calls=%async_computation.2 | async-start | bytes 524288 | tf_op jit(solution)/shard_map/quant_sum/all_to_all | solution.py:139
  152.3 11.3 %collective-permute-start.2 = (bf16[128,512]{1,0:T(8,128)(2,1)S(1)}, bf16[128,512]{1,0:T(8,128)(2,1)S(1)}, u32[]{:S(2)}, u32[]{:S(2)}) collective-permute-start(bf16[128,512]{1,0:T(8,128)(2,1)S(1)} %fusion.16), channel_id=1, source_target_pairs={{0,24},{8,0},{16,8},{24,16},{32,56},{40,32},{48,40},{56,48},{64,88... | collective-permute-start | bytes 393224 | tf_op jit(solution)/shard_map/grad_gather/ppermute | solution.py:172
  152.4 11.2 %collective-permute-start.3 = (bf16[128,512]{1,0:T(8,128)(2,1)S(1)}, bf16[128,512]{1,0:T(8,128)(2,1)S(1)}, u32[]{:S(2)}, u32[]{:S(2)}) collective-permute-start(bf16[128,512]{1,0:T(8,128)(2,1)S(1)} %fusion.16), channel_id=1, source_target_pairs={{0,16},{8,24},{16,0},{24,8},{32,48},{40,56},{48,32},{56,40},{64,80... | collective-permute-start | bytes 393224 | tf_op jit(solution)/shard_map/grad_gather/ppermute | solution.py:172
  155.1 8.5 %collective-permute-start.4 = (bf16[128,512]{1,0:T(8,128)(2,1)S(1)}, bf16[128,512]{1,0:T(8,128)(2,1)S(1)}, u32[]{:S(2)}, u32[]{:S(2)}) collective-permute-start(bf16[128,512]{1,0:T(8,128)(2,1)S(1)} %fusion.16), channel_id=1, source_target_pairs={{0,8},{8,16},{16,24},{24,0},{32,40},{40,48},{48,56},{56,32},{64,72... | collective-permute-start | bytes 393224 | tf_op jit(solution)/shard_map/grad_gather/ppermute | solution.py:172
  163.7 15.7 %collective-permute-start.5 = (bf16[4,128,512]{2,1,0:T(8,128)(2,1)S(1)}, bf16[4,128,512]{2,1,0:T(8,128)(2,1)S(1)}, u32[]{:S(2)}, u32[]{:S(2)}) collective-permute-start(bf16[4,128,512]{2,1,0:T(8,128)(2,1)S(1)} %pad_maximum_fusion), channel_id=1, source_target_pairs={{0,96},{8,104},{16,112},{24,120},{32,0},{40,8},{48,16},{56,24},{64... | collective-permute-start | bytes 1572872 | tf_op jit(solution)/shard_map/grad_gather/ppermute | solution.py:174
  166.1 12.8 %collective-permute-start.6 = (bf16[4,128,512]{2,1,0:T(8,128)(2,1)S(1)}, bf16[4,128,512]{2,1,0:T(8,128)(2,1)S(1)}, u32[]{:S(2)}, u32[]{:S(2)}) collective-permute-start(bf16[4,128,512]{2,1,0:T(8,128)(2,1)S(1)} %pad_maximum_fusion), channel_id=1, source_target_pairs={{0,32},{8,40},{16,48},{24,56},{32,64},{40,72},{48,80},{56,88},{64,... | collective-permute-start | bytes 1572872 | tf_op jit(solution)/shard_map/grad_gather/ppermute | solution.py:175
  178.8 7.7 %collective-permute-start.7 = (bf16[2,128,512]{2,1,0:T(8,128)(2,1)S(1)}, bf16[2,128,512]{2,1,0:T(8,128)(2,1)S(1)}, u32[]{:S(2)}, u32[]{:S(2)}) collective-permute-start(bf16[2,128,512]{2,1,0:T(8,128)(2,1)S(1)} %slice.76), channel_id=1, source_target_pairs={{0,32},{8,40},{16,48},{24,56},{32,64},{40,72},{48,80},{56,88},{64,... | collective-permute-start | bytes 786440 | tf_op jit(solution)/shard_map/grad_gather/ppermute | solution.py:176
  179.4 7.5 %collective-permute-start.8 = (bf16[2,128,512]{2,1,0:T(8,128)(2,1)S(1)}, bf16[2,128,512]{2,1,0:T(8,128)(2,1)S(1)}, u32[]{:S(2)}, u32[]{:S(2)}) collective-permute-start(bf16[2,128,512]{2,1,0:T(8,128)(2,1)S(1)} %slice.78), channel_id=1, source_target_pairs={{0,96},{8,104},{16,112},{24,120},{32,0},{40,8},{48,16},{56,24},{64... | collective-permute-start | bytes 786440 | tf_op jit(solution)/shard_map/grad_gather/ppermute | solution.py:177
  187.2 2.5 %copy-start.3 = (bf16[256,512]{1,0:T(8,128)(2,1)S(1)}, bf16[256,512]{1,0:T(8,128)(2,1)}, u32[]{:S(2)}) copy-start(bf16[256,512]{1,0:T(8,128)(2,1)} %param.17) | copy-start | bytes 786436
  187.7 2.0 collective-permute-start.9
Sparse Core Ops, SparseCore 0:
  9.9 110.3 all-gather.1

commit v2 on v1

--- a/solution.py
+++ b/solution.py
@@ -6,8 +6,9 @@
 ACTIONS = 18
 COSINES = 64
 FRACS = 64
+X = 4
+Y = 4
 Z = 4
-Y = 4
 
 SWAP = [(0, 1), (1, 0)]
 
@@ -18,6 +19,10 @@
 
 def y_from(step):
     return [(f, (f - step * Z) % (Y * Z)) for f in range(Y * Z)]
+
+
+def x_from(step):
+    return [(t, (t - step * 2) % (X * 2)) for t in range(X * 2)]
 
 
 def roll_from(array, start, axis):
@@ -72,21 +77,34 @@
 
     with jax.named_scope("columns_exchange"):
         block = width // (2 * shard_total)
-        own_cols = lax.dynamic_slice_in_dim(normed_online, group * (width // 2), width // 2, 1)
-        other_cols = lax.dynamic_slice_in_dim(
-            normed_online, (1 - group) * (width // 2), width // 2, 1
-        )
+        strip = half // X
+        x_place = lax.axis_index("tp") // 2
+        mine = lax.dynamic_slice_in_dim(normed_online, x_place * strip, strip, 0)
+        own_cols = lax.dynamic_slice_in_dim(mine, group * (width // 2), width // 2, 1)
+        other_cols = lax.dynamic_slice_in_dim(mine, (1 - group) * (width // 2), width // 2, 1)
         pieces = jnp.stack(
             [
-                own_cols.reshape(half, shard_total, block),
-                other_cols.reshape(half, shard_total, block),
+                own_cols.reshape(strip, shard_total, block),
+                other_cols.reshape(strip, shard_total, block),
             ],
             2,
         )
-        pieces = jnp.transpose(pieces, (1, 0, 2, 3)).reshape(shard_total, half, 2 * block)
+        pieces = jnp.transpose(pieces, (1, 0, 2, 3)).reshape(shard_total, strip, 2 * block)
         columns = lax.all_to_all(pieces, "fsdp", 0, 0, tiled=True)
-        columns = columns.reshape(Y, Z, half, 2 * block)
-        columns = roll_from(roll_from(columns, place // Z, 0), place % Z, 1)
+        after = lax.ppermute(columns, "tp", x_from(1))
+        before = lax.ppermute(columns, "tp", x_from(3))
+        far = jnp.concatenate(
+            [
+                lax.ppermute(after[: shard_total // 2], "tp", x_from(1)),
+                lax.ppermute(before[shard_total // 2 :], "tp", x_from(3)),
+            ],
+            0,
+        )
+        columns = jnp.stack([columns, after, far, before])
+        columns = roll_from(columns, (X - x_place) % X, 0)
+        columns = columns.reshape(X, Y, Z, strip, 2 * block)
+        columns = roll_from(roll_from(columns, place // Z, 1), place % Z, 2)
+        columns = jnp.transpose(columns, (1, 2, 0, 3, 4)).reshape(Y, Z, half, 2 * block)
 
     with jax.named_scope("counts"):
         lanes = jnp.arange(shard_total, dtype=jnp.int32)

time: 218 us -> 188 us (0.86)
  waiting for transfers between devices: 111 us -> 74.8 us
  starting transfers between devices: 33 us -> 39.4 us
  other arithmetic: 14 us -> 11.7 us
    all_gather x1, waiting for transfers between devices: 74.1 us -> 5.73 us  [shards(): whole = lax.all_gather(torso_weight, ('grp', 'fsdp'), axis=0, tiled=True)]
    all_to_all x1, waiting for transfers between devices: 0.01 us -> 18.6 us  [shards(): columns = lax.all_to_all(pieces, 'fsdp', 0, 0, tiled=True)]
    ppermute x0 -> x4, waiting for transfers between devices: none -> 14.2 us  [the longest x1 8.34 us: shards(): after = lax.ppermute(columns, 'tp', x_from(1))]
    ppermute x0 -> x4, starting transfers between devices: none -> 6.66 us  [the longest x1 3.77 us: shards(): lax.ppermute(after[:shard_total // 2], 'tp', x_from(1))]
    unnamed x24 -> x45, local copies, waits for them, and re-layouts: 0.84 us -> 5.9 us
    dynamic_slice x3 -> x2, local copies, waits for them, and re-layouts: 4.76 us -> 2.05 us  [the longest x1 1.79 us: roll_from(): lax.dynamic_slice_in_dim(jnp.concatenate([array, array], axis), start, si...]
  transfers between devices with their start and end apart: 14 -> 18, of which waited for: 7 -> 10; matrix products, arithmetic and copies ran while one was open for 16% -> 14% of each run, Pallas kernels for 0% -> 0%
where the time goes in v2:
time: 188 us; the launch traced here: 187 us
  waiting for transfers between devices  74.8 us (40%)
  starting transfers between devices  39.4 us (21%)
  blocking collectives  17.8 us (9%)
  local copies, waits for them, and re-layouts  16.4 us (9%)
  between operations  14.6 us (8%)
  matrix products  12 us (6%)
  other arithmetic  11.7 us (6%)
    all_to_all x1, waiting for transfers between devices, shards(): columns = lax.all_to_all(pieces, 'fsdp', 0, 0, tiled=True)  18.6 us
    all_to_all x1, blocking collectives, shards(): lax.all_to_all(updated, 'tp', split_axis=0, concat_axis=1, tiled=True)  17.8 us
    ppermute x1, waiting for transfers between devices, shards(): above = lax.ppermute(quad, 'fsdp', y_from(3))  11.8 us
    all_to_all x1, waiting for transfers between devices, shards(): lax.all_to_all(jnp.broadcast_to(partial_quant[None], (tp_total,) + partia...  10.9 us
    all_to_all x1, starting transfers between devices, shards(): lax.all_to_all(jnp.broadcast_to(local_counts[None, :], (shard_total, shar...  8.65 us
    ppermute x1, waiting for transfers between devices, shards(): after = lax.ppermute(columns, 'tp', x_from(1))  8.34 us
    ppermute x3, waiting for transfers between devices, shards(): lax.ppermute(grad_preact, 'fsdp', z_from(k))  7.75 us
    all_to_all x1, starting transfers between devices, shards(): lax.all_to_all(jnp.broadcast_to(partial_quant[None], (tp_total,) + partia...  7.69 us
  transfers between devices with their start and end apart: 18, of which 10 were waited for; matrix products, arithmetic and copies ran while one was open for 14% of the time, Pallas kernels for 0%

profile of v2, /device:TPU:32, one launch (start us, length us, event | category | flops | bytes accessed | tf_op | source)
XLA Modules:
  0.0 186.8 jit_solution(13764654004235056272)
XLA Ops:
  7.9 3.2 %dynamic-slice_bitcast_fusion = bf16[128,8192]{1,0:T(8,128)(2,1)} fusion(bf16[1,256,8192]{2,1,0:T(8,128)(2,1)} %param.10, s32[]{:T(128)S(6)} %select_n.93), kind=kLoop, calls=%fused_computation.25 | loop fusion | bytes 4194308 | tf_op jit(solution)/shard_map/rows_swap/dynamic_slice | solution.py:57
  11.8 8.7 %all-to-all-start.1 = ((f32[16,1,16]{2,1,0:T(1,128)}), f32[16,1,16]{2,1,0:T(1,128)S(1)}, u32[]{:S(2)}, u32[]{:S(2)}) async-start(f32[16,1,16]{2,1,0:T(1,128)} %broadcast_in_dim.46), calls=%async_computation.1 | async-start | bytes 16384 | tf_op jit(solution)/shard_map/counts/all_to_all | solution.py:114
  20.5 3.3 %fusion.3 = (f32[128]{0:T(128)S(1)}, f32[128]{0:T(128)S(1)}) fusion(bf16[128,8192]{1,0:T(8,128)(2,1)S(1)} %collective-permute-done, bf16[1,256,8192]{2,1,0:T(8,128)(2,1)} %param.10, s32[]{:T(128)S(6)} %select_n.94, pred[]{:T(512)S(6)} %eq.33), kind=kLoop, calls=%fused_computation.7 | loop fusion | flops 8388352 | bytes 4195333 | tf_op jit(solution)/shard_map/reduce_sum | solution.py:71
  23.8 2.7 %fusion.5 = (bf16[128,8192]{1,0:T(8,128)(2,1)}, bf16[128,8192]{1,0:T(8,128)(2,1)S(1)}) fusion(f32[128]{0:T(128)S(1)} %get-tuple-element.19, f32[8192]{0:T(1024)S(1)} %copy-done.11, bf16[128,8192]{1,0:T(8,128)(2,1)S(1)} %collective-permute-done, bf16[1,256,8192]{2,1,0:T(8,128)(2,1)S(1)} %copy-done.1, s32[]{:T(128)S(6)} %select_n.94, pred[]{:T(512)S(6)} %eq.33, ...), kind=kLoop, calls=%fused_computation.9 | loop fusion | flops 10485760 | bytes 8422405 | tf_op jit(solution)/shard_map/convert_element_type | solution.py:72
  26.6 1.3 copy-done.2
  28.9 1.1 reshape.104
  30.0 7.5 %all-to-all-start = ((bf16[16,32,512]{2,1,0:T(8,128)(2,1)}), bf16[16,32,512]{2,1,0:T(8,128)(2,1)S(1)}, u32[]{:S(2)}, u32[]{:S(2)}) async-start(bf16[16,32,512]{2,1,0:T(8,128)(2,1)} %reshape.104), calls=%async_computation | async-start | bytes 1048576 | tf_op jit(solution)/shard_map/columns_exchange/all_to_all | solution.py:93
  37.8 0.9 fusion.18
  38.9 18.6 %all-to-all-done = bf16[16,32,512]{2,1,0:T(8,128)(2,1)S(1)} async-done(((bf16[16,32,512]{2,1,0:T(8,128)(2,1)}), bf16[16,32,512]{2,1,0:T(8,128)(2,1)S(1)}, u32[]{:S(2)}, u32[]{:S(2)}) %all-to-all-start) | async-done | bytes 524320 | tf_op jit(solution)/shard_map/columns_exchange/all_to_all | solution.py:93
  57.6 2.6 %collective-permute-start.1 = (bf16[16,32,512]{2,1,0:T(8,128)(2,1)S(1)}, bf16[16,32,512]{2,1,0:T(8,128)(2,1)S(1)}, u32[]{:S(2)}, u32[]{:S(2)}) collective-permute-start(bf16[16,32,512]{2,1,0:T(8,128)(2,1)S(1)} %all-to-all-done), channel_id=1, source_target_pairs={{0,6},{1,7},{2,0},{3,1},{4,2},{5,3},{6,4},{7,5},{8,14},{9,15},{10,... | collective-permute-start | bytes 1572872 | tf_op jit(solution)/shard_map/columns_exchange/ppermute | solution.py:94
  60.5 1.1 fusion.24
  61.6 8.3 %collective-permute-done.1 = bf16[16,32,512]{2,1,0:T(8,128)(2,1)S(1)} collective-permute-done((bf16[16,32,512]{2,1,0:T(8,128)(2,1)S(1)}, bf16[16,32,512]{2,1,0:T(8,128)(2,1)S(1)}, u32[]{:S(2)}, u32[]{:S(2)}) %collective-permute-start.1) | collective-permute-done | bytes 524320 | tf_op jit(solution)/shard_map/columns_exchange/ppermute | solution.py:94
  70.0 3.8 %collective-permute-start.2 = (bf16[8,32,512]{2,1,0:T(8,128)(2,1)S(1)}, bf16[8,32,512]{2,1,0:T(8,128)(2,1)S(1)}, u32[]{:S(2)}, u32[]{:S(2)}) collective-permute-start(bf16[8,32,512]{2,1,0:T(8,128)(2,1)S(1)} %slice.76), channel_id=1, source_target_pairs={{0,6},{1,7},{2,0},{3,1},{4,2},{5,3},{6,4},{7,5},{8,14},{9,15},{10,... | collective-permute-start | bytes 786440 | tf_op jit(solution)/shard_map/columns_exchange/ppermute | solution.py:98
  74.0 0.9 bitcast_dynamic-update-slice_fusion.4
  75.8 1.8 collective-permute-done.2
  77.6 4.0 %collective-permute-done.4 = bf16[8,32,512]{2,1,0:T(8,128)(2,1)S(1)} collective-permute-done((bf16[8,32,512]{2,1,0:T(8,128)(2,1)S(1)}, bf16[8,32,512]{2,1,0:T(8,128)(2,1)S(1)}, u32[]{:S(2)}, u32[]{:S(2)}) %collective-permute-start.4) | collective-permute-done | bytes 262176 | tf_op jit(solution)/shard_map/columns_exchange/ppermute | solution.py:99
  81.6 0.9 fusion.21
  85.0 5.7 %all-gather.2.cloned.1.call-done = bf16[8192,512]{1,0:T(8,128)(2,1)} async-done(((bf16[256,512]{1,0:T(8,128)(2,1)}), bf16[8192,512]{1,0:T(8,128)(2,1)}) %all-gather.2.cloned.1.call-update) | async-done | bytes 8388624 | tf_op jit(solution)/shard_map/all_gather | solution.py:48
  90.8 6.4 %fusion.6 = f32[256,512]{1,0:T(8,128)S(1)} fusion(bf16[8192,512]{1,0:T(8,128)(2,1)} %all-gather.2.cloned.1.call-done, bf16[128,8192]{1,0:T(8,128)(2,1)S(1)} %copy-done.3, bf16[128,8192]{1,0:T(8,128)(2,1)} %get-tuple-element.6), kind=kOutput, calls=%fused_computation.14 | convolution fusion | flops 2155872256 | bytes 13107200 | tf_op jit(solution)/shard_map/dot_general | solution.py:143
  98.7 7.7 %all-to-all-start.2 = ((f32[8,32,256]{2,1,0:T(8,128)}), f32[8,32,256]{2,1,0:T(8,128)S(1)}, u32[]{:S(2)}, u32[]{:S(2)}) async-start(f32[8,32,256]{2,1,0:T(8,128)} %broadcast_in_dim.53), calls=%async_computation.2 | async-start | bytes 524288 | tf_op jit(solution)/shard_map/quant_sum/all_to_all | solution.py:157
  108.1 1.8 constant_dynamic-slice_fusion
  109.9 10.9 %all-to-all-done.2 = f32[8,32,256]{2,1,0:T(8,128)S(1)} async-done(((f32[8,32,256]{2,1,0:T(8,128)}), f32[8,32,256]{2,1,0:T(8,128)S(1)}, u32[]{:S(2)}, u32[]{:S(2)}) %all-to-all-start.2) | async-done | bytes 262176 | tf_op jit(solution)/shard_map/quant_sum/all_to_all | solution.py:157
  121.2 1.3 fusion.17
  122.6 3.1 %collective-permute-start.7 = (bf16[128,512]{1,0:T(8,128)(2,1)S(1)}, bf16[128,512]{1,0:T(8,128)(2,1)S(1)}, u32[]{:S(2)}, u32[]{:S(2)}) collective-permute-start(bf16[128,512]{1,0:T(8,128)(2,1)S(1)} %fusion.17), channel_id=1, source_target_pairs={{0,16},{8,24},{16,0},{24,8},{32,48},{40,56},{48,32},{56,40},{64,80... | collective-permute-start | bytes 393224 | tf_op jit(solution)/shard_map/grad_gather/ppermute | solution.py:190
  126.5 7.7 %collective-permute-done.6 = bf16[128,512]{1,0:T(8,128)(2,1)S(1)} collective-permute-done((bf16[128,512]{1,0:T(8,128)(2,1)S(1)}, bf16[128,512]{1,0:T(8,128)(2,1)S(1)}, u32[]{:S(2)}, u32[]{:S(2)}) %collective-permute-start.6) | collective-permute-done | bytes 131104 | tf_op jit(solution)/shard_map/grad_gather/ppermute | solution.py:190
  134.3 1.8 collective-permute-start.9
  137.8 11.8 %collective-permute-done.10 = bf16[4,128,512]{2,1,0:T(8,128)(2,1)S(1)} collective-permute-done((bf16[4,128,512]{2,1,0:T(8,128)(2,1)S(1)}, bf16[4,128,512]{2,1,0:T(8,128)(2,1)S(1)}, u32[]{:S(2)}, u32[]{:S(2)}) %collective-permute-start.10) | collective-permute-done | bytes 524320 | tf_op jit(solution)/shard_map/grad_gather/ppermute | solution.py:193
  149.8 3.3 %collective-permute-start.12 = (bf16[2,128,512]{2,1,0:T(8,128)(2,1)S(1)}, bf16[2,128,512]{2,1,0:T(8,128)(2,1)S(1)}, u32[]{:S(2)}, u32[]{:S(2)}) collective-permute-start(bf16[2,128,512]{2,1,0:T(8,128)(2,1)S(1)} %slice.91), channel_id=1, source_target_pairs={{0,96},{8,104},{16,112},{24,120},{32,0},{40,8},{48,16},{56,24},{64... | collective-permute-start | bytes 786440 | tf_op jit(solution)/shard_map/grad_gather/ppermute | solution.py:195
  154.0 3.3 %collective-permute-done.11 = bf16[2,128,512]{2,1,0:T(8,128)(2,1)S(1)} collective-permute-done((bf16[2,128,512]{2,1,0:T(8,128)(2,1)S(1)}, bf16[2,128,512]{2,1,0:T(8,128)(2,1)S(1)}, u32[]{:S(2)}, u32[]{:S(2)}) %collective-permute-start.11) | collective-permute-done | bytes 262176 | tf_op jit(solution)/shard_map/grad_gather/ppermute | solution.py:194
  158.6 1.9 %collective-permute-done.13 = f32[256,512]{1,0:T(8,128)S(1)} collective-permute-done((f32[256,512]{1,0:T(8,128)S(1)}, f32[256,512]{1,0:T(8,128)S(1)}, u32[]{:S(2)}, u32[]{:S(2)}) %collective-permute-start.13) | collective-permute-done | bytes 524320 | tf_op jit(solution)/shard_map/ppermute | solution.py:212
  160.5 0.9 subtract_convert_fusion
  161.4 17.8 %all_to_all.35 = bf16[8,32,512]{2,1,0:T(8,128)(2,1)S(1)} all-to-all(bf16[8,32,512]{2,1,0:T(8,128)(2,1)S(1)} %bitcast.107), channel_id=1, replica_groups=mesh['grp'=2,'fsdp'=16,'tp'=8] {'tp'}, dimensions={0} | all-to-all | bytes 524288 | tf_op jit(solution)/shard_map/all_to_all | solution.py:214
  (111 shorter events, 16.0 us)
Async XLA Ops:
  7.2 30.6 %copy-start = (bf16[64,512]{1,0:T(8,128)(2,1)S(1)}, bf16[64,512]{1,0:T(8,128)(2,1)}, u32[]{:S(2)}) copy-start(bf16[64,512]{1,0:T(8,128)(2,1)} %param.18) | copy-start | bytes 196612
  7.2 3.9 %copy-start.15 = (s32[256,1]{0,1:T(1,128)S(1)}, s32[256,1]{0,1:T(1,128)}, u32[]{:S(2)}) copy-start(s32[256,1]{0,1:T(1,128)} %param.14) | copy-start | bytes 3076
  7.2 83.6 %all-gather.2.cloned.1.call-start = ((), (), s32[]{:S(2)}) async-start(), calls=%async_computation.4 | async-start | bytes 8650752 | tf_op jit(solution)/shard_map/all_gather | solution.py:48
  7.9 15.9 %copy-start.11 = (f32[8192]{0:T(1024)S(1)}, f32[8192]{0:T(1024)}, u32[]{:S(2)}) copy-start(f32[8192]{0:T(1024)} %param.16) | copy-start | bytes 98308
  11.1 9.4 %collective-permute-start = (bf16[128,8192]{1,0:T(8,128)(2,1)}, bf16[128,8192]{1,0:T(8,128)(2,1)S(1)}, u32[]{:S(2)}, u32[]{:S(2)}) collective-permute-start(bf16[128,8192]{1,0:T(8,128)(2,1)} %dynamic-slice_bitcast_fusion), channel_id=1, source_target_pairs={{0,128},{128,0},{1,129},{129,1},{2,130},{130,2},{3,131},{131,3},{4... | collective-permute-start | bytes 6291464 | tf_op jit(solution)/shard_map/rows_swap/ppermute | solution.py:58
  11.8 18.1 %all-to-all-start.1 = ((f32[16,1,16]{2,1,0:T(1,128)}), f32[16,1,16]{2,1,0:T(1,128)S(1)}, u32[]{:S(2)}, u32[]{:S(2)}) async-start(f32[16,1,16]{2,1,0:T(1,128)} %broadcast_in_dim.46), calls=%async_computation.1 | async-start | bytes 16384 | tf_op jit(solution)/shard_map/counts/all_to_all | solution.py:114
  26.6 11.0 %copy-start.8 = (s32[1,256,32]{1,2,0:T(8,128)S(1)}, s32[1,256,32]{1,2,0:T(8,128)}, u32[]{:S(2)}) copy-start(s32[1,256,32]{1,2,0:T(8,128)} %param.13) | copy-start | bytes 98308
  26.6 11.0 %copy-start.13 = (s32[1,256]{1,0:T(1,128)S(1)}, s32[1,256]{1,0:T(1,128)}, u32[]{:S(2)}) copy-start(s32[1,256]{1,0:T(1,128)} %param.12) | copy-start | bytes 3076
  26.6 11.2 %copy-start.16 = (bf16[256]{0:T(256)(128)(2,1)S(1)}, bf16[256]{0:T(256)(128)(2,1)}, u32[]{:S(2)}) copy-start(bf16[256]{0:T(256)(128)(2,1)} %param.11) | copy-start | bytes 1540
  26.6 11.2 %copy-start.14 = (f32[64]{0:T(128)S(1)}, f32[64]{0:T(128)}, u32[]{:S(2)}) copy-start(f32[64]{0:T(128)} %param.15) | copy-start | bytes 772
  26.6 34.0 %copy-start.12 = (bf16[18,512]{1,0:T(8,128)(2,1)S(1)}, bf16[18,512]{1,0:T(8,128)(2,1)}, u32[]{:S(2)}) copy-start(bf16[18,512]{1,0:T(8,128)(2,1)} %param.19) | copy-start | bytes 55300
  30.0 27.6 %all-to-all-start = ((bf16[16,32,512]{2,1,0:T(8,128)(2,1)}), bf16[16,32,512]{2,1,0:T(8,128)(2,1)S(1)}, u32[]{:S(2)}, u32[]{:S(2)}) async-start(bf16[16,32,512]{2,1,0:T(8,128)(2,1)} %reshape.104), calls=%async_computation | async-start | bytes 1048576 | tf_op jit(solution)/shard_map/columns_exchange/all_to_all | solution.py:93
  37.5 22.7 %collective-permute-start.5 = (s32[128,33]{0,1:T(8,128)S(1)}, s32[128,33]{0,1:T(8,128)S(1)}, u32[]{:S(2)}, u32[]{:S(2)}) collective-permute-start(s32[128,33]{0,1:T(8,128)S(1)} %fusion.27), channel_id=1, source_target_pairs={{0,128},{128,0},{1,129},{129,1},{2,130},{130,2},{3,131},{131,3},{4... | collective-permute-start | bytes 50696 | tf_op jit(solution)/shard_map/rows_swap/ppermute | solution.py:58
  37.7 53.1 %copy-start.3 = (bf16[128,8192]{1,0:T(8,128)(2,1)S(1)}, bf16[128,8192]{1,0:T(8,128)(2,1)}, u32[]{:S(2)}) copy-start(bf16[128,8192]{1,0:T(8,128)(2,1)} %copy-done.2) | copy-start | bytes 6291460
  57.6 12.4 %collective-permute-start.1 = (bf16[16,32,512]{2,1,0:T(8,128)(2,1)S(1)}, bf16[16,32,512]{2,1,0:T(8,128)(2,1)S(1)}, u32[]{:S(2)}, u32[]{:S(2)}) collective-permute-start(bf16[16,32,512]{2,1,0:T(8,128)(2,1)S(1)} %all-to-all-done), channel_id=1, source_target_pairs={{0,6},{1,7},{2,0},{3,1},{4,2},{5,3},{6,4},{7,5},{8,14},{9,15},{10,... | collective-permute-start | bytes 1572872 | tf_op jit(solution)/shard_map/columns_exchange/ppermute | solution.py:94
  60.2 13.6 %collective-permute-start.3 = (bf16[16,32,512]{2,1,0:T(8,128)(2,1)S(1)}, bf16[16,32,512]{2,1,0:T(8,128)(2,1)S(1)}, u32[]{:S(2)}, u32[]{:S(2)}) collective-permute-start(bf16[16,32,512]{2,1,0:T(8,128)(2,1)S(1)} %all-to-all-done), channel_id=1, source_target_pairs={{0,2},{1,3},{2,4},{3,5},{4,6},{5,7},{6,0},{7,1},{8,10},{9,11},{10,... | collective-permute-start | bytes 1572872 | tf_op jit(solution)/shard_map/columns_exchange/ppermute | solution.py:95
  70.0 7.7 %collective-permute-start.2 = (bf16[8,32,512]{2,1,0:T(8,128)(2,1)S(1)}, bf16[8,32,512]{2,1,0:T(8,128)(2,1)S(1)}, u32[]{:S(2)}, u32[]{:S(2)}) collective-permute-start(bf16[8,32,512]{2,1,0:T(8,128)(2,1)S(1)} %slice.76), channel_id=1, source_target_pairs={{0,6},{1,7},{2,0},{3,1},{4,2},{5,3},{6,4},{7,5},{8,14},{9,15},{10,... | collective-permute-start | bytes 786440 | tf_op jit(solution)/shard_map/columns_exchange/ppermute | solution.py:98
  73.8 7.8 %collective-permute-start.4 = (bf16[8,32,512]{2,1,0:T(8,128)(2,1)S(1)}, bf16[8,32,512]{2,1,0:T(8,128)(2,1)S(1)}, u32[]{:S(2)}, u32[]{:S(2)}) collective-permute-start(bf16[8,32,512]{2,1,0:T(8,128)(2,1)S(1)} %slice.77), channel_id=1, source_target_pairs={{0,2},{1,3},{2,4},{3,5},{4,6},{5,7},{6,0},{7,1},{8,10},{9,11},{10,... | collective-permute-start | bytes 786440 | tf_op jit(solution)/shard_map/columns_exchange/ppermute | solution.py:99
  90.8 6.4 %copy-start.7 = (f32[256,512]{1,0:T(8,128)S(1)}, f32[256,512]{1,0:T(8,128)}, u32[]{:S(2)}) copy-start(f32[256,512]{1,0:T(8,128)} %fusion.24) | copy-start | bytes 1572868
  90.8 6.4 %copy-start.9 = (bf16[64,512]{1,0:T(8,128)(2,1)S(1)}, bf16[64,512]{1,0:T(8,128)(2,1)}, u32[]{:S(2)}) copy-start(bf16[64,512]{1,0:T(8,128)(2,1)} %fusion.18) | copy-start | bytes 196612
  90.8 15.7 %copy-start.5 = (bf16[8,32,512]{2,1,0:T(8,128)(2,1)S(1)}, bf16[8,32,512]{2,1,0:T(8,128)(2,1)}, u32[]{:S(2)}) copy-start(bf16[8,32,512]{2,1,0:T(8,128)(2,1)} %copy-done.4) | copy-start | bytes 786436
  97.5 23.7 %copy-start.10 = (bf16[64,512]{1,0:T(8,128)(2,1)S(1)}, bf16[64,512]{1,0:T(8,128)(2,1)}, u32[]{:S(2)}) copy-start(bf16[64,512]{1,0:T(8,128)(2,1)} %fusion.18) | copy-start | bytes 196612
  98.7 22.1 %all-to-all-start.2 = ((f32[8,32,256]{2,1,0:T(8,128)}), f32[8,32,256]{2,1,0:T(8,128)S(1)}, u32[]{:S(2)}, u32[]{:S(2)}) async-start(f32[8,32,256]{2,1,0:T(8,128)} %broadcast_in_dim.53), calls=%async_computation.2 | async-start | bytes 524288 | tf_op jit(solution)/shard_map/quant_sum/all_to_all | solution.py:157
  108.1 13.1 %copy-start.18 = (f32[256,512]{1,0:T(8,128)S(1)}, f32[256,512]{1,0:T(8,128)}, u32[]{:S(2)}) copy-start(f32[256,512]{1,0:T(8,128)} %copy-done.17) | copy-start | bytes 1572868
  122.5 11.7 %collective-permute-start.6 = (bf16[128,512]{1,0:T(8,128)(2,1)S(1)}, bf16[128,512]{1,0:T(8,128)(2,1)S(1)}, u32[]{:S(2)}, u32[]{:S(2)}) collective-permute-start(bf16[128,512]{1,0:T(8,128)(2,1)S(1)} %fusion.17), channel_id=1, source_target_pairs={{0,24},{8,0},{16,8},{24,16},{32,56},{40,32},{48,40},{56,48},{64,88... | collective-permute-start | bytes 393224 | tf_op jit(solution)/shard_map/grad_gather/ppermute | solution.py:190
  122.6 11.6 %collective-permute-start.7 = (bf16[128,512]{1,0:T(8,128)(2,1)S(1)}, bf16[128,512]{1,0:T(8,128)(2,1)S(1)}, u32[]{:S(2)}, u32[]{:S(2)}) collective-permute-start(bf16[128,512]{1,0:T(8,128)(2,1)S(1)} %fusion.17), channel_id=1, source_target_pairs={{0,16},{8,24},{16,0},{24,8},{32,48},{40,56},{48,32},{56,40},{64,80... | collective-permute-start | bytes 393224 | tf_op jit(solution)/shard_map/grad_gather/ppermute | solution.py:190
  125.8 8.5 %collective-permute-start.8 = (bf16[128,512]{1,0:T(8,128)(2,1)S(1)}, bf16[128,512]{1,0:T(8,128)(2,1)S(1)}, u32[]{:S(2)}, u32[]{:S(2)}) collective-permute-start(bf16[128,512]{1,0:T(8,128)(2,1)S(1)} %fusion.17), channel_id=1, source_target_pairs={{0,8},{8,16},{16,24},{24,0},{32,40},{40,48},{48,56},{56,32},{64,72... | collective-permute-start | bytes 393224 | tf_op jit(solution)/shard_map/grad_gather/ppermute | solution.py:190
  134.3 15.4 %collective-permute-start.9 = (bf16[4,128,512]{2,1,0:T(8,128)(2,1)S(1)}, bf16[4,128,512]{2,1,0:T(8,128)(2,1)S(1)}, u32[]{:S(2)}, u32[]{:S(2)}) collective-permute-start(bf16[4,128,512]{2,1,0:T(8,128)(2,1)S(1)} %pad_maximum_fusion), channel_id=1, source_target_pairs={{0,96},{8,104},{16,112},{24,120},{32,0},{40,8},{48,16},{56,24},{64... | collective-permute-start | bytes 1572872 | tf_op jit(solution)/shard_map/grad_gather/ppermute | solution.py:192
  136.1 13.5 %collective-permute-start.10 = (bf16[4,128,512]{2,1,0:T(8,128)(2,1)S(1)}, bf16[4,128,512]{2,1,0:T(8,128)(2,1)S(1)}, u32[]{:S(2)}, u32[]{:S(2)}) collective-permute-start(bf16[4,128,512]{2,1,0:T(8,128)(2,1)S(1)} %pad_maximum_fusion), channel_id=1, source_target_pairs={{0,32},{8,40},{16,48},{24,56},{32,64},{40,72},{48,80},{56,88},{64,... | collective-permute-start | bytes 1572872 | tf_op jit(solution)/shard_map/grad_gather/ppermute | solution.py:193
  149.6 7.7 %collective-permute-start.11 = (bf16[2,128,512]{2,1,0:T(8,128)(2,1)S(1)}, bf16[2,128,512]{2,1,0:T(8,128)(2,1)S(1)}, u32[]{:S(2)}, u32[]{:S(2)}) collective-permute-start(bf16[2,128,512]{2,1,0:T(8,128)(2,1)S(1)} %slice.89), channel_id=1, source_target_pairs={{0,32},{8,40},{16,48},{24,56},{32,64},{40,72},{48,80},{56,88},{64,... | collective-permute-start | bytes 786440 | tf_op jit(solution)/shard_map/grad_gather/ppermute | solution.py:194
  149.8 7.9 %collective-permute-start.12 = (bf16[2,128,512]{2,1,0:T(8,128)(2,1)S(1)}, bf16[2,128,512]{2,1,0:T(8,128)(2,1)S(1)}, u32[]{:S(2)}, u32[]{:S(2)}) collective-permute-start(bf16[2,128,512]{2,1,0:T(8,128)(2,1)S(1)} %slice.91), channel_id=1, source_target_pairs={{0,96},{8,104},{16,112},{24,120},{32,0},{40,8},{48,16},{56,24},{64... | collective-permute-start | bytes 786440 | tf_op jit(solution)/shard_map/grad_gather/ppermute | solution.py:195
  158.5 2.0 %collective-permute-start.13 = (f32[256,512]{1,0:T(8,128)S(1)}, f32[256,512]{1,0:T(8,128)S(1)}, u32[]{:S(2)}, u32[]{:S(2)}) collective-permute-start(f32[256,512]{1,0:T(8,128)S(1)} %slice.93), channel_id=1, source_target_pairs={{0,128},{128,0},{1,129},{129,1},{2,130},{130,2},{3,131},{131,3},{4... | collective-permute-start | bytes 1572872 | tf_op jit(solution)/shard_map/ppermute | solution.py:212
  (5 other events, 10.9 us)
Sparse Core Ops, SparseCore 0:
  9.9 80.8 all-gather.1

commit v3 on v1

v3 whole, which is shorter than its diff:
```python
import jax
import jax.numpy as jnp
from jax import lax
from jax.experimental import pallas as pl
from jax.experimental.pallas import tpu as pltpu
from jax.sharding import PartitionSpec as P

ACTIONS = 18
COSINES = 64
FRACS = 64
X = 4
Y = 4
Z = 4

SWAP = [(0, 1), (1, 0)]


def z_from(step):
    return [(f, (f // Z) * Z + (f % Z - step) % Z) for f in range(Y * Z)]


def y_from(step):
    return [(f, (f - step * Z) % (Y * Z)) for f in range(Y * Z)]


def x_from(step):
    return [(t, (t - step * 2) % (X * 2)) for t in range(X * 2)]


def round_y(block):
    half = block.shape[0] // 2
    below = lax.ppermute(block, "fsdp", y_from(1))
    above = lax.ppermute(block, "fsdp", y_from(3))
    low = lax.ppermute(above[:half], "fsdp", y_from(3))
    high = lax.ppermute(below[half:], "fsdp", y_from(1))
    return below, above, low, high


def preact_kernel(where_ref, own_ref, got_ref, *refs):
    weights = refs[: 5 * Z]
    keep_ref, send_ref, total = refs[5 * Z :]
    group, y, z = where_ref[0], where_ref[1], where_ref[2]
    rows = own_ref.shape[0]
    block = weights[0].shape[0]
    total[...] = jnp.zeros_like(total)
    for step_y in range(Y):
        for step_z in range(Z):
            place = lax.rem(y + step_y, Y) * Z + lax.rem(z + step_z, Z)
            cols = pl.ds(pl.multiple_of(place * block, block), block)
            if step_y == 0:
                weight = weights[step_z][...]
            elif step_y == 2:
                weight = jnp.concatenate(
                    [weights[3 * Z + step_z][...], weights[4 * Z + step_z][...]], 0
                )
            else:
                weight = weights[(1 if step_y == 1 else 2) * Z + step_z][...]
            total[:rows] += jnp.dot(own_ref[:, cols], weight, preferred_element_type=jnp.float32)
            total[rows:] += jnp.dot(got_ref[:, cols], weight, preferred_element_type=jnp.float32)
    half = rows // 2
    other = 1 - group
    for mine, part in ((True, group), (False, other)):
        base = 0 if mine else rows
        out = pl.ds(pl.multiple_of(part * half, half), half)
        keep_ref[out, :] = total[pl.ds(pl.multiple_of(base + group * half, half), half), :]
        send_ref[out, :] = total[pl.ds(pl.multiple_of(base + other * half, half), half), :]


def norm_kernel(where_ref, rows_ref, gain_ref, own_ref, send_ref):
    side = own_ref.shape[1]
    wide = rows_ref[...].astype(jnp.float32)
    scale = lax.rsqrt(jnp.mean(wide * wide, axis=-1, keepdims=True) + 1e-05)
    for part, out_ref in ((where_ref[0], own_ref), (1 - where_ref[0], send_ref)):
        cols = pl.ds(pl.multiple_of(part * side, side), side)
        values = rows_ref[:, cols].astype(jnp.float32)
        out_ref[...] = (values * scale * gain_ref[:, cols]).astype(jnp.bfloat16)


def pieces_kernel(where_ref, own_ref, got_ref, out_ref, held, sems):
    places, strip, block = out_ref.shape[1:]
    half = own_ref.shape[0] // 2

    def fetch(source):
        copies = []
        for k in range(2):
            row = pl.multiple_of(k * half + where_ref[3] * strip, strip)
            copies.append(
                pltpu.make_async_copy(source.at[pl.ds(row, strip), :], held.at[k], sems.at[k])
            )
            copies[-1].start()
        for copy in copies:
            copy.wait()

    @pl.when(where_ref[0] == 1)
    def _():
        fetch(own_ref)

    @pl.when(where_ref[0] == 0)
    def _():
        fetch(got_ref)

    for k in range(2):
        for place in range(places):
            out_ref[k, place] = held[k, :, place * block : (place + 1) * block]


def columns_kernel(where_ref, own_ref, after_ref, before_ref, far_a_ref, far_b_ref, out_ref, held):
    group, y, z, x = where_ref[0], where_ref[1], where_ref[2], where_ref[3]
    other = 1 - group
    strip, block = own_ref.shape[2], own_ref.shape[3]
    span = strip * X

    def body(step, carry):
        place = lax.rem(y + step // Z, Y) * Z + lax.rem(z + lax.rem(step, Z), Z)
        for shift, ref in ((0, own_ref), (1, after_ref), (3, before_ref)):
            rows = pl.ds(pl.multiple_of(lax.rem(x + shift, X) * strip, strip), strip)
            held[rows, :block] = ref[group, place]
            held[rows, block:] = ref[other, place]
        rows = pl.ds(pl.multiple_of(lax.rem(x + 2, X) * strip, strip), strip)
        held[rows, pl.ds(pl.multiple_of(group * block, block), block)] = far_a_ref[place]
        held[rows, pl.ds(pl.multiple_of(other * block, block), block)] = far_b_ref[place]
        out_ref[:, pl.ds(pl.multiple_of(step * span, span), span)] = held[...].T
        return carry

    lax.fori_loop(0, Y * Z, body, 0)


def near_kernel(cols_ref, own_ref, line_ref, b0_ref, b1_ref, a0_ref, a1_ref, out_ref):
    half = own_ref.shape[0]
    span = Z * half
    total = None
    for base, first, rest in (
        (0, own_ref, line_ref),
        (span, b0_ref, b1_ref),
        (3 * span, a0_ref, a1_ref),
    ):
        grads = jnp.concatenate([first[...], rest[...]], 0)
        term = jnp.dot(
            cols_ref[:, base : base + span], grads, preferred_element_type=jnp.float32
        )
        total = term if total is None else total + term
    out_ref[...] = total


def far_kernel(cols_ref, near_ref, l0_ref, h0_ref, l1_ref, h1_ref, own_ref, other_ref):
    grads = jnp.concatenate([l0_ref[...], h0_ref[...], l1_ref[...], h1_ref[...]], 0)
    span = grads.shape[0]
    block = own_ref.shape[0]
    cols = cols_ref[:, 2 * span : 3 * span]
    total = near_ref[...] + jnp.dot(cols, grads, preferred_element_type=jnp.float32)
    own_ref[...] = total[:block]
    other_ref[...] = total[block:]


def shards(
    frames,
    rewards,
    actions,
    fractions,
    episode_shard,
    table,
    norm_gain,
    torso_weight,
    embed_weight,
    value_weight,
):
    group = lax.axis_index("grp")
    place = lax.axis_index("fsdp")
    x_place = lax.axis_index("tp") // 2
    shard_total = lax.axis_size("fsdp")
    where = jnp.stack([group, place // Z, place % Z, x_place]).astype(jnp.int32)
    rows_block = frames.shape[1]
    width = frames.shape[2]
    features = torso_weight.shape[1]
    half = rows_block // 2
    side = width // 2
    block = side // shard_total
    strip = half // X
    own_rows = group * half
    other_rows = (1 - group) * half
    smem = pl.BlockSpec(memory_space=pltpu.SMEM)
    vmem = pl.BlockSpec(memory_space=pltpu.VMEM)

    with jax.named_scope("rows_swap"):
        values = frames[0]
        tile = 32
        normed_own, normed_send = pl.pallas_call(
            norm_kernel,
            grid=(rows_block // tile,),
            out_shape=(jax.ShapeDtypeStruct((rows_block, side), jnp.bfloat16),) * 2,
            in_specs=[
                smem,
                pl.BlockSpec((tile, width), lambda i: (i, 0)),
                pl.BlockSpec((1, width), lambda i: (0, 0)),
            ],
            out_specs=(pl.BlockSpec((tile, side), lambda i: (i, 0)),) * 2,
            compiler_params=pltpu.CompilerParams(vmem_limit_bytes=12 << 20),
            cost_estimate=pl.CostEstimate(
                flops=6 * rows_block * width,
                transcendentals=0,
                bytes_accessed=4 * rows_block * width,
            ),
            name="norm",
        )(where, values, norm_gain[None, :])
    with jax.named_scope("weight_gather"):
        own_weight, normed_send = lax.optimization_barrier((torso_weight, normed_send))
        lines = [own_weight] + [lax.ppermute(own_weight, "fsdp", z_from(k)) for k in range(1, Z)]
        rounds = [round_y(line) for line in lines]
        chunks = lines + [r[k] for k in range(4) for r in rounds]

    with jax.named_scope("rows_swap"):
        normed_got = lax.ppermute(normed_send, "grp", SWAP)
        ints = jnp.concatenate([fractions[0].T, actions[0][None, :]], 0)
        kept = lax.dynamic_slice_in_dim(ints, own_rows, half, 1)
        got = lax.ppermute(lax.dynamic_slice_in_dim(ints, other_rows, half, 1), "grp", SWAP)
        target_ints = jnp.where(group == 0, kept, got)
        online_ints = jnp.where(group == 0, got, kept)
        ints_all = jnp.concatenate([target_ints, online_ints], 1)
        fraction_rows = ints_all[:-1]
        action_rows = ints_all[-1]

    with jax.named_scope("columns_exchange"):

        pieces = pl.pallas_call(
            pieces_kernel,
            out_shape=jax.ShapeDtypeStruct((2, shard_total, strip, block), jnp.bfloat16),
            in_specs=[smem] + [pl.BlockSpec(memory_space=pl.ANY)] * 2,
            out_specs=vmem,
            scratch_shapes=[
                pltpu.VMEM((2, strip, side), jnp.bfloat16),
                pltpu.SemaphoreType.DMA((2,)),
            ],
            compiler_params=pltpu.CompilerParams(vmem_limit_bytes=4 << 20),
            cost_estimate=pl.CostEstimate(
                flops=0, transcendentals=0, bytes_accessed=8 * strip * side
            ),
            name="pieces",
        )(where, normed_own, normed_got)
        pieces = lax.all_to_all(
            pieces.reshape(2 * shard_total, strip, block), ("grp", "fsdp"), 0, 0, tiled=True
        ).reshape(2, shard_total, strip, block)
        after = lax.ppermute(pieces, "tp", x_from(1))
        before = lax.ppermute(pieces, "tp", x_from(3))
        far_a = lax.ppermute(after[0], "tp", x_from(1))
        far_b = lax.ppermute(before[1], "tp", x_from(3))
        columns = pl.pallas_call(
            columns_kernel,
            out_shape=jax.ShapeDtypeStruct((2 * block, shard_total * half), jnp.bfloat16),
            in_specs=[smem] + [vmem] * 5,
            out_specs=vmem,
            scratch_shapes=[pltpu.VMEM((half, 2 * block), jnp.bfloat16)],
            compiler_params=pltpu.CompilerParams(vmem_limit_bytes=8 << 20),
            cost_estimate=pl.CostEstimate(
                flops=0, transcendentals=0, bytes_accessed=8 * shard_total * half * block
            ),
            name="columns",
        )(where, pieces, after, before, far_a, far_b)

    with jax.named_scope("counts"):
        lanes = jnp.arange(shard_total, dtype=jnp.int32)
        onehot = episode_shard[:, :1] == lanes[None, :]
        local_counts = jnp.sum(onehot.astype(jnp.float32), axis=0)
        counts = jnp.sum(
            lax.all_to_all(
                jnp.broadcast_to(local_counts[None, :], (shard_total, shard_total)),
                "fsdp",
                0,
                0,
                tiled=True,
            ),
            axis=0,
        )
        inverse = float(rows_block) / counts
        row_weight = jnp.sum(jnp.where(onehot, inverse[None, :], 0.0), axis=1)
        row_weight = lax.dynamic_slice_in_dim(row_weight, own_rows, half, 0)

    choose_mask = (action_rows[:, None] == jnp.arange(ACTIONS, dtype=jnp.int32)[None, :]).astype(
        jnp.bfloat16
    )
    picked = jnp.dot(choose_mask, value_weight, preferred_element_type=jnp.float32)
    cosine = jnp.cos(
        jnp.pi * jnp.arange(COSINES, dtype=jnp.float32)[None, :] * table[:, None]
    ).astype(jnp.bfloat16)
    embedding = jax.nn.relu(
        jnp.dot(cosine, embed_weight, preferred_element_type=jnp.float32)
    ).astype(jnp.bfloat16)
    ids = jnp.arange(FRACS, dtype=jnp.int32)
    online_fractions = fraction_rows[:, half:]
    online_select = online_fractions[:, None, :] == ids[None, :, None]
    levels = jnp.sum(jnp.where(online_select, table[None, :, None], 0.0), axis=1)
    reward_rows = lax.dynamic_slice_in_dim(rewards, own_rows, half, 0).astype(jnp.float32)

    normed_own, _ = lax.optimization_barrier((normed_own, pieces))
    part_shape = jax.ShapeDtypeStruct((rows_block, features), jnp.float32)
    keep, send = pl.pallas_call(
        preact_kernel,
        out_shape=(part_shape, part_shape),
        in_specs=[smem] + [vmem] * (2 + 5 * Z),
        out_specs=(vmem, vmem),
        scratch_shapes=[pltpu.VMEM((2 * rows_block, features), jnp.float32)],
        compiler_params=pltpu.CompilerParams(vmem_limit_bytes=16 << 20),
        cost_estimate=pl.CostEstimate(
            flops=4 * rows_block * side * features,
            transcendentals=0,
            bytes_accessed=2 * side * features + 4 * side * rows_block + 8 * rows_block * features,
        ),
        name="preact",
    )(where, normed_own, normed_got, *chunks)
    preact = keep + lax.ppermute(send, "grp", SWAP)
    weighted = (jax.nn.silu(preact) * picked).astype(jnp.bfloat16)
    table_values = lax.dot_general(
        embedding, weighted, (((1,), (1,)), ((), ())), preferred_element_type=jnp.float32
    )
    partial_quant = jnp.sum(
        jnp.where(
            fraction_rows[:, None, :] == ids[None, :, None], table_values[None, :, :], 0.0
        ),
        axis=1,
    )
    with jax.named_scope("quant_sum"):
        tp_total = lax.axis_size("tp")
        quant = jnp.sum(
            lax.all_to_all(
                jnp.broadcast_to(partial_quant[None], (tp_total,) + partial_quant.shape),
                "tp",
                0,
                0,
                tiled=True,
            ),
            axis=0,
        )
    quant, _ = lax.optimization_barrier((quant, (after, before)))
    target_quant = quant[:, :half]
    online_quant = quant[:, half:]
    target_value = reward_rows[None, :] + 0.99 * target_quant
    errors = target_value[None, :, :] - online_quant[:, None, :]
    weight = jnp.abs(levels[:, None, :] - (errors < 0).astype(jnp.float32))
    grad_quant = -row_weight[None, :] * jnp.sum(weight * jnp.clip(errors, -1.0, 1.0), axis=1)
    grad_table = jnp.sum(jnp.where(online_select, grad_quant[:, None, :], 0.0), axis=0)
    grad_feature = lax.dot_general(
        grad_table,
        embedding.astype(jnp.float32),
        (((0,), (0,)), ((), ())),
        precision=lax.Precision.HIGHEST,
    )
    online_preact = preact[half:]
    gate_value = jax.nn.sigmoid(online_preact)
    grad_preact = (
        grad_feature
        * picked[half:]
        * gate_value
        * (1.0 + online_preact * (1.0 - gate_value))
    ).astype(jnp.bfloat16)

    with jax.named_scope("grad_gather"):
        first = round_y(grad_preact)
        pieces_z = tuple(lax.ppermute(grad_preact, "fsdp", z_from(k)) for k in range(1, Z))
        pieces_z, _ = lax.optimization_barrier((pieces_z, (first[0], first[1], far_a, far_b)))
        line = jnp.concatenate(pieces_z, 0)
        rest = round_y(line)

    near = pl.pallas_call(
        near_kernel,
        out_shape=jax.ShapeDtypeStruct((2 * block, features), jnp.float32),
        in_specs=[vmem] * 7,
        out_specs=vmem,
        compiler_params=pltpu.CompilerParams(vmem_limit_bytes=12 << 20),
        cost_estimate=pl.CostEstimate(
            flops=12 * Z * half * 2 * block * features // 2,
            transcendentals=0,
            bytes_accessed=6 * Z * half * (2 * block + features),
        ),
        name="near",
    )(columns, grad_preact, line, first[0], rest[0], first[1], rest[1])
    final_shape = jax.ShapeDtypeStruct((block, features), jnp.float32)
    mine, theirs = pl.pallas_call(
        far_kernel,
        out_shape=(final_shape, final_shape),
        in_specs=[vmem] * 6,
        out_specs=(vmem, vmem),
        compiler_params=pltpu.CompilerParams(vmem_limit_bytes=12 << 20),
        cost_estimate=pl.CostEstimate(
            flops=4 * Z * half * block * features,
            transcendentals=0,
            bytes_accessed=2 * Z * half * (2 * block + features) + 16 * block * features,
        ),
        name="far",
    )(columns, near, first[2], first[3], rest[2], rest[3])
    torso_grad = mine + lax.ppermute(theirs, "grp", SWAP)
    updated = (torso_weight.astype(jnp.float32) - 0.01 * torso_grad).astype(jnp.bfloat16)
    refreshed_weight = lax.all_to_all(updated, "tp", split_axis=0, concat_axis=1, tiled=True)
    return (torso_grad, refreshed_weight)


def solution(mesh):
    placed = (
        P("grp", "fsdp", None),
        P("fsdp"),
        P("grp", "fsdp"),
        P("grp", "fsdp", None),
        P("fsdp", None),
        P(),
        P(),
        P(("grp", "fsdp"), "tp"),
        P(None, "tp"),
        P(None, "tp"),
    )
    return jax.shard_map(
        shards,
        mesh=mesh,
        in_specs=placed,
        out_specs=(P(("grp", "fsdp"), "tp"), P(("grp", "fsdp", "tp"), None)),
        check_vma=False,
    )
```

time: 218 us -> 188 us (0.86)
  waiting for transfers between devices: 111 us -> 53.5 us
  starting transfers between devices: 33 us -> 72 us
  Pallas kernels: 0 us -> 16 us
  between operations: 14.4 us -> 1.18 us
  other arithmetic: 14 us -> 4.24 us
  matrix products: 10.6 us -> 3.54 us
  local copies, waits for them, and re-layouts: 15.3 us -> 19.4 us
    all_gather x1 -> x0, waiting for transfers between devices: 74.1 us -> none  [shards(): whole = lax.all_gather(torso_weight, ('grp', 'fsdp'), axis=0, tiled=True)]
    ppermute x7 -> x35, starting transfers between devices: 6.44 us -> 46.3 us  [the longest x6 15.7 us: round_y(): below = lax.ppermute(block, 'fsdp', y_from(1))]
    pallas_call x0 -> x6, Pallas kernels: none -> 16 us  [the longest x1 5.11 us: shards(): pl.pallas_call(norm_kernel, grid=(rows_block // tile,), out_shape=(jax.Sh...]
    ppermute x7 -> x35, waiting for transfers between devices: 17.3 us -> 31 us  [the longest x6 20.5 us: round_y(): above = lax.ppermute(block, 'fsdp', y_from(3))]
    all_to_all x1, waiting for transfers between devices: 0.01 us -> 8.76 us  [shards(): lax.all_to_all(jnp.broadcast_to(local_counts[None, :], (shard_total, shar...]
    unnamed x24 -> x52, local copies, waits for them, and re-layouts: 0.84 us -> 9.59 us
    dot_general x6 -> x0, matrix products: 8.41 us -> none  [the longest x1 6.33 us: shards(): preact = jnp.dot(normed, whole, preferred_element_type=jnp.float32)]
    dynamic_slice x4 -> x0, local copies, waits for them, and re-layouts: 7.91 us -> none  [the longest x2 3.45 us: shards(): lax.dynamic_slice_in_dim(normed_online, group * (width // 2), width // 2, 1)]
  transfers between devices with their start and end apart: 14 -> 41, of which waited for: 7 -> 13; matrix products, arithmetic and copies ran while one was open for 16% -> 8% of each run, Pallas kernels for 0% -> 3%
where the time goes in v3:
time: 188 us; the launch traced here: 187 us
  starting transfers between devices  72 us (38%)
  waiting for transfers between devices  53.5 us (28%)
  local copies, waits for them, and re-layouts  19.4 us (10%)
  blocking collectives  17.5 us (9%)
  Pallas kernels  16 us (9%)
  other arithmetic  4.24 us (2%)
  matrix products  3.54 us (2%)
    ppermute x6, waiting for transfers between devices, round_y(): above = lax.ppermute(block, 'fsdp', y_from(3))  20.5 us
    all_to_all x1, blocking collectives, shards(): lax.all_to_all(updated, 'tp', split_axis=0, concat_axis=1, tiled=True)  17.5 us
    ppermute x6, starting transfers between devices, round_y(): below = lax.ppermute(block, 'fsdp', y_from(1))  15.7 us
    ppermute x6, starting transfers between devices, round_y(): high = lax.ppermute(below[half:], 'fsdp', y_from(1))  11.7 us
    unnamed x52, local copies, waits for them, and re-layouts  9.59 us
    all_to_all x1, starting transfers between devices, shards(): lax.all_to_all(jnp.broadcast_to(partial_quant[None], (tp_total,) + partia...  9.13 us
    all_to_all x1, waiting for transfers between devices, shards(): lax.all_to_all(jnp.broadcast_to(local_counts[None, :], (shard_total, shar...  8.76 us
    all_to_all x1, waiting for transfers between devices, shards(): lax.all_to_all(jnp.broadcast_to(partial_quant[None], (tp_total,) + partia...  8.09 us
  transfers between devices with their start and end apart: 41, of which 13 were waited for; matrix products, arithmetic and copies ran while one was open for 8% of the time, Pallas kernels for 3%

profile of v3, /device:TPU:32, one launch (start us, length us, event | category | flops | bytes accessed | tf_op | source)
XLA Modules:
  0.0 187.3 jit_solution(119218785731245229)
XLA Ops:
  0.8 2.2 %copy-done.1 = bf16[1,256,8192]{2,1,0:T(8,128)(2,1)S(1)} copy-done((bf16[1,256,8192]{2,1,0:T(8,128)(2,1)S(1)}, bf16[1,256,8192]{2,1,0:T(8,128)(2,1)}, u32[]{:S(2)}) %copy-start.1) | copy-done | bytes 4194328
  3.7 5.1 %norm.1 = (bf16[256,4096]{1,0:T(8,128)(2,1)S(1)}, bf16[256,4096]{1,0:T(8,128)(2,1)}) custom-call(s32[4]{0:T(128)S(1)} %pad_add_fusion.1.where_ref, bf16[256,8192]{1,0:T(8,128)(2,1)S(1)} %bitcast.27, f32[1,8192]{1,0:T(1,128)S(1)} %bitcast.31), custom_call_target="tpu_custom_call" | custom-call | flops 12582912 | bytes 8388608 | tf_op jit(solution)/shard_map/rows_swap/norm/pallas_call | solution.py:187
  12.2 2.8 %collective-permute-start.8 = (bf16[256,512]{1,0:T(8,128)(2,1)S(1)}, bf16[256,512]{1,0:T(8,128)(2,1)}, u32[]{:S(2)}, u32[]{:S(2)}) collective-permute-start(bf16[256,512]{1,0:T(8,128)(2,1)S(1)} %copy-done.2), channel_id=1, source_target_pairs={{0,8},{8,16},{16,24},{24,0},{32,40},{40,48},{48,56},{56,32},{64,72... | collective-permute-start | bytes 786440 | tf_op jit(solution)/shard_map/weight_gather/ppermute | solution.py:207
  17.3 6.0 %all-to-all-start.1 = ((f32[16,1,16]{2,1,0:T(1,128)}), f32[16,1,16]{2,1,0:T(1,128)S(1)}, u32[]{:S(2)}, u32[]{:S(2)}) async-start(f32[16,1,16]{2,1,0:T(1,128)} %broadcast_in_dim.49), calls=%async_computation.1 | async-start | bytes 16384 | tf_op jit(solution)/shard_map/counts/all_to_all | solution.py:264
  23.3 2.8 %collective-permute-start.9 = (bf16[256,512]{1,0:T(8,128)(2,1)S(1)}, bf16[256,512]{1,0:T(8,128)(2,1)S(1)}, u32[]{:S(2)}, u32[]{:S(2)}) collective-permute-start(bf16[256,512]{1,0:T(8,128)(2,1)S(1)} %copy-done.2), channel_id=1, source_target_pairs={{0,96},{8,104},{16,112},{24,120},{32,0},{40,8},{48,16},{56,24},{64... | collective-permute-start | bytes 786440 | tf_op jit(solution)/shard_map/weight_gather/ppermute | solution.py:32
  26.1 2.4 %pieces.1 = bf16[2,16,32,256]{3,2,1,0:T(8,128)(2,1)} custom-call(s32[4]{0:T(128)S(1)} %pad_add_fusion.1.where_ref, bf16[256,4096]{1,0:T(8,128)(2,1)S(1)} %get-tuple-element.18.own_ref, bf16[256,4096]{1,0:T(8,128)(2,1)} %collective-permute-done.got_ref), custom_call_target="tpu_custom_call" | custom-call | bytes 1048576 | tf_op jit(solution)/shard_map/columns_exchange/pieces/pallas_call | solution.py:224
  28.6 8.8 %all-to-all-done.1 = f32[16,1,16]{2,1,0:T(1,128)S(1)} async-done(((f32[16,1,16]{2,1,0:T(1,128)}), f32[16,1,16]{2,1,0:T(1,128)S(1)}, u32[]{:S(2)}, u32[]{:S(2)}) %all-to-all-start.1) | async-done | bytes 1056 | tf_op jit(solution)/shard_map/counts/all_to_all | solution.py:264
  37.3 7.7 %all-to-all-start = ((bf16[32,32,256]{2,1,0:T(8,128)(2,1)}), bf16[32,32,256]{2,1,0:T(8,128)(2,1)S(1)}, u32[]{:S(2)}, u32[]{:S(2)}) async-start(bf16[32,32,256]{2,1,0:T(8,128)(2,1)} %bitcast.6), calls=%async_computation | async-start | bytes 1048576 | tf_op jit(solution)/shard_map/columns_exchange/all_to_all | solution.py:239
  46.0 2.8 %collective-permute-start.10 = (bf16[256,512]{1,0:T(8,128)(2,1)}, bf16[256,512]{1,0:T(8,128)(2,1)}, u32[]{:S(2)}, u32[]{:S(2)}) collective-permute-start(bf16[256,512]{1,0:T(8,128)(2,1)} %collective-permute-done.6.refs_1_), channel_id=1, source_target_pairs={{0,96},{8,104},{16,112},{24,120},{32,0},{40,8},{48,16},{56,24},{64... | collective-permute-start | bytes 786440 | tf_op jit(solution)/shard_map/weight_gather/ppermute | solution.py:32
  50.3 2.6 %collective-permute-start.11 = (bf16[256,512]{1,0:T(8,128)(2,1)}, bf16[256,512]{1,0:T(8,128)(2,1)S(1)}, u32[]{:S(2)}, u32[]{:S(2)}) collective-permute-start(bf16[256,512]{1,0:T(8,128)(2,1)} %collective-permute-done.7.refs_2_), channel_id=1, source_target_pairs={{0,96},{8,104},{16,112},{24,120},{32,0},{40,8},{48,16},{56,24},{64... | collective-permute-start | bytes 786440 | tf_op jit(solution)/shard_map/weight_gather/ppermute | solution.py:32
  52.8 1.9 %collective-permute-start.12 = (bf16[256,512]{1,0:T(8,128)(2,1)}, bf16[256,512]{1,0:T(8,128)(2,1)S(1)}, u32[]{:S(2)}, u32[]{:S(2)}) collective-permute-start(bf16[256,512]{1,0:T(8,128)(2,1)} %collective-permute-done.8.refs_3_), channel_id=1, source_target_pairs={{0,96},{8,104},{16,112},{24,120},{32,0},{40,8},{48,16},{56,24},{64... | collective-permute-start | bytes 786440 | tf_op jit(solution)/shard_map/weight_gather/ppermute | solution.py:32
  55.7 6.4 %collective-permute-done.15.refs_10_ = bf16[256,512]{1,0:T(8,128)(2,1)} collective-permute-done((bf16[256,512]{1,0:T(8,128)(2,1)}, bf16[256,512]{1,0:T(8,128)(2,1)}, u32[]{:S(2)}, u32[]{:S(2)}) %collective-permute-start.15) | collective-permute-done | bytes 262176 | tf_op jit(solution)/shard_map/weight_gather/ppermute | solution.py:33
  62.2 5.6 %collective-permute-done.16.refs_11_ = bf16[256,512]{1,0:T(8,128)(2,1)} collective-permute-done((bf16[256,512]{1,0:T(8,128)(2,1)}, bf16[256,512]{1,0:T(8,128)(2,1)}, u32[]{:S(2)}, u32[]{:S(2)}) %collective-permute-start.16) | collective-permute-done | bytes 262176 | tf_op jit(solution)/shard_map/weight_gather/ppermute | solution.py:33
  67.8 2.0 %collective-permute-start.18 = (bf16[128,512]{1,0:T(8,128)(2,1)S(1)}, bf16[128,512]{1,0:T(8,128)(2,1)S(1)}, u32[]{:S(2)}, u32[]{:S(2)}) collective-permute-start(bf16[128,512]{1,0:T(8,128)(2,1)S(1)} %slice.92), channel_id=1, source_target_pairs={{0,32},{8,40},{16,48},{24,56},{32,64},{40,72},{48,80},{56,88},{64,... | collective-permute-start | bytes 393224 | tf_op jit(solution)/shard_map/weight_gather/ppermute | solution.py:34
  77.4 3.2 %collective-permute-start.22 = (bf16[128,512]{1,0:T(8,128)(2,1)}, bf16[128,512]{1,0:T(8,128)(2,1)}, u32[]{:S(2)}, u32[]{:S(2)}) collective-permute-start(bf16[128,512]{1,0:T(8,128)(2,1)} %slice.96), channel_id=1, source_target_pairs={{0,96},{8,104},{16,112},{24,120},{32,0},{40,8},{48,16},{56,24},{64... | collective-permute-start | bytes 393224 | tf_op jit(solution)/shard_map/weight_gather/ppermute | solution.py:35
  81.2 2.0 %collective-permute-start.23 = (bf16[128,512]{1,0:T(8,128)(2,1)}, bf16[128,512]{1,0:T(8,128)(2,1)}, u32[]{:S(2)}, u32[]{:S(2)}) collective-permute-start(bf16[128,512]{1,0:T(8,128)(2,1)} %slice.97), channel_id=1, source_target_pairs={{0,96},{8,104},{16,112},{24,120},{32,0},{40,8},{48,16},{56,24},{64... | collective-permute-start | bytes 393224 | tf_op jit(solution)/shard_map/weight_gather/ppermute | solution.py:35
  83.9 2.3 %collective-permute-done.20.refs_15_ = bf16[128,512]{1,0:T(8,128)(2,1)} collective-permute-done((bf16[128,512]{1,0:T(8,128)(2,1)}, bf16[128,512]{1,0:T(8,128)(2,1)}, u32[]{:S(2)}, u32[]{:S(2)}) %collective-permute-start.20) | collective-permute-done | bytes 131104 | tf_op jit(solution)/shard_map/weight_gather/ppermute | solution.py:34
  87.6 2.1 %collective-permute-done.24.refs_19_ = bf16[128,512]{1,0:T(8,128)(2,1)} collective-permute-done((bf16[128,512]{1,0:T(8,128)(2,1)}, bf16[128,512]{1,0:T(8,128)(2,1)}, u32[]{:S(2)}, u32[]{:S(2)}) %collective-permute-start.24) | collective-permute-done | bytes 131104 | tf_op jit(solution)/shard_map/weight_gather/ppermute | solution.py:35
  94.3 4.7 %preact.1 = (f32[256,512]{1,0:T(8,128)S(1)}, f32[256,512]{1,0:T(8,128)S(1)}) custom-call(s32[4]{0:T(128)S(1)} %pad_add_fusion.1.where_ref, bf16[256,4096]{1,0:T(8,128)(2,1)S(1)} %get-tuple-element.18.own_ref, bf16[256,4096]{1,0:T(8,128)(2,1)} %collective-permute-done.got_ref, bf16[256,512]{1,0:T(8,128)(2,1)S(1)} %copy-done.2, ...), custom_call_target="tpu_custom_call" | custom-call | flops 2147483648 | bytes 9437184 | tf_op jit(solution)/shard_map/preact/pallas_call | solution.py:295
  101.0 2.8 %collective-permute-start.1 = (bf16[2,16,32,256]{3,2,1,0:T(8,128)(2,1)S(1)}, bf16[2,16,32,256]{3,2,1,0:T(8,128)(2,1)S(1)}, u32[]{:S(2)}, u32[]{:S(2)}) collective-permute-start(bf16[2,16,32,256]{3,2,1,0:T(8,128)(2,1)S(1)} %bitcast.28), channel_id=1, source_target_pairs={{0,6},{1,7},{2,0},{3,1},{4,2},{5,3},{6,4},{7,5},{8,14},{9,15},{10,... | collective-permute-start | bytes 1572872 | tf_op jit(solution)/shard_map/columns_exchange/ppermute | solution.py:242
  105.4 9.1 %all-to-all-start.2 = ((f32[8,32,256]{2,1,0:T(8,128)}), f32[8,32,256]{2,1,0:T(8,128)S(1)}, u32[]{:S(2)}, u32[]{:S(2)}) async-start(f32[8,32,256]{2,1,0:T(8,128)} %broadcast_in_dim.86), calls=%async_computation.2 | async-start | bytes 524288 | tf_op jit(solution)/shard_map/quant_sum/all_to_all | solution.py:323
  116.1 3.8 %collective-permute-start.3 = (bf16[16,32,256]{2,1,0:T(8,128)(2,1)S(1)}, bf16[16,32,256]{2,1,0:T(8,128)(2,1)S(1)}, u32[]{:S(2)}, u32[]{:S(2)}) collective-permute-start(bf16[16,32,256]{2,1,0:T(8,128)(2,1)S(1)} %slice_bitcast_fusion.1), channel_id=1, source_target_pairs={{0,6},{1,7},{2,0},{3,1},{4,2},{5,3},{6,4},{7,5},{8,14},{9,15},{10,... | collective-permute-start | bytes 786440 | tf_op jit(solution)/shard_map/columns_exchange/ppermute | solution.py:244
  120.5 8.1 %all-to-all-done.2 = f32[8,32,256]{2,1,0:T(8,128)S(1)} async-done(((f32[8,32,256]{2,1,0:T(8,128)}), f32[8,32,256]{2,1,0:T(8,128)S(1)}, u32[]{:S(2)}, u32[]{:S(2)}) %all-to-all-start.2) | async-done | bytes 262176 | tf_op jit(solution)/shard_map/quant_sum/all_to_all | solution.py:323
  130.7 2.6 %collective-permute-start.27 = (bf16[128,512]{1,0:T(8,128)(2,1)S(1)}, bf16[128,512]{1,0:T(8,128)(2,1)S(1)}, u32[]{:S(2)}, u32[]{:S(2)}) collective-permute-start(bf16[128,512]{1,0:T(8,128)(2,1)S(1)} %fusion.5.own_ref), channel_id=1, source_target_pairs={{0,16},{8,24},{16,0},{24,8},{32,48},{40,56},{48,32},{56,40},{64,80... | collective-permute-start | bytes 393224 | tf_op jit(solution)/shard_map/grad_gather/ppermute | solution.py:357
  133.3 3.6 %collective-permute-start.29 = (bf16[128,512]{1,0:T(8,128)(2,1)S(1)}, bf16[128,512]{1,0:T(8,128)(2,1)S(1)}, u32[]{:S(2)}, u32[]{:S(2)}) collective-permute-start(bf16[128,512]{1,0:T(8,128)(2,1)S(1)} %fusion.5.own_ref), channel_id=1, source_target_pairs={{0,96},{8,104},{16,112},{24,120},{32,0},{40,8},{48,16},{56,24},{64... | collective-permute-start | bytes 393224 | tf_op jit(solution)/shard_map/grad_gather/ppermute | solution.py:32
  136.9 5.6 %collective-permute-done.26 = bf16[128,512]{1,0:T(8,128)(2,1)S(1)} collective-permute-done((bf16[128,512]{1,0:T(8,128)(2,1)S(1)}, bf16[128,512]{1,0:T(8,128)(2,1)S(1)}, u32[]{:S(2)}, u32[]{:S(2)}) %collective-permute-start.26) | collective-permute-done | bytes 131104 | tf_op jit(solution)/shard_map/grad_gather/ppermute | solution.py:357
  144.4 2.0 %collective-permute-start.31 = (bf16[384,512]{1,0:T(8,128)(2,1)S(1)}, bf16[384,512]{1,0:T(8,128)(2,1)S(1)}, u32[]{:S(2)}, u32[]{:S(2)}) collective-permute-start(bf16[384,512]{1,0:T(8,128)(2,1)S(1)} %constant_dynamic-update-slice_fusion.line_ref), channel_id=1, source_target_pairs={{0,96},{8,104},{16,112},{24,120},{32,0},{40,8},{48,16},{56,24},{64... | collective-permute-start | bytes 1179656 | tf_op jit(solution)/shard_map/grad_gather/ppermute | solution.py:32
  146.4 7.9 %collective-permute-done.32.a1_ref = bf16[384,512]{1,0:T(8,128)(2,1)S(1)} collective-permute-done((bf16[384,512]{1,0:T(8,128)(2,1)S(1)}, bf16[384,512]{1,0:T(8,128)(2,1)S(1)}, u32[]{:S(2)}, u32[]{:S(2)}) %collective-permute-start.32) | collective-permute-done | bytes 393248 | tf_op jit(solution)/shard_map/grad_gather/ppermute | solution.py:33
  154.5 3.3 %collective-permute-start.36 = (bf16[192,512]{1,0:T(8,128)(2,1)S(1)}, bf16[192,512]{1,0:T(8,128)(2,1)S(1)}, u32[]{:S(2)}, u32[]{:S(2)}) collective-permute-start(bf16[192,512]{1,0:T(8,128)(2,1)S(1)} %slice.104), channel_id=1, source_target_pairs={{0,96},{8,104},{16,112},{24,120},{32,0},{40,8},{48,16},{56,24},{64... | collective-permute-start | bytes 589832 | tf_op jit(solution)/shard_map/grad_gather/ppermute | solution.py:35
  157.7 2.4 %columns.1.cols_ref = bf16[512,2048]{1,0:T(8,128)(2,1)S(1)} custom-call(s32[4]{0:T(128)S(1)} %pad_add_fusion.1.where_ref, bf16[2,16,32,256]{3,2,1,0:T(8,128)(2,1)S(1)} %bitcast.30, bf16[2,16,32,256]{3,2,1,0:T(8,128)(2,1)S(1)} %collective-permute-done.1.after_ref, bf16[2,16,32,256]{3,2,1,0:T(8,128)(2,1)S(1)} %collective-permute-done.2.before_ref, ...), custom_call_target="tpu_custom_call" | custom-call | bytes 4194304 | tf_op jit(solution)/shard_map/columns_exchange/columns/pallas_call | solution.py:246
  160.2 3.2 %collective-permute-start.34 = (bf16[64,512]{1,0:T(8,128)(2,1)S(1)}, bf16[64,512]{1,0:T(8,128)(2,1)S(1)}, u32[]{:S(2)}, u32[]{:S(2)}) collective-permute-start(bf16[64,512]{1,0:T(8,128)(2,1)S(1)} %slice.102), channel_id=1, source_target_pairs={{0,96},{8,104},{16,112},{24,120},{32,0},{40,8},{48,16},{56,24},{64... | collective-permute-start | bytes 196616 | tf_op jit(solution)/shard_map/grad_gather/ppermute | solution.py:35
  169.1 17.5 %all_to_all.35 = bf16[8,32,512]{2,1,0:T(8,128)(2,1)S(1)} all-to-all(bf16[8,32,512]{2,1,0:T(8,128)(2,1)S(1)} %bitcast.33), channel_id=1, replica_groups=mesh['grp'=2,'fsdp'=16,'tp'=8] {'tp'}, dimensions={0} | all-to-all | bytes 524288 | tf_op jit(solution)/shard_map/all_to_all | solution.py:391
  (153 shorter events, 41.0 us)
Async XLA Ops:
  8.8 17.3 %collective-permute-start = (bf16[256,4096]{1,0:T(8,128)(2,1)}, bf16[256,4096]{1,0:T(8,128)(2,1)}, u32[]{:S(2)}, u32[]{:S(2)}) collective-permute-start(bf16[256,4096]{1,0:T(8,128)(2,1)} %get-tuple-element.17), channel_id=1, source_target_pairs={{0,128},{128,0},{1,129},{129,1},{2,130},{130,2},{3,131},{131,3},{4... | collective-permute-start | bytes 6291464 | tf_op jit(solution)/shard_map/rows_swap/ppermute | solution.py:212
  8.8 14.5 %collective-permute-start.6 = (bf16[256,512]{1,0:T(8,128)(2,1)S(1)}, bf16[256,512]{1,0:T(8,128)(2,1)}, u32[]{:S(2)}, u32[]{:S(2)}) collective-permute-start(bf16[256,512]{1,0:T(8,128)(2,1)S(1)} %copy-done.2), channel_id=1, source_target_pairs={{0,24},{8,0},{16,8},{24,16},{32,56},{40,32},{48,40},{56,48},{64,88... | collective-permute-start | bytes 786440 | tf_op jit(solution)/shard_map/weight_gather/ppermute | solution.py:207
  10.7 35.3 %collective-permute-start.7 = (bf16[256,512]{1,0:T(8,128)(2,1)S(1)}, bf16[256,512]{1,0:T(8,128)(2,1)}, u32[]{:S(2)}, u32[]{:S(2)}) collective-permute-start(bf16[256,512]{1,0:T(8,128)(2,1)S(1)} %copy-done.2), channel_id=1, source_target_pairs={{0,16},{8,24},{16,0},{24,8},{32,48},{40,56},{48,32},{56,40},{64,80... | collective-permute-start | bytes 786440 | tf_op jit(solution)/shard_map/weight_gather/ppermute | solution.py:207
  12.2 36.5 %collective-permute-start.8 = (bf16[256,512]{1,0:T(8,128)(2,1)S(1)}, bf16[256,512]{1,0:T(8,128)(2,1)}, u32[]{:S(2)}, u32[]{:S(2)}) collective-permute-start(bf16[256,512]{1,0:T(8,128)(2,1)S(1)} %copy-done.2), channel_id=1, source_target_pairs={{0,8},{8,16},{16,24},{24,0},{32,40},{40,48},{48,56},{56,32},{64,72... | collective-permute-start | bytes 786440 | tf_op jit(solution)/shard_map/weight_gather/ppermute | solution.py:207
  15.0 33.7 %collective-permute-start.13 = (bf16[256,512]{1,0:T(8,128)(2,1)S(1)}, bf16[256,512]{1,0:T(8,128)(2,1)S(1)}, u32[]{:S(2)}, u32[]{:S(2)}) collective-permute-start(bf16[256,512]{1,0:T(8,128)(2,1)S(1)} %copy-done.2), channel_id=1, source_target_pairs={{0,32},{8,40},{16,48},{24,56},{32,64},{40,72},{48,80},{56,88},{64,... | collective-permute-start | bytes 786440 | tf_op jit(solution)/shard_map/weight_gather/ppermute | solution.py:33
  17.3 20.0 %all-to-all-start.1 = ((f32[16,1,16]{2,1,0:T(1,128)}), f32[16,1,16]{2,1,0:T(1,128)S(1)}, u32[]{:S(2)}, u32[]{:S(2)}) async-start(f32[16,1,16]{2,1,0:T(1,128)} %broadcast_in_dim.49), calls=%async_computation.1 | async-start | bytes 16384 | tf_op jit(solution)/shard_map/counts/all_to_all | solution.py:264
  23.3 26.9 %collective-permute-start.9 = (bf16[256,512]{1,0:T(8,128)(2,1)S(1)}, bf16[256,512]{1,0:T(8,128)(2,1)S(1)}, u32[]{:S(2)}, u32[]{:S(2)}) collective-permute-start(bf16[256,512]{1,0:T(8,128)(2,1)S(1)} %copy-done.2), channel_id=1, source_target_pairs={{0,96},{8,104},{16,112},{24,120},{32,0},{40,8},{48,16},{56,24},{64... | collective-permute-start | bytes 786440 | tf_op jit(solution)/shard_map/weight_gather/ppermute | solution.py:32
  26.1 26.8 %collective-permute-start.14 = (bf16[256,512]{1,0:T(8,128)(2,1)}, bf16[256,512]{1,0:T(8,128)(2,1)}, u32[]{:S(2)}, u32[]{:S(2)}) collective-permute-start(bf16[256,512]{1,0:T(8,128)(2,1)} %collective-permute-done.6.refs_1_), channel_id=1, source_target_pairs={{0,32},{8,40},{16,48},{24,56},{32,64},{40,72},{48,80},{56,88},{64,... | collective-permute-start | bytes 786440 | tf_op jit(solution)/shard_map/weight_gather/ppermute | solution.py:33
  37.3 46.6 %all-to-all-start = ((bf16[32,32,256]{2,1,0:T(8,128)(2,1)}), bf16[32,32,256]{2,1,0:T(8,128)(2,1)S(1)}, u32[]{:S(2)}, u32[]{:S(2)}) async-start(bf16[32,32,256]{2,1,0:T(8,128)(2,1)} %bitcast.6), calls=%async_computation | async-start | bytes 1048576 | tf_op jit(solution)/shard_map/columns_exchange/all_to_all | solution.py:239
  46.0 21.8 %collective-permute-start.10 = (bf16[256,512]{1,0:T(8,128)(2,1)}, bf16[256,512]{1,0:T(8,128)(2,1)}, u32[]{:S(2)}, u32[]{:S(2)}) collective-permute-start(bf16[256,512]{1,0:T(8,128)(2,1)} %collective-permute-done.6.refs_1_), channel_id=1, source_target_pairs={{0,96},{8,104},{16,112},{24,120},{32,0},{40,8},{48,16},{56,24},{64... | collective-permute-start | bytes 786440 | tf_op jit(solution)/shard_map/weight_gather/ppermute | solution.py:32
  48.8 13.4 %collective-permute-start.15 = (bf16[256,512]{1,0:T(8,128)(2,1)}, bf16[256,512]{1,0:T(8,128)(2,1)}, u32[]{:S(2)}, u32[]{:S(2)}) collective-permute-start(bf16[256,512]{1,0:T(8,128)(2,1)} %collective-permute-done.7.refs_2_), channel_id=1, source_target_pairs={{0,32},{8,40},{16,48},{24,56},{32,64},{40,72},{48,80},{56,88},{64,... | collective-permute-start | bytes 786440 | tf_op jit(solution)/shard_map/weight_gather/ppermute | solution.py:33
  48.8 19.0 %collective-permute-start.16 = (bf16[256,512]{1,0:T(8,128)(2,1)}, bf16[256,512]{1,0:T(8,128)(2,1)}, u32[]{:S(2)}, u32[]{:S(2)}) collective-permute-start(bf16[256,512]{1,0:T(8,128)(2,1)} %collective-permute-done.8.refs_3_), channel_id=1, source_target_pairs={{0,32},{8,40},{16,48},{24,56},{32,64},{40,72},{48,80},{56,88},{64,... | collective-permute-start | bytes 786440 | tf_op jit(solution)/shard_map/weight_gather/ppermute | solution.py:33
  50.3 19.7 %collective-permute-start.11 = (bf16[256,512]{1,0:T(8,128)(2,1)}, bf16[256,512]{1,0:T(8,128)(2,1)S(1)}, u32[]{:S(2)}, u32[]{:S(2)}) collective-permute-start(bf16[256,512]{1,0:T(8,128)(2,1)} %collective-permute-done.7.refs_2_), channel_id=1, source_target_pairs={{0,96},{8,104},{16,112},{24,120},{32,0},{40,8},{48,16},{56,24},{64... | collective-permute-start | bytes 786440 | tf_op jit(solution)/shard_map/weight_gather/ppermute | solution.py:32
  52.8 23.1 %collective-permute-start.12 = (bf16[256,512]{1,0:T(8,128)(2,1)}, bf16[256,512]{1,0:T(8,128)(2,1)S(1)}, u32[]{:S(2)}, u32[]{:S(2)}) collective-permute-start(bf16[256,512]{1,0:T(8,128)(2,1)} %collective-permute-done.8.refs_3_), channel_id=1, source_target_pairs={{0,96},{8,104},{16,112},{24,120},{32,0},{40,8},{48,16},{56,24},{64... | collective-permute-start | bytes 786440 | tf_op jit(solution)/shard_map/weight_gather/ppermute | solution.py:32
  62.2 14.5 %collective-permute-start.17 = (bf16[128,512]{1,0:T(8,128)(2,1)S(1)}, bf16[128,512]{1,0:T(8,128)(2,1)S(1)}, u32[]{:S(2)}, u32[]{:S(2)}) collective-permute-start(bf16[128,512]{1,0:T(8,128)(2,1)S(1)} %slice.91), channel_id=1, source_target_pairs={{0,32},{8,40},{16,48},{24,56},{32,64},{40,72},{48,80},{56,88},{64,... | collective-permute-start | bytes 393224 | tf_op jit(solution)/shard_map/weight_gather/ppermute | solution.py:34
  67.8 12.8 %collective-permute-start.21 = (bf16[128,512]{1,0:T(8,128)(2,1)S(1)}, bf16[128,512]{1,0:T(8,128)(2,1)S(1)}, u32[]{:S(2)}, u32[]{:S(2)}) collective-permute-start(bf16[128,512]{1,0:T(8,128)(2,1)S(1)} %slice.95), channel_id=1, source_target_pairs={{0,96},{8,104},{16,112},{24,120},{32,0},{40,8},{48,16},{56,24},{64... | collective-permute-start | bytes 393224 | tf_op jit(solution)/shard_map/weight_gather/ppermute | solution.py:35
  67.8 15.4 %collective-permute-start.18 = (bf16[128,512]{1,0:T(8,128)(2,1)S(1)}, bf16[128,512]{1,0:T(8,128)(2,1)S(1)}, u32[]{:S(2)}, u32[]{:S(2)}) collective-permute-start(bf16[128,512]{1,0:T(8,128)(2,1)S(1)} %slice.92), channel_id=1, source_target_pairs={{0,32},{8,40},{16,48},{24,56},{32,64},{40,72},{48,80},{56,88},{64,... | collective-permute-start | bytes 393224 | tf_op jit(solution)/shard_map/weight_gather/ppermute | solution.py:34
  76.7 9.5 %collective-permute-start.20 = (bf16[128,512]{1,0:T(8,128)(2,1)}, bf16[128,512]{1,0:T(8,128)(2,1)}, u32[]{:S(2)}, u32[]{:S(2)}) collective-permute-start(bf16[128,512]{1,0:T(8,128)(2,1)} %slice.94), channel_id=1, source_target_pairs={{0,32},{8,40},{16,48},{24,56},{32,64},{40,72},{48,80},{56,88},{64,... | collective-permute-start | bytes 393224 | tf_op jit(solution)/shard_map/weight_gather/ppermute | solution.py:34
  77.4 8.9 %collective-permute-start.22 = (bf16[128,512]{1,0:T(8,128)(2,1)}, bf16[128,512]{1,0:T(8,128)(2,1)}, u32[]{:S(2)}, u32[]{:S(2)}) collective-permute-start(bf16[128,512]{1,0:T(8,128)(2,1)} %slice.96), channel_id=1, source_target_pairs={{0,96},{8,104},{16,112},{24,120},{32,0},{40,8},{48,16},{56,24},{64... | collective-permute-start | bytes 393224 | tf_op jit(solution)/shard_map/weight_gather/ppermute | solution.py:35
  101.0 15.0 %collective-permute-start.1 = (bf16[2,16,32,256]{3,2,1,0:T(8,128)(2,1)S(1)}, bf16[2,16,32,256]{3,2,1,0:T(8,128)(2,1)S(1)}, u32[]{:S(2)}, u32[]{:S(2)}) collective-permute-start(bf16[2,16,32,256]{3,2,1,0:T(8,128)(2,1)S(1)} %bitcast.28), channel_id=1, source_target_pairs={{0,6},{1,7},{2,0},{3,1},{4,2},{5,3},{6,4},{7,5},{8,14},{9,15},{10,... | collective-permute-start | bytes 1572872 | tf_op jit(solution)/shard_map/columns_exchange/ppermute | solution.py:242
  103.9 16.0 %collective-permute-start.2 = (bf16[2,16,32,256]{3,2,1,0:T(8,128)(2,1)S(1)}, bf16[2,16,32,256]{3,2,1,0:T(8,128)(2,1)S(1)}, u32[]{:S(2)}, u32[]{:S(2)}) collective-permute-start(bf16[2,16,32,256]{3,2,1,0:T(8,128)(2,1)S(1)} %bitcast.29), channel_id=1, source_target_pairs={{0,2},{1,3},{2,4},{3,5},{4,6},{5,7},{6,0},{7,1},{8,10},{9,11},{10,... | collective-permute-start | bytes 1572872 | tf_op jit(solution)/shard_map/columns_exchange/ppermute | solution.py:243
  105.4 23.3 %all-to-all-start.2 = ((f32[8,32,256]{2,1,0:T(8,128)}), f32[8,32,256]{2,1,0:T(8,128)S(1)}, u32[]{:S(2)}, u32[]{:S(2)}) async-start(f32[8,32,256]{2,1,0:T(8,128)} %broadcast_in_dim.86), calls=%async_computation.2 | async-start | bytes 524288 | tf_op jit(solution)/shard_map/quant_sum/all_to_all | solution.py:323
  116.1 17.2 %collective-permute-start.3 = (bf16[16,32,256]{2,1,0:T(8,128)(2,1)S(1)}, bf16[16,32,256]{2,1,0:T(8,128)(2,1)S(1)}, u32[]{:S(2)}, u32[]{:S(2)}) collective-permute-start(bf16[16,32,256]{2,1,0:T(8,128)(2,1)S(1)} %slice_bitcast_fusion.1), channel_id=1, source_target_pairs={{0,6},{1,7},{2,0},{3,1},{4,2},{5,3},{6,4},{7,5},{8,14},{9,15},{10,... | collective-permute-start | bytes 786440 | tf_op jit(solution)/shard_map/columns_exchange/ppermute | solution.py:244
  120.5 16.3 %collective-permute-start.4 = (bf16[16,32,256]{2,1,0:T(8,128)(2,1)}, bf16[16,32,256]{2,1,0:T(8,128)(2,1)S(1)}, u32[]{:S(2)}, u32[]{:S(2)}) collective-permute-start(bf16[16,32,256]{2,1,0:T(8,128)(2,1)} %slice_bitcast_fusion), channel_id=1, source_target_pairs={{0,2},{1,3},{2,4},{3,5},{4,6},{5,7},{6,0},{7,1},{8,10},{9,11},{10,... | collective-permute-start | bytes 786440 | tf_op jit(solution)/shard_map/columns_exchange/ppermute | solution.py:245
  130.4 12.0 %collective-permute-start.26 = (bf16[128,512]{1,0:T(8,128)(2,1)S(1)}, bf16[128,512]{1,0:T(8,128)(2,1)S(1)}, u32[]{:S(2)}, u32[]{:S(2)}) collective-permute-start(bf16[128,512]{1,0:T(8,128)(2,1)S(1)} %fusion.5.own_ref), channel_id=1, source_target_pairs={{0,24},{8,0},{16,8},{24,16},{32,56},{40,32},{48,40},{56,48},{64,88... | collective-permute-start | bytes 393224 | tf_op jit(solution)/shard_map/grad_gather/ppermute | solution.py:357
  130.7 11.7 %collective-permute-start.27 = (bf16[128,512]{1,0:T(8,128)(2,1)S(1)}, bf16[128,512]{1,0:T(8,128)(2,1)S(1)}, u32[]{:S(2)}, u32[]{:S(2)}) collective-permute-start(bf16[128,512]{1,0:T(8,128)(2,1)S(1)} %fusion.5.own_ref), channel_id=1, source_target_pairs={{0,16},{8,24},{16,0},{24,8},{32,48},{40,56},{48,32},{56,40},{64,80... | collective-permute-start | bytes 393224 | tf_op jit(solution)/shard_map/grad_gather/ppermute | solution.py:357
  133.3 9.2 %collective-permute-start.28 = (bf16[128,512]{1,0:T(8,128)(2,1)S(1)}, bf16[128,512]{1,0:T(8,128)(2,1)S(1)}, u32[]{:S(2)}, u32[]{:S(2)}) collective-permute-start(bf16[128,512]{1,0:T(8,128)(2,1)S(1)} %fusion.5.own_ref), channel_id=1, source_target_pairs={{0,8},{8,16},{16,24},{24,0},{32,40},{40,48},{48,56},{56,32},{64,72... | collective-permute-start | bytes 393224 | tf_op jit(solution)/shard_map/grad_gather/ppermute | solution.py:357
  133.3 9.2 %collective-permute-start.29 = (bf16[128,512]{1,0:T(8,128)(2,1)S(1)}, bf16[128,512]{1,0:T(8,128)(2,1)S(1)}, u32[]{:S(2)}, u32[]{:S(2)}) collective-permute-start(bf16[128,512]{1,0:T(8,128)(2,1)S(1)} %fusion.5.own_ref), channel_id=1, source_target_pairs={{0,96},{8,104},{16,112},{24,120},{32,0},{40,8},{48,16},{56,24},{64... | collective-permute-start | bytes 393224 | tf_op jit(solution)/shard_map/grad_gather/ppermute | solution.py:32
  143.1 11.2 %collective-permute-start.32 = (bf16[384,512]{1,0:T(8,128)(2,1)S(1)}, bf16[384,512]{1,0:T(8,128)(2,1)S(1)}, u32[]{:S(2)}, u32[]{:S(2)}) collective-permute-start(bf16[384,512]{1,0:T(8,128)(2,1)S(1)} %constant_dynamic-update-slice_fusion.line_ref), channel_id=1, source_target_pairs={{0,32},{8,40},{16,48},{24,56},{32,64},{40,72},{48,80},{56,88},{64,... | collective-permute-start | bytes 1179656 | tf_op jit(solution)/shard_map/grad_gather/ppermute | solution.py:33
  144.4 10.1 %collective-permute-start.31 = (bf16[384,512]{1,0:T(8,128)(2,1)S(1)}, bf16[384,512]{1,0:T(8,128)(2,1)S(1)}, u32[]{:S(2)}, u32[]{:S(2)}) collective-permute-start(bf16[384,512]{1,0:T(8,128)(2,1)S(1)} %constant_dynamic-update-slice_fusion.line_ref), channel_id=1, source_target_pairs={{0,96},{8,104},{16,112},{24,120},{32,0},{40,8},{48,16},{56,24},{64... | collective-permute-start | bytes 1179656 | tf_op jit(solution)/shard_map/grad_gather/ppermute | solution.py:32
  154.3 11.4 %collective-permute-start.35 = (bf16[192,512]{1,0:T(8,128)(2,1)S(1)}, bf16[192,512]{1,0:T(8,128)(2,1)S(1)}, u32[]{:S(2)}, u32[]{:S(2)}) collective-permute-start(bf16[192,512]{1,0:T(8,128)(2,1)S(1)} %slice.103), channel_id=1, source_target_pairs={{0,32},{8,40},{16,48},{24,56},{32,64},{40,72},{48,80},{56,88},{64,... | collective-permute-start | bytes 589832 | tf_op jit(solution)/shard_map/grad_gather/ppermute | solution.py:34
  154.5 11.2 %collective-permute-start.36 = (bf16[192,512]{1,0:T(8,128)(2,1)S(1)}, bf16[192,512]{1,0:T(8,128)(2,1)S(1)}, u32[]{:S(2)}, u32[]{:S(2)}) collective-permute-start(bf16[192,512]{1,0:T(8,128)(2,1)S(1)} %slice.104), channel_id=1, source_target_pairs={{0,96},{8,104},{16,112},{24,120},{32,0},{40,8},{48,16},{56,24},{64... | collective-permute-start | bytes 589832 | tf_op jit(solution)/shard_map/grad_gather/ppermute | solution.py:35
  (34 other events, 325.0 us)

commit v4 on v3

--- a/solution.py
+++ b/solution.py
@@ -12,6 +12,7 @@
 Y = 4
 Z = 4
 
+
 SWAP = [(0, 1), (1, 0)]
 
 
@@ -27,40 +28,51 @@
     return [(t, (t - step * 2) % (X * 2)) for t in range(X * 2)]
 
 
-def round_y(block):
-    half = block.shape[0] // 2
+def round_y(block, upward):
     below = lax.ppermute(block, "fsdp", y_from(1))
     above = lax.ppermute(block, "fsdp", y_from(3))
-    low = lax.ppermute(above[:half], "fsdp", y_from(3))
-    high = lax.ppermute(below[half:], "fsdp", y_from(1))
-    return below, above, low, high
+    if upward:
+        return below, above, lax.ppermute(above, "fsdp", y_from(3))
+    return below, above, lax.ppermute(below, "fsdp", y_from(1))
 
 
 def preact_kernel(where_ref, own_ref, got_ref, *refs):
-    weights = refs[: 5 * Z]
-    keep_ref, send_ref, total = refs[5 * Z :]
+    weights = refs[: Y * Z]
+    keep_ref, send_ref, total, rows_held, held, sems = refs[Y * Z :]
     group, y, z = where_ref[0], where_ref[1], where_ref[2]
     rows = own_ref.shape[0]
     block = weights[0].shape[0]
-    total[...] = jnp.zeros_like(total)
-    for step_y in range(Y):
-        for step_z in range(Z):
-            place = lax.rem(y + step_y, Y) * Z + lax.rem(z + step_z, Z)
-            cols = pl.ds(pl.multiple_of(place * block, block), block)
-            if step_y == 0:
-                weight = weights[step_z][...]
-            elif step_y == 2:
-                weight = jnp.concatenate(
-                    [weights[3 * Z + step_z][...], weights[4 * Z + step_z][...]], 0
-                )
-            else:
-                weight = weights[(1 if step_y == 1 else 2) * Z + step_z][...]
-            total[:rows] += jnp.dot(own_ref[:, cols], weight, preferred_element_type=jnp.float32)
-            total[rows:] += jnp.dot(got_ref[:, cols], weight, preferred_element_type=jnp.float32)
+    order = [(0, k) for k in range(Z)] + [(j, k) for k in range(Z) for j in (1, 3)]
+    order += [(2, k) for k in range(Z)]
+    copies = []
+    for step, (step_y, step_z) in enumerate(order):
+        place = lax.rem(y + step_y, Y) * Z + lax.rem(z + step_z, Z)
+        cols = pl.ds(pl.multiple_of(place * block, block), block)
+        source = weights[step_y * Z + step_z]
+        copies.append(
+            (
+                pltpu.make_async_copy(
+                    own_ref.at[:, cols], rows_held.at[step, pl.ds(0, rows)], sems.at[0, step]
+                ),
+                pltpu.make_async_copy(
+                    got_ref.at[:, cols], rows_held.at[step, pl.ds(rows, rows)], sems.at[1, step]
+                ),
+                pltpu.make_async_copy(source, held.at[step], sems.at[2, step]),
+            )
+        )
+        for copy in copies[-1]:
+            copy.start()
+    for step in range(len(order)):
+        for copy in copies[step]:
+            copy.wait()
+        term = jnp.dot(rows_held[step], held[step], preferred_element_type=jnp.float32)
+        if step == 0:
+            total[...] = term
+        else:
+            total[...] += term
     half = rows // 2
     other = 1 - group
-    for mine, part in ((True, group), (False, other)):
-        base = 0 if mine else rows
+    for base, part in ((0, group), (rows, other)):
         out = pl.ds(pl.multiple_of(part * half, half), half)
         keep_ref[out, :] = total[pl.ds(pl.multiple_of(base + group * half, half), half), :]
         send_ref[out, :] = total[pl.ds(pl.multiple_of(base + other * half, half), half), :]
@@ -76,8 +88,9 @@
         out_ref[...] = (values * scale * gain_ref[:, cols]).astype(jnp.bfloat16)
 
 
-def pieces_kernel(where_ref, own_ref, got_ref, out_ref, held, sems):
-    places, strip, block = out_ref.shape[1:]
+def pieces_kernel(where_ref, own_ref, got_ref, count_ref, out_ref, held, sems):
+    places, _, block = out_ref.shape[1:]
+    strip = held.shape[1]
     half = own_ref.shape[0] // 2
 
     def fetch(source):
@@ -101,7 +114,8 @@
 
     for k in range(2):
         for place in range(places):
-            out_ref[k, place] = held[k, :, place * block : (place + 1) * block]
+            out_ref[k, place, :strip] = held[k, :, place * block : (place + 1) * block]
+            out_ref[k, place, strip:] = count_ref[...]
 
 
 def columns_kernel(where_ref, own_ref, after_ref, before_ref, far_a_ref, far_b_ref, out_ref, held):
@@ -142,8 +156,8 @@
     out_ref[...] = total
 
 
-def far_kernel(cols_ref, near_ref, l0_ref, h0_ref, l1_ref, h1_ref, own_ref, other_ref):
-    grads = jnp.concatenate([l0_ref[...], h0_ref[...], l1_ref[...], h1_ref[...]], 0)
+def far_kernel(cols_ref, near_ref, f0_ref, f1_ref, f2_ref, own_ref, other_ref):
+    grads = jnp.concatenate([f0_ref[...], f1_ref[...], f2_ref[...]], 0)
     span = grads.shape[0]
     block = own_ref.shape[0]
     cols = cols_ref[:, 2 * span : 3 * span]
@@ -203,10 +217,11 @@
             name="norm",
         )(where, values, norm_gain[None, :])
     with jax.named_scope("weight_gather"):
-        own_weight, normed_send = lax.optimization_barrier((torso_weight, normed_send))
-        lines = [own_weight] + [lax.ppermute(own_weight, "fsdp", z_from(k)) for k in range(1, Z)]
-        rounds = [round_y(line) for line in lines]
-        chunks = lines + [r[k] for k in range(4) for r in rounds]
+        lines = [torso_weight] + [
+            lax.ppermute(torso_weight, "fsdp", z_from(k)) for k in range(1, Z)
+        ]
+        rounds = [round_y(line, k < 2) for k, line in enumerate(lines)]
+        chunks = lines + [rounds[k][j] for j in (0, 2, 1) for k in range(Z)]
 
     with jax.named_scope("rows_swap"):
         normed_got = lax.ppermute(normed_send, "grp", SWAP)
@@ -221,10 +236,17 @@
 
     with jax.named_scope("columns_exchange"):
 
+        lanes = jnp.arange(shard_total, dtype=jnp.int32)
+        onehot = episode_shard[:, :1] == lanes[None, :]
+        local_counts = jnp.sum(onehot.astype(jnp.float32), axis=0).astype(jnp.bfloat16)
+        count_tile = jnp.pad(local_counts[None, :], ((0, 15), (0, block - shard_total)))
+        count_tile, _ = lax.optimization_barrier(
+            (count_tile, tuple(r[k] for r in rounds[:2] for k in range(2)))
+        )
         pieces = pl.pallas_call(
             pieces_kernel,
-            out_shape=jax.ShapeDtypeStruct((2, shard_total, strip, block), jnp.bfloat16),
-            in_specs=[smem] + [pl.BlockSpec(memory_space=pl.ANY)] * 2,
+            out_shape=jax.ShapeDtypeStruct((2, shard_total, strip + 16, block), jnp.bfloat16),
+            in_specs=[smem] + [pl.BlockSpec(memory_space=pl.ANY)] * 2 + [vmem],
             out_specs=vmem,
             scratch_shapes=[
                 pltpu.VMEM((2, strip, side), jnp.bfloat16),
@@ -235,10 +257,12 @@
                 flops=0, transcendentals=0, bytes_accessed=8 * strip * side
             ),
             name="pieces",
-        )(where, normed_own, normed_got)
+        )(where, normed_own, normed_got, count_tile)
         pieces = lax.all_to_all(
-            pieces.reshape(2 * shard_total, strip, block), ("grp", "fsdp"), 0, 0, tiled=True
-        ).reshape(2, shard_total, strip, block)
+            pieces.reshape(2 * shard_total, strip + 16, block), ("grp", "fsdp"), 0, 0, tiled=True
+        ).reshape(2, shard_total, strip + 16, block)
+        counts = jnp.sum(pieces[0, :, strip, :shard_total].astype(jnp.float32), axis=0)
+        pieces = pieces[:, :, :strip]
         after = lax.ppermute(pieces, "tp", x_from(1))
         before = lax.ppermute(pieces, "tp", x_from(3))
         far_a = lax.ppermute(after[0], "tp", x_from(1))
@@ -257,19 +281,6 @@
         )(where, pieces, after, before, far_a, far_b)
 
     with jax.named_scope("counts"):
-        lanes = jnp.arange(shard_total, dtype=jnp.int32)
-        onehot = episode_shard[:, :1] == lanes[None, :]
-        local_counts = jnp.sum(onehot.astype(jnp.float32), axis=0)
-        counts = jnp.sum(
-            lax.all_to_all(
-                jnp.broadcast_to(local_counts[None, :], (shard_total, shard_total)),
-                "fsdp",
-                0,
-                0,
-                tiled=True,
-            ),
-            axis=0,
-        )
         inverse = float(rows_block) / counts
         row_weight = jnp.sum(jnp.where(onehot, inverse[None, :], 0.0), axis=1)
         row_weight = lax.dynamic_slice_in_dim(row_weight, own_rows, half, 0)
@@ -290,15 +301,19 @@
     levels = jnp.sum(jnp.where(online_select, table[None, :, None], 0.0), axis=1)
     reward_rows = lax.dynamic_slice_in_dim(rewards, own_rows, half, 0).astype(jnp.float32)
 
-    normed_own, _ = lax.optimization_barrier((normed_own, pieces))
     part_shape = jax.ShapeDtypeStruct((rows_block, features), jnp.float32)
     keep, send = pl.pallas_call(
         preact_kernel,
         out_shape=(part_shape, part_shape),
-        in_specs=[smem] + [vmem] * (2 + 5 * Z),
+        in_specs=[smem] + [pl.BlockSpec(memory_space=pl.ANY)] * (2 + Y * Z),
         out_specs=(vmem, vmem),
-        scratch_shapes=[pltpu.VMEM((2 * rows_block, features), jnp.float32)],
-        compiler_params=pltpu.CompilerParams(vmem_limit_bytes=16 << 20),
+        scratch_shapes=[
+            pltpu.VMEM((2 * rows_block, features), jnp.float32),
+            pltpu.VMEM((Y * Z, 2 * rows_block, block), jnp.bfloat16),
+            pltpu.VMEM((Y * Z, block, features), jnp.bfloat16),
+            pltpu.SemaphoreType.DMA((3, Y * Z)),
+        ],
+        compiler_params=pltpu.CompilerParams(vmem_limit_bytes=14 << 20),
         cost_estimate=pl.CostEstimate(
             flops=4 * rows_block * side * features,
             transcendentals=0,
@@ -317,6 +332,7 @@
         ),
         axis=1,
     )
+    partial_quant, _ = lax.optimization_barrier((partial_quant, pieces))
     with jax.named_scope("quant_sum"):
         tp_total = lax.axis_size("tp")
         quant = jnp.sum(
@@ -353,11 +369,16 @@
     ).astype(jnp.bfloat16)
 
     with jax.named_scope("grad_gather"):
-        first = round_y(grad_preact)
+        b0 = lax.ppermute(grad_preact, "fsdp", y_from(1))
+        a0 = lax.ppermute(grad_preact, "fsdp", y_from(3))
         pieces_z = tuple(lax.ppermute(grad_preact, "fsdp", z_from(k)) for k in range(1, Z))
-        pieces_z, _ = lax.optimization_barrier((pieces_z, (first[0], first[1], far_a, far_b)))
+        pieces_z, _ = lax.optimization_barrier((pieces_z, (b0, a0)))
         line = jnp.concatenate(pieces_z, 0)
-        rest = round_y(line)
+        f0 = lax.ppermute(a0, "fsdp", y_from(3))
+        a1 = lax.ppermute(line, "fsdp", y_from(3))
+        b1 = lax.ppermute(line, "fsdp", y_from(1))
+        f1 = lax.ppermute(a1[:half], "fsdp", y_from(3))
+        f2 = lax.ppermute(b1[half:], "fsdp", y_from(1))
 
     near = pl.pallas_call(
         near_kernel,
@@ -371,12 +392,12 @@
             bytes_accessed=6 * Z * half * (2 * block + features),
         ),
         name="near",
-    )(columns, grad_preact, line, first[0], rest[0], first[1], rest[1])
+    )(columns, grad_preact, line, b0, b1, a0, a1)
     final_shape = jax.ShapeDtypeStruct((block, features), jnp.float32)
     mine, theirs = pl.pallas_call(
         far_kernel,
         out_shape=(final_shape, final_shape),
-        in_specs=[vmem] * 6,
+        in_specs=[vmem] * 5,
         out_specs=(vmem, vmem),
         compiler_params=pltpu.CompilerParams(vmem_limit_bytes=12 << 20),
         cost_estimate=pl.CostEstimate(
@@ -385,7 +406,7 @@
             bytes_accessed=2 * Z * half * (2 * block + features) + 16 * block * features,
         ),
         name="far",
-    )(columns, near, first[2], first[3], rest[2], rest[3])
+    )(columns, near, f0, f1, f2)
     torso_grad = mine + lax.ppermute(theirs, "grp", SWAP)
     updated = (torso_weight.astype(jnp.float32) - 0.01 * torso_grad).astype(jnp.bfloat16)
     refreshed_weight = lax.all_to_all(updated, "tp", split_axis=0, concat_axis=1, tiled=True)

time: 188 us -> 177 us (0.941)
  starting transfers between devices: 72 us -> 57.1 us
  waiting for transfers between devices: 53.5 us -> 68 us
  local copies, waits for them, and re-layouts: 19.4 us -> 9.56 us
    ppermute x15 -> x14, waiting for transfers between devices: 7.04 us -> 31.6 us  [the longest x3 14.1 us: shards(): lax.ppermute(torso_weight, 'fsdp', z_from(k))]
    ppermute x6 -> x4, waiting for transfers between devices: 20.5 us -> 11 us  [round_y(): above = lax.ppermute(block, 'fsdp', y_from(3))]
    all_to_all x2 -> x1, waiting for transfers between devices: 8.76 us -> 0.01 us  [shards(): lax.all_to_all(pieces.reshape(2 * shard_total, strip + 16, block), ('grp'...]
    ppermute x6 -> x4, starting transfers between devices: 15.7 us -> 7.22 us  [round_y(): below = lax.ppermute(block, 'fsdp', y_from(1))]
    slice x12 -> x3, local copies, waits for them, and re-layouts: 7.04 us -> 1.11 us  [the longest x1 1.08 us: shards(): pieces = pieces[:, :, :strip]]
    all_to_all x1, waiting for transfers between devices: 8.09 us -> 13.6 us  [shards(): lax.all_to_all(jnp.broadcast_to(partial_quant[None], (tp_total,) + partia...]
    all_to_all x2 -> x1, starting transfers between devices: 13.7 us -> 8.98 us  [shards(): lax.all_to_all(pieces.reshape(2 * shard_total, strip + 16, block), ('grp'...]
    unnamed x52 -> x36, local copies, waits for them, and re-layouts: 9.59 us -> 6.33 us
  transfers between devices with their start and end apart: 41 -> 35, of which waited for: 13 -> 14; matrix products, arithmetic and copies ran while one was open for 8% -> 4% of each run, Pallas kernels for 3% -> 6%
where the time goes in v4:
time: 177 us; the launch traced here: 176 us
  waiting for transfers between devices  68 us (38%)
  starting transfers between devices  57.1 us (32%)
  blocking collectives  16.7 us (9%)
  Pallas kernels  16.5 us (9%)
  local copies, waits for them, and re-layouts  9.56 us (5%)
  other arithmetic  5.18 us (3%)
  matrix products  1.85 us (1%)
    all_to_all x1, blocking collectives, shards(): lax.all_to_all(updated, 'tp', split_axis=0, concat_axis=1, tiled=True)  16.7 us
    ppermute x3, waiting for transfers between devices, shards(): lax.ppermute(torso_weight, 'fsdp', z_from(k))  14.1 us
    all_to_all x1, waiting for transfers between devices, shards(): lax.all_to_all(jnp.broadcast_to(partial_quant[None], (tp_total,) + partia...  13.6 us
    ppermute x4, waiting for transfers between devices, round_y(): above = lax.ppermute(block, 'fsdp', y_from(3))  11 us
    all_to_all x1, starting transfers between devices, shards(): lax.all_to_all(jnp.broadcast_to(partial_quant[None], (tp_total,) + partia...  9.1 us
    all_to_all x1, starting transfers between devices, shards(): lax.all_to_all(pieces.reshape(2 * shard_total, strip + 16, block), ('grp'...  8.98 us
    ppermute x4, starting transfers between devices, round_y(): below = lax.ppermute(block, 'fsdp', y_from(1))  7.22 us
    ppermute x3, waiting for transfers between devices, shards(): lax.ppermute(grad_preact, 'fsdp', z_from(k))  7.04 us
  transfers between devices with their start and end apart: 35, of which 14 were waited for; matrix products, arithmetic and copies ran while one was open for 4% of the time, Pallas kernels for 6%

profile of v4, /device:TPU:32, one launch (start us, length us, event | category | flops | bytes accessed | tf_op | source)
XLA Modules:
  0.0 175.8 jit_solution(4052201797650188114)
XLA Ops:
  0.8 2.2 %copy-done.1 = bf16[1,256,8192]{2,1,0:T(8,128)(2,1)S(1)} copy-done((bf16[1,256,8192]{2,1,0:T(8,128)(2,1)S(1)}, bf16[1,256,8192]{2,1,0:T(8,128)(2,1)}, u32[]{:S(2)}) %copy-start.1) | copy-done | bytes 4194328
  3.7 5.2 %norm.1 = (bf16[256,4096]{1,0:T(8,128)(2,1)S(1)}, bf16[256,4096]{1,0:T(8,128)(2,1)}) custom-call(s32[4]{0:T(128)S(1)} %pad_add_fusion.1.where_ref, bf16[256,8192]{1,0:T(8,128)(2,1)S(1)} %bitcast.29, f32[1,8192]{1,0:T(1,128)S(1)} %bitcast.30), custom_call_target="tpu_custom_call" | custom-call | flops 12582912 | bytes 8388608 | tf_op jit(solution)/shard_map/rows_swap/norm/pallas_call | solution.py:201
  8.9 1.8 %collective-permute-start.3 = (bf16[256,512]{1,0:T(8,128)(2,1)S(1)}, bf16[256,512]{1,0:T(8,128)(2,1)S(1)}, u32[]{:S(2)}, u32[]{:S(2)}) collective-permute-start(bf16[256,512]{1,0:T(8,128)(2,1)S(1)} %copy-done.2), channel_id=1, source_target_pairs={{0,24},{8,0},{16,8},{24,16},{32,56},{40,32},{48,40},{56,48},{64,88... | collective-permute-start | bytes 786440 | tf_op jit(solution)/shard_map/weight_gather/ppermute | solution.py:221
  10.7 1.5 collective-permute-start.11
  12.3 2.8 %collective-permute-start.12 = (bf16[256,512]{1,0:T(8,128)(2,1)S(1)}, bf16[256,512]{1,0:T(8,128)(2,1)S(1)}, u32[]{:S(2)}, u32[]{:S(2)}) collective-permute-start(bf16[256,512]{1,0:T(8,128)(2,1)S(1)} %copy-done.2), channel_id=1, source_target_pairs={{0,8},{8,16},{16,24},{24,0},{32,40},{40,48},{48,56},{56,32},{64,72... | collective-permute-start | bytes 786440 | tf_op jit(solution)/shard_map/weight_gather/ppermute | solution.py:221
  15.1 1.6 collective-permute-start.2
  18.1 3.0 %collective-permute-start.1 = (bf16[256,512]{1,0:T(8,128)(2,1)S(1)}, bf16[256,512]{1,0:T(8,128)(2,1)S(1)}, u32[]{:S(2)}, u32[]{:S(2)}) collective-permute-start(bf16[256,512]{1,0:T(8,128)(2,1)S(1)} %copy-done.2), channel_id=1, source_target_pairs={{0,96},{8,104},{16,112},{24,120},{32,0},{40,8},{48,16},{56,24},{64... | collective-permute-start | bytes 786440 | tf_op jit(solution)/shard_map/weight_gather/ppermute | solution.py:32
  21.1 9.1 %collective-permute-done.11.refs_2_ = bf16[256,512]{1,0:T(8,128)(2,1)S(1)} collective-permute-done((bf16[256,512]{1,0:T(8,128)(2,1)S(1)}, bf16[256,512]{1,0:T(8,128)(2,1)S(1)}, u32[]{:S(2)}, u32[]{:S(2)}) %collective-permute-start.11) | collective-permute-done | bytes 262176 | tf_op jit(solution)/shard_map/weight_gather/ppermute | solution.py:221
  30.2 1.6 collective-permute-start.5
  31.8 3.6 %collective-permute-done.12.refs_3_ = bf16[256,512]{1,0:T(8,128)(2,1)S(1)} collective-permute-done((bf16[256,512]{1,0:T(8,128)(2,1)S(1)}, bf16[256,512]{1,0:T(8,128)(2,1)S(1)}, u32[]{:S(2)}, u32[]{:S(2)}) %collective-permute-start.12) | collective-permute-done | bytes 262176 | tf_op jit(solution)/shard_map/weight_gather/ppermute | solution.py:221
  35.3 3.0 %collective-permute-start.4 = (bf16[256,512]{1,0:T(8,128)(2,1)S(1)}, bf16[256,512]{1,0:T(8,128)(2,1)}, u32[]{:S(2)}, u32[]{:S(2)}) collective-permute-start(bf16[256,512]{1,0:T(8,128)(2,1)S(1)} %collective-permute-done.3.refs_1_), channel_id=1, source_target_pairs={{0,96},{8,104},{16,112},{24,120},{32,0},{40,8},{48,16},{56,24},{64... | collective-permute-start | bytes 786440 | tf_op jit(solution)/shard_map/weight_gather/ppermute | solution.py:32
  40.9 1.6 collective-permute-start.15
  43.5 1.6 collective-permute-done.4.refs_5_
  48.2 2.5 %pieces.1 = bf16[2,16,48,256]{3,2,1,0:T(8,128)(2,1)} custom-call(s32[4]{0:T(128)S(1)} %pad_add_fusion.1.where_ref, bf16[256,4096]{1,0:T(8,128)(2,1)S(1)} %get-tuple-element.14.own_ref, bf16[256,4096]{1,0:T(8,128)(2,1)} %collective-permute-done.got_ref, bf16[16,256]{1,0:T(8,128)(2,1)S(1)} %pad.4.count_ref), custom_call_target="tpu_custom_call" | custom-call | bytes 1048576 | tf_op jit(solution)/shard_map/columns_exchange/pieces/pallas_call | solution.py:246
  50.7 9.0 %all-to-all-start = ((bf16[32,48,256]{2,1,0:T(8,128)(2,1)}), bf16[32,48,256]{2,1,0:T(8,128)(2,1)}, u32[]{:S(2)}, u32[]{:S(2)}) async-start(bf16[32,48,256]{2,1,0:T(8,128)(2,1)} %bitcast.8), calls=%async_computation | async-start | bytes 1572864 | tf_op jit(solution)/shard_map/columns_exchange/all_to_all | solution.py:261
  59.7 1.5 collective-permute-start.20
  62.7 1.8 %collective-permute-start.17 = (bf16[256,512]{1,0:T(8,128)(2,1)}, bf16[256,512]{1,0:T(8,128)(2,1)}, u32[]{:S(2)}, u32[]{:S(2)}) collective-permute-start(bf16[256,512]{1,0:T(8,128)(2,1)} %collective-permute-done.13.refs_6_), channel_id=1, source_target_pairs={{0,96},{8,104},{16,112},{24,120},{32,0},{40,8},{48,16},{56,24},{64... | collective-permute-start | bytes 786440 | tf_op jit(solution)/shard_map/weight_gather/ppermute | solution.py:36
  65.8 11.0 %collective-permute-done.20.refs_15_ = bf16[256,512]{1,0:T(8,128)(2,1)} collective-permute-done((bf16[256,512]{1,0:T(8,128)(2,1)S(1)}, bf16[256,512]{1,0:T(8,128)(2,1)}, u32[]{:S(2)}, u32[]{:S(2)}) %collective-permute-start.20) | collective-permute-done | bytes 262176 | tf_op jit(solution)/shard_map/weight_gather/ppermute | solution.py:33
  76.8 6.4 %collective-permute-done.16.refs_9_ = bf16[256,512]{1,0:T(8,128)(2,1)} collective-permute-done((bf16[256,512]{1,0:T(8,128)(2,1)}, bf16[256,512]{1,0:T(8,128)(2,1)}, u32[]{:S(2)}, u32[]{:S(2)}) %collective-permute-start.16) | collective-permute-done | bytes 262176 | tf_op jit(solution)/shard_map/weight_gather/ppermute | solution.py:35
  85.2 5.0 %preact.1 = (f32[256,512]{1,0:T(8,128)S(1)}, f32[256,512]{1,0:T(8,128)S(1)}) custom-call(s32[4]{0:T(128)S(1)} %pad_add_fusion.1.where_ref, bf16[256,4096]{1,0:T(8,128)(2,1)S(1)} %get-tuple-element.14.own_ref, bf16[256,4096]{1,0:T(8,128)(2,1)} %collective-permute-done.got_ref, bf16[256,512]{1,0:T(8,128)(2,1)S(1)} %copy-done.2, ...), custom_call_target="tpu_custom_call" | custom-call | flops 2147483648 | bytes 9437184 | tf_op jit(solution)/shard_map/preact/pallas_call | solution.py:305
  94.1 2.8 %collective-permute-start.6 = (bf16[2,16,32,256]{3,2,1,0:T(8,128)(2,1)S(1)}, bf16[2,16,32,256]{3,2,1,0:T(8,128)(2,1)S(1)}, u32[]{:S(2)}, u32[]{:S(2)}) collective-permute-start(bf16[2,16,32,256]{3,2,1,0:T(8,128)(2,1)S(1)} %slice.54.own_ref), channel_id=1, source_target_pairs={{0,6},{1,7},{2,0},{3,1},{4,2},{5,3},{6,4},{7,5},{8,14},{9,15},{10,... | collective-permute-start | bytes 1572872 | tf_op jit(solution)/shard_map/columns_exchange/ppermute | solution.py:266
  97.6 9.1 %all-to-all-start.1 = ((f32[8,32,256]{2,1,0:T(8,128)}), f32[8,32,256]{2,1,0:T(8,128)S(1)}, u32[]{:S(2)}, u32[]{:S(2)}) async-start(f32[8,32,256]{2,1,0:T(8,128)} %broadcast_in_dim.80), calls=%async_computation.1 | async-start | bytes 524288 | tf_op jit(solution)/shard_map/quant_sum/all_to_all | solution.py:339
  107.7 13.6 %all-to-all-done.1 = f32[8,32,256]{2,1,0:T(8,128)S(1)} async-done(((f32[8,32,256]{2,1,0:T(8,128)}), f32[8,32,256]{2,1,0:T(8,128)S(1)}, u32[]{:S(2)}, u32[]{:S(2)}) %all-to-all-start.1) | async-done | bytes 262176 | tf_op jit(solution)/shard_map/quant_sum/all_to_all | solution.py:339
  122.2 2.1 %collective-permute-start.23 = (bf16[128,512]{1,0:T(8,128)(2,1)S(1)}, bf16[128,512]{1,0:T(8,128)(2,1)S(1)}, u32[]{:S(2)}, u32[]{:S(2)}) collective-permute-start(bf16[128,512]{1,0:T(8,128)(2,1)S(1)} %fusion.5.own_ref), channel_id=1, source_target_pairs={{0,16},{8,24},{16,0},{24,8},{32,48},{40,56},{48,32},{56,40},{64,80... | collective-permute-start | bytes 393224 | tf_op jit(solution)/shard_map/grad_gather/ppermute | solution.py:374
  124.3 1.5 collective-permute-start.25
  126.3 7.0 %collective-permute-done.22 = bf16[128,512]{1,0:T(8,128)(2,1)S(1)} collective-permute-done((bf16[128,512]{1,0:T(8,128)(2,1)S(1)}, bf16[128,512]{1,0:T(8,128)(2,1)S(1)}, u32[]{:S(2)}, u32[]{:S(2)}) %collective-permute-start.22) | collective-permute-done | bytes 131104 | tf_op jit(solution)/shard_map/grad_gather/ppermute | solution.py:374
  137.9 6.2 %collective-permute-done.27.b1_ref = bf16[384,512]{1,0:T(8,128)(2,1)S(1)} collective-permute-done((bf16[384,512]{1,0:T(8,128)(2,1)S(1)}, bf16[384,512]{1,0:T(8,128)(2,1)S(1)}, u32[]{:S(2)}, u32[]{:S(2)}) %collective-permute-start.27) | collective-permute-done | bytes 393248 | tf_op jit(solution)/shard_map/grad_gather/ppermute | solution.py:379
  144.2 2.6 %collective-permute-start.31 = (bf16[256,512]{1,0:T(8,128)(2,1)S(1)}, bf16[256,512]{1,0:T(8,128)(2,1)S(1)}, u32[]{:S(2)}, u32[]{:S(2)}) collective-permute-start(bf16[256,512]{1,0:T(8,128)(2,1)S(1)} %slice.64), channel_id=1, source_target_pairs={{0,96},{8,104},{16,112},{24,120},{32,0},{40,8},{48,16},{56,24},{64... | collective-permute-start | bytes 786440 | tf_op jit(solution)/shard_map/grad_gather/ppermute | solution.py:381
  147.4 2.4 %columns.1.cols_ref = bf16[512,2048]{1,0:T(8,128)(2,1)S(1)} custom-call(s32[4]{0:T(128)S(1)} %pad_add_fusion.1.where_ref, bf16[2,16,32,256]{3,2,1,0:T(8,128)(2,1)S(1)} %slice.54.own_ref, bf16[2,16,32,256]{3,2,1,0:T(8,128)(2,1)S(1)} %collective-permute-done.6.after_ref, bf16[2,16,32,256]{3,2,1,0:T(8,128)(2,1)S(1)} %collective-permute-done.7.before_ref, ...), custom_call_target="tpu_custom_call" | custom-call | bytes 4194304 | tf_op jit(solution)/shard_map/columns_exchange/columns/pallas_call | solution.py:270
  150.8 2.9 %collective-permute-done.29.f0_ref = bf16[128,512]{1,0:T(8,128)(2,1)S(1)} collective-permute-done((bf16[128,512]{1,0:T(8,128)(2,1)S(1)}, bf16[128,512]{1,0:T(8,128)(2,1)S(1)}, u32[]{:S(2)}, u32[]{:S(2)}) %collective-permute-start.29) | collective-permute-done | bytes 131104 | tf_op jit(solution)/shard_map/grad_gather/ppermute | solution.py:377
  155.6 1.9 %collective-permute-done.32 = f32[256,512]{1,0:T(8,128)S(1)} collective-permute-done((f32[256,512]{1,0:T(8,128)S(1)}, f32[256,512]{1,0:T(8,128)S(1)}, u32[]{:S(2)}, u32[]{:S(2)}) %collective-permute-start.32) | collective-permute-done | bytes 524320 | tf_op jit(solution)/shard_map/ppermute | solution.py:410
  158.5 16.7 %all_to_all.29 = bf16[8,32,512]{2,1,0:T(8,128)(2,1)S(1)} all-to-all(bf16[8,32,512]{2,1,0:T(8,128)(2,1)S(1)} %bitcast.32), channel_id=1, replica_groups=mesh['grp'=2,'fsdp'=16,'tp'=8] {'tp'}, dimensions={0} | all-to-all | bytes 524288 | tf_op jit(solution)/shard_map/all_to_all | solution.py:412
  (116 shorter events, 30.3 us)
Async XLA Ops:
  8.9 38.2 %collective-permute-start = (bf16[256,4096]{1,0:T(8,128)(2,1)}, bf16[256,4096]{1,0:T(8,128)(2,1)}, u32[]{:S(2)}, u32[]{:S(2)}) collective-permute-start(bf16[256,4096]{1,0:T(8,128)(2,1)} %get-tuple-element.15), channel_id=1, source_target_pairs={{0,128},{128,0},{1,129},{129,1},{2,130},{130,2},{3,131},{131,3},{4... | collective-permute-start | bytes 6291464 | tf_op jit(solution)/shard_map/rows_swap/ppermute | solution.py:227
  8.9 9.2 %collective-permute-start.3 = (bf16[256,512]{1,0:T(8,128)(2,1)S(1)}, bf16[256,512]{1,0:T(8,128)(2,1)S(1)}, u32[]{:S(2)}, u32[]{:S(2)}) collective-permute-start(bf16[256,512]{1,0:T(8,128)(2,1)S(1)} %copy-done.2), channel_id=1, source_target_pairs={{0,24},{8,0},{16,8},{24,16},{32,56},{40,32},{48,40},{56,48},{64,88... | collective-permute-start | bytes 786440 | tf_op jit(solution)/shard_map/weight_gather/ppermute | solution.py:221
  10.7 19.4 %collective-permute-start.11 = (bf16[256,512]{1,0:T(8,128)(2,1)S(1)}, bf16[256,512]{1,0:T(8,128)(2,1)S(1)}, u32[]{:S(2)}, u32[]{:S(2)}) collective-permute-start(bf16[256,512]{1,0:T(8,128)(2,1)S(1)} %copy-done.2), channel_id=1, source_target_pairs={{0,16},{8,24},{16,0},{24,8},{32,48},{40,56},{48,32},{56,40},{64,80... | collective-permute-start | bytes 786440 | tf_op jit(solution)/shard_map/weight_gather/ppermute | solution.py:221
  12.3 23.1 %collective-permute-start.12 = (bf16[256,512]{1,0:T(8,128)(2,1)S(1)}, bf16[256,512]{1,0:T(8,128)(2,1)S(1)}, u32[]{:S(2)}, u32[]{:S(2)}) collective-permute-start(bf16[256,512]{1,0:T(8,128)(2,1)S(1)} %copy-done.2), channel_id=1, source_target_pairs={{0,8},{8,16},{16,24},{24,0},{32,40},{40,48},{48,56},{56,32},{64,72... | collective-permute-start | bytes 786440 | tf_op jit(solution)/shard_map/weight_gather/ppermute | solution.py:221
  15.1 23.3 %collective-permute-start.2 = (bf16[256,512]{1,0:T(8,128)(2,1)S(1)}, bf16[256,512]{1,0:T(8,128)(2,1)S(1)}, u32[]{:S(2)}, u32[]{:S(2)}) collective-permute-start(bf16[256,512]{1,0:T(8,128)(2,1)S(1)} %copy-done.2), channel_id=1, source_target_pairs={{0,32},{8,40},{16,48},{24,56},{32,64},{40,72},{48,80},{56,88},{64,... | collective-permute-start | bytes 786440 | tf_op jit(solution)/shard_map/weight_gather/ppermute | solution.py:33
  18.1 21.0 %collective-permute-start.1 = (bf16[256,512]{1,0:T(8,128)(2,1)S(1)}, bf16[256,512]{1,0:T(8,128)(2,1)S(1)}, u32[]{:S(2)}, u32[]{:S(2)}) collective-permute-start(bf16[256,512]{1,0:T(8,128)(2,1)S(1)} %copy-done.2), channel_id=1, source_target_pairs={{0,96},{8,104},{16,112},{24,120},{32,0},{40,8},{48,16},{56,24},{64... | collective-permute-start | bytes 786440 | tf_op jit(solution)/shard_map/weight_gather/ppermute | solution.py:32
  30.2 10.1 %collective-permute-start.5 = (bf16[256,512]{1,0:T(8,128)(2,1)S(1)}, bf16[256,512]{1,0:T(8,128)(2,1)S(1)}, u32[]{:S(2)}, u32[]{:S(2)}) collective-permute-start(bf16[256,512]{1,0:T(8,128)(2,1)S(1)} %collective-permute-done.3.refs_1_), channel_id=1, source_target_pairs={{0,32},{8,40},{16,48},{24,56},{32,64},{40,72},{48,80},{56,88},{64,... | collective-permute-start | bytes 786440 | tf_op jit(solution)/shard_map/weight_gather/ppermute | solution.py:33
  35.3 9.8 %collective-permute-start.4 = (bf16[256,512]{1,0:T(8,128)(2,1)S(1)}, bf16[256,512]{1,0:T(8,128)(2,1)}, u32[]{:S(2)}, u32[]{:S(2)}) collective-permute-start(bf16[256,512]{1,0:T(8,128)(2,1)S(1)} %collective-permute-done.3.refs_1_), channel_id=1, source_target_pairs={{0,96},{8,104},{16,112},{24,120},{32,0},{40,8},{48,16},{56,24},{64... | collective-permute-start | bytes 786440 | tf_op jit(solution)/shard_map/weight_gather/ppermute | solution.py:32
  38.3 22.9 %collective-permute-start.13 = (bf16[256,512]{1,0:T(8,128)(2,1)S(1)}, bf16[256,512]{1,0:T(8,128)(2,1)}, u32[]{:S(2)}, u32[]{:S(2)}) collective-permute-start(bf16[256,512]{1,0:T(8,128)(2,1)S(1)} %collective-permute-done.11.refs_2_), channel_id=1, source_target_pairs={{0,96},{8,104},{16,112},{24,120},{32,0},{40,8},{48,16},{56,24},{64... | collective-permute-start | bytes 786440 | tf_op jit(solution)/shard_map/weight_gather/ppermute | solution.py:32
  39.8 23.0 %collective-permute-start.14 = (bf16[256,512]{1,0:T(8,128)(2,1)S(1)}, bf16[256,512]{1,0:T(8,128)(2,1)}, u32[]{:S(2)}, u32[]{:S(2)}) collective-permute-start(bf16[256,512]{1,0:T(8,128)(2,1)S(1)} %collective-permute-done.12.refs_3_), channel_id=1, source_target_pairs={{0,96},{8,104},{16,112},{24,120},{32,0},{40,8},{48,16},{56,24},{64... | collective-permute-start | bytes 786440 | tf_op jit(solution)/shard_map/weight_gather/ppermute | solution.py:32
  40.9 23.6 %collective-permute-start.15 = (bf16[256,512]{1,0:T(8,128)(2,1)S(1)}, bf16[256,512]{1,0:T(8,128)(2,1)}, u32[]{:S(2)}, u32[]{:S(2)}) collective-permute-start(bf16[256,512]{1,0:T(8,128)(2,1)S(1)} %collective-permute-done.2.refs_12_), channel_id=1, source_target_pairs={{0,32},{8,40},{16,48},{24,56},{32,64},{40,72},{48,80},{56,88},{64,... | collective-permute-start | bytes 786440 | tf_op jit(solution)/shard_map/weight_gather/ppermute | solution.py:35
  45.1 14.7 %collective-permute-start.10 = (s32[33,128]{1,0:T(8,128)S(1)}, s32[33,128]{1,0:T(8,128)S(1)}, u32[]{:S(2)}, u32[]{:S(2)}) collective-permute-start(s32[33,128]{1,0:T(8,128)S(1)} %fusion.11), channel_id=1, source_target_pairs={{0,128},{128,0},{1,129},{129,1},{2,130},{130,2},{3,131},{131,3},{4... | collective-permute-start | bytes 50696 | tf_op jit(solution)/shard_map/rows_swap/ppermute | solution.py:230
  47.0 18.8 %collective-permute-start.19 = (bf16[256,512]{1,0:T(8,128)(2,1)S(1)}, bf16[256,512]{1,0:T(8,128)(2,1)}, u32[]{:S(2)}, u32[]{:S(2)}) collective-permute-start(bf16[256,512]{1,0:T(8,128)(2,1)S(1)} %collective-permute-done.11.refs_2_), channel_id=1, source_target_pairs={{0,32},{8,40},{16,48},{24,56},{32,64},{40,72},{48,80},{56,88},{64,... | collective-permute-start | bytes 786440 | tf_op jit(solution)/shard_map/weight_gather/ppermute | solution.py:33
  50.7 42.2 %all-to-all-start = ((bf16[32,48,256]{2,1,0:T(8,128)(2,1)}), bf16[32,48,256]{2,1,0:T(8,128)(2,1)}, u32[]{:S(2)}, u32[]{:S(2)}) async-start(bf16[32,48,256]{2,1,0:T(8,128)(2,1)} %bitcast.8), calls=%async_computation | async-start | bytes 1572864 | tf_op jit(solution)/shard_map/columns_exchange/all_to_all | solution.py:261
  59.7 17.1 %collective-permute-start.20 = (bf16[256,512]{1,0:T(8,128)(2,1)S(1)}, bf16[256,512]{1,0:T(8,128)(2,1)}, u32[]{:S(2)}, u32[]{:S(2)}) collective-permute-start(bf16[256,512]{1,0:T(8,128)(2,1)S(1)} %collective-permute-done.12.refs_3_), channel_id=1, source_target_pairs={{0,32},{8,40},{16,48},{24,56},{32,64},{40,72},{48,80},{56,88},{64,... | collective-permute-start | bytes 786440 | tf_op jit(solution)/shard_map/weight_gather/ppermute | solution.py:33
  61.3 22.0 %collective-permute-start.16 = (bf16[256,512]{1,0:T(8,128)(2,1)}, bf16[256,512]{1,0:T(8,128)(2,1)}, u32[]{:S(2)}, u32[]{:S(2)}) collective-permute-start(bf16[256,512]{1,0:T(8,128)(2,1)} %copy-done.5), channel_id=1, source_target_pairs={{0,32},{8,40},{16,48},{24,56},{32,64},{40,72},{48,80},{56,88},{64,... | collective-permute-start | bytes 786440 | tf_op jit(solution)/shard_map/weight_gather/ppermute | solution.py:35
  62.7 20.5 %collective-permute-start.17 = (bf16[256,512]{1,0:T(8,128)(2,1)}, bf16[256,512]{1,0:T(8,128)(2,1)}, u32[]{:S(2)}, u32[]{:S(2)}) collective-permute-start(bf16[256,512]{1,0:T(8,128)(2,1)} %collective-permute-done.13.refs_6_), channel_id=1, source_target_pairs={{0,96},{8,104},{16,112},{24,120},{32,0},{40,8},{48,16},{56,24},{64... | collective-permute-start | bytes 786440 | tf_op jit(solution)/shard_map/weight_gather/ppermute | solution.py:36
  64.5 18.7 %collective-permute-start.18 = (bf16[256,512]{1,0:T(8,128)(2,1)}, bf16[256,512]{1,0:T(8,128)(2,1)}, u32[]{:S(2)}, u32[]{:S(2)}) collective-permute-start(bf16[256,512]{1,0:T(8,128)(2,1)} %collective-permute-done.14.refs_7_), channel_id=1, source_target_pairs={{0,96},{8,104},{16,112},{24,120},{32,0},{40,8},{48,16},{56,24},{64... | collective-permute-start | bytes 786440 | tf_op jit(solution)/shard_map/weight_gather/ppermute | solution.py:36
  94.1 27.3 %collective-permute-start.6 = (bf16[2,16,32,256]{3,2,1,0:T(8,128)(2,1)S(1)}, bf16[2,16,32,256]{3,2,1,0:T(8,128)(2,1)S(1)}, u32[]{:S(2)}, u32[]{:S(2)}) collective-permute-start(bf16[2,16,32,256]{3,2,1,0:T(8,128)(2,1)S(1)} %slice.54.own_ref), channel_id=1, source_target_pairs={{0,6},{1,7},{2,0},{3,1},{4,2},{5,3},{6,4},{7,5},{8,14},{9,15},{10,... | collective-permute-start | bytes 1572872 | tf_op jit(solution)/shard_map/columns_exchange/ppermute | solution.py:266
  96.9 24.4 %collective-permute-start.7 = (bf16[2,16,32,256]{3,2,1,0:T(8,128)(2,1)S(1)}, bf16[2,16,32,256]{3,2,1,0:T(8,128)(2,1)S(1)}, u32[]{:S(2)}, u32[]{:S(2)}) collective-permute-start(bf16[2,16,32,256]{3,2,1,0:T(8,128)(2,1)S(1)} %slice.54.own_ref), channel_id=1, source_target_pairs={{0,2},{1,3},{2,4},{3,5},{4,6},{5,7},{6,0},{7,1},{8,10},{9,11},{10,... | collective-permute-start | bytes 1572872 | tf_op jit(solution)/shard_map/columns_exchange/ppermute | solution.py:267
  97.6 23.7 %all-to-all-start.1 = ((f32[8,32,256]{2,1,0:T(8,128)}), f32[8,32,256]{2,1,0:T(8,128)S(1)}, u32[]{:S(2)}, u32[]{:S(2)}) async-start(f32[8,32,256]{2,1,0:T(8,128)} %broadcast_in_dim.80), calls=%async_computation.1 | async-start | bytes 524288 | tf_op jit(solution)/shard_map/quant_sum/all_to_all | solution.py:339
  122.1 11.2 %collective-permute-start.22 = (bf16[128,512]{1,0:T(8,128)(2,1)S(1)}, bf16[128,512]{1,0:T(8,128)(2,1)S(1)}, u32[]{:S(2)}, u32[]{:S(2)}) collective-permute-start(bf16[128,512]{1,0:T(8,128)(2,1)S(1)} %fusion.5.own_ref), channel_id=1, source_target_pairs={{0,24},{8,0},{16,8},{24,16},{32,56},{40,32},{48,40},{56,48},{64,88... | collective-permute-start | bytes 393224 | tf_op jit(solution)/shard_map/grad_gather/ppermute | solution.py:374
  122.2 11.1 %collective-permute-start.23 = (bf16[128,512]{1,0:T(8,128)(2,1)S(1)}, bf16[128,512]{1,0:T(8,128)(2,1)S(1)}, u32[]{:S(2)}, u32[]{:S(2)}) collective-permute-start(bf16[128,512]{1,0:T(8,128)(2,1)S(1)} %fusion.5.own_ref), channel_id=1, source_target_pairs={{0,16},{8,24},{16,0},{24,8},{32,48},{40,56},{48,32},{56,40},{64,80... | collective-permute-start | bytes 393224 | tf_op jit(solution)/shard_map/grad_gather/ppermute | solution.py:374
  124.3 9.1 %collective-permute-start.24 = (bf16[128,512]{1,0:T(8,128)(2,1)S(1)}, bf16[128,512]{1,0:T(8,128)(2,1)S(1)}, u32[]{:S(2)}, u32[]{:S(2)}) collective-permute-start(bf16[128,512]{1,0:T(8,128)(2,1)S(1)} %fusion.5.own_ref), channel_id=1, source_target_pairs={{0,8},{8,16},{16,24},{24,0},{32,40},{40,48},{48,56},{56,32},{64,72... | collective-permute-start | bytes 393224 | tf_op jit(solution)/shard_map/grad_gather/ppermute | solution.py:374
  124.3 9.1 %collective-permute-start.25 = (bf16[128,512]{1,0:T(8,128)(2,1)S(1)}, bf16[128,512]{1,0:T(8,128)(2,1)S(1)}, u32[]{:S(2)}, u32[]{:S(2)}) collective-permute-start(bf16[128,512]{1,0:T(8,128)(2,1)S(1)} %fusion.5.own_ref), channel_id=1, source_target_pairs={{0,96},{8,104},{16,112},{24,120},{32,0},{40,8},{48,16},{56,24},{64... | collective-permute-start | bytes 393224 | tf_op jit(solution)/shard_map/grad_gather/ppermute | solution.py:372
  125.7 7.6 %collective-permute-start.26 = (bf16[128,512]{1,0:T(8,128)(2,1)S(1)}, bf16[128,512]{1,0:T(8,128)(2,1)S(1)}, u32[]{:S(2)}, u32[]{:S(2)}) collective-permute-start(bf16[128,512]{1,0:T(8,128)(2,1)S(1)} %fusion.5.own_ref), channel_id=1, source_target_pairs={{0,32},{8,40},{16,48},{24,56},{32,64},{40,72},{48,80},{56,88},{64,... | collective-permute-start | bytes 393224 | tf_op jit(solution)/shard_map/grad_gather/ppermute | solution.py:373
  133.4 10.8 %collective-permute-start.27 = (bf16[384,512]{1,0:T(8,128)(2,1)S(1)}, bf16[384,512]{1,0:T(8,128)(2,1)S(1)}, u32[]{:S(2)}, u32[]{:S(2)}) collective-permute-start(bf16[384,512]{1,0:T(8,128)(2,1)S(1)} %constant_dynamic-update-slice_fusion.line_ref), channel_id=1, source_target_pairs={{0,96},{8,104},{16,112},{24,120},{32,0},{40,8},{48,16},{56,24},{64... | collective-permute-start | bytes 1179656 | tf_op jit(solution)/shard_map/grad_gather/ppermute | solution.py:379
  134.4 13.0 %collective-permute-start.8 = (bf16[16,32,256]{2,1,0:T(8,128)(2,1)S(1)}, bf16[16,32,256]{2,1,0:T(8,128)(2,1)S(1)}, u32[]{:S(2)}, u32[]{:S(2)}) collective-permute-start(bf16[16,32,256]{2,1,0:T(8,128)(2,1)S(1)} %slice_bitcast_fusion.1), channel_id=1, source_target_pairs={{0,6},{1,7},{2,0},{3,1},{4,2},{5,3},{6,4},{7,5},{8,14},{9,15},{10,... | collective-permute-start | bytes 786440 | tf_op jit(solution)/shard_map/columns_exchange/ppermute | solution.py:268
  135.6 11.7 %collective-permute-start.28 = (bf16[384,512]{1,0:T(8,128)(2,1)S(1)}, bf16[384,512]{1,0:T(8,128)(2,1)S(1)}, u32[]{:S(2)}, u32[]{:S(2)}) collective-permute-start(bf16[384,512]{1,0:T(8,128)(2,1)S(1)} %constant_dynamic-update-slice_fusion.line_ref), channel_id=1, source_target_pairs={{0,32},{8,40},{16,48},{24,56},{32,64},{40,72},{48,80},{56,88},{64,... | collective-permute-start | bytes 1179656 | tf_op jit(solution)/shard_map/grad_gather/ppermute | solution.py:378
  136.7 10.7 %collective-permute-start.9 = (bf16[16,32,256]{2,1,0:T(8,128)(2,1)S(1)}, bf16[16,32,256]{2,1,0:T(8,128)(2,1)S(1)}, u32[]{:S(2)}, u32[]{:S(2)}) collective-permute-start(bf16[16,32,256]{2,1,0:T(8,128)(2,1)S(1)} %slice_bitcast_fusion), channel_id=1, source_target_pairs={{0,2},{1,3},{2,4},{3,5},{4,6},{5,7},{6,0},{7,1},{8,10},{9,11},{10,... | collective-permute-start | bytes 786440 | tf_op jit(solution)/shard_map/columns_exchange/ppermute | solution.py:269
  144.2 10.9 %collective-permute-start.31 = (bf16[256,512]{1,0:T(8,128)(2,1)S(1)}, bf16[256,512]{1,0:T(8,128)(2,1)S(1)}, u32[]{:S(2)}, u32[]{:S(2)}) collective-permute-start(bf16[256,512]{1,0:T(8,128)(2,1)S(1)} %slice.64), channel_id=1, source_target_pairs={{0,96},{8,104},{16,112},{24,120},{32,0},{40,8},{48,16},{56,24},{64... | collective-permute-start | bytes 786440 | tf_op jit(solution)/shard_map/grad_gather/ppermute | solution.py:381
  147.3 7.8 %collective-permute-start.30 = (bf16[128,512]{1,0:T(8,128)(2,1)S(1)}, bf16[128,512]{1,0:T(8,128)(2,1)S(1)}, u32[]{:S(2)}, u32[]{:S(2)}) collective-permute-start(bf16[128,512]{1,0:T(8,128)(2,1)S(1)} %slice.63), channel_id=1, source_target_pairs={{0,32},{8,40},{16,48},{24,56},{32,64},{40,72},{48,80},{56,88},{64,... | collective-permute-start | bytes 393224 | tf_op jit(solution)/shard_map/grad_gather/ppermute | solution.py:380
  (20 other events, 279.7 us)

commit v5 on v4

--- a/solution.py
+++ b/solution.py
@@ -195,8 +195,15 @@
     smem = pl.BlockSpec(memory_space=pltpu.SMEM)
     vmem = pl.BlockSpec(memory_space=pltpu.VMEM)
 
+    with jax.named_scope("weight_gather"):
+        lines = [torso_weight] + [
+            lax.ppermute(torso_weight, "fsdp", z_from(k)) for k in range(1, Z)
+        ]
+        rounds = [round_y(line, k < 2) for k, line in enumerate(lines)]
+        chunks = lines + [rounds[k][j] for j in (0, 2, 1) for k in range(Z)]
+
     with jax.named_scope("rows_swap"):
-        values = frames[0]
+        values, _ = lax.optimization_barrier((frames[0], (lines[1:], rounds[0][:2], rounds[1][:2])))
         tile = 32
         normed_own, normed_send = pl.pallas_call(
             norm_kernel,
@@ -216,13 +223,6 @@
             ),
             name="norm",
         )(where, values, norm_gain[None, :])
-    with jax.named_scope("weight_gather"):
-        lines = [torso_weight] + [
-            lax.ppermute(torso_weight, "fsdp", z_from(k)) for k in range(1, Z)
-        ]
-        rounds = [round_y(line, k < 2) for k, line in enumerate(lines)]
-        chunks = lines + [rounds[k][j] for j in (0, 2, 1) for k in range(Z)]
-
     with jax.named_scope("rows_swap"):
         normed_got = lax.ppermute(normed_send, "grp", SWAP)
         ints = jnp.concatenate([fractions[0].T, actions[0][None, :]], 0)
@@ -241,7 +241,7 @@
         local_counts = jnp.sum(onehot.astype(jnp.float32), axis=0).astype(jnp.bfloat16)
         count_tile = jnp.pad(local_counts[None, :], ((0, 15), (0, block - shard_total)))
         count_tile, _ = lax.optimization_barrier(
-            (count_tile, tuple(r[k] for r in rounds[:2] for k in range(2)))
+            (count_tile, tuple(r[k] for r in rounds for k in range(2)))
         )
         pieces = pl.pallas_call(
             pieces_kernel,
@@ -263,22 +263,6 @@
         ).reshape(2, shard_total, strip + 16, block)
         counts = jnp.sum(pieces[0, :, strip, :shard_total].astype(jnp.float32), axis=0)
         pieces = pieces[:, :, :strip]
-        after = lax.ppermute(pieces, "tp", x_from(1))
-        before = lax.ppermute(pieces, "tp", x_from(3))
-        far_a = lax.ppermute(after[0], "tp", x_from(1))
-        far_b = lax.ppermute(before[1], "tp", x_from(3))
-        columns = pl.pallas_call(
-            columns_kernel,
-            out_shape=jax.ShapeDtypeStruct((2 * block, shard_total * half), jnp.bfloat16),
-            in_specs=[smem] + [vmem] * 5,
-            out_specs=vmem,
-            scratch_shapes=[pltpu.VMEM((half, 2 * block), jnp.bfloat16)],
-            compiler_params=pltpu.CompilerParams(vmem_limit_bytes=8 << 20),
-            cost_estimate=pl.CostEstimate(
-                flops=0, transcendentals=0, bytes_accessed=8 * shard_total * half * block
-            ),
-            name="columns",
-        )(where, pieces, after, before, far_a, far_b)
 
     with jax.named_scope("counts"):
         inverse = float(rows_block) / counts
@@ -332,20 +316,12 @@
         ),
         axis=1,
     )
-    partial_quant, _ = lax.optimization_barrier((partial_quant, pieces))
     with jax.named_scope("quant_sum"):
-        tp_total = lax.axis_size("tp")
-        quant = jnp.sum(
-            lax.all_to_all(
-                jnp.broadcast_to(partial_quant[None], (tp_total,) + partial_quant.shape),
-                "tp",
-                0,
-                0,
-                tiled=True,
-            ),
-            axis=0,
-        )
-    quant, _ = lax.optimization_barrier((quant, (after, before)))
+        quant = partial_quant
+        for flip in (2, 4):
+            quant = quant + lax.ppermute(quant, "tp", [(t, t ^ flip) for t in range(2 * X)])
+        quant = quant + lax.ppermute(quant, "tp", [(t, t ^ 1) for t in range(2 * X)])
+    quant, pieces = lax.optimization_barrier((quant, pieces))
     target_quant = quant[:, :half]
     online_quant = quant[:, half:]
     target_value = reward_rows[None, :] + 0.99 * target_quant
@@ -368,11 +344,30 @@
         * (1.0 + online_preact * (1.0 - gate_value))
     ).astype(jnp.bfloat16)
 
+    grad_preact, pieces = lax.optimization_barrier((grad_preact, pieces))
+    with jax.named_scope("columns_round_x"):
+        after = lax.ppermute(pieces, "tp", x_from(1))
+        before = lax.ppermute(pieces, "tp", x_from(3))
+        far_a = lax.ppermute(after[0], "tp", x_from(1))
+        far_b = lax.ppermute(before[1], "tp", x_from(3))
+        columns = pl.pallas_call(
+            columns_kernel,
+            out_shape=jax.ShapeDtypeStruct((2 * block, shard_total * half), jnp.bfloat16),
+            in_specs=[smem] + [vmem] * 5,
+            out_specs=vmem,
+            scratch_shapes=[pltpu.VMEM((half, 2 * block), jnp.bfloat16)],
+            compiler_params=pltpu.CompilerParams(vmem_limit_bytes=8 << 20),
+            cost_estimate=pl.CostEstimate(
+                flops=0, transcendentals=0, bytes_accessed=8 * shard_total * half * block
+            ),
+            name="columns",
+        )(where, pieces, after, before, far_a, far_b)
+
     with jax.named_scope("grad_gather"):
         b0 = lax.ppermute(grad_preact, "fsdp", y_from(1))
         a0 = lax.ppermute(grad_preact, "fsdp", y_from(3))
         pieces_z = tuple(lax.ppermute(grad_preact, "fsdp", z_from(k)) for k in range(1, Z))
-        pieces_z, _ = lax.optimization_barrier((pieces_z, (b0, a0)))
+        pieces_z, _ = lax.optimization_barrier((pieces_z, (b0, a0, after, before)))
         line = jnp.concatenate(pieces_z, 0)
         f0 = lax.ppermute(a0, "fsdp", y_from(3))
         a1 = lax.ppermute(line, "fsdp", y_from(3))

time: 177 us -> 174 us (0.983)
  waiting for transfers between devices: 68 us -> 54.4 us
  starting transfers between devices: 57.1 us -> 64.2 us
  blocking collectives: 16.7 us -> 23.3 us
    all_to_all x1 -> x0, waiting for transfers between devices: 13.6 us -> none  [shards(): lax.all_to_all(jnp.broadcast_to(partial_quant[None], (tp_total,) + partia...]
    ppermute x0 -> x3, starting transfers between devices: none -> 10.5 us  [the longest x1 5.91 us: shards(): lax.ppermute(quant, 'tp', [(t, t ^ 1) for t in range(2 * X)])]
    all_to_all x1 -> x0, starting transfers between devices: 9.1 us -> none  [shards(): lax.all_to_all(jnp.broadcast_to(partial_quant[None], (tp_total,) + partia...]
    ppermute x4, waiting for transfers between devices: 1.6 us -> 9.94 us  [round_y(): below = lax.ppermute(block, 'fsdp', y_from(1))]
    ppermute x4, waiting for transfers between devices: 11 us -> 2.67 us  [round_y(): above = lax.ppermute(block, 'fsdp', y_from(3))]
    ppermute x0 -> x3, waiting for transfers between devices: none -> 6.63 us  [the longest x2 4.73 us: shards(): lax.ppermute(quant, 'tp', [(t, t ^ flip) for t in range(2 * X)])]
    all_to_all x1, blocking collectives: 16.7 us -> 23.3 us  [shards(): lax.all_to_all(updated, 'tp', split_axis=0, concat_axis=1, tiled=True)]
    ppermute x2, waiting for transfers between devices: 6.42 us -> 0.01 us  [round_y(): return (below, above, lax.ppermute(above, 'fsdp', y_from(3)))]
  transfers between devices with their start and end apart: 35 -> 37, of which waited for: 14 -> 19; matrix products, arithmetic and copies ran while one was open for 4% -> 2% of each run, Pallas kernels for 6% -> 6%
where the time goes in v5:
time: 174 us; the launch traced here: 173 us
  starting transfers between devices  64.2 us (37%)
  waiting for transfers between devices  54.4 us (31%)
  blocking collectives  23.3 us (13%)
  Pallas kernels  16.4 us (9%)
  local copies, waits for them, and re-layouts  8.2 us (5%)
  other arithmetic  4.05 us (2%)
  matrix products  1.83 us (1%)
    all_to_all x1, blocking collectives, shards(): lax.all_to_all(updated, 'tp', split_axis=0, concat_axis=1, tiled=True)  23.3 us
    ppermute x3, waiting for transfers between devices, shards(): lax.ppermute(torso_weight, 'fsdp', z_from(k))  12.3 us
    all_to_all x1, starting transfers between devices, shards(): lax.all_to_all(pieces.reshape(2 * shard_total, strip + 16, block), ('grp'...  10.4 us
    ppermute x4, waiting for transfers between devices, round_y(): below = lax.ppermute(block, 'fsdp', y_from(1))  9.94 us
    ppermute x4, starting transfers between devices, round_y(): below = lax.ppermute(block, 'fsdp', y_from(1))  8.51 us
    unnamed x36, local copies, waits for them, and re-layouts  6.31 us
    ppermute x3, starting transfers between devices, shards(): lax.ppermute(torso_weight, 'fsdp', z_from(k))  6.27 us
    ppermute x1, starting transfers between devices, shards(): lax.ppermute(quant, 'tp', [(t, t ^ 1) for t in range(2 * X)])  5.91 us
  transfers between devices with their start and end apart: 37, of which 19 were waited for; matrix products, arithmetic and copies ran while one was open for 2% of the time, Pallas kernels for 6%

profile of v5, /device:TPU:32, one launch (start us, length us, event | category | flops | bytes accessed | tf_op | source)
XLA Modules:
  0.0 173.4 jit_solution(4409205114585515734)
XLA Ops:
  0.6 1.9 %collective-permute-start.1 = (bf16[256,512]{1,0:T(8,128)(2,1)}, bf16[256,512]{1,0:T(8,128)(2,1)S(1)}, u32[]{:S(2)}, u32[]{:S(2)}) collective-permute-start(bf16[256,512]{1,0:T(8,128)(2,1)} %refs_0_.1), channel_id=1, source_target_pairs={{0,24},{8,0},{16,8},{24,16},{32,56},{40,32},{48,40},{56,48},{64,88... | collective-permute-start | bytes 786440 | tf_op jit(solution)/shard_map/weight_gather/ppermute | solution.py:200
  4.1 2.8 %collective-permute-start.3 = (bf16[256,512]{1,0:T(8,128)(2,1)}, bf16[256,512]{1,0:T(8,128)(2,1)S(1)}, u32[]{:S(2)}, u32[]{:S(2)}) collective-permute-start(bf16[256,512]{1,0:T(8,128)(2,1)} %refs_0_.1), channel_id=1, source_target_pairs={{0,8},{8,16},{16,24},{24,0},{32,40},{40,48},{48,56},{56,32},{64,72... | collective-permute-start | bytes 786440 | tf_op jit(solution)/shard_map/weight_gather/ppermute | solution.py:200
  6.9 3.0 %collective-permute-start.4 = (bf16[256,512]{1,0:T(8,128)(2,1)}, bf16[256,512]{1,0:T(8,128)(2,1)S(1)}, u32[]{:S(2)}, u32[]{:S(2)}) collective-permute-start(bf16[256,512]{1,0:T(8,128)(2,1)} %refs_0_.1), channel_id=1, source_target_pairs={{0,96},{8,104},{16,112},{24,120},{32,0},{40,8},{48,16},{56,24},{64... | collective-permute-start | bytes 786440 | tf_op jit(solution)/shard_map/weight_gather/ppermute | solution.py:32
  10.6 3.0 %collective-permute-start.6 = (bf16[256,512]{1,0:T(8,128)(2,1)S(1)}, bf16[256,512]{1,0:T(8,128)(2,1)S(1)}, u32[]{:S(2)}, u32[]{:S(2)}) collective-permute-start(bf16[256,512]{1,0:T(8,128)(2,1)S(1)} %collective-permute-done.1.refs_1_), channel_id=1, source_target_pairs={{0,96},{8,104},{16,112},{24,120},{32,0},{40,8},{48,16},{56,24},{64... | collective-permute-start | bytes 786440 | tf_op jit(solution)/shard_map/weight_gather/ppermute | solution.py:32
  13.6 8.5 %collective-permute-done.2.refs_2_ = bf16[256,512]{1,0:T(8,128)(2,1)S(1)} collective-permute-done((bf16[256,512]{1,0:T(8,128)(2,1)}, bf16[256,512]{1,0:T(8,128)(2,1)S(1)}, u32[]{:S(2)}, u32[]{:S(2)}) %collective-permute-start.2) | collective-permute-done | bytes 262176 | tf_op jit(solution)/shard_map/weight_gather/ppermute | solution.py:200
  23.8 3.1 %collective-permute-done.3.refs_3_ = bf16[256,512]{1,0:T(8,128)(2,1)S(1)} collective-permute-done((bf16[256,512]{1,0:T(8,128)(2,1)}, bf16[256,512]{1,0:T(8,128)(2,1)S(1)}, u32[]{:S(2)}, u32[]{:S(2)}) %collective-permute-start.3) | collective-permute-done | bytes 262176 | tf_op jit(solution)/shard_map/weight_gather/ppermute | solution.py:200
  27.6 2.5 %collective-permute-done.7.refs_13_ = bf16[256,512]{1,0:T(8,128)(2,1)} collective-permute-done((bf16[256,512]{1,0:T(8,128)(2,1)S(1)}, bf16[256,512]{1,0:T(8,128)(2,1)}, u32[]{:S(2)}, u32[]{:S(2)}) %collective-permute-start.7) | collective-permute-done | bytes 262176 | tf_op jit(solution)/shard_map/weight_gather/ppermute | solution.py:33
  30.0 2.2 %copy-done.1 = bf16[1,256,8192]{2,1,0:T(8,128)(2,1)S(1)} copy-done((bf16[1,256,8192]{2,1,0:T(8,128)(2,1)S(1)}, bf16[1,256,8192]{2,1,0:T(8,128)(2,1)}, u32[]{:S(2)}) %copy-start.1) | copy-done | bytes 4194328
  33.0 5.1 %norm.1 = (bf16[256,4096]{1,0:T(8,128)(2,1)S(1)}, bf16[256,4096]{1,0:T(8,128)(2,1)}) custom-call(s32[4]{0:T(128)S(1)} %pad_add_fusion.1.where_ref, bf16[256,8192]{1,0:T(8,128)(2,1)S(1)} %bitcast.29, f32[1,8192]{1,0:T(1,128)S(1)} %bitcast.30), custom_call_target="tpu_custom_call" | custom-call | flops 12582912 | bytes 8388608 | tf_op jit(solution)/shard_map/rows_swap/norm/pallas_call | solution.py:208
  42.3 5.0 %collective-permute-done.9.refs_6_ = bf16[256,512]{1,0:T(8,128)(2,1)} collective-permute-done((bf16[256,512]{1,0:T(8,128)(2,1)S(1)}, bf16[256,512]{1,0:T(8,128)(2,1)}, u32[]{:S(2)}, u32[]{:S(2)}) %collective-permute-start.9) | collective-permute-done | bytes 262176 | tf_op jit(solution)/shard_map/weight_gather/ppermute | solution.py:32
  47.7 4.9 %collective-permute-done.11.refs_7_ = bf16[256,512]{1,0:T(8,128)(2,1)} collective-permute-done((bf16[256,512]{1,0:T(8,128)(2,1)S(1)}, bf16[256,512]{1,0:T(8,128)(2,1)}, u32[]{:S(2)}, u32[]{:S(2)}) %collective-permute-start.11) | collective-permute-done | bytes 262176 | tf_op jit(solution)/shard_map/weight_gather/ppermute | solution.py:32
  53.6 2.9 %collective-permute-start.15 = (bf16[256,512]{1,0:T(8,128)(2,1)}, bf16[256,512]{1,0:T(8,128)(2,1)}, u32[]{:S(2)}, u32[]{:S(2)}) collective-permute-start(bf16[256,512]{1,0:T(8,128)(2,1)} %collective-permute-done.9.refs_6_), channel_id=1, source_target_pairs={{0,96},{8,104},{16,112},{24,120},{32,0},{40,8},{48,16},{56,24},{64... | collective-permute-start | bytes 786440 | tf_op jit(solution)/shard_map/weight_gather/ppermute | solution.py:36
  59.3 2.5 %pieces.1 = bf16[2,16,48,256]{3,2,1,0:T(8,128)(2,1)} custom-call(s32[4]{0:T(128)S(1)} %pad_add_fusion.1.where_ref, bf16[256,4096]{1,0:T(8,128)(2,1)S(1)} %get-tuple-element.18.own_ref, bf16[256,4096]{1,0:T(8,128)(2,1)} %collective-permute-done.8.got_ref, bf16[16,256]{1,0:T(8,128)(2,1)S(1)} %pad.4.count_ref), custom_call_target="tpu_custom_call" | custom-call | bytes 1048576 | tf_op jit(solution)/shard_map/columns_exchange/pieces/pallas_call | solution.py:246
  61.8 10.4 %all-to-all-start = ((bf16[32,48,256]{2,1,0:T(8,128)(2,1)}), bf16[32,48,256]{2,1,0:T(8,128)(2,1)}, u32[]{:S(2)}, u32[]{:S(2)}) async-start(bf16[32,48,256]{2,1,0:T(8,128)(2,1)} %bitcast.10), calls=%async_computation | async-start | bytes 1572864 | tf_op jit(solution)/shard_map/columns_exchange/all_to_all | solution.py:261
  74.2 5.0 %preact.1 = (f32[256,512]{1,0:T(8,128)S(1)}, f32[256,512]{1,0:T(8,128)S(1)}) custom-call(s32[4]{0:T(128)S(1)} %pad_add_fusion.1.where_ref, bf16[256,4096]{1,0:T(8,128)(2,1)S(1)} %get-tuple-element.18.own_ref, bf16[256,4096]{1,0:T(8,128)(2,1)} %collective-permute-done.8.got_ref, bf16[256,512]{1,0:T(8,128)(2,1)S(1)} %copy-done.2, ...), custom_call_target="tpu_custom_call" | custom-call | flops 2147483648 | bytes 9437184 | tf_op jit(solution)/shard_map/preact/pallas_call | solution.py:289
  83.5 2.4 %collective-permute-done.18 = f32[32,256]{1,0:T(8,128)S(1)} collective-permute-done((f32[32,256]{1,0:T(8,128)S(1)}, f32[32,256]{1,0:T(8,128)S(1)}, u32[]{:S(2)}, u32[]{:S(2)}) %collective-permute-start.18) | collective-permute-done | bytes 32800 | tf_op jit(solution)/shard_map/quant_sum/ppermute | solution.py:322
  85.9 3.0 %collective-permute-start.19 = (f32[32,256]{1,0:T(8,128)S(1)}, f32[32,256]{1,0:T(8,128)S(1)}, u32[]{:S(2)}, u32[]{:S(2)}) collective-permute-start(f32[32,256]{1,0:T(8,128)S(1)} %add.55), channel_id=1, source_target_pairs={{0,4},{1,5},{2,6},{3,7},{4,0},{5,1},{6,2},{7,3},{8,12},{9,13},{10,... | collective-permute-start | bytes 98312 | tf_op jit(solution)/shard_map/quant_sum/ppermute | solution.py:322
  89.1 2.3 %collective-permute-done.19 = f32[32,256]{1,0:T(8,128)S(1)} collective-permute-done((f32[32,256]{1,0:T(8,128)S(1)}, f32[32,256]{1,0:T(8,128)S(1)}, u32[]{:S(2)}, u32[]{:S(2)}) %collective-permute-start.19) | collective-permute-done | bytes 32800 | tf_op jit(solution)/shard_map/quant_sum/ppermute | solution.py:322
  91.4 5.9 %collective-permute-start.20 = (f32[32,256]{1,0:T(8,128)S(1)}, f32[32,256]{1,0:T(8,128)S(1)}, u32[]{:S(2)}, u32[]{:S(2)}) collective-permute-start(f32[32,256]{1,0:T(8,128)S(1)} %add.56), channel_id=1, source_target_pairs={{0,1},{1,0},{2,3},{3,2},{4,5},{5,4},{6,7},{7,6},{8,9},{9,8},{10,11... | collective-permute-start | bytes 98312 | tf_op jit(solution)/shard_map/quant_sum/ppermute | solution.py:323
  102.3 2.8 %collective-permute-start.21 = (bf16[2,16,32,256]{3,2,1,0:T(8,128)(2,1)S(1)}, bf16[2,16,32,256]{3,2,1,0:T(8,128)(2,1)S(1)}, u32[]{:S(2)}, u32[]{:S(2)}) collective-permute-start(bf16[2,16,32,256]{3,2,1,0:T(8,128)(2,1)S(1)} %slice.58.own_ref), channel_id=1, source_target_pairs={{0,6},{1,7},{2,0},{3,1},{4,2},{5,3},{6,4},{7,5},{8,14},{9,15},{10,... | collective-permute-start | bytes 1572872 | tf_op jit(solution)/shard_map/columns_round_x/ppermute | solution.py:349
  107.8 2.4 %collective-permute-start.27 = (bf16[128,512]{1,0:T(8,128)(2,1)S(1)}, bf16[128,512]{1,0:T(8,128)(2,1)S(1)}, u32[]{:S(2)}, u32[]{:S(2)}) collective-permute-start(bf16[128,512]{1,0:T(8,128)(2,1)S(1)} %fusion.5.own_ref), channel_id=1, source_target_pairs={{0,8},{8,16},{16,24},{24,0},{32,40},{40,48},{48,56},{56,32},{64,72... | collective-permute-start | bytes 393224 | tf_op jit(solution)/shard_map/grad_gather/ppermute | solution.py:369
  110.2 5.7 %collective-permute-done.25 = bf16[128,512]{1,0:T(8,128)(2,1)S(1)} collective-permute-done((bf16[128,512]{1,0:T(8,128)(2,1)S(1)}, bf16[128,512]{1,0:T(8,128)(2,1)S(1)}, u32[]{:S(2)}, u32[]{:S(2)}) %collective-permute-start.25) | collective-permute-done | bytes 131104 | tf_op jit(solution)/shard_map/grad_gather/ppermute | solution.py:369
  115.9 2.9 %collective-permute-start.28 = (bf16[128,512]{1,0:T(8,128)(2,1)S(1)}, bf16[128,512]{1,0:T(8,128)(2,1)S(1)}, u32[]{:S(2)}, u32[]{:S(2)}) collective-permute-start(bf16[128,512]{1,0:T(8,128)(2,1)S(1)} %fusion.5.own_ref), channel_id=1, source_target_pairs={{0,96},{8,104},{16,112},{24,120},{32,0},{40,8},{48,16},{56,24},{64... | collective-permute-start | bytes 393224 | tf_op jit(solution)/shard_map/grad_gather/ppermute | solution.py:367
  118.8 3.9 %collective-permute-done.28.b0_ref = bf16[128,512]{1,0:T(8,128)(2,1)S(1)} collective-permute-done((bf16[128,512]{1,0:T(8,128)(2,1)S(1)}, bf16[128,512]{1,0:T(8,128)(2,1)S(1)}, u32[]{:S(2)}, u32[]{:S(2)}) %collective-permute-start.28) | collective-permute-done | bytes 131104 | tf_op jit(solution)/shard_map/grad_gather/ppermute | solution.py:367
  122.7 3.7 %collective-permute-done.29.a0_ref = bf16[128,512]{1,0:T(8,128)(2,1)S(1)} collective-permute-done((bf16[128,512]{1,0:T(8,128)(2,1)S(1)}, bf16[128,512]{1,0:T(8,128)(2,1)S(1)}, u32[]{:S(2)}, u32[]{:S(2)}) %collective-permute-start.29) | collective-permute-done | bytes 131104 | tf_op jit(solution)/shard_map/grad_gather/ppermute | solution.py:368
  126.6 2.0 %collective-permute-start.31 = (bf16[384,512]{1,0:T(8,128)(2,1)S(1)}, bf16[384,512]{1,0:T(8,128)(2,1)S(1)}, u32[]{:S(2)}, u32[]{:S(2)}) collective-permute-start(bf16[384,512]{1,0:T(8,128)(2,1)S(1)} %constant_dynamic-update-slice_fusion.line_ref), channel_id=1, source_target_pairs={{0,32},{8,40},{16,48},{24,56},{32,64},{40,72},{48,80},{56,88},{64,... | collective-permute-start | bytes 1179656 | tf_op jit(solution)/shard_map/grad_gather/ppermute | solution.py:373
  128.6 3.0 %collective-permute-start.23 = (bf16[16,32,256]{2,1,0:T(8,128)(2,1)S(1)}, bf16[16,32,256]{2,1,0:T(8,128)(2,1)S(1)}, u32[]{:S(2)}, u32[]{:S(2)}) collective-permute-start(bf16[16,32,256]{2,1,0:T(8,128)(2,1)S(1)} %slice_bitcast_fusion.1), channel_id=1, source_target_pairs={{0,6},{1,7},{2,0},{3,1},{4,2},{5,3},{6,4},{7,5},{8,14},{9,15},{10,... | collective-permute-start | bytes 786440 | tf_op jit(solution)/shard_map/columns_round_x/ppermute | solution.py:351
  131.8 2.9 %collective-permute-done.30.b1_ref = bf16[384,512]{1,0:T(8,128)(2,1)S(1)} collective-permute-done((bf16[384,512]{1,0:T(8,128)(2,1)S(1)}, bf16[384,512]{1,0:T(8,128)(2,1)S(1)}, u32[]{:S(2)}, u32[]{:S(2)}) %collective-permute-start.30) | collective-permute-done | bytes 393248 | tf_op jit(solution)/shard_map/grad_gather/ppermute | solution.py:374
  134.7 3.8 %collective-permute-start.34 = (bf16[256,512]{1,0:T(8,128)(2,1)S(1)}, bf16[256,512]{1,0:T(8,128)(2,1)S(1)}, u32[]{:S(2)}, u32[]{:S(2)}) collective-permute-start(bf16[256,512]{1,0:T(8,128)(2,1)S(1)} %slice.64), channel_id=1, source_target_pairs={{0,96},{8,104},{16,112},{24,120},{32,0},{40,8},{48,16},{56,24},{64... | collective-permute-start | bytes 786440 | tf_op jit(solution)/shard_map/grad_gather/ppermute | solution.py:376
  139.3 2.4 %columns.1.cols_ref = bf16[512,2048]{1,0:T(8,128)(2,1)S(1)} custom-call(s32[4]{0:T(128)S(1)} %pad_add_fusion.1.where_ref, bf16[2,16,32,256]{3,2,1,0:T(8,128)(2,1)S(1)} %slice.58.own_ref, bf16[2,16,32,256]{3,2,1,0:T(8,128)(2,1)S(1)} %collective-permute-done.21.after_ref, bf16[2,16,32,256]{3,2,1,0:T(8,128)(2,1)S(1)} %collective-permute-done.22.before_ref, ...), custom_call_target="tpu_custom_call" | custom-call | bytes 4194304 | tf_op jit(solution)/shard_map/columns_round_x/columns/pallas_call | solution.py:353
  142.7 2.0 %collective-permute-done.32.f0_ref = bf16[128,512]{1,0:T(8,128)(2,1)S(1)} collective-permute-done((bf16[128,512]{1,0:T(8,128)(2,1)S(1)}, bf16[128,512]{1,0:T(8,128)(2,1)S(1)}, u32[]{:S(2)}, u32[]{:S(2)}) %collective-permute-start.32) | collective-permute-done | bytes 131104 | tf_op jit(solution)/shard_map/grad_gather/ppermute | solution.py:372
  149.4 23.3 %all_to_all.24 = bf16[8,32,512]{2,1,0:T(8,128)(2,1)S(1)} all-to-all(bf16[8,32,512]{2,1,0:T(8,128)(2,1)S(1)} %bitcast.32), channel_id=1, replica_groups=mesh['grp'=2,'fsdp'=16,'tp'=8] {'tp'}, dimensions={0} | all-to-all | bytes 524288 | tf_op jit(solution)/shard_map/all_to_all | solution.py:407
  (121 shorter events, 35.1 us)
Async XLA Ops:
  0.6 10.0 %collective-permute-start.1 = (bf16[256,512]{1,0:T(8,128)(2,1)}, bf16[256,512]{1,0:T(8,128)(2,1)S(1)}, u32[]{:S(2)}, u32[]{:S(2)}) collective-permute-start(bf16[256,512]{1,0:T(8,128)(2,1)} %refs_0_.1), channel_id=1, source_target_pairs={{0,24},{8,0},{16,8},{24,16},{32,56},{40,32},{48,40},{56,48},{64,88... | collective-permute-start | bytes 786440 | tf_op jit(solution)/shard_map/weight_gather/ppermute | solution.py:200
  2.6 19.6 %collective-permute-start.2 = (bf16[256,512]{1,0:T(8,128)(2,1)}, bf16[256,512]{1,0:T(8,128)(2,1)S(1)}, u32[]{:S(2)}, u32[]{:S(2)}) collective-permute-start(bf16[256,512]{1,0:T(8,128)(2,1)} %refs_0_.1), channel_id=1, source_target_pairs={{0,16},{8,24},{16,0},{24,8},{32,48},{40,56},{48,32},{56,40},{64,80... | collective-permute-start | bytes 786440 | tf_op jit(solution)/shard_map/weight_gather/ppermute | solution.py:200
  4.1 22.8 %collective-permute-start.3 = (bf16[256,512]{1,0:T(8,128)(2,1)}, bf16[256,512]{1,0:T(8,128)(2,1)S(1)}, u32[]{:S(2)}, u32[]{:S(2)}) collective-permute-start(bf16[256,512]{1,0:T(8,128)(2,1)} %refs_0_.1), channel_id=1, source_target_pairs={{0,8},{8,16},{16,24},{24,0},{32,40},{40,48},{48,56},{56,32},{64,72... | collective-permute-start | bytes 786440 | tf_op jit(solution)/shard_map/weight_gather/ppermute | solution.py:200
  6.9 20.0 %collective-permute-start.4 = (bf16[256,512]{1,0:T(8,128)(2,1)}, bf16[256,512]{1,0:T(8,128)(2,1)S(1)}, u32[]{:S(2)}, u32[]{:S(2)}) collective-permute-start(bf16[256,512]{1,0:T(8,128)(2,1)} %refs_0_.1), channel_id=1, source_target_pairs={{0,96},{8,104},{16,112},{24,120},{32,0},{40,8},{48,16},{56,24},{64... | collective-permute-start | bytes 786440 | tf_op jit(solution)/shard_map/weight_gather/ppermute | solution.py:32
  9.9 16.9 %collective-permute-start.5 = (bf16[256,512]{1,0:T(8,128)(2,1)}, bf16[256,512]{1,0:T(8,128)(2,1)}, u32[]{:S(2)}, u32[]{:S(2)}) collective-permute-start(bf16[256,512]{1,0:T(8,128)(2,1)} %refs_0_.1), channel_id=1, source_target_pairs={{0,32},{8,40},{16,48},{24,56},{32,64},{40,72},{48,80},{56,88},{64,... | collective-permute-start | bytes 786440 | tf_op jit(solution)/shard_map/weight_gather/ppermute | solution.py:33
  10.6 16.2 %collective-permute-start.6 = (bf16[256,512]{1,0:T(8,128)(2,1)S(1)}, bf16[256,512]{1,0:T(8,128)(2,1)S(1)}, u32[]{:S(2)}, u32[]{:S(2)}) collective-permute-start(bf16[256,512]{1,0:T(8,128)(2,1)S(1)} %collective-permute-done.1.refs_1_), channel_id=1, source_target_pairs={{0,96},{8,104},{16,112},{24,120},{32,0},{40,8},{48,16},{56,24},{64... | collective-permute-start | bytes 786440 | tf_op jit(solution)/shard_map/weight_gather/ppermute | solution.py:32
  22.2 7.9 %collective-permute-start.7 = (bf16[256,512]{1,0:T(8,128)(2,1)S(1)}, bf16[256,512]{1,0:T(8,128)(2,1)}, u32[]{:S(2)}, u32[]{:S(2)}) collective-permute-start(bf16[256,512]{1,0:T(8,128)(2,1)S(1)} %collective-permute-done.1.refs_1_), channel_id=1, source_target_pairs={{0,32},{8,40},{16,48},{24,56},{32,64},{40,72},{48,80},{56,88},{64,... | collective-permute-start | bytes 786440 | tf_op jit(solution)/shard_map/weight_gather/ppermute | solution.py:33
  38.1 21.1 %collective-permute-start.8 = (bf16[256,4096]{1,0:T(8,128)(2,1)}, bf16[256,4096]{1,0:T(8,128)(2,1)}, u32[]{:S(2)}, u32[]{:S(2)}) collective-permute-start(bf16[256,4096]{1,0:T(8,128)(2,1)} %get-tuple-element.19), channel_id=1, source_target_pairs={{0,128},{128,0},{1,129},{129,1},{2,130},{130,2},{3,131},{131,3},{4... | collective-permute-start | bytes 6291464 | tf_op jit(solution)/shard_map/rows_swap/ppermute | solution.py:227
  38.1 9.2 %collective-permute-start.9 = (bf16[256,512]{1,0:T(8,128)(2,1)S(1)}, bf16[256,512]{1,0:T(8,128)(2,1)}, u32[]{:S(2)}, u32[]{:S(2)}) collective-permute-start(bf16[256,512]{1,0:T(8,128)(2,1)S(1)} %collective-permute-done.2.refs_2_), channel_id=1, source_target_pairs={{0,96},{8,104},{16,112},{24,120},{32,0},{40,8},{48,16},{56,24},{64... | collective-permute-start | bytes 786440 | tf_op jit(solution)/shard_map/weight_gather/ppermute | solution.py:32
  39.9 12.7 %collective-permute-start.11 = (bf16[256,512]{1,0:T(8,128)(2,1)S(1)}, bf16[256,512]{1,0:T(8,128)(2,1)}, u32[]{:S(2)}, u32[]{:S(2)}) collective-permute-start(bf16[256,512]{1,0:T(8,128)(2,1)S(1)} %collective-permute-done.3.refs_3_), channel_id=1, source_target_pairs={{0,96},{8,104},{16,112},{24,120},{32,0},{40,8},{48,16},{56,24},{64... | collective-permute-start | bytes 786440 | tf_op jit(solution)/shard_map/weight_gather/ppermute | solution.py:32
  40.6 12.3 %collective-permute-start.10 = (bf16[256,512]{1,0:T(8,128)(2,1)S(1)}, bf16[256,512]{1,0:T(8,128)(2,1)S(1)}, u32[]{:S(2)}, u32[]{:S(2)}) collective-permute-start(bf16[256,512]{1,0:T(8,128)(2,1)S(1)} %collective-permute-done.2.refs_2_), channel_id=1, source_target_pairs={{0,32},{8,40},{16,48},{24,56},{32,64},{40,72},{48,80},{56,88},{64,... | collective-permute-start | bytes 786440 | tf_op jit(solution)/shard_map/weight_gather/ppermute | solution.py:33
  41.9 14.8 %collective-permute-start.12 = (bf16[256,512]{1,0:T(8,128)(2,1)S(1)}, bf16[256,512]{1,0:T(8,128)(2,1)}, u32[]{:S(2)}, u32[]{:S(2)}) collective-permute-start(bf16[256,512]{1,0:T(8,128)(2,1)S(1)} %collective-permute-done.3.refs_3_), channel_id=1, source_target_pairs={{0,32},{8,40},{16,48},{24,56},{32,64},{40,72},{48,80},{56,88},{64,... | collective-permute-start | bytes 786440 | tf_op jit(solution)/shard_map/weight_gather/ppermute | solution.py:33
  47.3 24.9 %collective-permute-start.13 = (bf16[256,512]{1,0:T(8,128)(2,1)}, bf16[256,512]{1,0:T(8,128)(2,1)}, u32[]{:S(2)}, u32[]{:S(2)}) collective-permute-start(bf16[256,512]{1,0:T(8,128)(2,1)} %collective-permute-done.5.refs_12_), channel_id=1, source_target_pairs={{0,32},{8,40},{16,48},{24,56},{32,64},{40,72},{48,80},{56,88},{64,... | collective-permute-start | bytes 786440 | tf_op jit(solution)/shard_map/weight_gather/ppermute | solution.py:35
  52.6 19.7 %collective-permute-start.14 = (bf16[256,512]{1,0:T(8,128)(2,1)}, bf16[256,512]{1,0:T(8,128)(2,1)}, u32[]{:S(2)}, u32[]{:S(2)}) collective-permute-start(bf16[256,512]{1,0:T(8,128)(2,1)} %collective-permute-done.7.refs_13_), channel_id=1, source_target_pairs={{0,32},{8,40},{16,48},{24,56},{32,64},{40,72},{48,80},{56,88},{64,... | collective-permute-start | bytes 786440 | tf_op jit(solution)/shard_map/weight_gather/ppermute | solution.py:35
  53.6 18.7 %collective-permute-start.15 = (bf16[256,512]{1,0:T(8,128)(2,1)}, bf16[256,512]{1,0:T(8,128)(2,1)}, u32[]{:S(2)}, u32[]{:S(2)}) collective-permute-start(bf16[256,512]{1,0:T(8,128)(2,1)} %collective-permute-done.9.refs_6_), channel_id=1, source_target_pairs={{0,96},{8,104},{16,112},{24,120},{32,0},{40,8},{48,16},{56,24},{64... | collective-permute-start | bytes 786440 | tf_op jit(solution)/shard_map/weight_gather/ppermute | solution.py:36
  56.7 15.5 %collective-permute-start.16 = (bf16[256,512]{1,0:T(8,128)(2,1)}, bf16[256,512]{1,0:T(8,128)(2,1)}, u32[]{:S(2)}, u32[]{:S(2)}) collective-permute-start(bf16[256,512]{1,0:T(8,128)(2,1)} %collective-permute-done.11.refs_7_), channel_id=1, source_target_pairs={{0,96},{8,104},{16,112},{24,120},{32,0},{40,8},{48,16},{56,24},{64... | collective-permute-start | bytes 786440 | tf_op jit(solution)/shard_map/weight_gather/ppermute | solution.py:36
  59.2 20.3 %collective-permute-start = (s32[33,128]{1,0:T(8,128)S(1)}, s32[33,128]{1,0:T(8,128)}, u32[]{:S(2)}, u32[]{:S(2)}) collective-permute-start(s32[33,128]{1,0:T(8,128)S(1)} %fusion.11), channel_id=1, source_target_pairs={{0,128},{128,0},{1,129},{129,1},{2,130},{130,2},{3,131},{131,3},{4... | collective-permute-start | bytes 50696 | tf_op jit(solution)/shard_map/rows_swap/ppermute | solution.py:230
  61.8 37.7 %all-to-all-start = ((bf16[32,48,256]{2,1,0:T(8,128)(2,1)}), bf16[32,48,256]{2,1,0:T(8,128)(2,1)}, u32[]{:S(2)}, u32[]{:S(2)}) async-start(bf16[32,48,256]{2,1,0:T(8,128)(2,1)} %bitcast.10), calls=%async_computation | async-start | bytes 1572864 | tf_op jit(solution)/shard_map/columns_exchange/all_to_all | solution.py:261
  91.4 8.1 %collective-permute-start.20 = (f32[32,256]{1,0:T(8,128)S(1)}, f32[32,256]{1,0:T(8,128)S(1)}, u32[]{:S(2)}, u32[]{:S(2)}) collective-permute-start(f32[32,256]{1,0:T(8,128)S(1)} %add.56), channel_id=1, source_target_pairs={{0,1},{1,0},{2,3},{3,2},{4,5},{5,4},{6,7},{7,6},{8,9},{9,8},{10,11... | collective-permute-start | bytes 98312 | tf_op jit(solution)/shard_map/quant_sum/ppermute | solution.py:323
  102.3 24.1 %collective-permute-start.21 = (bf16[2,16,32,256]{3,2,1,0:T(8,128)(2,1)S(1)}, bf16[2,16,32,256]{3,2,1,0:T(8,128)(2,1)S(1)}, u32[]{:S(2)}, u32[]{:S(2)}) collective-permute-start(bf16[2,16,32,256]{3,2,1,0:T(8,128)(2,1)S(1)} %slice.58.own_ref), channel_id=1, source_target_pairs={{0,6},{1,7},{2,0},{3,1},{4,2},{5,3},{6,4},{7,5},{8,14},{9,15},{10,... | collective-permute-start | bytes 1572872 | tf_op jit(solution)/shard_map/columns_round_x/ppermute | solution.py:349
  105.1 21.3 %collective-permute-start.22 = (bf16[2,16,32,256]{3,2,1,0:T(8,128)(2,1)S(1)}, bf16[2,16,32,256]{3,2,1,0:T(8,128)(2,1)S(1)}, u32[]{:S(2)}, u32[]{:S(2)}) collective-permute-start(bf16[2,16,32,256]{3,2,1,0:T(8,128)(2,1)S(1)} %slice.58.own_ref), channel_id=1, source_target_pairs={{0,2},{1,3},{2,4},{3,5},{4,6},{5,7},{6,0},{7,1},{8,10},{9,11},{10,... | collective-permute-start | bytes 1572872 | tf_op jit(solution)/shard_map/columns_round_x/ppermute | solution.py:350
  105.1 10.7 %collective-permute-start.25 = (bf16[128,512]{1,0:T(8,128)(2,1)S(1)}, bf16[128,512]{1,0:T(8,128)(2,1)S(1)}, u32[]{:S(2)}, u32[]{:S(2)}) collective-permute-start(bf16[128,512]{1,0:T(8,128)(2,1)S(1)} %fusion.5.own_ref), channel_id=1, source_target_pairs={{0,24},{8,0},{16,8},{24,16},{32,56},{40,32},{48,40},{56,48},{64,88... | collective-permute-start | bytes 393224 | tf_op jit(solution)/shard_map/grad_gather/ppermute | solution.py:369
  106.8 12.0 %collective-permute-start.26 = (bf16[128,512]{1,0:T(8,128)(2,1)S(1)}, bf16[128,512]{1,0:T(8,128)(2,1)S(1)}, u32[]{:S(2)}, u32[]{:S(2)}) collective-permute-start(bf16[128,512]{1,0:T(8,128)(2,1)S(1)} %fusion.5.own_ref), channel_id=1, source_target_pairs={{0,16},{8,24},{16,0},{24,8},{32,48},{40,56},{48,32},{56,40},{64,80... | collective-permute-start | bytes 393224 | tf_op jit(solution)/shard_map/grad_gather/ppermute | solution.py:369
  107.8 11.0 %collective-permute-start.27 = (bf16[128,512]{1,0:T(8,128)(2,1)S(1)}, bf16[128,512]{1,0:T(8,128)(2,1)S(1)}, u32[]{:S(2)}, u32[]{:S(2)}) collective-permute-start(bf16[128,512]{1,0:T(8,128)(2,1)S(1)} %fusion.5.own_ref), channel_id=1, source_target_pairs={{0,8},{8,16},{16,24},{24,0},{32,40},{40,48},{48,56},{56,32},{64,72... | collective-permute-start | bytes 393224 | tf_op jit(solution)/shard_map/grad_gather/ppermute | solution.py:369
  115.9 6.9 %collective-permute-start.28 = (bf16[128,512]{1,0:T(8,128)(2,1)S(1)}, bf16[128,512]{1,0:T(8,128)(2,1)S(1)}, u32[]{:S(2)}, u32[]{:S(2)}) collective-permute-start(bf16[128,512]{1,0:T(8,128)(2,1)S(1)} %fusion.5.own_ref), channel_id=1, source_target_pairs={{0,96},{8,104},{16,112},{24,120},{32,0},{40,8},{48,16},{56,24},{64... | collective-permute-start | bytes 393224 | tf_op jit(solution)/shard_map/grad_gather/ppermute | solution.py:367
  118.8 7.6 %collective-permute-start.29 = (bf16[128,512]{1,0:T(8,128)(2,1)S(1)}, bf16[128,512]{1,0:T(8,128)(2,1)S(1)}, u32[]{:S(2)}, u32[]{:S(2)}) collective-permute-start(bf16[128,512]{1,0:T(8,128)(2,1)S(1)} %fusion.5.own_ref), channel_id=1, source_target_pairs={{0,32},{8,40},{16,48},{24,56},{32,64},{40,72},{48,80},{56,88},{64,... | collective-permute-start | bytes 393224 | tf_op jit(solution)/shard_map/grad_gather/ppermute | solution.py:368
  126.5 8.2 %collective-permute-start.30 = (bf16[384,512]{1,0:T(8,128)(2,1)S(1)}, bf16[384,512]{1,0:T(8,128)(2,1)S(1)}, u32[]{:S(2)}, u32[]{:S(2)}) collective-permute-start(bf16[384,512]{1,0:T(8,128)(2,1)S(1)} %constant_dynamic-update-slice_fusion.line_ref), channel_id=1, source_target_pairs={{0,96},{8,104},{16,112},{24,120},{32,0},{40,8},{48,16},{56,24},{64... | collective-permute-start | bytes 1179656 | tf_op jit(solution)/shard_map/grad_gather/ppermute | solution.py:374
  126.6 11.9 %collective-permute-start.31 = (bf16[384,512]{1,0:T(8,128)(2,1)S(1)}, bf16[384,512]{1,0:T(8,128)(2,1)S(1)}, u32[]{:S(2)}, u32[]{:S(2)}) collective-permute-start(bf16[384,512]{1,0:T(8,128)(2,1)S(1)} %constant_dynamic-update-slice_fusion.line_ref), channel_id=1, source_target_pairs={{0,32},{8,40},{16,48},{24,56},{32,64},{40,72},{48,80},{56,88},{64,... | collective-permute-start | bytes 1179656 | tf_op jit(solution)/shard_map/grad_gather/ppermute | solution.py:373
  128.6 10.0 %collective-permute-start.23 = (bf16[16,32,256]{2,1,0:T(8,128)(2,1)S(1)}, bf16[16,32,256]{2,1,0:T(8,128)(2,1)S(1)}, u32[]{:S(2)}, u32[]{:S(2)}) collective-permute-start(bf16[16,32,256]{2,1,0:T(8,128)(2,1)S(1)} %slice_bitcast_fusion.1), channel_id=1, source_target_pairs={{0,6},{1,7},{2,0},{3,1},{4,2},{5,3},{6,4},{7,5},{8,14},{9,15},{10,... | collective-permute-start | bytes 786440 | tf_op jit(solution)/shard_map/columns_round_x/ppermute | solution.py:351
  131.7 7.7 %collective-permute-start.24 = (bf16[16,32,256]{2,1,0:T(8,128)(2,1)S(1)}, bf16[16,32,256]{2,1,0:T(8,128)(2,1)S(1)}, u32[]{:S(2)}, u32[]{:S(2)}) collective-permute-start(bf16[16,32,256]{2,1,0:T(8,128)(2,1)S(1)} %slice_bitcast_fusion), channel_id=1, source_target_pairs={{0,2},{1,3},{2,4},{3,5},{4,6},{5,7},{6,0},{7,1},{8,10},{9,11},{10,... | collective-permute-start | bytes 786440 | tf_op jit(solution)/shard_map/columns_round_x/ppermute | solution.py:352
  134.7 11.4 %collective-permute-start.34 = (bf16[256,512]{1,0:T(8,128)(2,1)S(1)}, bf16[256,512]{1,0:T(8,128)(2,1)S(1)}, u32[]{:S(2)}, u32[]{:S(2)}) collective-permute-start(bf16[256,512]{1,0:T(8,128)(2,1)S(1)} %slice.64), channel_id=1, source_target_pairs={{0,96},{8,104},{16,112},{24,120},{32,0},{40,8},{48,16},{56,24},{64... | collective-permute-start | bytes 786440 | tf_op jit(solution)/shard_map/grad_gather/ppermute | solution.py:376
  138.5 7.6 %collective-permute-start.33 = (bf16[128,512]{1,0:T(8,128)(2,1)S(1)}, bf16[128,512]{1,0:T(8,128)(2,1)S(1)}, u32[]{:S(2)}, u32[]{:S(2)}) collective-permute-start(bf16[128,512]{1,0:T(8,128)(2,1)S(1)} %slice.63), channel_id=1, source_target_pairs={{0,32},{8,40},{16,48},{24,56},{32,64},{40,72},{48,80},{56,88},{64,... | collective-permute-start | bytes 393224 | tf_op jit(solution)/shard_map/grad_gather/ppermute | solution.py:375
  (22 other events, 214.3 us)

commit v6 on v5

--- a/solution.py
+++ b/solution.py
@@ -34,6 +34,10 @@
     if upward:
         return below, above, lax.ppermute(above, "fsdp", y_from(3))
     return below, above, lax.ppermute(below, "fsdp", y_from(1))
+
+
+def in_hbm(*arrays):
+    return [pltpu.with_memory_space_constraint(array, pltpu.HBM) for array in arrays]
 
 
 def preact_kernel(where_ref, own_ref, got_ref, *refs):
@@ -203,8 +207,8 @@
         chunks = lines + [rounds[k][j] for j in (0, 2, 1) for k in range(Z)]
 
     with jax.named_scope("rows_swap"):
-        values, _ = lax.optimization_barrier((frames[0], (lines[1:], rounds[0][:2], rounds[1][:2])))
-        tile = 32
+        values = frames[0]
+        tile = 64
         normed_own, normed_send = pl.pallas_call(
             norm_kernel,
             grid=(rows_block // tile,),
@@ -222,7 +226,7 @@
                 bytes_accessed=4 * rows_block * width,
             ),
             name="norm",
-        )(where, values, norm_gain[None, :])
+        )(where, *in_hbm(values, norm_gain[None, :]))
     with jax.named_scope("rows_swap"):
         normed_got = lax.ppermute(normed_send, "grp", SWAP)
         ints = jnp.concatenate([fractions[0].T, actions[0][None, :]], 0)
@@ -304,7 +308,7 @@
             bytes_accessed=2 * side * features + 4 * side * rows_block + 8 * rows_block * features,
         ),
         name="preact",
-    )(where, normed_own, normed_got, *chunks)
+    )(where, *in_hbm(normed_own, normed_got, *chunks))
     preact = keep + lax.ppermute(send, "grp", SWAP)
     weighted = (jax.nn.silu(preact) * picked).astype(jnp.bfloat16)
     table_values = lax.dot_general(
@@ -344,7 +348,19 @@
         * (1.0 + online_preact * (1.0 - gate_value))
     ).astype(jnp.bfloat16)
 
-    grad_preact, pieces = lax.optimization_barrier((grad_preact, pieces))
+    with jax.named_scope("grad_gather"):
+        b0 = lax.ppermute(grad_preact, "fsdp", y_from(1))
+        a0 = lax.ppermute(grad_preact, "fsdp", y_from(3))
+        pieces_z = tuple(lax.ppermute(grad_preact, "fsdp", z_from(k)) for k in range(1, Z))
+        pieces_z, _ = lax.optimization_barrier((pieces_z, (b0, a0)))
+        line = jnp.concatenate(pieces_z, 0)
+        f0 = lax.ppermute(a0, "fsdp", y_from(3))
+        a1 = lax.ppermute(line, "fsdp", y_from(3))
+        b1 = lax.ppermute(line, "fsdp", y_from(1))
+        f1 = lax.ppermute(a1[:half], "fsdp", y_from(3))
+        f2 = lax.ppermute(b1[half:], "fsdp", y_from(1))
+
+    pieces, _ = lax.optimization_barrier((pieces, (b0, a0, pieces_z[0])))
     with jax.named_scope("columns_round_x"):
         after = lax.ppermute(pieces, "tp", x_from(1))
         before = lax.ppermute(pieces, "tp", x_from(3))
@@ -362,18 +378,6 @@
             ),
             name="columns",
         )(where, pieces, after, before, far_a, far_b)
-
-    with jax.named_scope("grad_gather"):
-        b0 = lax.ppermute(grad_preact, "fsdp", y_from(1))
-        a0 = lax.ppermute(grad_preact, "fsdp", y_from(3))
-        pieces_z = tuple(lax.ppermute(grad_preact, "fsdp", z_from(k)) for k in range(1, Z))
-        pieces_z, _ = lax.optimization_barrier((pieces_z, (b0, a0, after, before)))
-        line = jnp.concatenate(pieces_z, 0)
-        f0 = lax.ppermute(a0, "fsdp", y_from(3))
-        a1 = lax.ppermute(line, "fsdp", y_from(3))
-        b1 = lax.ppermute(line, "fsdp", y_from(1))
-        f1 = lax.ppermute(a1[:half], "fsdp", y_from(3))
-        f2 = lax.ppermute(b1[half:], "fsdp", y_from(1))
 
     near = pl.pallas_call(
         near_kernel,

time: 174 us -> 164 us (0.943)
  local copies, waits for them, and re-layouts: 8.2 us -> 1.67 us
  starting transfers between devices: 64.2 us -> 60.6 us
  waiting for transfers between devices: 54.4 us -> 56.3 us
    ppermute x1, waiting for transfers between devices: 0.01 us -> 6.92 us  [shards(): after = lax.ppermute(pieces, 'tp', x_from(1))]
    ppermute x4, waiting for transfers between devices: 2.67 us -> 8.96 us  [round_y(): above = lax.ppermute(block, 'fsdp', y_from(3))]
    unnamed x36 -> x42, local copies, waits for them, and re-layouts: 6.31 us -> 0.81 us
    ppermute x2, starting transfers between devices: 4.46 us -> 0.01 us  [round_y(): return (below, above, lax.ppermute(below, 'fsdp', y_from(1)))]
    ppermute x1, waiting for transfers between devices: 3.94 us -> 0.01 us  [shards(): b0 = lax.ppermute(grad_preact, 'fsdp', y_from(1))]
    all_to_all x1, starting transfers between devices: 10.4 us -> 6.94 us  [shards(): lax.all_to_all(pieces.reshape(2 * shard_total, strip + 16, block), ('grp'...]
    ppermute x4, waiting for transfers between devices: 9.94 us -> 6.82 us  [round_y(): below = lax.ppermute(block, 'fsdp', y_from(1))]
    ppermute x1, waiting for transfers between devices: 0.74 us -> 3.79 us  [shards(): far_b = lax.ppermute(before[1], 'tp', x_from(3))]
  transfers between devices with their start and end apart: 37 -> 37, of which waited for: 19 -> 17; matrix products, arithmetic and copies ran while one was open for 2% -> 2% of each run, Pallas kernels for 6% -> 7%
where the time goes in v6:
time: 164 us; the launch traced here: 163 us
  starting transfers between devices  60.6 us (37%)
  waiting for transfers between devices  56.3 us (34%)
  blocking collectives  21.7 us (13%)
  Pallas kernels  17.3 us (11%)
  other arithmetic  2.55 us (2%)
  matrix products  1.83 us (1%)
  local copies, waits for them, and re-layouts  1.67 us (1%)
    all_to_all x1, blocking collectives, shards(): lax.all_to_all(updated, 'tp', split_axis=0, concat_axis=1, tiled=True)  21.7 us
    ppermute x3, waiting for transfers between devices, shards(): lax.ppermute(torso_weight, 'fsdp', z_from(k))  12.7 us
    ppermute x4, starting transfers between devices, round_y(): below = lax.ppermute(block, 'fsdp', y_from(1))  9.79 us
    ppermute x4, waiting for transfers between devices, round_y(): above = lax.ppermute(block, 'fsdp', y_from(3))  8.96 us
    all_to_all x1, starting transfers between devices, shards(): lax.all_to_all(pieces.reshape(2 * shard_total, strip + 16, block), ('grp'...  6.94 us
    ppermute x1, waiting for transfers between devices, shards(): after = lax.ppermute(pieces, 'tp', x_from(1))  6.92 us
    ppermute x4, waiting for transfers between devices, round_y(): below = lax.ppermute(block, 'fsdp', y_from(1))  6.82 us
    ppermute x3, starting transfers between devices, shards(): lax.ppermute(torso_weight, 'fsdp', z_from(k))  6.27 us
  transfers between devices with their start and end apart: 37, of which 17 were waited for; matrix products, arithmetic and copies ran while one was open for 2% of the time, Pallas kernels for 7%

profile of v6, /device:TPU:32, one launch (start us, length us, event | category | flops | bytes accessed | tf_op | source)
XLA Modules:
  0.0 163.1 jit_solution(17213068187263488522)
XLA Ops:
  0.8 5.8 %norm.1 = (bf16[256,4096]{1,0:T(8,128)(2,1)S(1)}, bf16[256,4096]{1,0:T(8,128)(2,1)}) custom-call(s32[4]{0:T(128)S(1)} %pad_add_fusion.1.where_ref, bf16[256,8192]{1,0:T(8,128)(2,1)} %bitcast.29, f32[1,8192]{1,0:T(1,128)} %bitcast.37), custom_call_target="tpu_custom_call" | custom-call | flops 12582912 | bytes 8388608 | tf_op jit(solution)/shard_map/rows_swap/norm/pallas_call | solution.py:212
  6.6 1.9 %collective-permute-start.2 = (bf16[256,512]{1,0:T(8,128)(2,1)S(1)}, bf16[256,512]{1,0:T(8,128)(2,1)S(1)}, u32[]{:S(2)}, u32[]{:S(2)}) collective-permute-start(bf16[256,512]{1,0:T(8,128)(2,1)S(1)} %copy-done.2), channel_id=1, source_target_pairs={{0,24},{8,0},{16,8},{24,16},{32,56},{40,32},{48,40},{56,48},{64,88... | collective-permute-start | bytes 786440 | tf_op jit(solution)/shard_map/weight_gather/ppermute | solution.py:204
  10.0 2.8 %collective-permute-start.4 = (bf16[256,512]{1,0:T(8,128)(2,1)S(1)}, bf16[256,512]{1,0:T(8,128)(2,1)S(1)}, u32[]{:S(2)}, u32[]{:S(2)}) collective-permute-start(bf16[256,512]{1,0:T(8,128)(2,1)S(1)} %copy-done.2), channel_id=1, source_target_pairs={{0,8},{8,16},{16,24},{24,0},{32,40},{40,48},{48,56},{56,32},{64,72... | collective-permute-start | bytes 786440 | tf_op jit(solution)/shard_map/weight_gather/ppermute | solution.py:204
  12.8 3.0 %collective-permute-start.5 = (bf16[256,512]{1,0:T(8,128)(2,1)S(1)}, bf16[256,512]{1,0:T(8,128)(2,1)S(1)}, u32[]{:S(2)}, u32[]{:S(2)}) collective-permute-start(bf16[256,512]{1,0:T(8,128)(2,1)S(1)} %copy-done.2), channel_id=1, source_target_pairs={{0,96},{8,104},{16,112},{24,120},{32,0},{40,8},{48,16},{56,24},{64... | collective-permute-start | bytes 786440 | tf_op jit(solution)/shard_map/weight_gather/ppermute | solution.py:32
  17.3 10.6 %collective-permute-done.3.refs_2_ = bf16[256,512]{1,0:T(8,128)(2,1)S(1)} collective-permute-done((bf16[256,512]{1,0:T(8,128)(2,1)S(1)}, bf16[256,512]{1,0:T(8,128)(2,1)S(1)}, u32[]{:S(2)}, u32[]{:S(2)}) %collective-permute-start.3) | collective-permute-done | bytes 262176 | tf_op jit(solution)/shard_map/weight_gather/ppermute | solution.py:204
  27.9 3.0 %collective-permute-start.6 = (bf16[256,512]{1,0:T(8,128)(2,1)S(1)}, bf16[256,512]{1,0:T(8,128)(2,1)S(1)}, u32[]{:S(2)}, u32[]{:S(2)}) collective-permute-start(bf16[256,512]{1,0:T(8,128)(2,1)S(1)} %collective-permute-done.2.refs_1_), channel_id=1, source_target_pairs={{0,96},{8,104},{16,112},{24,120},{32,0},{40,8},{48,16},{56,24},{64... | collective-permute-start | bytes 786440 | tf_op jit(solution)/shard_map/weight_gather/ppermute | solution.py:32
  31.0 2.0 %collective-permute-done.4.refs_3_ = bf16[256,512]{1,0:T(8,128)(2,1)S(1)} collective-permute-done((bf16[256,512]{1,0:T(8,128)(2,1)S(1)}, bf16[256,512]{1,0:T(8,128)(2,1)S(1)}, u32[]{:S(2)}, u32[]{:S(2)}) %collective-permute-start.4) | collective-permute-done | bytes 262176 | tf_op jit(solution)/shard_map/weight_gather/ppermute | solution.py:204
  33.0 3.0 %collective-permute-start.7 = (bf16[256,512]{1,0:T(8,128)(2,1)S(1)}, bf16[256,512]{1,0:T(8,128)(2,1)S(1)}, u32[]{:S(2)}, u32[]{:S(2)}) collective-permute-start(bf16[256,512]{1,0:T(8,128)(2,1)S(1)} %collective-permute-done.3.refs_2_), channel_id=1, source_target_pairs={{0,96},{8,104},{16,112},{24,120},{32,0},{40,8},{48,16},{56,24},{64... | collective-permute-start | bytes 786440 | tf_op jit(solution)/shard_map/weight_gather/ppermute | solution.py:32
  38.1 4.6 %collective-permute-done.7.refs_6_ = bf16[256,512]{1,0:T(8,128)(2,1)S(1)} collective-permute-done((bf16[256,512]{1,0:T(8,128)(2,1)S(1)}, bf16[256,512]{1,0:T(8,128)(2,1)S(1)}, u32[]{:S(2)}, u32[]{:S(2)}) %collective-permute-start.7) | collective-permute-done | bytes 262176 | tf_op jit(solution)/shard_map/weight_gather/ppermute | solution.py:32
  44.6 2.2 %collective-permute-done.8.refs_7_ = bf16[256,512]{1,0:T(8,128)(2,1)} collective-permute-done((bf16[256,512]{1,0:T(8,128)(2,1)S(1)}, bf16[256,512]{1,0:T(8,128)(2,1)}, u32[]{:S(2)}, u32[]{:S(2)}) %collective-permute-start.8) | collective-permute-done | bytes 262176 | tf_op jit(solution)/shard_map/weight_gather/ppermute | solution.py:32
  49.6 3.3 %collective-permute-done.15.refs_14_ = bf16[256,512]{1,0:T(8,128)(2,1)} collective-permute-done((bf16[256,512]{1,0:T(8,128)(2,1)S(1)}, bf16[256,512]{1,0:T(8,128)(2,1)}, u32[]{:S(2)}, u32[]{:S(2)}) %collective-permute-start.15) | collective-permute-done | bytes 262176 | tf_op jit(solution)/shard_map/weight_gather/ppermute | solution.py:33
  52.9 5.6 %collective-permute-done.16.refs_15_ = bf16[256,512]{1,0:T(8,128)(2,1)} collective-permute-done((bf16[256,512]{1,0:T(8,128)(2,1)S(1)}, bf16[256,512]{1,0:T(8,128)(2,1)}, u32[]{:S(2)}, u32[]{:S(2)}) %collective-permute-start.16) | collective-permute-done | bytes 262176 | tf_op jit(solution)/shard_map/weight_gather/ppermute | solution.py:33
  59.5 2.6 %pieces.1 = bf16[2,16,48,256]{3,2,1,0:T(8,128)(2,1)} custom-call(s32[4]{0:T(128)S(1)} %pad_add_fusion.1.where_ref, bf16[256,4096]{1,0:T(8,128)(2,1)S(1)} %get-tuple-element.15.own_ref, bf16[256,4096]{1,0:T(8,128)(2,1)} %collective-permute-done.1.got_ref, bf16[16,256]{1,0:T(8,128)(2,1)S(1)} %pad.4.count_ref), custom_call_target="tpu_custom_call" | custom-call | bytes 1048576 | tf_op jit(solution)/shard_map/columns_exchange/pieces/pallas_call | solution.py:250
  62.1 6.9 %all-to-all-start = ((bf16[32,48,256]{2,1,0:T(8,128)(2,1)}), bf16[32,48,256]{2,1,0:T(8,128)(2,1)S(1)}, u32[]{:S(2)}, u32[]{:S(2)}) async-start(bf16[32,48,256]{2,1,0:T(8,128)(2,1)} %bitcast.11), calls=%async_computation | async-start | bytes 1572864 | tf_op jit(solution)/shard_map/columns_exchange/all_to_all | solution.py:265
  69.2 5.2 %preact.1 = (f32[256,512]{1,0:T(8,128)S(1)}, f32[256,512]{1,0:T(8,128)S(1)}) custom-call(s32[4]{0:T(128)S(1)} %pad_add_fusion.1.where_ref, bf16[256,4096]{1,0:T(8,128)(2,1)} %copy-done.1, bf16[256,4096]{1,0:T(8,128)(2,1)} %collective-permute-done.1.got_ref, bf16[256,512]{1,0:T(8,128)(2,1)} %refs_0_.1, bf16[256,512]{1,0:T(8,128)(2,1)} %copy-done.4, ...), custom_call_target="tpu_custom_call" | custom-call | flops 2147483648 | bytes 9437184 | tf_op jit(solution)/shard_map/preact/pallas_call | solution.py:293
  78.7 2.4 %collective-permute-done.18 = f32[32,256]{1,0:T(8,128)S(1)} collective-permute-done((f32[32,256]{1,0:T(8,128)S(1)}, f32[32,256]{1,0:T(8,128)S(1)}, u32[]{:S(2)}, u32[]{:S(2)}) %collective-permute-start.18) | collective-permute-done | bytes 32800 | tf_op jit(solution)/shard_map/quant_sum/ppermute | solution.py:326
  81.1 3.0 %collective-permute-start.19 = (f32[32,256]{1,0:T(8,128)S(1)}, f32[32,256]{1,0:T(8,128)S(1)}, u32[]{:S(2)}, u32[]{:S(2)}) collective-permute-start(f32[32,256]{1,0:T(8,128)S(1)} %add.54), channel_id=1, source_target_pairs={{0,4},{1,5},{2,6},{3,7},{4,0},{5,1},{6,2},{7,3},{8,12},{9,13},{10,... | collective-permute-start | bytes 98312 | tf_op jit(solution)/shard_map/quant_sum/ppermute | solution.py:326
  84.2 2.3 %collective-permute-done.19 = f32[32,256]{1,0:T(8,128)S(1)} collective-permute-done((f32[32,256]{1,0:T(8,128)S(1)}, f32[32,256]{1,0:T(8,128)S(1)}, u32[]{:S(2)}, u32[]{:S(2)}) %collective-permute-start.19) | collective-permute-done | bytes 32800 | tf_op jit(solution)/shard_map/quant_sum/ppermute | solution.py:326
  86.5 5.6 %collective-permute-start.20 = (f32[32,256]{1,0:T(8,128)S(1)}, f32[32,256]{1,0:T(8,128)S(1)}, u32[]{:S(2)}, u32[]{:S(2)}) collective-permute-start(f32[32,256]{1,0:T(8,128)S(1)} %add.55), channel_id=1, source_target_pairs={{0,1},{1,0},{2,3},{3,2},{4,5},{5,4},{6,7},{7,6},{8,9},{9,8},{10,11... | collective-permute-start | bytes 98312 | tf_op jit(solution)/shard_map/quant_sum/ppermute | solution.py:327
  92.4 2.0 %collective-permute-done.20 = f32[32,256]{1,0:T(8,128)S(1)} collective-permute-done((f32[32,256]{1,0:T(8,128)S(1)}, f32[32,256]{1,0:T(8,128)S(1)}, u32[]{:S(2)}, u32[]{:S(2)}) %collective-permute-start.20) | collective-permute-done | bytes 32800 | tf_op jit(solution)/shard_map/quant_sum/ppermute | solution.py:327
  95.4 2.8 %collective-permute-start.21 = (bf16[128,512]{1,0:T(8,128)(2,1)S(1)}, bf16[128,512]{1,0:T(8,128)(2,1)S(1)}, u32[]{:S(2)}, u32[]{:S(2)}) collective-permute-start(bf16[128,512]{1,0:T(8,128)(2,1)S(1)} %fusion.5.own_ref), channel_id=1, source_target_pairs={{0,96},{8,104},{16,112},{24,120},{32,0},{40,8},{48,16},{56,24},{64... | collective-permute-start | bytes 393224 | tf_op jit(solution)/shard_map/grad_gather/ppermute | solution.py:352
  98.7 2.8 %collective-permute-start.24 = (bf16[128,512]{1,0:T(8,128)(2,1)S(1)}, bf16[128,512]{1,0:T(8,128)(2,1)S(1)}, u32[]{:S(2)}, u32[]{:S(2)}) collective-permute-start(bf16[128,512]{1,0:T(8,128)(2,1)S(1)} %fusion.5.own_ref), channel_id=1, source_target_pairs={{0,16},{8,24},{16,0},{24,8},{32,48},{40,56},{48,32},{56,40},{64,80... | collective-permute-start | bytes 393224 | tf_op jit(solution)/shard_map/grad_gather/ppermute | solution.py:354
  101.5 1.9 %collective-permute-start.25 = (bf16[128,512]{1,0:T(8,128)(2,1)S(1)}, bf16[128,512]{1,0:T(8,128)(2,1)S(1)}, u32[]{:S(2)}, u32[]{:S(2)}) collective-permute-start(bf16[128,512]{1,0:T(8,128)(2,1)S(1)} %fusion.5.own_ref), channel_id=1, source_target_pairs={{0,8},{8,16},{16,24},{24,0},{32,40},{40,48},{48,56},{56,32},{64,72... | collective-permute-start | bytes 393224 | tf_op jit(solution)/shard_map/grad_gather/ppermute | solution.py:354
  104.3 4.7 %collective-permute-done.23 = bf16[128,512]{1,0:T(8,128)(2,1)S(1)} collective-permute-done((bf16[128,512]{1,0:T(8,128)(2,1)S(1)}, bf16[128,512]{1,0:T(8,128)(2,1)S(1)}, u32[]{:S(2)}, u32[]{:S(2)}) %collective-permute-start.23) | collective-permute-done | bytes 131104 | tf_op jit(solution)/shard_map/grad_gather/ppermute | solution.py:354
  109.6 2.8 %collective-permute-start.26 = (bf16[2,16,32,256]{3,2,1,0:T(8,128)(2,1)S(1)}, bf16[2,16,32,256]{3,2,1,0:T(8,128)(2,1)S(1)}, u32[]{:S(2)}, u32[]{:S(2)}) collective-permute-start(bf16[2,16,32,256]{3,2,1,0:T(8,128)(2,1)S(1)} %slice.56.own_ref), channel_id=1, source_target_pairs={{0,6},{1,7},{2,0},{3,1},{4,2},{5,3},{6,4},{7,5},{8,14},{9,15},{10,... | collective-permute-start | bytes 1572872 | tf_op jit(solution)/shard_map/columns_round_x/ppermute | solution.py:365
  112.4 3.0 %collective-permute-start.30 = (bf16[384,512]{1,0:T(8,128)(2,1)S(1)}, bf16[384,512]{1,0:T(8,128)(2,1)S(1)}, u32[]{:S(2)}, u32[]{:S(2)}) collective-permute-start(bf16[384,512]{1,0:T(8,128)(2,1)S(1)} %constant_dynamic-update-slice_fusion.line_ref), channel_id=1, source_target_pairs={{0,96},{8,104},{16,112},{24,120},{32,0},{40,8},{48,16},{56,24},{64... | collective-permute-start | bytes 1179656 | tf_op jit(solution)/shard_map/grad_gather/ppermute | solution.py:359
  115.5 6.9 %collective-permute-done.26.after_ref = bf16[2,16,32,256]{3,2,1,0:T(8,128)(2,1)S(1)} collective-permute-done((bf16[2,16,32,256]{3,2,1,0:T(8,128)(2,1)S(1)}, bf16[2,16,32,256]{3,2,1,0:T(8,128)(2,1)S(1)}, u32[]{:S(2)}, u32[]{:S(2)}) %collective-permute-start.26) | collective-permute-done | bytes 524320 | tf_op jit(solution)/shard_map/columns_round_x/ppermute | solution.py:365
  122.4 3.8 %collective-permute-start.28 = (bf16[16,32,256]{2,1,0:T(8,128)(2,1)S(1)}, bf16[16,32,256]{2,1,0:T(8,128)(2,1)S(1)}, u32[]{:S(2)}, u32[]{:S(2)}) collective-permute-start(bf16[16,32,256]{2,1,0:T(8,128)(2,1)S(1)} %slice_bitcast_fusion.1), channel_id=1, source_target_pairs={{0,6},{1,7},{2,0},{3,1},{4,2},{5,3},{6,4},{7,5},{8,14},{9,15},{10,... | collective-permute-start | bytes 786440 | tf_op jit(solution)/shard_map/columns_round_x/ppermute | solution.py:367
  126.3 2.7 %collective-permute-start.34 = (bf16[256,512]{1,0:T(8,128)(2,1)S(1)}, bf16[256,512]{1,0:T(8,128)(2,1)S(1)}, u32[]{:S(2)}, u32[]{:S(2)}) collective-permute-start(bf16[256,512]{1,0:T(8,128)(2,1)S(1)} %slice.64), channel_id=1, source_target_pairs={{0,96},{8,104},{16,112},{24,120},{32,0},{40,8},{48,16},{56,24},{64... | collective-permute-start | bytes 786440 | tf_op jit(solution)/shard_map/grad_gather/ppermute | solution.py:361
  130.1 3.8 %collective-permute-done.29.far_b_ref = bf16[16,32,256]{2,1,0:T(8,128)(2,1)S(1)} collective-permute-done((bf16[16,32,256]{2,1,0:T(8,128)(2,1)S(1)}, bf16[16,32,256]{2,1,0:T(8,128)(2,1)S(1)}, u32[]{:S(2)}, u32[]{:S(2)}) %collective-permute-start.29) | collective-permute-done | bytes 262176 | tf_op jit(solution)/shard_map/columns_round_x/ppermute | solution.py:368
  133.9 2.4 %columns.1.cols_ref = bf16[512,2048]{1,0:T(8,128)(2,1)S(1)} custom-call(s32[4]{0:T(128)S(1)} %pad_add_fusion.1.where_ref, bf16[2,16,32,256]{3,2,1,0:T(8,128)(2,1)S(1)} %slice.56.own_ref, bf16[2,16,32,256]{3,2,1,0:T(8,128)(2,1)S(1)} %collective-permute-done.26.after_ref, bf16[2,16,32,256]{3,2,1,0:T(8,128)(2,1)S(1)} %collective-permute-done.27.before_ref, ...), custom_call_target="tpu_custom_call" | custom-call | bytes 4194304 | tf_op jit(solution)/shard_map/columns_round_x/columns/pallas_call | solution.py:369
  140.7 21.7 %all_to_all.24 = bf16[8,32,512]{2,1,0:T(8,128)(2,1)S(1)} all-to-all(bf16[8,32,512]{2,1,0:T(8,128)(2,1)S(1)} %bitcast.33), channel_id=1, replica_groups=mesh['grp'=2,'fsdp'=16,'tp'=8] {'tp'}, dimensions={0} | all-to-all | bytes 524288 | tf_op jit(solution)/shard_map/all_to_all | solution.py:411
  (127 shorter events, 24.8 us)
Async XLA Ops:
  6.6 53.0 %collective-permute-start.1 = (bf16[256,4096]{1,0:T(8,128)(2,1)}, bf16[256,4096]{1,0:T(8,128)(2,1)}, u32[]{:S(2)}, u32[]{:S(2)}) collective-permute-start(bf16[256,4096]{1,0:T(8,128)(2,1)} %get-tuple-element.16), channel_id=1, source_target_pairs={{0,128},{128,0},{1,129},{129,1},{2,130},{130,2},{3,131},{131,3},{4... | collective-permute-start | bytes 6291464 | tf_op jit(solution)/shard_map/rows_swap/ppermute | solution.py:231
  6.6 9.3 %collective-permute-start.2 = (bf16[256,512]{1,0:T(8,128)(2,1)S(1)}, bf16[256,512]{1,0:T(8,128)(2,1)S(1)}, u32[]{:S(2)}, u32[]{:S(2)}) collective-permute-start(bf16[256,512]{1,0:T(8,128)(2,1)S(1)} %copy-done.2), channel_id=1, source_target_pairs={{0,24},{8,0},{16,8},{24,16},{32,56},{40,32},{48,40},{56,48},{64,88... | collective-permute-start | bytes 786440 | tf_op jit(solution)/shard_map/weight_gather/ppermute | solution.py:204
  8.5 19.5 %collective-permute-start.3 = (bf16[256,512]{1,0:T(8,128)(2,1)S(1)}, bf16[256,512]{1,0:T(8,128)(2,1)S(1)}, u32[]{:S(2)}, u32[]{:S(2)}) collective-permute-start(bf16[256,512]{1,0:T(8,128)(2,1)S(1)} %copy-done.2), channel_id=1, source_target_pairs={{0,16},{8,24},{16,0},{24,8},{32,48},{40,56},{48,32},{56,40},{64,80... | collective-permute-start | bytes 786440 | tf_op jit(solution)/shard_map/weight_gather/ppermute | solution.py:204
  10.0 22.9 %collective-permute-start.4 = (bf16[256,512]{1,0:T(8,128)(2,1)S(1)}, bf16[256,512]{1,0:T(8,128)(2,1)S(1)}, u32[]{:S(2)}, u32[]{:S(2)}) collective-permute-start(bf16[256,512]{1,0:T(8,128)(2,1)S(1)} %copy-done.2), channel_id=1, source_target_pairs={{0,8},{8,16},{16,24},{24,0},{32,40},{40,48},{48,56},{56,32},{64,72... | collective-permute-start | bytes 786440 | tf_op jit(solution)/shard_map/weight_gather/ppermute | solution.py:204
  12.8 23.2 %collective-permute-start.5 = (bf16[256,512]{1,0:T(8,128)(2,1)S(1)}, bf16[256,512]{1,0:T(8,128)(2,1)S(1)}, u32[]{:S(2)}, u32[]{:S(2)}) collective-permute-start(bf16[256,512]{1,0:T(8,128)(2,1)S(1)} %copy-done.2), channel_id=1, source_target_pairs={{0,96},{8,104},{16,112},{24,120},{32,0},{40,8},{48,16},{56,24},{64... | collective-permute-start | bytes 786440 | tf_op jit(solution)/shard_map/weight_gather/ppermute | solution.py:32
  15.9 20.9 %collective-permute-start.9 = (bf16[256,512]{1,0:T(8,128)(2,1)S(1)}, bf16[256,512]{1,0:T(8,128)(2,1)S(1)}, u32[]{:S(2)}, u32[]{:S(2)}) collective-permute-start(bf16[256,512]{1,0:T(8,128)(2,1)S(1)} %copy-done.2), channel_id=1, source_target_pairs={{0,32},{8,40},{16,48},{24,56},{32,64},{40,72},{48,80},{56,88},{64,... | collective-permute-start | bytes 786440 | tf_op jit(solution)/shard_map/weight_gather/ppermute | solution.py:33
  27.9 10.1 %collective-permute-start.6 = (bf16[256,512]{1,0:T(8,128)(2,1)S(1)}, bf16[256,512]{1,0:T(8,128)(2,1)S(1)}, u32[]{:S(2)}, u32[]{:S(2)}) collective-permute-start(bf16[256,512]{1,0:T(8,128)(2,1)S(1)} %collective-permute-done.2.refs_1_), channel_id=1, source_target_pairs={{0,96},{8,104},{16,112},{24,120},{32,0},{40,8},{48,16},{56,24},{64... | collective-permute-start | bytes 786440 | tf_op jit(solution)/shard_map/weight_gather/ppermute | solution.py:32
  33.0 9.8 %collective-permute-start.7 = (bf16[256,512]{1,0:T(8,128)(2,1)S(1)}, bf16[256,512]{1,0:T(8,128)(2,1)S(1)}, u32[]{:S(2)}, u32[]{:S(2)}) collective-permute-start(bf16[256,512]{1,0:T(8,128)(2,1)S(1)} %collective-permute-done.3.refs_2_), channel_id=1, source_target_pairs={{0,96},{8,104},{16,112},{24,120},{32,0},{40,8},{48,16},{56,24},{64... | collective-permute-start | bytes 786440 | tf_op jit(solution)/shard_map/weight_gather/ppermute | solution.py:32
  36.0 10.9 %collective-permute-start.8 = (bf16[256,512]{1,0:T(8,128)(2,1)S(1)}, bf16[256,512]{1,0:T(8,128)(2,1)}, u32[]{:S(2)}, u32[]{:S(2)}) collective-permute-start(bf16[256,512]{1,0:T(8,128)(2,1)S(1)} %collective-permute-done.4.refs_3_), channel_id=1, source_target_pairs={{0,96},{8,104},{16,112},{24,120},{32,0},{40,8},{48,16},{56,24},{64... | collective-permute-start | bytes 786440 | tf_op jit(solution)/shard_map/weight_gather/ppermute | solution.py:32
  36.7 11.3 %collective-permute-start.11 = (bf16[256,512]{1,0:T(8,128)(2,1)S(1)}, bf16[256,512]{1,0:T(8,128)(2,1)}, u32[]{:S(2)}, u32[]{:S(2)}) collective-permute-start(bf16[256,512]{1,0:T(8,128)(2,1)S(1)} %collective-permute-done.2.refs_1_), channel_id=1, source_target_pairs={{0,32},{8,40},{16,48},{24,56},{32,64},{40,72},{48,80},{56,88},{64,... | collective-permute-start | bytes 786440 | tf_op jit(solution)/shard_map/weight_gather/ppermute | solution.py:33
  38.0 14.9 %collective-permute-start.15 = (bf16[256,512]{1,0:T(8,128)(2,1)S(1)}, bf16[256,512]{1,0:T(8,128)(2,1)}, u32[]{:S(2)}, u32[]{:S(2)}) collective-permute-start(bf16[256,512]{1,0:T(8,128)(2,1)S(1)} %collective-permute-done.3.refs_2_), channel_id=1, source_target_pairs={{0,32},{8,40},{16,48},{24,56},{32,64},{40,72},{48,80},{56,88},{64,... | collective-permute-start | bytes 786440 | tf_op jit(solution)/shard_map/weight_gather/ppermute | solution.py:33
  43.4 15.1 %collective-permute-start.16 = (bf16[256,512]{1,0:T(8,128)(2,1)S(1)}, bf16[256,512]{1,0:T(8,128)(2,1)}, u32[]{:S(2)}, u32[]{:S(2)}) collective-permute-start(bf16[256,512]{1,0:T(8,128)(2,1)S(1)} %collective-permute-done.4.refs_3_), channel_id=1, source_target_pairs={{0,32},{8,40},{16,48},{24,56},{32,64},{40,72},{48,80},{56,88},{64,... | collective-permute-start | bytes 786440 | tf_op jit(solution)/shard_map/weight_gather/ppermute | solution.py:33
  46.8 22.3 %collective-permute-start.10 = (bf16[256,512]{1,0:T(8,128)(2,1)S(1)}, bf16[256,512]{1,0:T(8,128)(2,1)}, u32[]{:S(2)}, u32[]{:S(2)}) collective-permute-start(bf16[256,512]{1,0:T(8,128)(2,1)S(1)} %collective-permute-done.9.refs_12_), channel_id=1, source_target_pairs={{0,32},{8,40},{16,48},{24,56},{32,64},{40,72},{48,80},{56,88},{64,... | collective-permute-start | bytes 786440 | tf_op jit(solution)/shard_map/weight_gather/ppermute | solution.py:35
  48.0 21.1 %collective-permute-start.12 = (bf16[256,512]{1,0:T(8,128)(2,1)}, bf16[256,512]{1,0:T(8,128)(2,1)}, u32[]{:S(2)}, u32[]{:S(2)}) collective-permute-start(bf16[256,512]{1,0:T(8,128)(2,1)} %collective-permute-done.11.refs_13_), channel_id=1, source_target_pairs={{0,32},{8,40},{16,48},{24,56},{32,64},{40,72},{48,80},{56,88},{64,... | collective-permute-start | bytes 786440 | tf_op jit(solution)/shard_map/weight_gather/ppermute | solution.py:35
  52.9 16.2 %collective-permute-start.13 = (bf16[256,512]{1,0:T(8,128)(2,1)}, bf16[256,512]{1,0:T(8,128)(2,1)}, u32[]{:S(2)}, u32[]{:S(2)}) collective-permute-start(bf16[256,512]{1,0:T(8,128)(2,1)} %copy-done.10), channel_id=1, source_target_pairs={{0,96},{8,104},{16,112},{24,120},{32,0},{40,8},{48,16},{56,24},{64... | collective-permute-start | bytes 786440 | tf_op jit(solution)/shard_map/weight_gather/ppermute | solution.py:36
  58.5 10.6 %collective-permute-start.14 = (bf16[256,512]{1,0:T(8,128)(2,1)}, bf16[256,512]{1,0:T(8,128)(2,1)}, u32[]{:S(2)}, u32[]{:S(2)}) collective-permute-start(bf16[256,512]{1,0:T(8,128)(2,1)} %collective-permute-done.8.refs_7_), channel_id=1, source_target_pairs={{0,96},{8,104},{16,112},{24,120},{32,0},{40,8},{48,16},{56,24},{64... | collective-permute-start | bytes 786440 | tf_op jit(solution)/shard_map/weight_gather/ppermute | solution.py:36
  59.5 15.0 %collective-permute-start = (s32[33,128]{1,0:T(8,128)S(1)}, s32[33,128]{1,0:T(8,128)S(1)}, u32[]{:S(2)}, u32[]{:S(2)}) collective-permute-start(s32[33,128]{1,0:T(8,128)S(1)} %fusion.10), channel_id=1, source_target_pairs={{0,128},{128,0},{1,129},{129,1},{2,130},{130,2},{3,131},{131,3},{4... | collective-permute-start | bytes 50696 | tf_op jit(solution)/shard_map/rows_swap/ppermute | solution.py:234
  62.1 32.2 %all-to-all-start = ((bf16[32,48,256]{2,1,0:T(8,128)(2,1)}), bf16[32,48,256]{2,1,0:T(8,128)(2,1)S(1)}, u32[]{:S(2)}, u32[]{:S(2)}) async-start(bf16[32,48,256]{2,1,0:T(8,128)(2,1)} %bitcast.11), calls=%async_computation | async-start | bytes 1572864 | tf_op jit(solution)/shard_map/columns_exchange/all_to_all | solution.py:265
  86.5 7.8 %collective-permute-start.20 = (f32[32,256]{1,0:T(8,128)S(1)}, f32[32,256]{1,0:T(8,128)S(1)}, u32[]{:S(2)}, u32[]{:S(2)}) collective-permute-start(f32[32,256]{1,0:T(8,128)S(1)} %add.55), channel_id=1, source_target_pairs={{0,1},{1,0},{2,3},{3,2},{4,5},{5,4},{6,7},{7,6},{8,9},{9,8},{10,11... | collective-permute-start | bytes 98312 | tf_op jit(solution)/shard_map/quant_sum/ppermute | solution.py:327
  95.4 8.1 %collective-permute-start.21 = (bf16[128,512]{1,0:T(8,128)(2,1)S(1)}, bf16[128,512]{1,0:T(8,128)(2,1)S(1)}, u32[]{:S(2)}, u32[]{:S(2)}) collective-permute-start(bf16[128,512]{1,0:T(8,128)(2,1)S(1)} %fusion.5.own_ref), channel_id=1, source_target_pairs={{0,96},{8,104},{16,112},{24,120},{32,0},{40,8},{48,16},{56,24},{64... | collective-permute-start | bytes 393224 | tf_op jit(solution)/shard_map/grad_gather/ppermute | solution.py:352
  98.1 10.8 %collective-permute-start.23 = (bf16[128,512]{1,0:T(8,128)(2,1)S(1)}, bf16[128,512]{1,0:T(8,128)(2,1)S(1)}, u32[]{:S(2)}, u32[]{:S(2)}) collective-permute-start(bf16[128,512]{1,0:T(8,128)(2,1)S(1)} %fusion.5.own_ref), channel_id=1, source_target_pairs={{0,24},{8,0},{16,8},{24,16},{32,56},{40,32},{48,40},{56,48},{64,88... | collective-permute-start | bytes 393224 | tf_op jit(solution)/shard_map/grad_gather/ppermute | solution.py:354
  98.7 10.2 %collective-permute-start.24 = (bf16[128,512]{1,0:T(8,128)(2,1)S(1)}, bf16[128,512]{1,0:T(8,128)(2,1)S(1)}, u32[]{:S(2)}, u32[]{:S(2)}) collective-permute-start(bf16[128,512]{1,0:T(8,128)(2,1)S(1)} %fusion.5.own_ref), channel_id=1, source_target_pairs={{0,16},{8,24},{16,0},{24,8},{32,48},{40,56},{48,32},{56,40},{64,80... | collective-permute-start | bytes 393224 | tf_op jit(solution)/shard_map/grad_gather/ppermute | solution.py:354
  101.5 8.1 %collective-permute-start.25 = (bf16[128,512]{1,0:T(8,128)(2,1)S(1)}, bf16[128,512]{1,0:T(8,128)(2,1)S(1)}, u32[]{:S(2)}, u32[]{:S(2)}) collective-permute-start(bf16[128,512]{1,0:T(8,128)(2,1)S(1)} %fusion.5.own_ref), channel_id=1, source_target_pairs={{0,8},{8,16},{16,24},{24,0},{32,40},{40,48},{48,56},{56,32},{64,72... | collective-permute-start | bytes 393224 | tf_op jit(solution)/shard_map/grad_gather/ppermute | solution.py:354
  109.6 12.8 %collective-permute-start.26 = (bf16[2,16,32,256]{3,2,1,0:T(8,128)(2,1)S(1)}, bf16[2,16,32,256]{3,2,1,0:T(8,128)(2,1)S(1)}, u32[]{:S(2)}, u32[]{:S(2)}) collective-permute-start(bf16[2,16,32,256]{3,2,1,0:T(8,128)(2,1)S(1)} %slice.56.own_ref), channel_id=1, source_target_pairs={{0,6},{1,7},{2,0},{3,1},{4,2},{5,3},{6,4},{7,5},{8,14},{9,15},{10,... | collective-permute-start | bytes 1572872 | tf_op jit(solution)/shard_map/columns_round_x/ppermute | solution.py:365
  112.4 13.8 %collective-permute-start.27 = (bf16[2,16,32,256]{3,2,1,0:T(8,128)(2,1)S(1)}, bf16[2,16,32,256]{3,2,1,0:T(8,128)(2,1)S(1)}, u32[]{:S(2)}, u32[]{:S(2)}) collective-permute-start(bf16[2,16,32,256]{3,2,1,0:T(8,128)(2,1)S(1)} %slice.56.own_ref), channel_id=1, source_target_pairs={{0,2},{1,3},{2,4},{3,5},{4,6},{5,7},{6,0},{7,1},{8,10},{9,11},{10,... | collective-permute-start | bytes 1572872 | tf_op jit(solution)/shard_map/columns_round_x/ppermute | solution.py:366
  112.4 13.9 %collective-permute-start.30 = (bf16[384,512]{1,0:T(8,128)(2,1)S(1)}, bf16[384,512]{1,0:T(8,128)(2,1)S(1)}, u32[]{:S(2)}, u32[]{:S(2)}) collective-permute-start(bf16[384,512]{1,0:T(8,128)(2,1)S(1)} %constant_dynamic-update-slice_fusion.line_ref), channel_id=1, source_target_pairs={{0,96},{8,104},{16,112},{24,120},{32,0},{40,8},{48,16},{56,24},{64... | collective-permute-start | bytes 1179656 | tf_op jit(solution)/shard_map/grad_gather/ppermute | solution.py:359
  115.5 13.6 %collective-permute-start.31 = (bf16[384,512]{1,0:T(8,128)(2,1)S(1)}, bf16[384,512]{1,0:T(8,128)(2,1)S(1)}, u32[]{:S(2)}, u32[]{:S(2)}) collective-permute-start(bf16[384,512]{1,0:T(8,128)(2,1)S(1)} %constant_dynamic-update-slice_fusion.line_ref), channel_id=1, source_target_pairs={{0,32},{8,40},{16,48},{24,56},{32,64},{40,72},{48,80},{56,88},{64,... | collective-permute-start | bytes 1179656 | tf_op jit(solution)/shard_map/grad_gather/ppermute | solution.py:358
  122.4 7.7 %collective-permute-start.28 = (bf16[16,32,256]{2,1,0:T(8,128)(2,1)S(1)}, bf16[16,32,256]{2,1,0:T(8,128)(2,1)S(1)}, u32[]{:S(2)}, u32[]{:S(2)}) collective-permute-start(bf16[16,32,256]{2,1,0:T(8,128)(2,1)S(1)} %slice_bitcast_fusion.1), channel_id=1, source_target_pairs={{0,6},{1,7},{2,0},{3,1},{4,2},{5,3},{6,4},{7,5},{8,14},{9,15},{10,... | collective-permute-start | bytes 786440 | tf_op jit(solution)/shard_map/columns_round_x/ppermute | solution.py:367
  126.2 7.7 %collective-permute-start.29 = (bf16[16,32,256]{2,1,0:T(8,128)(2,1)S(1)}, bf16[16,32,256]{2,1,0:T(8,128)(2,1)S(1)}, u32[]{:S(2)}, u32[]{:S(2)}) collective-permute-start(bf16[16,32,256]{2,1,0:T(8,128)(2,1)S(1)} %slice_bitcast_fusion), channel_id=1, source_target_pairs={{0,2},{1,3},{2,4},{3,5},{4,6},{5,7},{6,0},{7,1},{8,10},{9,11},{10,... | collective-permute-start | bytes 786440 | tf_op jit(solution)/shard_map/columns_round_x/ppermute | solution.py:368
  126.3 10.9 %collective-permute-start.34 = (bf16[256,512]{1,0:T(8,128)(2,1)S(1)}, bf16[256,512]{1,0:T(8,128)(2,1)S(1)}, u32[]{:S(2)}, u32[]{:S(2)}) collective-permute-start(bf16[256,512]{1,0:T(8,128)(2,1)S(1)} %slice.64), channel_id=1, source_target_pairs={{0,96},{8,104},{16,112},{24,120},{32,0},{40,8},{48,16},{56,24},{64... | collective-permute-start | bytes 786440 | tf_op jit(solution)/shard_map/grad_gather/ppermute | solution.py:361
  129.1 8.2 %collective-permute-start.32 = (bf16[128,512]{1,0:T(8,128)(2,1)S(1)}, bf16[128,512]{1,0:T(8,128)(2,1)S(1)}, u32[]{:S(2)}, u32[]{:S(2)}) collective-permute-start(bf16[128,512]{1,0:T(8,128)(2,1)S(1)} %collective-permute-done.22.a0_ref), channel_id=1, source_target_pairs={{0,32},{8,40},{16,48},{24,56},{32,64},{40,72},{48,80},{56,88},{64,... | collective-permute-start | bytes 393224 | tf_op jit(solution)/shard_map/grad_gather/ppermute | solution.py:357
  129.1 8.1 %collective-permute-start.33 = (bf16[128,512]{1,0:T(8,128)(2,1)S(1)}, bf16[128,512]{1,0:T(8,128)(2,1)S(1)}, u32[]{:S(2)}, u32[]{:S(2)}) collective-permute-start(bf16[128,512]{1,0:T(8,128)(2,1)S(1)} %slice.63), channel_id=1, source_target_pairs={{0,32},{8,40},{16,48},{24,56},{32,64},{40,72},{48,80},{56,88},{64,... | collective-permute-start | bytes 393224 | tf_op jit(solution)/shard_map/grad_gather/ppermute | solution.py:360
  (25 other events, 553.4 us)

commit v7 on v6

--- a/solution.py
+++ b/solution.py
@@ -26,14 +26,6 @@
 
 def x_from(step):
     return [(t, (t - step * 2) % (X * 2)) for t in range(X * 2)]
-
-
-def round_y(block, upward):
-    below = lax.ppermute(block, "fsdp", y_from(1))
-    above = lax.ppermute(block, "fsdp", y_from(3))
-    if upward:
-        return below, above, lax.ppermute(above, "fsdp", y_from(3))
-    return below, above, lax.ppermute(below, "fsdp", y_from(1))
 
 
 def in_hbm(*arrays):
@@ -125,18 +117,19 @@
 def columns_kernel(where_ref, own_ref, after_ref, before_ref, far_a_ref, far_b_ref, out_ref, held):
     group, y, z, x = where_ref[0], where_ref[1], where_ref[2], where_ref[3]
     other = 1 - group
-    strip, block = own_ref.shape[2], own_ref.shape[3]
-    span = strip * X
+    block = own_ref.shape[3]
+    span = held.shape[0]
+    strip = span // X
 
     def body(step, carry):
         place = lax.rem(y + step // Z, Y) * Z + lax.rem(z + lax.rem(step, Z), Z)
         for shift, ref in ((0, own_ref), (1, after_ref), (3, before_ref)):
             rows = pl.ds(pl.multiple_of(lax.rem(x + shift, X) * strip, strip), strip)
-            held[rows, :block] = ref[group, place]
-            held[rows, block:] = ref[other, place]
+            held[rows, :block] = ref[group, place, :strip]
+            held[rows, block:] = ref[other, place, :strip]
         rows = pl.ds(pl.multiple_of(lax.rem(x + 2, X) * strip, strip), strip)
-        held[rows, pl.ds(pl.multiple_of(group * block, block), block)] = far_a_ref[place]
-        held[rows, pl.ds(pl.multiple_of(other * block, block), block)] = far_b_ref[place]
+        held[rows, pl.ds(pl.multiple_of(group * block, block), block)] = far_a_ref[place, :strip]
+        held[rows, pl.ds(pl.multiple_of(other * block, block), block)] = far_b_ref[place, :strip]
         out_ref[:, pl.ds(pl.multiple_of(step * span, span), span)] = held[...].T
         return carry
 
@@ -203,7 +196,16 @@
         lines = [torso_weight] + [
             lax.ppermute(torso_weight, "fsdp", z_from(k)) for k in range(1, Z)
         ]
-        rounds = [round_y(line, k < 2) for k, line in enumerate(lines)]
+        near = [
+            (lax.ppermute(line, "fsdp", y_from(1)), lax.ppermute(line, "fsdp", y_from(3)))
+            for line in lines
+        ]
+        near = lax.optimization_barrier(near)
+        far = [
+            lax.ppermute(above, "fsdp", y_from(3)) if k < 2 else lax.ppermute(below, "fsdp", y_from(1))
+            for k, (below, above) in enumerate(near)
+        ]
+        rounds = [(below, above, last) for (below, above), last in zip(near, far)]
         chunks = lines + [rounds[k][j] for j in (0, 2, 1) for k in range(Z)]
 
     with jax.named_scope("rows_swap"):
@@ -228,6 +230,7 @@
             name="norm",
         )(where, *in_hbm(values, norm_gain[None, :]))
     with jax.named_scope("rows_swap"):
+        normed_send, _ = lax.optimization_barrier((normed_send, near[0]))
         normed_got = lax.ppermute(normed_send, "grp", SWAP)
         ints = jnp.concatenate([fractions[0].T, actions[0][None, :]], 0)
         kept = lax.dynamic_slice_in_dim(ints, own_rows, half, 1)
@@ -266,7 +269,6 @@
             pieces.reshape(2 * shard_total, strip + 16, block), ("grp", "fsdp"), 0, 0, tiled=True
         ).reshape(2, shard_total, strip + 16, block)
         counts = jnp.sum(pieces[0, :, strip, :shard_total].astype(jnp.float32), axis=0)
-        pieces = pieces[:, :, :strip]
 
     with jax.named_scope("counts"):
         inverse = float(rows_block) / counts
@@ -308,7 +310,7 @@
             bytes_accessed=2 * side * features + 4 * side * rows_block + 8 * rows_block * features,
         ),
         name="preact",
-    )(where, *in_hbm(normed_own, normed_got, *chunks))
+    )(where, *in_hbm(normed_own, normed_got, *chunks[:8]), *chunks[8:12], *in_hbm(*chunks[12:]))
     preact = keep + lax.ppermute(send, "grp", SWAP)
     weighted = (jax.nn.silu(preact) * picked).astype(jnp.bfloat16)
     table_values = lax.dot_general(
@@ -360,7 +362,7 @@
         f1 = lax.ppermute(a1[:half], "fsdp", y_from(3))
         f2 = lax.ppermute(b1[half:], "fsdp", y_from(1))
 
-    pieces, _ = lax.optimization_barrier((pieces, (b0, a0, pieces_z[0])))
+    pieces, _ = lax.optimization_barrier((pieces, grad_preact))
     with jax.named_scope("columns_round_x"):
         after = lax.ppermute(pieces, "tp", x_from(1))
         before = lax.ppermute(pieces, "tp", x_from(3))

time: 164 us -> 154 us (0.939)
  waiting for transfers between devices: 56.3 us -> 43.5 us
  starting transfers between devices: 60.6 us -> 66.1 us
    ppermute x12, waiting for transfers between devices: 15.8 us -> 2.93 us  [the longest x4 2.91 us: shards(): lax.ppermute(line, 'fsdp', y_from(3))]
    ppermute x1, waiting for transfers between devices: 6.92 us -> 0.01 us  [shards(): after = lax.ppermute(pieces, 'tp', x_from(1))]
    ppermute x1, waiting for transfers between devices: 0.01 us -> 5.64 us  [shards(): b1 = lax.ppermute(line, 'fsdp', y_from(1))]
    ppermute x1, waiting for transfers between devices: 3.79 us -> 0.01 us  [shards(): far_b = lax.ppermute(before[1], 'tp', x_from(3))]
    ppermute x1, starting transfers between devices: 3.77 us -> 0.19 us  [shards(): far_a = lax.ppermute(after[0], 'tp', x_from(1))]
    ppermute x1, waiting for transfers between devices: 0.88 us -> 4.02 us  [shards(): a0 = lax.ppermute(grad_preact, 'fsdp', y_from(3))]
    ppermute x3, starting transfers between devices: 5.29 us -> 8.07 us  [shards(): lax.ppermute(grad_preact, 'fsdp', z_from(k))]
    ppermute x1, waiting for transfers between devices: 0.01 us -> 2.66 us  [shards(): b0 = lax.ppermute(grad_preact, 'fsdp', y_from(1))]
  transfers between devices with their start and end apart: 37 -> 37, of which waited for: 17 -> 16; matrix products, arithmetic and copies ran while one was open for 2% -> 1% of each run, Pallas kernels for 7% -> 11%
where the time goes in v7:
time: 154 us
  starting transfers between devices  66.1 us (43%)
  waiting for transfers between devices  43.5 us (28%)
  blocking collectives  21.2 us (14%)
  Pallas kernels  17.2 us (11%)
  other arithmetic  2.54 us (2%)
    all_to_all x1, blocking collectives, shards(): lax.all_to_all(updated, 'tp', split_axis=0, concat_axis=1, tiled=True)  21.2 us
    ppermute x3, waiting for transfers between devices, shards(): lax.ppermute(torso_weight, 'fsdp', z_from(k))  10.9 us
    ppermute x4, starting transfers between devices, shards(): lax.ppermute(line, 'fsdp', y_from(1))  10.8 us
    all_to_all x1, starting transfers between devices, shards(): lax.all_to_all(pieces.reshape(2 * shard_total, strip + 16, block), ('grp'...  8.92 us
    ppermute x3, starting transfers between devices, shards(): lax.ppermute(grad_preact, 'fsdp', z_from(k))  8.07 us
    ppermute x3, starting transfers between devices, shards(): lax.ppermute(torso_weight, 'fsdp', z_from(k))  8.01 us
    ppermute x1, starting transfers between devices, shards(): lax.ppermute(quant, 'tp', [(t, t ^ 1) for t in range(2 * X)])  6.54 us
    pallas_call x1, Pallas kernels, shards(): pl.pallas_call(norm_kernel, grid=(rows_block // tile,), out_shape=(jax.Sh...  5.73 us
  transfers between devices with their start and end apart: 37, of which 16 were waited for; matrix products, arithmetic and copies ran while one was open for 1% of the time, Pallas kernels for 11%

profile of v7, /device:TPU:32, one launch (start us, length us, event | category | flops | bytes accessed | tf_op | source)
XLA Modules:
  0.0 153.8 jit_solution(15704750476700551615)
XLA Ops:
  0.6 1.9 %collective-permute-start.3 = (bf16[256,512]{1,0:T(8,128)(2,1)}, bf16[256,512]{1,0:T(8,128)(2,1)S(1)}, u32[]{:S(2)}, u32[]{:S(2)}) collective-permute-start(bf16[256,512]{1,0:T(8,128)(2,1)} %refs_0_.1), channel_id=1, source_target_pairs={{0,24},{8,0},{16,8},{24,16},{32,56},{40,32},{48,40},{56,48},{64,88... | collective-permute-start | bytes 786440 | tf_op jit(solution)/shard_map/weight_gather/ppermute | solution.py:197
  3.8 3.3 %collective-permute-start.6 = (bf16[256,512]{1,0:T(8,128)(2,1)}, bf16[256,512]{1,0:T(8,128)(2,1)S(1)}, u32[]{:S(2)}, u32[]{:S(2)}) collective-permute-start(bf16[256,512]{1,0:T(8,128)(2,1)} %refs_0_.1), channel_id=1, source_target_pairs={{0,16},{8,24},{16,0},{24,8},{32,48},{40,56},{48,32},{56,40},{64,80... | collective-permute-start | bytes 786440 | tf_op jit(solution)/shard_map/weight_gather/ppermute | solution.py:197
  7.1 2.8 %collective-permute-start.9 = (bf16[256,512]{1,0:T(8,128)(2,1)}, bf16[256,512]{1,0:T(8,128)(2,1)S(1)}, u32[]{:S(2)}, u32[]{:S(2)}) collective-permute-start(bf16[256,512]{1,0:T(8,128)(2,1)} %refs_0_.1), channel_id=1, source_target_pairs={{0,8},{8,16},{16,24},{24,0},{32,40},{40,48},{48,56},{56,32},{64,72... | collective-permute-start | bytes 786440 | tf_op jit(solution)/shard_map/weight_gather/ppermute | solution.py:197
  9.9 3.7 %collective-permute-start.4 = (bf16[256,512]{1,0:T(8,128)(2,1)S(1)}, bf16[256,512]{1,0:T(8,128)(2,1)S(1)}, u32[]{:S(2)}, u32[]{:S(2)}) collective-permute-start(bf16[256,512]{1,0:T(8,128)(2,1)S(1)} %collective-permute-done.3.refs_1_), channel_id=1, source_target_pairs={{0,96},{8,104},{16,112},{24,120},{32,0},{40,8},{48,16},{56,24},{64... | collective-permute-start | bytes 786440 | tf_op jit(solution)/shard_map/weight_gather/ppermute | solution.py:200
  13.7 8.4 %collective-permute-done.6.refs_2_ = bf16[256,512]{1,0:T(8,128)(2,1)S(1)} collective-permute-done((bf16[256,512]{1,0:T(8,128)(2,1)}, bf16[256,512]{1,0:T(8,128)(2,1)S(1)}, u32[]{:S(2)}, u32[]{:S(2)}) %collective-permute-start.6) | collective-permute-done | bytes 262176 | tf_op jit(solution)/shard_map/weight_gather/ppermute | solution.py:197
  22.1 3.1 %collective-permute-start.7 = (bf16[256,512]{1,0:T(8,128)(2,1)S(1)}, bf16[256,512]{1,0:T(8,128)(2,1)}, u32[]{:S(2)}, u32[]{:S(2)}) collective-permute-start(bf16[256,512]{1,0:T(8,128)(2,1)S(1)} %collective-permute-done.6.refs_2_), channel_id=1, source_target_pairs={{0,96},{8,104},{16,112},{24,120},{32,0},{40,8},{48,16},{56,24},{64... | collective-permute-start | bytes 786440 | tf_op jit(solution)/shard_map/weight_gather/ppermute | solution.py:200
  25.2 2.4 %collective-permute-done.9.refs_3_ = bf16[256,512]{1,0:T(8,128)(2,1)S(1)} collective-permute-done((bf16[256,512]{1,0:T(8,128)(2,1)}, bf16[256,512]{1,0:T(8,128)(2,1)S(1)}, u32[]{:S(2)}, u32[]{:S(2)}) %collective-permute-start.9) | collective-permute-done | bytes 262176 | tf_op jit(solution)/shard_map/weight_gather/ppermute | solution.py:197
  27.6 2.7 %collective-permute-start.10 = (bf16[256,512]{1,0:T(8,128)(2,1)S(1)}, bf16[256,512]{1,0:T(8,128)(2,1)}, u32[]{:S(2)}, u32[]{:S(2)}) collective-permute-start(bf16[256,512]{1,0:T(8,128)(2,1)S(1)} %collective-permute-done.9.refs_3_), channel_id=1, source_target_pairs={{0,96},{8,104},{16,112},{24,120},{32,0},{40,8},{48,16},{56,24},{64... | collective-permute-start | bytes 786440 | tf_op jit(solution)/shard_map/weight_gather/ppermute | solution.py:200
  30.5 5.7 %norm.1 = (bf16[256,4096]{1,0:T(8,128)(2,1)S(1)}, bf16[256,4096]{1,0:T(8,128)(2,1)}) custom-call(s32[4]{0:T(128)S(1)} %pad_add_fusion.1.where_ref, bf16[256,8192]{1,0:T(8,128)(2,1)} %bitcast.33, f32[1,8192]{1,0:T(1,128)} %bitcast.39), custom_call_target="tpu_custom_call" | custom-call | flops 12582912 | bytes 8388608 | tf_op jit(solution)/shard_map/rows_swap/norm/pallas_call | solution.py:214
  36.3 2.9 %collective-permute-done.11.refs_15_ = bf16[256,512]{1,0:T(8,128)(2,1)} collective-permute-done((bf16[256,512]{1,0:T(8,128)(2,1)S(1)}, bf16[256,512]{1,0:T(8,128)(2,1)}, u32[]{:S(2)}, u32[]{:S(2)}) %collective-permute-start.11) | collective-permute-done | bytes 262176 | tf_op jit(solution)/shard_map/weight_gather/ppermute | solution.py:200
  39.5 3.2 %collective-permute-start.15 = (bf16[256,512]{1,0:T(8,128)(2,1)}, bf16[256,512]{1,0:T(8,128)(2,1)S(1)}, u32[]{:S(2)}, u32[]{:S(2)}) collective-permute-start(bf16[256,512]{1,0:T(8,128)(2,1)} %collective-permute-done.7.refs_6_), channel_id=1, source_target_pairs={{0,96},{8,104},{16,112},{24,120},{32,0},{40,8},{48,16},{56,24},{64... | collective-permute-start | bytes 786440 | tf_op jit(solution)/shard_map/weight_gather/ppermute | solution.py:205
  42.7 1.9 %collective-permute-start.16 = (bf16[256,512]{1,0:T(8,128)(2,1)}, bf16[256,512]{1,0:T(8,128)(2,1)S(1)}, u32[]{:S(2)}, u32[]{:S(2)}) collective-permute-start(bf16[256,512]{1,0:T(8,128)(2,1)} %collective-permute-done.10.refs_7_), channel_id=1, source_target_pairs={{0,96},{8,104},{16,112},{24,120},{32,0},{40,8},{48,16},{56,24},{64... | collective-permute-start | bytes 786440 | tf_op jit(solution)/shard_map/weight_gather/ppermute | solution.py:205
  45.1 2.6 %pieces.1 = bf16[2,16,48,256]{3,2,1,0:T(8,128)(2,1)} custom-call(s32[4]{0:T(128)S(1)} %pad_add_fusion.1.where_ref, bf16[256,4096]{1,0:T(8,128)(2,1)S(1)} %get-tuple-element.24.own_ref, bf16[256,4096]{1,0:T(8,128)(2,1)} %collective-permute-done.12.got_ref, bf16[16,256]{1,0:T(8,128)(2,1)S(1)} %pad.4.count_ref), custom_call_target="tpu_custom_call" | custom-call | bytes 1048576 | tf_op jit(solution)/shard_map/columns_exchange/pieces/pallas_call | solution.py:253
  47.7 8.9 %all-to-all-start = ((bf16[32,48,256]{2,1,0:T(8,128)(2,1)}), bf16[32,48,256]{2,1,0:T(8,128)(2,1)S(1)}, u32[]{:S(2)}, u32[]{:S(2)}) async-start(bf16[32,48,256]{2,1,0:T(8,128)(2,1)} %bitcast.11), calls=%async_computation | async-start | bytes 1572864 | tf_op jit(solution)/shard_map/columns_exchange/all_to_all | solution.py:268
  56.7 5.2 %preact.1 = (f32[256,512]{1,0:T(8,128)S(1)}, f32[256,512]{1,0:T(8,128)S(1)}) custom-call(s32[4]{0:T(128)S(1)} %pad_add_fusion.1.where_ref, bf16[256,4096]{1,0:T(8,128)(2,1)} %copy-done.1, bf16[256,4096]{1,0:T(8,128)(2,1)} %collective-permute-done.12.got_ref, bf16[256,512]{1,0:T(8,128)(2,1)} %refs_0_.1, bf16[256,512]{1,0:T(8,128)(2,1)} %copy-done.3, ...), custom_call_target="tpu_custom_call" | custom-call | flops 2147483648 | bytes 9437184 | tf_op jit(solution)/shard_map/preact/pallas_call | solution.py:295
  66.2 2.4 %collective-permute-done.18 = f32[32,256]{1,0:T(8,128)S(1)} collective-permute-done((f32[32,256]{1,0:T(8,128)S(1)}, f32[32,256]{1,0:T(8,128)S(1)}, u32[]{:S(2)}, u32[]{:S(2)}) %collective-permute-start.18) | collective-permute-done | bytes 32800 | tf_op jit(solution)/shard_map/quant_sum/ppermute | solution.py:328
  68.6 3.0 %collective-permute-start.19 = (f32[32,256]{1,0:T(8,128)S(1)}, f32[32,256]{1,0:T(8,128)S(1)}, u32[]{:S(2)}, u32[]{:S(2)}) collective-permute-start(f32[32,256]{1,0:T(8,128)S(1)} %add.54), channel_id=1, source_target_pairs={{0,4},{1,5},{2,6},{3,7},{4,0},{5,1},{6,2},{7,3},{8,12},{9,13},{10,... | collective-permute-start | bytes 98312 | tf_op jit(solution)/shard_map/quant_sum/ppermute | solution.py:328
  71.7 2.3 %collective-permute-done.19 = f32[32,256]{1,0:T(8,128)S(1)} collective-permute-done((f32[32,256]{1,0:T(8,128)S(1)}, f32[32,256]{1,0:T(8,128)S(1)}, u32[]{:S(2)}, u32[]{:S(2)}) %collective-permute-start.19) | collective-permute-done | bytes 32800 | tf_op jit(solution)/shard_map/quant_sum/ppermute | solution.py:328
  74.0 6.5 %collective-permute-start.20 = (f32[32,256]{1,0:T(8,128)S(1)}, f32[32,256]{1,0:T(8,128)S(1)}, u32[]{:S(2)}, u32[]{:S(2)}) collective-permute-start(f32[32,256]{1,0:T(8,128)S(1)} %add.55), channel_id=1, source_target_pairs={{0,1},{1,0},{2,3},{3,2},{4,5},{5,4},{6,7},{7,6},{8,9},{9,8},{10,11... | collective-permute-start | bytes 98312 | tf_op jit(solution)/shard_map/quant_sum/ppermute | solution.py:329
  83.4 2.8 %collective-permute-start.21 = (bf16[2,16,48,256]{3,2,1,0:T(8,128)(2,1)S(1)}, bf16[2,16,48,256]{3,2,1,0:T(8,128)(2,1)S(1)}, u32[]{:S(2)}, u32[]{:S(2)}) collective-permute-start(bf16[2,16,48,256]{3,2,1,0:T(8,128)(2,1)S(1)} %bitcast.30), channel_id=1, source_target_pairs={{0,6},{1,7},{2,0},{3,1},{4,2},{5,3},{6,4},{7,5},{8,14},{9,15},{10,... | collective-permute-start | bytes 2359304 | tf_op jit(solution)/shard_map/columns_round_x/ppermute | solution.py:367
  86.2 6.6 %collective-permute-start.25 = (bf16[128,512]{1,0:T(8,128)(2,1)S(1)}, bf16[128,512]{1,0:T(8,128)(2,1)S(1)}, u32[]{:S(2)}, u32[]{:S(2)}) collective-permute-start(bf16[128,512]{1,0:T(8,128)(2,1)S(1)} %fusion.5.own_ref), channel_id=1, source_target_pairs={{0,24},{8,0},{16,8},{24,16},{32,56},{40,32},{48,40},{56,48},{64,88... | collective-permute-start | bytes 393224 | tf_op jit(solution)/shard_map/grad_gather/ppermute | solution.py:356
  94.3 3.4 %collective-permute-done.25 = bf16[128,512]{1,0:T(8,128)(2,1)S(1)} collective-permute-done((bf16[128,512]{1,0:T(8,128)(2,1)S(1)}, bf16[128,512]{1,0:T(8,128)(2,1)S(1)}, u32[]{:S(2)}, u32[]{:S(2)}) %collective-permute-start.25) | collective-permute-done | bytes 131104 | tf_op jit(solution)/shard_map/grad_gather/ppermute | solution.py:356
  97.8 3.3 %collective-permute-start.28 = (bf16[128,512]{1,0:T(8,128)(2,1)S(1)}, bf16[128,512]{1,0:T(8,128)(2,1)S(1)}, u32[]{:S(2)}, u32[]{:S(2)}) collective-permute-start(bf16[128,512]{1,0:T(8,128)(2,1)S(1)} %fusion.5.own_ref), channel_id=1, source_target_pairs={{0,96},{8,104},{16,112},{24,120},{32,0},{40,8},{48,16},{56,24},{64... | collective-permute-start | bytes 393224 | tf_op jit(solution)/shard_map/grad_gather/ppermute | solution.py:354
  101.1 2.7 %collective-permute-done.28.b0_ref = bf16[128,512]{1,0:T(8,128)(2,1)S(1)} collective-permute-done((bf16[128,512]{1,0:T(8,128)(2,1)S(1)}, bf16[128,512]{1,0:T(8,128)(2,1)S(1)}, u32[]{:S(2)}, u32[]{:S(2)}) %collective-permute-start.28) | collective-permute-done | bytes 131104 | tf_op jit(solution)/shard_map/grad_gather/ppermute | solution.py:354
  103.8 4.0 %collective-permute-done.29.a0_ref = bf16[128,512]{1,0:T(8,128)(2,1)S(1)} collective-permute-done((bf16[128,512]{1,0:T(8,128)(2,1)S(1)}, bf16[128,512]{1,0:T(8,128)(2,1)S(1)}, u32[]{:S(2)}, u32[]{:S(2)}) %collective-permute-start.29) | collective-permute-done | bytes 131104 | tf_op jit(solution)/shard_map/grad_gather/ppermute | solution.py:355
  110.5 1.7 %collective-permute-start.24 = (bf16[16,48,256]{2,1,0:T(8,128)(2,1)S(1)}, bf16[16,48,256]{2,1,0:T(8,128)(2,1)S(1)}, u32[]{:S(2)}, u32[]{:S(2)}) collective-permute-start(bf16[16,48,256]{2,1,0:T(8,128)(2,1)S(1)} %slice_bitcast_fusion), channel_id=1, source_target_pairs={{0,2},{1,3},{2,4},{3,5},{4,6},{5,7},{6,0},{7,1},{8,10},{9,11},{10,... | collective-permute-start | bytes 1179656 | tf_op jit(solution)/shard_map/columns_round_x/ppermute | solution.py:370
  112.2 5.6 %collective-permute-done.30.b1_ref = bf16[384,512]{1,0:T(8,128)(2,1)S(1)} collective-permute-done((bf16[384,512]{1,0:T(8,128)(2,1)S(1)}, bf16[384,512]{1,0:T(8,128)(2,1)S(1)}, u32[]{:S(2)}, u32[]{:S(2)}) %collective-permute-start.30) | collective-permute-done | bytes 393248 | tf_op jit(solution)/shard_map/grad_gather/ppermute | solution.py:361
  117.9 3.1 %collective-permute-start.34 = (bf16[256,512]{1,0:T(8,128)(2,1)S(1)}, bf16[256,512]{1,0:T(8,128)(2,1)S(1)}, u32[]{:S(2)}, u32[]{:S(2)}) collective-permute-start(bf16[256,512]{1,0:T(8,128)(2,1)S(1)} %slice.59), channel_id=1, source_target_pairs={{0,96},{8,104},{16,112},{24,120},{32,0},{40,8},{48,16},{56,24},{64... | collective-permute-start | bytes 786440 | tf_op jit(solution)/shard_map/grad_gather/ppermute | solution.py:363
  121.1 2.4 %columns.1.cols_ref = bf16[512,2048]{1,0:T(8,128)(2,1)S(1)} custom-call(s32[4]{0:T(128)S(1)} %pad_add_fusion.1.where_ref, bf16[2,16,48,256]{3,2,1,0:T(8,128)(2,1)S(1)} %bitcast.32, bf16[2,16,48,256]{3,2,1,0:T(8,128)(2,1)S(1)} %collective-permute-done.21.after_ref, bf16[2,16,48,256]{3,2,1,0:T(8,128)(2,1)S(1)} %collective-permute-done.22.before_ref, ...), custom_call_target="tpu_custom_call" | custom-call | bytes 4194304 | tf_op jit(solution)/shard_map/columns_round_x/columns/pallas_call | solution.py:371
  124.5 2.6 %collective-permute-done.32.f0_ref = bf16[128,512]{1,0:T(8,128)(2,1)S(1)} collective-permute-done((bf16[128,512]{1,0:T(8,128)(2,1)S(1)}, bf16[128,512]{1,0:T(8,128)(2,1)S(1)}, u32[]{:S(2)}, u32[]{:S(2)}) %collective-permute-start.32) | collective-permute-done | bytes 131104 | tf_op jit(solution)/shard_map/grad_gather/ppermute | solution.py:359
  129.0 1.9 %collective-permute-done.35 = f32[256,512]{1,0:T(8,128)S(1)} collective-permute-done((f32[256,512]{1,0:T(8,128)S(1)}, f32[256,512]{1,0:T(8,128)S(1)}, u32[]{:S(2)}, u32[]{:S(2)}) %collective-permute-start.35) | collective-permute-done | bytes 524320 | tf_op jit(solution)/shard_map/ppermute | solution.py:411
  131.9 21.2 %all_to_all.24 = bf16[8,32,512]{2,1,0:T(8,128)(2,1)S(1)} all-to-all(bf16[8,32,512]{2,1,0:T(8,128)(2,1)S(1)} %bitcast.35), channel_id=1, replica_groups=mesh['grp'=2,'fsdp'=16,'tp'=8] {'tp'}, dimensions={0} | all-to-all | bytes 524288 | tf_op jit(solution)/shard_map/all_to_all | solution.py:413
  (116 shorter events, 18.3 us)
Async XLA Ops:
  0.6 9.3 %collective-permute-start.3 = (bf16[256,512]{1,0:T(8,128)(2,1)}, bf16[256,512]{1,0:T(8,128)(2,1)S(1)}, u32[]{:S(2)}, u32[]{:S(2)}) collective-permute-start(bf16[256,512]{1,0:T(8,128)(2,1)} %refs_0_.1), channel_id=1, source_target_pairs={{0,24},{8,0},{16,8},{24,16},{32,56},{40,32},{48,40},{56,48},{64,88... | collective-permute-start | bytes 786440 | tf_op jit(solution)/shard_map/weight_gather/ppermute | solution.py:197
  2.6 11.1 %collective-permute-start.1 = (bf16[256,512]{1,0:T(8,128)(2,1)}, bf16[256,512]{1,0:T(8,128)(2,1)S(1)}, u32[]{:S(2)}, u32[]{:S(2)}) collective-permute-start(bf16[256,512]{1,0:T(8,128)(2,1)} %refs_0_.1), channel_id=1, source_target_pairs={{0,96},{8,104},{16,112},{24,120},{32,0},{40,8},{48,16},{56,24},{64... | collective-permute-start | bytes 786440 | tf_op jit(solution)/shard_map/weight_gather/ppermute | solution.py:200
  3.8 18.3 %collective-permute-start.6 = (bf16[256,512]{1,0:T(8,128)(2,1)}, bf16[256,512]{1,0:T(8,128)(2,1)S(1)}, u32[]{:S(2)}, u32[]{:S(2)}) collective-permute-start(bf16[256,512]{1,0:T(8,128)(2,1)} %refs_0_.1), channel_id=1, source_target_pairs={{0,16},{8,24},{16,0},{24,8},{32,48},{40,56},{48,32},{56,40},{64,80... | collective-permute-start | bytes 786440 | tf_op jit(solution)/shard_map/weight_gather/ppermute | solution.py:197
  7.1 18.1 %collective-permute-start.2 = (bf16[256,512]{1,0:T(8,128)(2,1)}, bf16[256,512]{1,0:T(8,128)(2,1)}, u32[]{:S(2)}, u32[]{:S(2)}) collective-permute-start(bf16[256,512]{1,0:T(8,128)(2,1)} %refs_0_.1), channel_id=1, source_target_pairs={{0,32},{8,40},{16,48},{24,56},{32,64},{40,72},{48,80},{56,88},{64,... | collective-permute-start | bytes 786440 | tf_op jit(solution)/shard_map/weight_gather/ppermute | solution.py:200
  7.1 20.5 %collective-permute-start.9 = (bf16[256,512]{1,0:T(8,128)(2,1)}, bf16[256,512]{1,0:T(8,128)(2,1)S(1)}, u32[]{:S(2)}, u32[]{:S(2)}) collective-permute-start(bf16[256,512]{1,0:T(8,128)(2,1)} %refs_0_.1), channel_id=1, source_target_pairs={{0,8},{8,16},{16,24},{24,0},{32,40},{40,48},{48,56},{56,32},{64,72... | collective-permute-start | bytes 786440 | tf_op jit(solution)/shard_map/weight_gather/ppermute | solution.py:197
  9.9 20.4 %collective-permute-start.4 = (bf16[256,512]{1,0:T(8,128)(2,1)S(1)}, bf16[256,512]{1,0:T(8,128)(2,1)S(1)}, u32[]{:S(2)}, u32[]{:S(2)}) collective-permute-start(bf16[256,512]{1,0:T(8,128)(2,1)S(1)} %collective-permute-done.3.refs_1_), channel_id=1, source_target_pairs={{0,96},{8,104},{16,112},{24,120},{32,0},{40,8},{48,16},{56,24},{64... | collective-permute-start | bytes 786440 | tf_op jit(solution)/shard_map/weight_gather/ppermute | solution.py:200
  13.7 22.6 %collective-permute-start.5 = (bf16[256,512]{1,0:T(8,128)(2,1)S(1)}, bf16[256,512]{1,0:T(8,128)(2,1)}, u32[]{:S(2)}, u32[]{:S(2)}) collective-permute-start(bf16[256,512]{1,0:T(8,128)(2,1)S(1)} %collective-permute-done.3.refs_1_), channel_id=1, source_target_pairs={{0,32},{8,40},{16,48},{24,56},{32,64},{40,72},{48,80},{56,88},{64,... | collective-permute-start | bytes 786440 | tf_op jit(solution)/shard_map/weight_gather/ppermute | solution.py:200
  22.1 14.1 %collective-permute-start.7 = (bf16[256,512]{1,0:T(8,128)(2,1)S(1)}, bf16[256,512]{1,0:T(8,128)(2,1)}, u32[]{:S(2)}, u32[]{:S(2)}) collective-permute-start(bf16[256,512]{1,0:T(8,128)(2,1)S(1)} %collective-permute-done.6.refs_2_), channel_id=1, source_target_pairs={{0,96},{8,104},{16,112},{24,120},{32,0},{40,8},{48,16},{56,24},{64... | collective-permute-start | bytes 786440 | tf_op jit(solution)/shard_map/weight_gather/ppermute | solution.py:200
  25.2 11.1 %collective-permute-start.8 = (bf16[256,512]{1,0:T(8,128)(2,1)S(1)}, bf16[256,512]{1,0:T(8,128)(2,1)S(1)}, u32[]{:S(2)}, u32[]{:S(2)}) collective-permute-start(bf16[256,512]{1,0:T(8,128)(2,1)S(1)} %collective-permute-done.6.refs_2_), channel_id=1, source_target_pairs={{0,32},{8,40},{16,48},{24,56},{32,64},{40,72},{48,80},{56,88},{64,... | collective-permute-start | bytes 786440 | tf_op jit(solution)/shard_map/weight_gather/ppermute | solution.py:200
  27.6 8.6 %collective-permute-start.10 = (bf16[256,512]{1,0:T(8,128)(2,1)S(1)}, bf16[256,512]{1,0:T(8,128)(2,1)}, u32[]{:S(2)}, u32[]{:S(2)}) collective-permute-start(bf16[256,512]{1,0:T(8,128)(2,1)S(1)} %collective-permute-done.9.refs_3_), channel_id=1, source_target_pairs={{0,96},{8,104},{16,112},{24,120},{32,0},{40,8},{48,16},{56,24},{64... | collective-permute-start | bytes 786440 | tf_op jit(solution)/shard_map/weight_gather/ppermute | solution.py:200
  30.3 8.9 %collective-permute-start.11 = (bf16[256,512]{1,0:T(8,128)(2,1)S(1)}, bf16[256,512]{1,0:T(8,128)(2,1)}, u32[]{:S(2)}, u32[]{:S(2)}) collective-permute-start(bf16[256,512]{1,0:T(8,128)(2,1)S(1)} %collective-permute-done.9.refs_3_), channel_id=1, source_target_pairs={{0,32},{8,40},{16,48},{24,56},{32,64},{40,72},{48,80},{56,88},{64,... | collective-permute-start | bytes 786440 | tf_op jit(solution)/shard_map/weight_gather/ppermute | solution.py:200
  39.3 17.3 %collective-permute-start.13 = (bf16[256,512]{1,0:T(8,128)(2,1)}, bf16[256,512]{1,0:T(8,128)(2,1)S(1)}, u32[]{:S(2)}, u32[]{:S(2)}) collective-permute-start(bf16[256,512]{1,0:T(8,128)(2,1)} %collective-permute-done.2.refs_12_), channel_id=1, source_target_pairs={{0,32},{8,40},{16,48},{24,56},{32,64},{40,72},{48,80},{56,88},{64,... | collective-permute-start | bytes 786440 | tf_op jit(solution)/shard_map/weight_gather/ppermute | solution.py:205
  39.4 17.2 %collective-permute-start.14 = (bf16[256,512]{1,0:T(8,128)(2,1)}, bf16[256,512]{1,0:T(8,128)(2,1)S(1)}, u32[]{:S(2)}, u32[]{:S(2)}) collective-permute-start(bf16[256,512]{1,0:T(8,128)(2,1)} %collective-permute-done.5.refs_13_), channel_id=1, source_target_pairs={{0,32},{8,40},{16,48},{24,56},{32,64},{40,72},{48,80},{56,88},{64,... | collective-permute-start | bytes 786440 | tf_op jit(solution)/shard_map/weight_gather/ppermute | solution.py:205
  39.5 17.1 %collective-permute-start.15 = (bf16[256,512]{1,0:T(8,128)(2,1)}, bf16[256,512]{1,0:T(8,128)(2,1)S(1)}, u32[]{:S(2)}, u32[]{:S(2)}) collective-permute-start(bf16[256,512]{1,0:T(8,128)(2,1)} %collective-permute-done.7.refs_6_), channel_id=1, source_target_pairs={{0,96},{8,104},{16,112},{24,120},{32,0},{40,8},{48,16},{56,24},{64... | collective-permute-start | bytes 786440 | tf_op jit(solution)/shard_map/weight_gather/ppermute | solution.py:205
  42.7 13.9 %collective-permute-start.16 = (bf16[256,512]{1,0:T(8,128)(2,1)}, bf16[256,512]{1,0:T(8,128)(2,1)S(1)}, u32[]{:S(2)}, u32[]{:S(2)}) collective-permute-start(bf16[256,512]{1,0:T(8,128)(2,1)} %collective-permute-done.10.refs_7_), channel_id=1, source_target_pairs={{0,96},{8,104},{16,112},{24,120},{32,0},{40,8},{48,16},{56,24},{64... | collective-permute-start | bytes 786440 | tf_op jit(solution)/shard_map/weight_gather/ppermute | solution.py:205
  45.0 17.1 %collective-permute-start = (s32[33,128]{1,0:T(8,128)S(1)}, s32[33,128]{1,0:T(8,128)S(1)}, u32[]{:S(2)}, u32[]{:S(2)}) collective-permute-start(s32[33,128]{1,0:T(8,128)S(1)} %fusion.10), channel_id=1, source_target_pairs={{0,128},{128,0},{1,129},{129,1},{2,130},{130,2},{3,131},{131,3},{4... | collective-permute-start | bytes 50696 | tf_op jit(solution)/shard_map/rows_swap/ppermute | solution.py:237
  47.7 34.8 %all-to-all-start = ((bf16[32,48,256]{2,1,0:T(8,128)(2,1)}), bf16[32,48,256]{2,1,0:T(8,128)(2,1)S(1)}, u32[]{:S(2)}, u32[]{:S(2)}) async-start(bf16[32,48,256]{2,1,0:T(8,128)(2,1)} %bitcast.11), calls=%async_computation | async-start | bytes 1572864 | tf_op jit(solution)/shard_map/columns_exchange/all_to_all | solution.py:268
  74.0 8.4 %collective-permute-start.20 = (f32[32,256]{1,0:T(8,128)S(1)}, f32[32,256]{1,0:T(8,128)S(1)}, u32[]{:S(2)}, u32[]{:S(2)}) collective-permute-start(f32[32,256]{1,0:T(8,128)S(1)} %add.55), channel_id=1, source_target_pairs={{0,1},{1,0},{2,3},{3,2},{4,5},{5,4},{6,7},{7,6},{8,9},{9,8},{10,11... | collective-permute-start | bytes 98312 | tf_op jit(solution)/shard_map/quant_sum/ppermute | solution.py:329
  83.4 26.5 %collective-permute-start.21 = (bf16[2,16,48,256]{3,2,1,0:T(8,128)(2,1)S(1)}, bf16[2,16,48,256]{3,2,1,0:T(8,128)(2,1)S(1)}, u32[]{:S(2)}, u32[]{:S(2)}) collective-permute-start(bf16[2,16,48,256]{3,2,1,0:T(8,128)(2,1)S(1)} %bitcast.30), channel_id=1, source_target_pairs={{0,6},{1,7},{2,0},{3,1},{4,2},{5,3},{6,4},{7,5},{8,14},{9,15},{10,... | collective-permute-start | bytes 2359304 | tf_op jit(solution)/shard_map/columns_round_x/ppermute | solution.py:367
  86.2 11.5 %collective-permute-start.25 = (bf16[128,512]{1,0:T(8,128)(2,1)S(1)}, bf16[128,512]{1,0:T(8,128)(2,1)S(1)}, u32[]{:S(2)}, u32[]{:S(2)}) collective-permute-start(bf16[128,512]{1,0:T(8,128)(2,1)S(1)} %fusion.5.own_ref), channel_id=1, source_target_pairs={{0,24},{8,0},{16,8},{24,16},{32,56},{40,32},{48,40},{56,48},{64,88... | collective-permute-start | bytes 393224 | tf_op jit(solution)/shard_map/grad_gather/ppermute | solution.py:356
  92.8 8.2 %collective-permute-start.26 = (bf16[128,512]{1,0:T(8,128)(2,1)S(1)}, bf16[128,512]{1,0:T(8,128)(2,1)S(1)}, u32[]{:S(2)}, u32[]{:S(2)}) collective-permute-start(bf16[128,512]{1,0:T(8,128)(2,1)S(1)} %fusion.5.own_ref), channel_id=1, source_target_pairs={{0,16},{8,24},{16,0},{24,8},{32,48},{40,56},{48,32},{56,40},{64,80... | collective-permute-start | bytes 393224 | tf_op jit(solution)/shard_map/grad_gather/ppermute | solution.py:356
  92.8 17.6 %collective-permute-start.22 = (bf16[2,16,48,256]{3,2,1,0:T(8,128)(2,1)S(1)}, bf16[2,16,48,256]{3,2,1,0:T(8,128)(2,1)S(1)}, u32[]{:S(2)}, u32[]{:S(2)}) collective-permute-start(bf16[2,16,48,256]{3,2,1,0:T(8,128)(2,1)S(1)} %bitcast.31), channel_id=1, source_target_pairs={{0,2},{1,3},{2,4},{3,5},{4,6},{5,7},{6,0},{7,1},{8,10},{9,11},{10,... | collective-permute-start | bytes 2359304 | tf_op jit(solution)/shard_map/columns_round_x/ppermute | solution.py:368
  92.9 8.3 %collective-permute-start.27 = (bf16[128,512]{1,0:T(8,128)(2,1)S(1)}, bf16[128,512]{1,0:T(8,128)(2,1)S(1)}, u32[]{:S(2)}, u32[]{:S(2)}) collective-permute-start(bf16[128,512]{1,0:T(8,128)(2,1)S(1)} %fusion.5.own_ref), channel_id=1, source_target_pairs={{0,8},{8,16},{16,24},{24,0},{32,40},{40,48},{48,56},{56,32},{64,72... | collective-permute-start | bytes 393224 | tf_op jit(solution)/shard_map/grad_gather/ppermute | solution.py:356
  97.8 6.0 %collective-permute-start.28 = (bf16[128,512]{1,0:T(8,128)(2,1)S(1)}, bf16[128,512]{1,0:T(8,128)(2,1)S(1)}, u32[]{:S(2)}, u32[]{:S(2)}) collective-permute-start(bf16[128,512]{1,0:T(8,128)(2,1)S(1)} %fusion.5.own_ref), channel_id=1, source_target_pairs={{0,96},{8,104},{16,112},{24,120},{32,0},{40,8},{48,16},{56,24},{64... | collective-permute-start | bytes 393224 | tf_op jit(solution)/shard_map/grad_gather/ppermute | solution.py:354
  101.1 6.7 %collective-permute-start.29 = (bf16[128,512]{1,0:T(8,128)(2,1)S(1)}, bf16[128,512]{1,0:T(8,128)(2,1)S(1)}, u32[]{:S(2)}, u32[]{:S(2)}) collective-permute-start(bf16[128,512]{1,0:T(8,128)(2,1)S(1)} %fusion.5.own_ref), channel_id=1, source_target_pairs={{0,32},{8,40},{16,48},{24,56},{32,64},{40,72},{48,80},{56,88},{64,... | collective-permute-start | bytes 393224 | tf_op jit(solution)/shard_map/grad_gather/ppermute | solution.py:355
  107.8 10.0 %collective-permute-start.30 = (bf16[384,512]{1,0:T(8,128)(2,1)S(1)}, bf16[384,512]{1,0:T(8,128)(2,1)S(1)}, u32[]{:S(2)}, u32[]{:S(2)}) collective-permute-start(bf16[384,512]{1,0:T(8,128)(2,1)S(1)} %constant_dynamic-update-slice_fusion.line_ref), channel_id=1, source_target_pairs={{0,96},{8,104},{16,112},{24,120},{32,0},{40,8},{48,16},{56,24},{64... | collective-permute-start | bytes 1179656 | tf_op jit(solution)/shard_map/grad_gather/ppermute | solution.py:361
  109.2 11.8 %collective-permute-start.31 = (bf16[384,512]{1,0:T(8,128)(2,1)S(1)}, bf16[384,512]{1,0:T(8,128)(2,1)S(1)}, u32[]{:S(2)}, u32[]{:S(2)}) collective-permute-start(bf16[384,512]{1,0:T(8,128)(2,1)S(1)} %constant_dynamic-update-slice_fusion.line_ref), channel_id=1, source_target_pairs={{0,32},{8,40},{16,48},{24,56},{32,64},{40,72},{48,80},{56,88},{64,... | collective-permute-start | bytes 1179656 | tf_op jit(solution)/shard_map/grad_gather/ppermute | solution.py:360
  110.0 11.1 %collective-permute-start.23 = (bf16[16,48,256]{2,1,0:T(8,128)(2,1)S(1)}, bf16[16,48,256]{2,1,0:T(8,128)(2,1)S(1)}, u32[]{:S(2)}, u32[]{:S(2)}) collective-permute-start(bf16[16,48,256]{2,1,0:T(8,128)(2,1)S(1)} %slice_bitcast_fusion.1), channel_id=1, source_target_pairs={{0,6},{1,7},{2,0},{3,1},{4,2},{5,3},{6,4},{7,5},{8,14},{9,15},{10,... | collective-permute-start | bytes 1179656 | tf_op jit(solution)/shard_map/columns_round_x/ppermute | solution.py:369
  110.5 10.6 %collective-permute-start.24 = (bf16[16,48,256]{2,1,0:T(8,128)(2,1)S(1)}, bf16[16,48,256]{2,1,0:T(8,128)(2,1)S(1)}, u32[]{:S(2)}, u32[]{:S(2)}) collective-permute-start(bf16[16,48,256]{2,1,0:T(8,128)(2,1)S(1)} %slice_bitcast_fusion), channel_id=1, source_target_pairs={{0,2},{1,3},{2,4},{3,5},{4,6},{5,7},{6,0},{7,1},{8,10},{9,11},{10,... | collective-permute-start | bytes 1179656 | tf_op jit(solution)/shard_map/columns_round_x/ppermute | solution.py:370
  117.9 10.6 %collective-permute-start.34 = (bf16[256,512]{1,0:T(8,128)(2,1)S(1)}, bf16[256,512]{1,0:T(8,128)(2,1)S(1)}, u32[]{:S(2)}, u32[]{:S(2)}) collective-permute-start(bf16[256,512]{1,0:T(8,128)(2,1)S(1)} %slice.59), channel_id=1, source_target_pairs={{0,96},{8,104},{16,112},{24,120},{32,0},{40,8},{48,16},{56,24},{64... | collective-permute-start | bytes 786440 | tf_op jit(solution)/shard_map/grad_gather/ppermute | solution.py:363
  120.9 6.2 %collective-permute-start.32 = (bf16[128,512]{1,0:T(8,128)(2,1)S(1)}, bf16[128,512]{1,0:T(8,128)(2,1)S(1)}, u32[]{:S(2)}, u32[]{:S(2)}) collective-permute-start(bf16[128,512]{1,0:T(8,128)(2,1)S(1)} %collective-permute-done.29.a0_ref), channel_id=1, source_target_pairs={{0,32},{8,40},{16,48},{24,56},{32,64},{40,72},{48,80},{56,88},{64,... | collective-permute-start | bytes 393224 | tf_op jit(solution)/shard_map/grad_gather/ppermute | solution.py:359
  121.0 7.5 %collective-permute-start.33 = (bf16[128,512]{1,0:T(8,128)(2,1)S(1)}, bf16[128,512]{1,0:T(8,128)(2,1)S(1)}, u32[]{:S(2)}, u32[]{:S(2)}) collective-permute-start(bf16[128,512]{1,0:T(8,128)(2,1)S(1)} %slice.58), channel_id=1, source_target_pairs={{0,32},{8,40},{16,48},{24,56},{32,64},{40,72},{48,80},{56,88},{64,... | collective-permute-start | bytes 393224 | tf_op jit(solution)/shard_map/grad_gather/ppermute | solution.py:362
  (20 other events, 210.2 us)

commit v8 on v7

--- a/solution.py
+++ b/solution.py
@@ -32,19 +32,14 @@
     return [pltpu.with_memory_space_constraint(array, pltpu.HBM) for array in arrays]
 
 
-def preact_kernel(where_ref, own_ref, got_ref, *refs):
-    weights = refs[: Y * Z]
-    keep_ref, send_ref, total, rows_held, held, sems = refs[Y * Z :]
-    group, y, z = where_ref[0], where_ref[1], where_ref[2]
+def multiply_chunks(where_ref, own_ref, got_ref, order, sources, total, rows_held, held, sems):
+    y, z = where_ref[1], where_ref[2]
     rows = own_ref.shape[0]
-    block = weights[0].shape[0]
-    order = [(0, k) for k in range(Z)] + [(j, k) for k in range(Z) for j in (1, 3)]
-    order += [(2, k) for k in range(Z)]
+    block = sources[0].shape[0]
     copies = []
     for step, (step_y, step_z) in enumerate(order):
         place = lax.rem(y + step_y, Y) * Z + lax.rem(z + step_z, Z)
         cols = pl.ds(pl.multiple_of(place * block, block), block)
-        source = weights[step_y * Z + step_z]
         copies.append(
             (
                 pltpu.make_async_copy(
@@ -53,7 +48,7 @@
                 pltpu.make_async_copy(
                     got_ref.at[:, cols], rows_held.at[step, pl.ds(rows, rows)], sems.at[1, step]
                 ),
-                pltpu.make_async_copy(source, held.at[step], sems.at[2, step]),
+                pltpu.make_async_copy(sources[step], held.at[step], sems.at[2, step]),
             )
         )
         for copy in copies[-1]:
@@ -66,12 +61,26 @@
             total[...] = term
         else:
             total[...] += term
+
+
+def early_kernel(where_ref, own_ref, got_ref, *refs):
+    order = [(j, k) for j in (0, 1, 3) for k in range(Z)]
+    multiply_chunks(where_ref, own_ref, got_ref, order, refs[: len(order)], *refs[len(order) :])
+
+
+def late_kernel(where_ref, own_ref, got_ref, early_ref, *refs):
+    order = [(2, k) for k in range(Z)]
+    keep_ref, send_ref, total = refs[Z : Z + 3]
+    multiply_chunks(where_ref, own_ref, got_ref, order, refs[:Z], total, *refs[Z + 3 :])
+    group = where_ref[0]
+    rows = own_ref.shape[0]
     half = rows // 2
     other = 1 - group
     for base, part in ((0, group), (rows, other)):
         out = pl.ds(pl.multiple_of(part * half, half), half)
-        keep_ref[out, :] = total[pl.ds(pl.multiple_of(base + group * half, half), half), :]
-        send_ref[out, :] = total[pl.ds(pl.multiple_of(base + other * half, half), half), :]
+        for half_of, out_ref in ((group, keep_ref), (other, send_ref)):
+            source = pl.ds(pl.multiple_of(base + half_of * half, half), half)
+            out_ref[out, :] = early_ref[source, :] + total[source, :]
 
 
 def norm_kernel(where_ref, rows_ref, gain_ref, own_ref, send_ref):
@@ -192,22 +201,6 @@
     smem = pl.BlockSpec(memory_space=pltpu.SMEM)
     vmem = pl.BlockSpec(memory_space=pltpu.VMEM)
 
-    with jax.named_scope("weight_gather"):
-        lines = [torso_weight] + [
-            lax.ppermute(torso_weight, "fsdp", z_from(k)) for k in range(1, Z)
-        ]
-        near = [
-            (lax.ppermute(line, "fsdp", y_from(1)), lax.ppermute(line, "fsdp", y_from(3)))
-            for line in lines
-        ]
-        near = lax.optimization_barrier(near)
-        far = [
-            lax.ppermute(above, "fsdp", y_from(3)) if k < 2 else lax.ppermute(below, "fsdp", y_from(1))
-            for k, (below, above) in enumerate(near)
-        ]
-        rounds = [(below, above, last) for (below, above), last in zip(near, far)]
-        chunks = lines + [rounds[k][j] for j in (0, 2, 1) for k in range(Z)]
-
     with jax.named_scope("rows_swap"):
         values = frames[0]
         tile = 64
@@ -229,6 +222,21 @@
             ),
             name="norm",
         )(where, *in_hbm(values, norm_gain[None, :]))
+    with jax.named_scope("weight_gather"):
+        after_z = lax.ppermute(torso_weight, "fsdp", z_from(1))
+        before_z = lax.ppermute(torso_weight, "fsdp", z_from(3))
+        after_z, normed_send = lax.optimization_barrier((after_z, normed_send))
+        lines = [torso_weight, after_z, lax.ppermute(after_z, "fsdp", z_from(1)), before_z]
+        near = [
+            (lax.ppermute(line, "fsdp", y_from(1)), lax.ppermute(line, "fsdp", y_from(3)))
+            for line in lines
+        ]
+        near = lax.optimization_barrier(near)
+        far = [
+            lax.ppermute(above, "fsdp", y_from(3)) if k < 2 else lax.ppermute(below, "fsdp", y_from(1))
+            for k, (below, above) in enumerate(near)
+        ]
+
     with jax.named_scope("rows_swap"):
         normed_send, _ = lax.optimization_barrier((normed_send, near[0]))
         normed_got = lax.ppermute(normed_send, "grp", SWAP)
@@ -248,7 +256,7 @@
         local_counts = jnp.sum(onehot.astype(jnp.float32), axis=0).astype(jnp.bfloat16)
         count_tile = jnp.pad(local_counts[None, :], ((0, 15), (0, block - shard_total)))
         count_tile, _ = lax.optimization_barrier(
-            (count_tile, tuple(r[k] for r in rounds for k in range(2)))
+            (count_tile, near)
         )
         pieces = pl.pallas_call(
             pieces_kernel,
@@ -291,26 +299,46 @@
     levels = jnp.sum(jnp.where(online_select, table[None, :, None], 0.0), axis=1)
     reward_rows = lax.dynamic_slice_in_dim(rewards, own_rows, half, 0).astype(jnp.float32)
 
+    any_space = pl.BlockSpec(memory_space=pl.ANY)
+
+    def held(count):
+        return [
+            pltpu.VMEM((count, 2 * rows_block, block), jnp.bfloat16),
+            pltpu.VMEM((count, block, features), jnp.bfloat16),
+            pltpu.SemaphoreType.DMA((3, count)),
+        ]
+
+    def work(count):
+        return pl.CostEstimate(
+            flops=4 * count * rows_block * block * features,
+            transcendentals=0,
+            bytes_accessed=2 * count * block * (features + 2 * rows_block)
+            + 8 * rows_block * features,
+        )
+
+    total_shape = jax.ShapeDtypeStruct((2 * rows_block, features), jnp.float32)
     part_shape = jax.ShapeDtypeStruct((rows_block, features), jnp.float32)
+    near_chunks = lines + [pair[0] for pair in near] + [pair[1] for pair in near]
+    early = pl.pallas_call(
+        early_kernel,
+        out_shape=total_shape,
+        in_specs=[smem] + [any_space] * (2 + 3 * Z),
+        out_specs=vmem,
+        scratch_shapes=held(3 * Z),
+        compiler_params=pltpu.CompilerParams(vmem_limit_bytes=12 << 20),
+        cost_estimate=work(3 * Z),
+        name="early",
+    )(where, *in_hbm(normed_own, normed_got, *near_chunks))
     keep, send = pl.pallas_call(
-        preact_kernel,
+        late_kernel,
         out_shape=(part_shape, part_shape),
-        in_specs=[smem] + [pl.BlockSpec(memory_space=pl.ANY)] * (2 + Y * Z),
+        in_specs=[smem] + [any_space] * 2 + [vmem] + [any_space] * Z,
         out_specs=(vmem, vmem),
-        scratch_shapes=[
-            pltpu.VMEM((2 * rows_block, features), jnp.float32),
-            pltpu.VMEM((Y * Z, 2 * rows_block, block), jnp.bfloat16),
-            pltpu.VMEM((Y * Z, block, features), jnp.bfloat16),
-            pltpu.SemaphoreType.DMA((3, Y * Z)),
-        ],
-        compiler_params=pltpu.CompilerParams(vmem_limit_bytes=14 << 20),
-        cost_estimate=pl.CostEstimate(
-            flops=4 * rows_block * side * features,
-            transcendentals=0,
-            bytes_accessed=2 * side * features + 4 * side * rows_block + 8 * rows_block * features,
-        ),
-        name="preact",
-    )(where, *in_hbm(normed_own, normed_got, *chunks[:8]), *chunks[8:12], *in_hbm(*chunks[12:]))
+        scratch_shapes=[pltpu.VMEM((2 * rows_block, features), jnp.float32)] + held(Z),
+        compiler_params=pltpu.CompilerParams(vmem_limit_bytes=8 << 20),
+        cost_estimate=work(Z),
+        name="late",
+    )(where, *in_hbm(normed_own, normed_got), early, *far)
     preact = keep + lax.ppermute(send, "grp", SWAP)
     weighted = (jax.nn.silu(preact) * picked).astype(jnp.bfloat16)
     table_values = lax.dot_general(
@@ -326,43 +354,8 @@
         quant = partial_quant
         for flip in (2, 4):
             quant = quant + lax.ppermute(quant, "tp", [(t, t ^ flip) for t in range(2 * X)])
+        quant, pieces = lax.optimization_barrier((quant, pieces))
         quant = quant + lax.ppermute(quant, "tp", [(t, t ^ 1) for t in range(2 * X)])
-    quant, pieces = lax.optimization_barrier((quant, pieces))
-    target_quant = quant[:, :half]
-    online_quant = quant[:, half:]
-    target_value = reward_rows[None, :] + 0.99 * target_quant
-    errors = target_value[None, :, :] - online_quant[:, None, :]
-    weight = jnp.abs(levels[:, None, :] - (errors < 0).astype(jnp.float32))
-    grad_quant = -row_weight[None, :] * jnp.sum(weight * jnp.clip(errors, -1.0, 1.0), axis=1)
-    grad_table = jnp.sum(jnp.where(online_select, grad_quant[:, None, :], 0.0), axis=0)
-    grad_feature = lax.dot_general(
-        grad_table,
-        embedding.astype(jnp.float32),
-        (((0,), (0,)), ((), ())),
-        precision=lax.Precision.HIGHEST,
-    )
-    online_preact = preact[half:]
-    gate_value = jax.nn.sigmoid(online_preact)
-    grad_preact = (
-        grad_feature
-        * picked[half:]
-        * gate_value
-        * (1.0 + online_preact * (1.0 - gate_value))
-    ).astype(jnp.bfloat16)
-
-    with jax.named_scope("grad_gather"):
-        b0 = lax.ppermute(grad_preact, "fsdp", y_from(1))
-        a0 = lax.ppermute(grad_preact, "fsdp", y_from(3))
-        pieces_z = tuple(lax.ppermute(grad_preact, "fsdp", z_from(k)) for k in range(1, Z))
-        pieces_z, _ = lax.optimization_barrier((pieces_z, (b0, a0)))
-        line = jnp.concatenate(pieces_z, 0)
-        f0 = lax.ppermute(a0, "fsdp", y_from(3))
-        a1 = lax.ppermute(line, "fsdp", y_from(3))
-        b1 = lax.ppermute(line, "fsdp", y_from(1))
-        f1 = lax.ppermute(a1[:half], "fsdp", y_from(3))
-        f2 = lax.ppermute(b1[half:], "fsdp", y_from(1))
-
-    pieces, _ = lax.optimization_barrier((pieces, grad_preact))
     with jax.named_scope("columns_round_x"):
         after = lax.ppermute(pieces, "tp", x_from(1))
         before = lax.ppermute(pieces, "tp", x_from(3))
@@ -380,6 +373,39 @@
             ),
             name="columns",
         )(where, pieces, after, before, far_a, far_b)
+    target_quant = quant[:, :half]
+    online_quant = quant[:, half:]
+    target_value = reward_rows[None, :] + 0.99 * target_quant
+    errors = target_value[None, :, :] - online_quant[:, None, :]
+    weight = jnp.abs(levels[:, None, :] - (errors < 0).astype(jnp.float32))
+    grad_quant = -row_weight[None, :] * jnp.sum(weight * jnp.clip(errors, -1.0, 1.0), axis=1)
+    grad_table = jnp.sum(jnp.where(online_select, grad_quant[:, None, :], 0.0), axis=0)
+    grad_feature = lax.dot_general(
+        grad_table,
+        embedding.astype(jnp.float32),
+        (((0,), (0,)), ((), ())),
+        precision=lax.Precision.HIGHEST,
+    )
+    online_preact = preact[half:]
+    gate_value = jax.nn.sigmoid(online_preact)
+    grad_preact = (
+        grad_feature
+        * picked[half:]
+        * gate_value
+        * (1.0 + online_preact * (1.0 - gate_value))
+    ).astype(jnp.bfloat16)
+
+    with jax.named_scope("grad_gather"):
+        b0 = lax.ppermute(grad_preact, "fsdp", y_from(1))
+        a0 = lax.ppermute(grad_preact, "fsdp", y_from(3))
+        pieces_z = tuple(lax.ppermute(grad_preact, "fsdp", z_from(k)) for k in range(1, Z))
+        pieces_z, _ = lax.optimization_barrier((pieces_z, (b0, a0)))
+        line = jnp.concatenate(pieces_z, 0)
+        f0 = lax.ppermute(a0, "fsdp", y_from(3))
+        a1 = lax.ppermute(line, "fsdp", y_from(3))
+        b1 = lax.ppermute(line, "fsdp", y_from(1))
+        f1 = lax.ppermute(a1[:half], "fsdp", y_from(3))
+        f2 = lax.ppermute(b1[half:], "fsdp", y_from(1))
 
     near = pl.pallas_call(
         near_kernel,

time: 154 us -> 149 us (0.968)
  starting transfers between devices: 66.1 us -> 58.1 us
  Pallas kernels: 17.2 us -> 18.9 us
    ppermute x3, waiting for transfers between devices: 10.9 us -> 0.05 us  [the longest x1 0.04 us: shards(): lax.ppermute(after_z, 'fsdp', z_from(1))]
    ppermute x4, waiting for transfers between devices: 2.91 us -> 10.5 us  [shards(): lax.ppermute(line, 'fsdp', y_from(3))]
    ppermute x3, starting transfers between devices: 8.07 us -> 4.85 us  [shards(): lax.ppermute(grad_preact, 'fsdp', z_from(k))]
    ppermute x3, starting transfers between devices: 8.01 us -> 4.89 us  [the longest x1 2.79 us: shards(): lax.ppermute(after_z, 'fsdp', z_from(1))]
    ppermute x4, starting transfers between devices: 0.01 us -> 2.8 us  [shards(): lax.ppermute(line, 'fsdp', y_from(3))]
    ppermute x1, starting transfers between devices: 0.19 us -> 2.45 us  [shards(): far_a = lax.ppermute(after[0], 'tp', x_from(1))]
    all_to_all x1, waiting for transfers between devices: 0.01 us -> 2.22 us  [shards(): lax.all_to_all(pieces.reshape(2 * shard_total, strip + 16, block), ('grp'...]
    all_to_all x1, starting transfers between devices: 8.92 us -> 6.8 us  [shards(): lax.all_to_all(pieces.reshape(2 * shard_total, strip + 16, block), ('grp'...]
  transfers between devices with their start and end apart: 37 -> 37, of which waited for: 16 -> 17; matrix products, arithmetic and copies ran while one was open for 1% -> 3% of each run, Pallas kernels for 11% -> 13%
where the time goes in v8:
time: 149 us; the launch traced here: 148 us
  starting transfers between devices  58.1 us (39%)
  waiting for transfers between devices  43.1 us (29%)
  blocking collectives  20.3 us (14%)
  Pallas kernels  18.9 us (13%)
  other arithmetic  3.26 us (2%)
  matrix products  1.84 us (1%)
  local copies, waits for them, and re-layouts  1.63 us (1%)
    all_to_all x1, blocking collectives, shards(): lax.all_to_all(updated, 'tp', split_axis=0, concat_axis=1, tiled=True)  20.3 us
    ppermute x4, starting transfers between devices, shards(): lax.ppermute(line, 'fsdp', y_from(1))  10.5 us
    ppermute x4, waiting for transfers between devices, shards(): lax.ppermute(line, 'fsdp', y_from(3))  10.5 us
    all_to_all x1, starting transfers between devices, shards(): lax.all_to_all(pieces.reshape(2 * shard_total, strip + 16, block), ('grp'...  6.8 us
    pallas_call x1, Pallas kernels, shards(): pl.pallas_call(norm_kernel, grid=(rows_block // tile,), out_shape=(jax.Sh...  5.77 us
    ppermute x3, waiting for transfers between devices, shards(): lax.ppermute(grad_preact, 'fsdp', z_from(k))  5.44 us
    ppermute x1, waiting for transfers between devices, shards(): b1 = lax.ppermute(line, 'fsdp', y_from(1))  5.4 us
    ppermute x3, starting transfers between devices, shards(): lax.ppermute(grad_preact, 'fsdp', z_from(k))  4.85 us
  transfers between devices with their start and end apart: 37, of which 17 were waited for; matrix products, arithmetic and copies ran while one was open for 3% of the time, Pallas kernels for 13%

profile of v8, /device:TPU:32, one launch (start us, length us, event | category | flops | bytes accessed | tf_op | source)
XLA Modules:
  0.0 148.1 jit_solution(9179746265515904341)
XLA Ops:
  0.6 1.9 %collective-permute-start.1 = (bf16[256,512]{1,0:T(8,128)(2,1)}, bf16[256,512]{1,0:T(8,128)(2,1)S(1)}, u32[]{:S(2)}, u32[]{:S(2)}) collective-permute-start(bf16[256,512]{1,0:T(8,128)(2,1)} %refs_0_.1), channel_id=1, source_target_pairs={{0,24},{8,0},{16,8},{24,16},{32,56},{40,32},{48,40},{56,48},{64,88... | collective-permute-start | bytes 786440 | tf_op jit(solution)/shard_map/weight_gather/ppermute | solution.py:226
  2.7 3.0 %collective-permute-start.2 = (bf16[256,512]{1,0:T(8,128)(2,1)}, bf16[256,512]{1,0:T(8,128)(2,1)S(1)}, u32[]{:S(2)}, u32[]{:S(2)}) collective-permute-start(bf16[256,512]{1,0:T(8,128)(2,1)} %refs_0_.1), channel_id=1, source_target_pairs={{0,96},{8,104},{16,112},{24,120},{32,0},{40,8},{48,16},{56,24},{64... | collective-permute-start | bytes 786440 | tf_op jit(solution)/shard_map/weight_gather/ppermute | solution.py:231
  5.9 5.8 %norm.1 = (bf16[256,4096]{1,0:T(8,128)(2,1)S(1)}, bf16[256,4096]{1,0:T(8,128)(2,1)}) custom-call(s32[4]{0:T(128)S(1)} %pad_add_fusion.1.where_ref, bf16[256,8192]{1,0:T(8,128)(2,1)} %bitcast.33, f32[1,8192]{1,0:T(1,128)} %bitcast.39), custom_call_target="tpu_custom_call" | custom-call | flops 12582912 | bytes 8388608 | tf_op jit(solution)/shard_map/rows_swap/norm/pallas_call | solution.py:207
  11.6 2.8 %collective-permute-start.6 = (bf16[256,512]{1,0:T(8,128)(2,1)S(1)}, bf16[256,512]{1,0:T(8,128)(2,1)S(1)}, u32[]{:S(2)}, u32[]{:S(2)}) collective-permute-start(bf16[256,512]{1,0:T(8,128)(2,1)S(1)} %collective-permute-done.1.refs_1_), channel_id=1, source_target_pairs={{0,24},{8,0},{16,8},{24,16},{32,56},{40,32},{48,40},{56,48},{64,88... | collective-permute-start | bytes 786440 | tf_op jit(solution)/shard_map/weight_gather/ppermute | solution.py:229
  14.4 3.2 %collective-permute-start.4 = (bf16[256,512]{1,0:T(8,128)(2,1)S(1)}, bf16[256,512]{1,0:T(8,128)(2,1)S(1)}, u32[]{:S(2)}, u32[]{:S(2)}) collective-permute-start(bf16[256,512]{1,0:T(8,128)(2,1)S(1)} %collective-permute-done.1.refs_1_), channel_id=1, source_target_pairs={{0,96},{8,104},{16,112},{24,120},{32,0},{40,8},{48,16},{56,24},{64... | collective-permute-start | bytes 786440 | tf_op jit(solution)/shard_map/weight_gather/ppermute | solution.py:231
  17.7 2.0 %collective-permute-start.5 = (bf16[256,512]{1,0:T(8,128)(2,1)S(1)}, bf16[256,512]{1,0:T(8,128)(2,1)}, u32[]{:S(2)}, u32[]{:S(2)}) collective-permute-start(bf16[256,512]{1,0:T(8,128)(2,1)S(1)} %collective-permute-done.1.refs_1_), channel_id=1, source_target_pairs={{0,32},{8,40},{16,48},{24,56},{32,64},{40,72},{48,80},{56,88},{64,... | collective-permute-start | bytes 786440 | tf_op jit(solution)/shard_map/weight_gather/ppermute | solution.py:231
  21.7 3.0 %collective-permute-start.7 = (bf16[256,512]{1,0:T(8,128)(2,1)S(1)}, bf16[256,512]{1,0:T(8,128)(2,1)}, u32[]{:S(2)}, u32[]{:S(2)}) collective-permute-start(bf16[256,512]{1,0:T(8,128)(2,1)S(1)} %collective-permute-done.6.refs_2_), channel_id=1, source_target_pairs={{0,96},{8,104},{16,112},{24,120},{32,0},{40,8},{48,16},{56,24},{64... | collective-permute-start | bytes 786440 | tf_op jit(solution)/shard_map/weight_gather/ppermute | solution.py:231
  24.8 3.5 %collective-permute-done.5.refs_9_ = bf16[256,512]{1,0:T(8,128)(2,1)} collective-permute-done((bf16[256,512]{1,0:T(8,128)(2,1)S(1)}, bf16[256,512]{1,0:T(8,128)(2,1)}, u32[]{:S(2)}, u32[]{:S(2)}) %collective-permute-start.5) | collective-permute-done | bytes 262176 | tf_op jit(solution)/shard_map/weight_gather/ppermute | solution.py:231
  28.2 1.8 %collective-permute-done.10.refs_7_ = bf16[256,512]{1,0:T(8,128)(2,1)} collective-permute-done((bf16[256,512]{1,0:T(8,128)(2,1)S(1)}, bf16[256,512]{1,0:T(8,128)(2,1)}, u32[]{:S(2)}, u32[]{:S(2)}) %collective-permute-start.10) | collective-permute-done | bytes 262176 | tf_op jit(solution)/shard_map/weight_gather/ppermute | solution.py:231
  30.0 3.7 %collective-permute-done.11.refs_11_ = bf16[256,512]{1,0:T(8,128)(2,1)S(1)} collective-permute-done((bf16[256,512]{1,0:T(8,128)(2,1)S(1)}, bf16[256,512]{1,0:T(8,128)(2,1)S(1)}, u32[]{:S(2)}, u32[]{:S(2)}) %collective-permute-start.11) | collective-permute-done | bytes 262176 | tf_op jit(solution)/shard_map/weight_gather/ppermute | solution.py:231
  33.7 3.3 %collective-permute-done.8.refs_10_ = bf16[256,512]{1,0:T(8,128)(2,1)S(1)} collective-permute-done((bf16[256,512]{1,0:T(8,128)(2,1)S(1)}, bf16[256,512]{1,0:T(8,128)(2,1)S(1)}, u32[]{:S(2)}, u32[]{:S(2)}) %collective-permute-start.8) | collective-permute-done | bytes 262176 | tf_op jit(solution)/shard_map/weight_gather/ppermute | solution.py:231
  44.3 2.6 %pieces.1 = bf16[2,16,48,256]{3,2,1,0:T(8,128)(2,1)} custom-call(s32[4]{0:T(128)S(1)} %pad_add_fusion.1.where_ref, bf16[256,4096]{1,0:T(8,128)(2,1)S(1)} %get-tuple-element.25.own_ref, bf16[256,4096]{1,0:T(8,128)(2,1)} %collective-permute-done.12.got_ref, bf16[16,256]{1,0:T(8,128)(2,1)S(1)} %pad.4.count_ref), custom_call_target="tpu_custom_call" | custom-call | bytes 1048576 | tf_op jit(solution)/shard_map/columns_exchange/pieces/pallas_call | solution.py:261
  46.9 6.8 %all-to-all-start = ((bf16[32,48,256]{2,1,0:T(8,128)(2,1)}), bf16[32,48,256]{2,1,0:T(8,128)(2,1)S(1)}, u32[]{:S(2)}, u32[]{:S(2)}) async-start(bf16[32,48,256]{2,1,0:T(8,128)(2,1)} %bitcast.11), calls=%async_computation | async-start | bytes 1572864 | tf_op jit(solution)/shard_map/columns_exchange/all_to_all | solution.py:276
  53.7 4.2 %early.1.early_ref = f32[512,512]{1,0:T(8,128)S(1)} custom-call(s32[4]{0:T(128)S(1)} %pad_add_fusion.1.where_ref, bf16[256,4096]{1,0:T(8,128)(2,1)} %copy-done.1, bf16[256,4096]{1,0:T(8,128)(2,1)} %collective-permute-done.12.got_ref, bf16[256,512]{1,0:T(8,128)(2,1)} %refs_0_.1, bf16[256,512]{1,0:T(8,128)(2,1)} %copy-done.3, bf16[256,512]{1,0:T(8,128)(2,1)} %copy-done.6, ...), custom_call_target="tpu_custom_call" | custom-call | flops 1610612736 | bytes 7340032 | tf_op jit(solution)/shard_map/early/pallas_call | solution.py:322
  58.0 2.6 %late.1 = (f32[256,512]{1,0:T(8,128)S(1)}, f32[256,512]{1,0:T(8,128)S(1)}) custom-call(s32[4]{0:T(128)S(1)} %pad_add_fusion.1.where_ref, bf16[256,4096]{1,0:T(8,128)(2,1)} %copy-done.1, bf16[256,4096]{1,0:T(8,128)(2,1)} %collective-permute-done.12.got_ref, f32[512,512]{1,0:T(8,128)S(1)} %early.1.early_ref, ...), custom_call_target="tpu_custom_call" | custom-call | flops 536870912 | bytes 3145728 | tf_op jit(solution)/shard_map/late/pallas_call | solution.py:332
  65.0 2.3 %collective-permute-done.18 = f32[32,256]{1,0:T(8,128)S(1)} collective-permute-done((f32[32,256]{1,0:T(8,128)S(1)}, f32[32,256]{1,0:T(8,128)S(1)}, u32[]{:S(2)}, u32[]{:S(2)}) %collective-permute-start.18) | collective-permute-done | bytes 32800 | tf_op jit(solution)/shard_map/quant_sum/ppermute | solution.py:356
  67.4 3.0 %collective-permute-start.19 = (f32[32,256]{1,0:T(8,128)S(1)}, f32[32,256]{1,0:T(8,128)S(1)}, u32[]{:S(2)}, u32[]{:S(2)}) collective-permute-start(f32[32,256]{1,0:T(8,128)S(1)} %add.54), channel_id=1, source_target_pairs={{0,4},{1,5},{2,6},{3,7},{4,0},{5,1},{6,2},{7,3},{8,12},{9,13},{10,... | collective-permute-start | bytes 98312 | tf_op jit(solution)/shard_map/quant_sum/ppermute | solution.py:356
  70.7 2.1 %collective-permute-done.19 = f32[32,256]{1,0:T(8,128)S(1)} collective-permute-done((f32[32,256]{1,0:T(8,128)S(1)}, f32[32,256]{1,0:T(8,128)S(1)}, u32[]{:S(2)}, u32[]{:S(2)}) %collective-permute-start.19) | collective-permute-done | bytes 32800 | tf_op jit(solution)/shard_map/quant_sum/ppermute | solution.py:356
  72.8 2.2 %all-to-all-done = bf16[32,48,256]{2,1,0:T(8,128)(2,1)S(1)} async-done(((bf16[32,48,256]{2,1,0:T(8,128)(2,1)}), bf16[32,48,256]{2,1,0:T(8,128)(2,1)S(1)}, u32[]{:S(2)}, u32[]{:S(2)}) %all-to-all-start) | async-done | bytes 786464 | tf_op jit(solution)/shard_map/columns_exchange/all_to_all | solution.py:276
  75.0 4.6 %collective-permute-start.24 = (f32[32,256]{1,0:T(8,128)S(1)}, f32[32,256]{1,0:T(8,128)S(1)}, u32[]{:S(2)}, u32[]{:S(2)}) collective-permute-start(f32[32,256]{1,0:T(8,128)S(1)} %add.55), channel_id=1, source_target_pairs={{0,1},{1,0},{2,3},{3,2},{4,5},{5,4},{6,7},{7,6},{8,9},{9,8},{10,11... | collective-permute-start | bytes 98312 | tf_op jit(solution)/shard_map/quant_sum/ppermute | solution.py:358
  79.8 2.8 %collective-permute-start.20 = (bf16[2,16,48,256]{3,2,1,0:T(8,128)(2,1)S(1)}, bf16[2,16,48,256]{3,2,1,0:T(8,128)(2,1)S(1)}, u32[]{:S(2)}, u32[]{:S(2)}) collective-permute-start(bf16[2,16,48,256]{3,2,1,0:T(8,128)(2,1)S(1)} %bitcast.30), channel_id=1, source_target_pairs={{0,6},{1,7},{2,0},{3,1},{4,2},{5,3},{6,4},{7,5},{8,14},{9,15},{10,... | collective-permute-start | bytes 2359304 | tf_op jit(solution)/shard_map/columns_round_x/ppermute | solution.py:360
  87.7 2.4 %collective-permute-start.27 = (bf16[128,512]{1,0:T(8,128)(2,1)S(1)}, bf16[128,512]{1,0:T(8,128)(2,1)S(1)}, u32[]{:S(2)}, u32[]{:S(2)}) collective-permute-start(bf16[128,512]{1,0:T(8,128)(2,1)S(1)} %fusion.5.own_ref), channel_id=1, source_target_pairs={{0,8},{8,16},{16,24},{24,0},{32,40},{40,48},{48,56},{56,32},{64,72... | collective-permute-start | bytes 393224 | tf_op jit(solution)/shard_map/grad_gather/ppermute | solution.py:401
  90.0 5.4 %collective-permute-done.25 = bf16[128,512]{1,0:T(8,128)(2,1)S(1)} collective-permute-done((bf16[128,512]{1,0:T(8,128)(2,1)S(1)}, bf16[128,512]{1,0:T(8,128)(2,1)S(1)}, u32[]{:S(2)}, u32[]{:S(2)}) %collective-permute-start.25) | collective-permute-done | bytes 131104 | tf_op jit(solution)/shard_map/grad_gather/ppermute | solution.py:401
  95.5 1.9 %collective-permute-start.28 = (bf16[128,512]{1,0:T(8,128)(2,1)S(1)}, bf16[128,512]{1,0:T(8,128)(2,1)S(1)}, u32[]{:S(2)}, u32[]{:S(2)}) collective-permute-start(bf16[128,512]{1,0:T(8,128)(2,1)S(1)} %fusion.5.own_ref), channel_id=1, source_target_pairs={{0,96},{8,104},{16,112},{24,120},{32,0},{40,8},{48,16},{56,24},{64... | collective-permute-start | bytes 393224 | tf_op jit(solution)/shard_map/grad_gather/ppermute | solution.py:399
  97.5 3.4 %collective-permute-done.28.b0_ref = bf16[128,512]{1,0:T(8,128)(2,1)S(1)} collective-permute-done((bf16[128,512]{1,0:T(8,128)(2,1)S(1)}, bf16[128,512]{1,0:T(8,128)(2,1)S(1)}, u32[]{:S(2)}, u32[]{:S(2)}) %collective-permute-start.28) | collective-permute-done | bytes 131104 | tf_op jit(solution)/shard_map/grad_gather/ppermute | solution.py:399
  100.9 3.8 %collective-permute-done.29.a0_ref = bf16[128,512]{1,0:T(8,128)(2,1)S(1)} collective-permute-done((bf16[128,512]{1,0:T(8,128)(2,1)S(1)}, bf16[128,512]{1,0:T(8,128)(2,1)S(1)}, u32[]{:S(2)}, u32[]{:S(2)}) %collective-permute-start.29) | collective-permute-done | bytes 131104 | tf_op jit(solution)/shard_map/grad_gather/ppermute | solution.py:400
  104.8 2.0 %collective-permute-start.31 = (bf16[384,512]{1,0:T(8,128)(2,1)S(1)}, bf16[384,512]{1,0:T(8,128)(2,1)S(1)}, u32[]{:S(2)}, u32[]{:S(2)}) collective-permute-start(bf16[384,512]{1,0:T(8,128)(2,1)S(1)} %constant_dynamic-update-slice_fusion.line_ref), channel_id=1, source_target_pairs={{0,32},{8,40},{16,48},{24,56},{32,64},{40,72},{48,80},{56,88},{64,... | collective-permute-start | bytes 1179656 | tf_op jit(solution)/shard_map/grad_gather/ppermute | solution.py:405
  106.9 2.5 %collective-permute-start.22 = (bf16[16,48,256]{2,1,0:T(8,128)(2,1)S(1)}, bf16[16,48,256]{2,1,0:T(8,128)(2,1)S(1)}, u32[]{:S(2)}, u32[]{:S(2)}) collective-permute-start(bf16[16,48,256]{2,1,0:T(8,128)(2,1)S(1)} %slice_bitcast_fusion.1), channel_id=1, source_target_pairs={{0,6},{1,7},{2,0},{3,1},{4,2},{5,3},{6,4},{7,5},{8,14},{9,15},{10,... | collective-permute-start | bytes 1179656 | tf_op jit(solution)/shard_map/columns_round_x/ppermute | solution.py:362
  109.5 5.4 %collective-permute-done.30.b1_ref = bf16[384,512]{1,0:T(8,128)(2,1)S(1)} collective-permute-done((bf16[384,512]{1,0:T(8,128)(2,1)S(1)}, bf16[384,512]{1,0:T(8,128)(2,1)S(1)}, u32[]{:S(2)}, u32[]{:S(2)}) %collective-permute-start.30) | collective-permute-done | bytes 393248 | tf_op jit(solution)/shard_map/grad_gather/ppermute | solution.py:406
  118.4 2.4 %columns.1.cols_ref = bf16[512,2048]{1,0:T(8,128)(2,1)S(1)} custom-call(s32[4]{0:T(128)S(1)} %pad_add_fusion.1.where_ref, bf16[2,16,48,256]{3,2,1,0:T(8,128)(2,1)S(1)} %bitcast.32, bf16[2,16,48,256]{3,2,1,0:T(8,128)(2,1)S(1)} %collective-permute-done.20.after_ref, bf16[2,16,48,256]{3,2,1,0:T(8,128)(2,1)S(1)} %collective-permute-done.21.before_ref, ...), custom_call_target="tpu_custom_call" | custom-call | bytes 4194304 | tf_op jit(solution)/shard_map/columns_round_x/columns/pallas_call | solution.py:364
  124.3 1.9 %collective-permute-done.35 = f32[256,512]{1,0:T(8,128)S(1)} collective-permute-done((f32[256,512]{1,0:T(8,128)S(1)}, f32[256,512]{1,0:T(8,128)S(1)}, u32[]{:S(2)}, u32[]{:S(2)}) %collective-permute-start.35) | collective-permute-done | bytes 524320 | tf_op jit(solution)/shard_map/ppermute | solution.py:437
  127.2 20.3 %all_to_all.24 = bf16[8,32,512]{2,1,0:T(8,128)(2,1)S(1)} all-to-all(bf16[8,32,512]{2,1,0:T(8,128)(2,1)S(1)} %bitcast.35), channel_id=1, replica_groups=mesh['grp'=2,'fsdp'=16,'tp'=8] {'tp'}, dimensions={0} | all-to-all | bytes 524288 | tf_op jit(solution)/shard_map/all_to_all | solution.py:439
  (121 shorter events, 28.6 us)
Async XLA Ops:
  0.6 11.0 %collective-permute-start.1 = (bf16[256,512]{1,0:T(8,128)(2,1)}, bf16[256,512]{1,0:T(8,128)(2,1)S(1)}, u32[]{:S(2)}, u32[]{:S(2)}) collective-permute-start(bf16[256,512]{1,0:T(8,128)(2,1)} %refs_0_.1), channel_id=1, source_target_pairs={{0,24},{8,0},{16,8},{24,16},{32,56},{40,32},{48,40},{56,48},{64,88... | collective-permute-start | bytes 786440 | tf_op jit(solution)/shard_map/weight_gather/ppermute | solution.py:226
  2.6 15.1 %collective-permute-start.9 = (bf16[256,512]{1,0:T(8,128)(2,1)}, bf16[256,512]{1,0:T(8,128)(2,1)S(1)}, u32[]{:S(2)}, u32[]{:S(2)}) collective-permute-start(bf16[256,512]{1,0:T(8,128)(2,1)} %refs_0_.1), channel_id=1, source_target_pairs={{0,8},{8,16},{16,24},{24,0},{32,40},{40,48},{48,56},{56,32},{64,72... | collective-permute-start | bytes 786440 | tf_op jit(solution)/shard_map/weight_gather/ppermute | solution.py:227
  2.7 16.9 %collective-permute-start.2 = (bf16[256,512]{1,0:T(8,128)(2,1)}, bf16[256,512]{1,0:T(8,128)(2,1)S(1)}, u32[]{:S(2)}, u32[]{:S(2)}) collective-permute-start(bf16[256,512]{1,0:T(8,128)(2,1)} %refs_0_.1), channel_id=1, source_target_pairs={{0,96},{8,104},{16,112},{24,120},{32,0},{40,8},{48,16},{56,24},{64... | collective-permute-start | bytes 786440 | tf_op jit(solution)/shard_map/weight_gather/ppermute | solution.py:231
  5.8 15.1 %collective-permute-start.3 = (bf16[256,512]{1,0:T(8,128)(2,1)}, bf16[256,512]{1,0:T(8,128)(2,1)}, u32[]{:S(2)}, u32[]{:S(2)}) collective-permute-start(bf16[256,512]{1,0:T(8,128)(2,1)} %refs_0_.1), channel_id=1, source_target_pairs={{0,32},{8,40},{16,48},{24,56},{32,64},{40,72},{48,80},{56,88},{64,... | collective-permute-start | bytes 786440 | tf_op jit(solution)/shard_map/weight_gather/ppermute | solution.py:231
  11.6 10.1 %collective-permute-start.6 = (bf16[256,512]{1,0:T(8,128)(2,1)S(1)}, bf16[256,512]{1,0:T(8,128)(2,1)S(1)}, u32[]{:S(2)}, u32[]{:S(2)}) collective-permute-start(bf16[256,512]{1,0:T(8,128)(2,1)S(1)} %collective-permute-done.1.refs_1_), channel_id=1, source_target_pairs={{0,24},{8,0},{16,8},{24,16},{32,56},{40,32},{48,40},{56,48},{64,88... | collective-permute-start | bytes 786440 | tf_op jit(solution)/shard_map/weight_gather/ppermute | solution.py:229
  14.4 10.3 %collective-permute-start.4 = (bf16[256,512]{1,0:T(8,128)(2,1)S(1)}, bf16[256,512]{1,0:T(8,128)(2,1)S(1)}, u32[]{:S(2)}, u32[]{:S(2)}) collective-permute-start(bf16[256,512]{1,0:T(8,128)(2,1)S(1)} %collective-permute-done.1.refs_1_), channel_id=1, source_target_pairs={{0,96},{8,104},{16,112},{24,120},{32,0},{40,8},{48,16},{56,24},{64... | collective-permute-start | bytes 786440 | tf_op jit(solution)/shard_map/weight_gather/ppermute | solution.py:231
  17.7 10.6 %collective-permute-start.5 = (bf16[256,512]{1,0:T(8,128)(2,1)S(1)}, bf16[256,512]{1,0:T(8,128)(2,1)}, u32[]{:S(2)}, u32[]{:S(2)}) collective-permute-start(bf16[256,512]{1,0:T(8,128)(2,1)S(1)} %collective-permute-done.1.refs_1_), channel_id=1, source_target_pairs={{0,32},{8,40},{16,48},{24,56},{32,64},{40,72},{48,80},{56,88},{64,... | collective-permute-start | bytes 786440 | tf_op jit(solution)/shard_map/weight_gather/ppermute | solution.py:231
  19.7 10.4 %collective-permute-start.10 = (bf16[256,512]{1,0:T(8,128)(2,1)S(1)}, bf16[256,512]{1,0:T(8,128)(2,1)}, u32[]{:S(2)}, u32[]{:S(2)}) collective-permute-start(bf16[256,512]{1,0:T(8,128)(2,1)S(1)} %collective-permute-done.9.refs_3_), channel_id=1, source_target_pairs={{0,96},{8,104},{16,112},{24,120},{32,0},{40,8},{48,16},{56,24},{64... | collective-permute-start | bytes 786440 | tf_op jit(solution)/shard_map/weight_gather/ppermute | solution.py:231
  20.9 12.8 %collective-permute-start.11 = (bf16[256,512]{1,0:T(8,128)(2,1)S(1)}, bf16[256,512]{1,0:T(8,128)(2,1)S(1)}, u32[]{:S(2)}, u32[]{:S(2)}) collective-permute-start(bf16[256,512]{1,0:T(8,128)(2,1)S(1)} %collective-permute-done.9.refs_3_), channel_id=1, source_target_pairs={{0,32},{8,40},{16,48},{24,56},{32,64},{40,72},{48,80},{56,88},{64,... | collective-permute-start | bytes 786440 | tf_op jit(solution)/shard_map/weight_gather/ppermute | solution.py:231
  21.7 12.0 %collective-permute-start.7 = (bf16[256,512]{1,0:T(8,128)(2,1)S(1)}, bf16[256,512]{1,0:T(8,128)(2,1)}, u32[]{:S(2)}, u32[]{:S(2)}) collective-permute-start(bf16[256,512]{1,0:T(8,128)(2,1)S(1)} %collective-permute-done.6.refs_2_), channel_id=1, source_target_pairs={{0,96},{8,104},{16,112},{24,120},{32,0},{40,8},{48,16},{56,24},{64... | collective-permute-start | bytes 786440 | tf_op jit(solution)/shard_map/weight_gather/ppermute | solution.py:231
  24.8 12.3 %collective-permute-start.8 = (bf16[256,512]{1,0:T(8,128)(2,1)S(1)}, bf16[256,512]{1,0:T(8,128)(2,1)S(1)}, u32[]{:S(2)}, u32[]{:S(2)}) collective-permute-start(bf16[256,512]{1,0:T(8,128)(2,1)S(1)} %collective-permute-done.6.refs_2_), channel_id=1, source_target_pairs={{0,32},{8,40},{16,48},{24,56},{32,64},{40,72},{48,80},{56,88},{64,... | collective-permute-start | bytes 786440 | tf_op jit(solution)/shard_map/weight_gather/ppermute | solution.py:231
  37.8 6.4 %collective-permute-start.12 = (bf16[256,4096]{1,0:T(8,128)(2,1)}, bf16[256,4096]{1,0:T(8,128)(2,1)}, u32[]{:S(2)}, u32[]{:S(2)}) collective-permute-start(bf16[256,4096]{1,0:T(8,128)(2,1)} %get-tuple-element.31), channel_id=1, source_target_pairs={{0,128},{128,0},{1,129},{129,1},{2,130},{130,2},{3,131},{131,3},{4... | collective-permute-start | bytes 6291464 | tf_op jit(solution)/shard_map/rows_swap/ppermute | solution.py:242
  38.9 19.1 %collective-permute-start.13 = (bf16[256,512]{1,0:T(8,128)(2,1)}, bf16[256,512]{1,0:T(8,128)(2,1)S(1)}, u32[]{:S(2)}, u32[]{:S(2)}) collective-permute-start(bf16[256,512]{1,0:T(8,128)(2,1)} %collective-permute-done.3.refs_8_), channel_id=1, source_target_pairs={{0,32},{8,40},{16,48},{24,56},{32,64},{40,72},{48,80},{56,88},{64,... | collective-permute-start | bytes 786440 | tf_op jit(solution)/shard_map/weight_gather/ppermute | solution.py:236
  39.2 18.8 %collective-permute-start.14 = (bf16[256,512]{1,0:T(8,128)(2,1)}, bf16[256,512]{1,0:T(8,128)(2,1)S(1)}, u32[]{:S(2)}, u32[]{:S(2)}) collective-permute-start(bf16[256,512]{1,0:T(8,128)(2,1)} %collective-permute-done.5.refs_9_), channel_id=1, source_target_pairs={{0,32},{8,40},{16,48},{24,56},{32,64},{40,72},{48,80},{56,88},{64,... | collective-permute-start | bytes 786440 | tf_op jit(solution)/shard_map/weight_gather/ppermute | solution.py:236
  40.8 17.2 %collective-permute-start.15 = (bf16[256,512]{1,0:T(8,128)(2,1)}, bf16[256,512]{1,0:T(8,128)(2,1)S(1)}, u32[]{:S(2)}, u32[]{:S(2)}) collective-permute-start(bf16[256,512]{1,0:T(8,128)(2,1)} %collective-permute-done.7.refs_6_), channel_id=1, source_target_pairs={{0,96},{8,104},{16,112},{24,120},{32,0},{40,8},{48,16},{56,24},{64... | collective-permute-start | bytes 786440 | tf_op jit(solution)/shard_map/weight_gather/ppermute | solution.py:236
  42.5 15.6 %collective-permute-start.16 = (bf16[256,512]{1,0:T(8,128)(2,1)}, bf16[256,512]{1,0:T(8,128)(2,1)S(1)}, u32[]{:S(2)}, u32[]{:S(2)}) collective-permute-start(bf16[256,512]{1,0:T(8,128)(2,1)} %collective-permute-done.10.refs_7_), channel_id=1, source_target_pairs={{0,96},{8,104},{16,112},{24,120},{32,0},{40,8},{48,16},{56,24},{64... | collective-permute-start | bytes 786440 | tf_op jit(solution)/shard_map/weight_gather/ppermute | solution.py:236
  44.2 16.7 %collective-permute-start = (s32[33,128]{1,0:T(8,128)S(1)}, s32[33,128]{1,0:T(8,128)}, u32[]{:S(2)}, u32[]{:S(2)}) collective-permute-start(s32[33,128]{1,0:T(8,128)S(1)} %fusion.10), channel_id=1, source_target_pairs={{0,128},{128,0},{1,129},{129,1},{2,130},{130,2},{3,131},{131,3},{4... | collective-permute-start | bytes 50696 | tf_op jit(solution)/shard_map/rows_swap/ppermute | solution.py:245
  46.9 28.1 %all-to-all-start = ((bf16[32,48,256]{2,1,0:T(8,128)(2,1)}), bf16[32,48,256]{2,1,0:T(8,128)(2,1)S(1)}, u32[]{:S(2)}, u32[]{:S(2)}) async-start(bf16[32,48,256]{2,1,0:T(8,128)(2,1)} %bitcast.11), calls=%async_computation | async-start | bytes 1572864 | tf_op jit(solution)/shard_map/columns_exchange/all_to_all | solution.py:276
  75.0 7.9 %collective-permute-start.24 = (f32[32,256]{1,0:T(8,128)S(1)}, f32[32,256]{1,0:T(8,128)S(1)}, u32[]{:S(2)}, u32[]{:S(2)}) collective-permute-start(f32[32,256]{1,0:T(8,128)S(1)} %add.55), channel_id=1, source_target_pairs={{0,1},{1,0},{2,3},{3,2},{4,5},{5,4},{6,7},{7,6},{8,9},{9,8},{10,11... | collective-permute-start | bytes 98312 | tf_op jit(solution)/shard_map/quant_sum/ppermute | solution.py:358
  79.8 27.1 %collective-permute-start.20 = (bf16[2,16,48,256]{3,2,1,0:T(8,128)(2,1)S(1)}, bf16[2,16,48,256]{3,2,1,0:T(8,128)(2,1)S(1)}, u32[]{:S(2)}, u32[]{:S(2)}) collective-permute-start(bf16[2,16,48,256]{3,2,1,0:T(8,128)(2,1)S(1)} %bitcast.30), channel_id=1, source_target_pairs={{0,6},{1,7},{2,0},{3,1},{4,2},{5,3},{6,4},{7,5},{8,14},{9,15},{10,... | collective-permute-start | bytes 2359304 | tf_op jit(solution)/shard_map/columns_round_x/ppermute | solution.py:360
  83.7 11.8 %collective-permute-start.25 = (bf16[128,512]{1,0:T(8,128)(2,1)S(1)}, bf16[128,512]{1,0:T(8,128)(2,1)S(1)}, u32[]{:S(2)}, u32[]{:S(2)}) collective-permute-start(bf16[128,512]{1,0:T(8,128)(2,1)S(1)} %fusion.5.own_ref), channel_id=1, source_target_pairs={{0,24},{8,0},{16,8},{24,16},{32,56},{40,32},{48,40},{56,48},{64,88... | collective-permute-start | bytes 393224 | tf_op jit(solution)/shard_map/grad_gather/ppermute | solution.py:401
  85.2 12.1 %collective-permute-start.26 = (bf16[128,512]{1,0:T(8,128)(2,1)S(1)}, bf16[128,512]{1,0:T(8,128)(2,1)S(1)}, u32[]{:S(2)}, u32[]{:S(2)}) collective-permute-start(bf16[128,512]{1,0:T(8,128)(2,1)S(1)} %fusion.5.own_ref), channel_id=1, source_target_pairs={{0,16},{8,24},{16,0},{24,8},{32,48},{40,56},{48,32},{56,40},{64,80... | collective-permute-start | bytes 393224 | tf_op jit(solution)/shard_map/grad_gather/ppermute | solution.py:401
  86.2 23.2 %collective-permute-start.21 = (bf16[2,16,48,256]{3,2,1,0:T(8,128)(2,1)S(1)}, bf16[2,16,48,256]{3,2,1,0:T(8,128)(2,1)S(1)}, u32[]{:S(2)}, u32[]{:S(2)}) collective-permute-start(bf16[2,16,48,256]{3,2,1,0:T(8,128)(2,1)S(1)} %bitcast.31), channel_id=1, source_target_pairs={{0,2},{1,3},{2,4},{3,5},{4,6},{5,7},{6,0},{7,1},{8,10},{9,11},{10,... | collective-permute-start | bytes 2359304 | tf_op jit(solution)/shard_map/columns_round_x/ppermute | solution.py:361
  87.7 9.8 %collective-permute-start.27 = (bf16[128,512]{1,0:T(8,128)(2,1)S(1)}, bf16[128,512]{1,0:T(8,128)(2,1)S(1)}, u32[]{:S(2)}, u32[]{:S(2)}) collective-permute-start(bf16[128,512]{1,0:T(8,128)(2,1)S(1)} %fusion.5.own_ref), channel_id=1, source_target_pairs={{0,8},{8,16},{16,24},{24,0},{32,40},{40,48},{48,56},{56,32},{64,72... | collective-permute-start | bytes 393224 | tf_op jit(solution)/shard_map/grad_gather/ppermute | solution.py:401
  97.3 7.4 %collective-permute-start.29 = (bf16[128,512]{1,0:T(8,128)(2,1)S(1)}, bf16[128,512]{1,0:T(8,128)(2,1)S(1)}, u32[]{:S(2)}, u32[]{:S(2)}) collective-permute-start(bf16[128,512]{1,0:T(8,128)(2,1)S(1)} %fusion.5.own_ref), channel_id=1, source_target_pairs={{0,32},{8,40},{16,48},{24,56},{32,64},{40,72},{48,80},{56,88},{64,... | collective-permute-start | bytes 393224 | tf_op jit(solution)/shard_map/grad_gather/ppermute | solution.py:400
  104.7 10.1 %collective-permute-start.30 = (bf16[384,512]{1,0:T(8,128)(2,1)S(1)}, bf16[384,512]{1,0:T(8,128)(2,1)S(1)}, u32[]{:S(2)}, u32[]{:S(2)}) collective-permute-start(bf16[384,512]{1,0:T(8,128)(2,1)S(1)} %constant_dynamic-update-slice_fusion.line_ref), channel_id=1, source_target_pairs={{0,96},{8,104},{16,112},{24,120},{32,0},{40,8},{48,16},{56,24},{64... | collective-permute-start | bytes 1179656 | tf_op jit(solution)/shard_map/grad_gather/ppermute | solution.py:406
  104.8 12.2 %collective-permute-start.31 = (bf16[384,512]{1,0:T(8,128)(2,1)S(1)}, bf16[384,512]{1,0:T(8,128)(2,1)S(1)}, u32[]{:S(2)}, u32[]{:S(2)}) collective-permute-start(bf16[384,512]{1,0:T(8,128)(2,1)S(1)} %constant_dynamic-update-slice_fusion.line_ref), channel_id=1, source_target_pairs={{0,32},{8,40},{16,48},{24,56},{32,64},{40,72},{48,80},{56,88},{64,... | collective-permute-start | bytes 1179656 | tf_op jit(solution)/shard_map/grad_gather/ppermute | solution.py:405
  106.9 10.5 %collective-permute-start.22 = (bf16[16,48,256]{2,1,0:T(8,128)(2,1)S(1)}, bf16[16,48,256]{2,1,0:T(8,128)(2,1)S(1)}, u32[]{:S(2)}, u32[]{:S(2)}) collective-permute-start(bf16[16,48,256]{2,1,0:T(8,128)(2,1)S(1)} %slice_bitcast_fusion.1), channel_id=1, source_target_pairs={{0,6},{1,7},{2,0},{3,1},{4,2},{5,3},{6,4},{7,5},{8,14},{9,15},{10,... | collective-permute-start | bytes 1179656 | tf_op jit(solution)/shard_map/columns_round_x/ppermute | solution.py:362
  109.4 9.1 %collective-permute-start.23 = (bf16[16,48,256]{2,1,0:T(8,128)(2,1)S(1)}, bf16[16,48,256]{2,1,0:T(8,128)(2,1)S(1)}, u32[]{:S(2)}, u32[]{:S(2)}) collective-permute-start(bf16[16,48,256]{2,1,0:T(8,128)(2,1)S(1)} %slice_bitcast_fusion), channel_id=1, source_target_pairs={{0,2},{1,3},{2,4},{3,5},{4,6},{5,7},{6,0},{7,1},{8,10},{9,11},{10,... | collective-permute-start | bytes 1179656 | tf_op jit(solution)/shard_map/columns_round_x/ppermute | solution.py:363
  114.9 8.9 %collective-permute-start.34 = (bf16[256,512]{1,0:T(8,128)(2,1)S(1)}, bf16[256,512]{1,0:T(8,128)(2,1)S(1)}, u32[]{:S(2)}, u32[]{:S(2)}) collective-permute-start(bf16[256,512]{1,0:T(8,128)(2,1)S(1)} %slice.61), channel_id=1, source_target_pairs={{0,96},{8,104},{16,112},{24,120},{32,0},{40,8},{48,16},{56,24},{64... | collective-permute-start | bytes 786440 | tf_op jit(solution)/shard_map/grad_gather/ppermute | solution.py:408
  116.2 6.2 %collective-permute-start.32 = (bf16[128,512]{1,0:T(8,128)(2,1)S(1)}, bf16[128,512]{1,0:T(8,128)(2,1)S(1)}, u32[]{:S(2)}, u32[]{:S(2)}) collective-permute-start(bf16[128,512]{1,0:T(8,128)(2,1)S(1)} %collective-permute-done.29.a0_ref), channel_id=1, source_target_pairs={{0,32},{8,40},{16,48},{24,56},{32,64},{40,72},{48,80},{56,88},{64,... | collective-permute-start | bytes 393224 | tf_op jit(solution)/shard_map/grad_gather/ppermute | solution.py:404
  117.0 6.8 %collective-permute-start.33 = (bf16[128,512]{1,0:T(8,128)(2,1)S(1)}, bf16[128,512]{1,0:T(8,128)(2,1)S(1)}, u32[]{:S(2)}, u32[]{:S(2)}) collective-permute-start(bf16[128,512]{1,0:T(8,128)(2,1)S(1)} %slice.60), channel_id=1, source_target_pairs={{0,32},{8,40},{16,48},{24,56},{32,64},{40,72},{48,80},{56,88},{64,... | collective-permute-start | bytes 393224 | tf_op jit(solution)/shard_map/grad_gather/ppermute | solution.py:407
  (22 other events, 357.7 us)

commit v9 on v8

--- a/solution.py
+++ b/solution.py
@@ -223,24 +223,31 @@
             name="norm",
         )(where, *in_hbm(values, norm_gain[None, :]))
     with jax.named_scope("weight_gather"):
-        after_z = lax.ppermute(torso_weight, "fsdp", z_from(1))
-        before_z = lax.ppermute(torso_weight, "fsdp", z_from(3))
-        after_z, normed_send = lax.optimization_barrier((after_z, normed_send))
-        lines = [torso_weight, after_z, lax.ppermute(after_z, "fsdp", z_from(1)), before_z]
-        near = [
+        first = (
+            lax.ppermute(torso_weight, "fsdp", z_from(1)),
+            lax.ppermute(torso_weight, "fsdp", z_from(3)),
+            lax.ppermute(torso_weight, "fsdp", y_from(1)),
+            lax.ppermute(torso_weight, "fsdp", y_from(3)),
+        )
+        first, normed_send = lax.optimization_barrier((first, normed_send))
+        after_z, before_z = first[:2]
+        normed_got = lax.ppermute(normed_send, "grp", SWAP)
+        twice_z = lax.ppermute(after_z, "fsdp", z_from(1))
+        lines = [torso_weight, after_z, twice_z, before_z]
+        near = [first[2:]] + [
             (lax.ppermute(line, "fsdp", y_from(1)), lax.ppermute(line, "fsdp", y_from(3)))
-            for line in lines
+            for line in lines[1:]
         ]
-        near = lax.optimization_barrier(near)
+        sent = list(near)
+        near[2:], normed_got = lax.optimization_barrier((near[2:], normed_got))
         far = [
-            lax.ppermute(above, "fsdp", y_from(3)) if k < 2 else lax.ppermute(below, "fsdp", y_from(1))
+            lax.ppermute(above, "fsdp", y_from(3)) if k % 2 == 0 else lax.ppermute(below, "fsdp", y_from(1))
             for k, (below, above) in enumerate(near)
         ]
 
     with jax.named_scope("rows_swap"):
-        normed_send, _ = lax.optimization_barrier((normed_send, near[0]))
-        normed_got = lax.ppermute(normed_send, "grp", SWAP)
         ints = jnp.concatenate([fractions[0].T, actions[0][None, :]], 0)
+        ints, _ = lax.optimization_barrier((ints, sent))
         kept = lax.dynamic_slice_in_dim(ints, own_rows, half, 1)
         got = lax.ppermute(lax.dynamic_slice_in_dim(ints, other_rows, half, 1), "grp", SWAP)
         target_ints = jnp.where(group == 0, kept, got)
@@ -256,7 +263,7 @@
         local_counts = jnp.sum(onehot.astype(jnp.float32), axis=0).astype(jnp.bfloat16)
         count_tile = jnp.pad(local_counts[None, :], ((0, 15), (0, block - shard_total)))
         count_tile, _ = lax.optimization_barrier(
-            (count_tile, near)
+            (count_tile, got)
         )
         pieces = pl.pallas_call(
             pieces_kernel,
@@ -277,6 +284,7 @@
             pieces.reshape(2 * shard_total, strip + 16, block), ("grp", "fsdp"), 0, 0, tiled=True
         ).reshape(2, shard_total, strip + 16, block)
         counts = jnp.sum(pieces[0, :, strip, :shard_total].astype(jnp.float32), axis=0)
+        pieces = pieces[:, :, :strip]
 
     with jax.named_scope("counts"):
         inverse = float(rows_block) / counts
@@ -329,6 +337,7 @@
         cost_estimate=work(3 * Z),
         name="early",
     )(where, *in_hbm(normed_own, normed_got, *near_chunks))
+    early, pieces = lax.optimization_barrier((early, pieces))
     keep, send = pl.pallas_call(
         late_kernel,
         out_shape=(part_shape, part_shape),
@@ -350,12 +359,6 @@
         ),
         axis=1,
     )
-    with jax.named_scope("quant_sum"):
-        quant = partial_quant
-        for flip in (2, 4):
-            quant = quant + lax.ppermute(quant, "tp", [(t, t ^ flip) for t in range(2 * X)])
-        quant, pieces = lax.optimization_barrier((quant, pieces))
-        quant = quant + lax.ppermute(quant, "tp", [(t, t ^ 1) for t in range(2 * X)])
     with jax.named_scope("columns_round_x"):
         after = lax.ppermute(pieces, "tp", x_from(1))
         before = lax.ppermute(pieces, "tp", x_from(3))
@@ -373,6 +376,11 @@
             ),
             name="columns",
         )(where, pieces, after, before, far_a, far_b)
+    with jax.named_scope("quant_sum"):
+        quant = partial_quant
+        for flip in (1, 2, 4):
+            quant = quant + lax.ppermute(quant, "tp", [(t, t ^ flip) for t in range(2 * X)])
+    quant, _ = lax.optimization_barrier((quant, (far_a, far_b)))
     target_quant = quant[:, :half]
     online_quant = quant[:, half:]
     target_value = reward_rows[None, :] + 0.99 * target_quant

time: 149 us -> 169 us (1.13)
  waiting for transfers between devices: 43.1 us -> 62.4 us
  starting transfers between devices: 58.1 us -> 55.7 us
  blocking collectives: 20.3 us -> 22.3 us
    ppermute x4 -> x5, waiting for transfers between devices: 0.43 us -> 8.02 us  [the longest x1 5.76 us: shards(): lax.ppermute(torso_weight, 'fsdp', z_from(3))]
    all_to_all x1, waiting for transfers between devices: 2.22 us -> 8.77 us  [shards(): lax.all_to_all(pieces.reshape(2 * shard_total, strip + 16, block), ('grp'...]
    ppermute x1, waiting for transfers between devices: 0.01 us -> 5.84 us  [shards(): after = lax.ppermute(pieces, 'tp', x_from(1))]
    ppermute x2 -> x3, waiting for transfers between devices: 4.46 us -> 9.13 us  [shards(): lax.ppermute(quant, 'tp', [(t, t ^ flip) for t in range(2 * X)])]
    ppermute x4 -> x5, starting transfers between devices: 9.46 us -> 5.44 us  [the longest x1 3.01 us: shards(): lax.ppermute(torso_weight, 'fsdp', y_from(1))]
    ppermute x1, waiting for transfers between devices: 3.37 us -> 0.01 us  [shards(): b0 = lax.ppermute(grad_preact, 'fsdp', y_from(1))]
    ppermute x4 -> x3, waiting for transfers between devices: 10.5 us -> 7.15 us  [shards(): lax.ppermute(line, 'fsdp', y_from(3))]
    ppermute x2 -> x3, starting transfers between devices: 4.6 us -> 7.36 us  [shards(): lax.ppermute(quant, 'tp', [(t, t ^ flip) for t in range(2 * X)])]
  transfers between devices with their start and end apart: 37 -> 37, of which waited for: 17 -> 19; matrix products, arithmetic and copies ran while one was open for 3% -> 2% of each run, Pallas kernels for 13% -> 8%
where the time goes in v9:
time: 169 us; the launch traced here: 168 us
  waiting for transfers between devices  62.4 us (37%)
  starting transfers between devices  55.7 us (33%)
  blocking collectives  22.3 us (13%)
  Pallas kernels  18.9 us (11%)
  other arithmetic  3.81 us (2%)
  matrix products  1.84 us (1%)
    all_to_all x1, blocking collectives, shards(): lax.all_to_all(updated, 'tp', split_axis=0, concat_axis=1, tiled=True)  22.3 us
    ppermute x3, starting transfers between devices, shards(): lax.ppermute(line, 'fsdp', y_from(1))  9.53 us
    ppermute x3, waiting for transfers between devices, shards(): lax.ppermute(quant, 'tp', [(t, t ^ flip) for t in range(2 * X)])  9.13 us
    all_to_all x1, waiting for transfers between devices, shards(): lax.all_to_all(pieces.reshape(2 * shard_total, strip + 16, block), ('grp'...  8.77 us
    ppermute x3, starting transfers between devices, shards(): lax.ppermute(quant, 'tp', [(t, t ^ flip) for t in range(2 * X)])  7.36 us
    ppermute x1, waiting for transfers between devices, shards(): b1 = lax.ppermute(line, 'fsdp', y_from(1))  7.16 us
    ppermute x3, waiting for transfers between devices, shards(): lax.ppermute(line, 'fsdp', y_from(3))  7.15 us
    all_to_all x1, starting transfers between devices, shards(): lax.all_to_all(pieces.reshape(2 * shard_total, strip + 16, block), ('grp'...  6.39 us
  transfers between devices with their start and end apart: 37, of which 19 were waited for; matrix products, arithmetic and copies ran while one was open for 2% of the time, Pallas kernels for 8%

profile of v9, /device:TPU:32, one launch (start us, length us, event | category | flops | bytes accessed | tf_op | source)
XLA Modules:
  0.0 167.8 jit_solution(2642896844184152008)
XLA Ops:
  2.7 3.0 %collective-permute-start.2 = (bf16[256,512]{1,0:T(8,128)(2,1)}, bf16[256,512]{1,0:T(8,128)(2,1)S(1)}, u32[]{:S(2)}, u32[]{:S(2)}) collective-permute-start(bf16[256,512]{1,0:T(8,128)(2,1)} %refs_0_.1), channel_id=1, source_target_pairs={{0,96},{8,104},{16,112},{24,120},{32,0},{40,8},{48,16},{56,24},{64... | collective-permute-start | bytes 786440 | tf_op jit(solution)/shard_map/weight_gather/ppermute | solution.py:229
  5.8 5.7 %norm.1 = (bf16[256,4096]{1,0:T(8,128)(2,1)S(1)}, bf16[256,4096]{1,0:T(8,128)(2,1)}) custom-call(s32[4]{0:T(128)S(1)} %pad_add_fusion.2.where_ref, bf16[256,8192]{1,0:T(8,128)(2,1)} %bitcast.29, f32[1,8192]{1,0:T(1,128)} %bitcast.35), custom_call_target="tpu_custom_call" | custom-call | flops 12582912 | bytes 8388608 | tf_op jit(solution)/shard_map/rows_swap/norm/pallas_call | solution.py:207
  11.6 5.8 %collective-permute-done.1.refs_3_ = bf16[256,512]{1,0:T(8,128)(2,1)S(1)} collective-permute-done((bf16[256,512]{1,0:T(8,128)(2,1)}, bf16[256,512]{1,0:T(8,128)(2,1)S(1)}, u32[]{:S(2)}, u32[]{:S(2)}) %collective-permute-start.1) | collective-permute-done | bytes 262176 | tf_op jit(solution)/shard_map/weight_gather/ppermute | solution.py:228
  17.8 3.0 %collective-permute-start.10 = (bf16[256,512]{1,0:T(8,128)(2,1)S(1)}, bf16[256,512]{1,0:T(8,128)(2,1)S(1)}, u32[]{:S(2)}, u32[]{:S(2)}) collective-permute-start(bf16[256,512]{1,0:T(8,128)(2,1)S(1)} %collective-permute-done.refs_1_), channel_id=1, source_target_pairs={{0,96},{8,104},{16,112},{24,120},{32,0},{40,8},{48,16},{56,24},{64... | collective-permute-start | bytes 786440 | tf_op jit(solution)/shard_map/weight_gather/ppermute | solution.py:238
  20.8 3.2 %collective-permute-start.7 = (bf16[256,512]{1,0:T(8,128)(2,1)S(1)}, bf16[256,512]{1,0:T(8,128)(2,1)}, u32[]{:S(2)}, u32[]{:S(2)}) collective-permute-start(bf16[256,512]{1,0:T(8,128)(2,1)S(1)} %collective-permute-done.1.refs_3_), channel_id=1, source_target_pairs={{0,96},{8,104},{16,112},{24,120},{32,0},{40,8},{48,16},{56,24},{64... | collective-permute-start | bytes 786440 | tf_op jit(solution)/shard_map/weight_gather/ppermute | solution.py:238
  24.0 2.3 %collective-permute-done.4.refs_2_ = bf16[256,512]{1,0:T(8,128)(2,1)} collective-permute-done((bf16[256,512]{1,0:T(8,128)(2,1)S(1)}, bf16[256,512]{1,0:T(8,128)(2,1)}, u32[]{:S(2)}, u32[]{:S(2)}) %collective-permute-start.4) | collective-permute-done | bytes 262176 | tf_op jit(solution)/shard_map/weight_gather/ppermute | solution.py:235
  27.9 3.3 %collective-permute-start.5 = (bf16[256,512]{1,0:T(8,128)(2,1)}, bf16[256,512]{1,0:T(8,128)(2,1)}, u32[]{:S(2)}, u32[]{:S(2)}) collective-permute-start(bf16[256,512]{1,0:T(8,128)(2,1)} %collective-permute-done.4.refs_2_), channel_id=1, source_target_pairs={{0,96},{8,104},{16,112},{24,120},{32,0},{40,8},{48,16},{56,24},{64... | collective-permute-start | bytes 786440 | tf_op jit(solution)/shard_map/weight_gather/ppermute | solution.py:238
  33.1 3.7 %collective-permute-done.8.refs_11_ = bf16[256,512]{1,0:T(8,128)(2,1)} collective-permute-done((bf16[256,512]{1,0:T(8,128)(2,1)S(1)}, bf16[256,512]{1,0:T(8,128)(2,1)}, u32[]{:S(2)}, u32[]{:S(2)}) %collective-permute-start.8) | collective-permute-done | bytes 262176 | tf_op jit(solution)/shard_map/weight_gather/ppermute | solution.py:238
  38.1 3.4 %collective-permute-done.6.refs_10_ = bf16[256,512]{1,0:T(8,128)(2,1)} collective-permute-done((bf16[256,512]{1,0:T(8,128)(2,1)}, bf16[256,512]{1,0:T(8,128)(2,1)}, u32[]{:S(2)}, u32[]{:S(2)}) %collective-permute-start.6) | collective-permute-done | bytes 262176 | tf_op jit(solution)/shard_map/weight_gather/ppermute | solution.py:238
  42.7 2.6 %pieces.1 = bf16[2,16,48,256]{3,2,1,0:T(8,128)(2,1)} custom-call(s32[4]{0:T(128)S(1)} %pad_add_fusion.2.where_ref, bf16[256,4096]{1,0:T(8,128)(2,1)S(1)} %get-tuple-element.26.own_ref, bf16[256,4096]{1,0:T(8,128)(2,1)} %collective-permute-done.9.got_ref, bf16[16,256]{1,0:T(8,128)(2,1)S(1)} %pad.4.count_ref), custom_call_target="tpu_custom_call" | custom-call | bytes 1048576 | tf_op jit(solution)/shard_map/columns_exchange/pieces/pallas_call | solution.py:268
  45.3 6.4 %all-to-all-start = ((bf16[32,48,256]{2,1,0:T(8,128)(2,1)}), bf16[32,48,256]{2,1,0:T(8,128)(2,1)S(1)}, u32[]{:S(2)}, u32[]{:S(2)}) async-start(bf16[32,48,256]{2,1,0:T(8,128)(2,1)} %bitcast.10), calls=%async_computation | async-start | bytes 1572864 | tf_op jit(solution)/shard_map/columns_exchange/all_to_all | solution.py:283
  56.8 3.0 %collective-permute-start.20 = (bf16[256,512]{1,0:T(8,128)(2,1)}, bf16[256,512]{1,0:T(8,128)(2,1)S(1)}, u32[]{:S(2)}, u32[]{:S(2)}) collective-permute-start(bf16[256,512]{1,0:T(8,128)(2,1)} %collective-permute-done.7.refs_7_), channel_id=1, source_target_pairs={{0,96},{8,104},{16,112},{24,120},{32,0},{40,8},{48,16},{56,24},{64... | collective-permute-start | bytes 786440 | tf_op jit(solution)/shard_map/weight_gather/ppermute | solution.py:244
  59.8 4.2 %early.1.early_ref = f32[512,512]{1,0:T(8,128)S(1)} custom-call(s32[4]{0:T(128)S(1)} %pad_add_fusion.2.where_ref, bf16[256,4096]{1,0:T(8,128)(2,1)} %copy-done.1, bf16[256,4096]{1,0:T(8,128)(2,1)} %collective-permute-done.9.got_ref, bf16[256,512]{1,0:T(8,128)(2,1)} %refs_0_.1, bf16[256,512]{1,0:T(8,128)(2,1)} %copy-done.4, ...), custom_call_target="tpu_custom_call" | custom-call | flops 1610612736 | bytes 7340032 | tf_op jit(solution)/shard_map/early/pallas_call | solution.py:330
  64.1 8.8 %all-to-all-done = bf16[32,48,256]{2,1,0:T(8,128)(2,1)S(1)} async-done(((bf16[32,48,256]{2,1,0:T(8,128)(2,1)}), bf16[32,48,256]{2,1,0:T(8,128)(2,1)S(1)}, u32[]{:S(2)}, u32[]{:S(2)}) %all-to-all-start) | async-done | bytes 786464 | tf_op jit(solution)/shard_map/columns_exchange/all_to_all | solution.py:283
  72.9 2.2 %collective-permute-done.19.refs_2_ = bf16[256,512]{1,0:T(8,128)(2,1)S(1)} collective-permute-done((bf16[256,512]{1,0:T(8,128)(2,1)}, bf16[256,512]{1,0:T(8,128)(2,1)S(1)}, u32[]{:S(2)}, u32[]{:S(2)}) %collective-permute-start.19) | collective-permute-done | bytes 262176 | tf_op jit(solution)/shard_map/weight_gather/ppermute | solution.py:244
  75.2 2.6 %late.1 = (f32[256,512]{1,0:T(8,128)S(1)}, f32[256,512]{1,0:T(8,128)S(1)}) custom-call(s32[4]{0:T(128)S(1)} %pad_add_fusion.2.where_ref, bf16[256,4096]{1,0:T(8,128)(2,1)} %copy-done.1, bf16[256,4096]{1,0:T(8,128)(2,1)} %collective-permute-done.9.got_ref, f32[512,512]{1,0:T(8,128)S(1)} %early.1.early_ref, ...), custom_call_target="tpu_custom_call" | custom-call | flops 536870912 | bytes 3145728 | tf_op jit(solution)/shard_map/late/pallas_call | solution.py:341
  78.5 2.8 %collective-permute-start.13 = (bf16[2,16,32,256]{3,2,1,0:T(8,128)(2,1)S(1)}, bf16[2,16,32,256]{3,2,1,0:T(8,128)(2,1)S(1)}, u32[]{:S(2)}, u32[]{:S(2)}) collective-permute-start(bf16[2,16,32,256]{3,2,1,0:T(8,128)(2,1)S(1)} %slice.54.own_ref), channel_id=1, source_target_pairs={{0,6},{1,7},{2,0},{3,1},{4,2},{5,3},{6,4},{7,5},{8,14},{9,15},{10,... | collective-permute-start | bytes 1572872 | tf_op jit(solution)/shard_map/columns_round_x/ppermute | solution.py:363
  82.1 5.2 %collective-permute-start.22 = (f32[32,256]{1,0:T(8,128)S(1)}, f32[32,256]{1,0:T(8,128)S(1)}, u32[]{:S(2)}, u32[]{:S(2)}) collective-permute-start(f32[32,256]{1,0:T(8,128)S(1)} %select_reduce_fusion), channel_id=1, source_target_pairs={{0,1},{1,0},{2,3},{3,2},{4,5},{5,4},{6,7},{7,6},{8,9},{9,8},{10,11... | collective-permute-start | bytes 98312 | tf_op jit(solution)/shard_map/quant_sum/ppermute | solution.py:382
  87.3 5.8 %collective-permute-done.13.after_ref = bf16[2,16,32,256]{3,2,1,0:T(8,128)(2,1)S(1)} collective-permute-done((bf16[2,16,32,256]{3,2,1,0:T(8,128)(2,1)S(1)}, bf16[2,16,32,256]{3,2,1,0:T(8,128)(2,1)S(1)}, u32[]{:S(2)}, u32[]{:S(2)}) %collective-permute-start.13) | collective-permute-done | bytes 524320 | tf_op jit(solution)/shard_map/columns_round_x/ppermute | solution.py:363
  93.2 3.8 %collective-permute-start.15 = (bf16[16,32,256]{2,1,0:T(8,128)(2,1)S(1)}, bf16[16,32,256]{2,1,0:T(8,128)(2,1)S(1)}, u32[]{:S(2)}, u32[]{:S(2)}) collective-permute-start(bf16[16,32,256]{2,1,0:T(8,128)(2,1)S(1)} %slice_bitcast_fusion.1), channel_id=1, source_target_pairs={{0,6},{1,7},{2,0},{3,1},{4,2},{5,3},{6,4},{7,5},{8,14},{9,15},{10,... | collective-permute-start | bytes 786440 | tf_op jit(solution)/shard_map/columns_round_x/ppermute | solution.py:365
  97.3 5.9 %collective-permute-done.23 = f32[32,256]{1,0:T(8,128)S(1)} collective-permute-done((f32[32,256]{1,0:T(8,128)S(1)}, f32[32,256]{1,0:T(8,128)S(1)}, u32[]{:S(2)}, u32[]{:S(2)}) %collective-permute-start.23) | collective-permute-done | bytes 32800 | tf_op jit(solution)/shard_map/quant_sum/ppermute | solution.py:382
  103.2 2.1 %collective-permute-start.24 = (f32[32,256]{1,0:T(8,128)S(1)}, f32[32,256]{1,0:T(8,128)S(1)}, u32[]{:S(2)}, u32[]{:S(2)}) collective-permute-start(f32[32,256]{1,0:T(8,128)S(1)} %add.56), channel_id=1, source_target_pairs={{0,4},{1,5},{2,6},{3,7},{4,0},{5,1},{6,2},{7,3},{8,12},{9,13},{10,... | collective-permute-start | bytes 98312 | tf_op jit(solution)/shard_map/quant_sum/ppermute | solution.py:382
  105.3 3.2 %collective-permute-done.24 = f32[32,256]{1,0:T(8,128)S(1)} collective-permute-done((f32[32,256]{1,0:T(8,128)S(1)}, f32[32,256]{1,0:T(8,128)S(1)}, u32[]{:S(2)}, u32[]{:S(2)}) %collective-permute-start.24) | collective-permute-done | bytes 32800 | tf_op jit(solution)/shard_map/quant_sum/ppermute | solution.py:382
  110.0 2.4 %collective-permute-start.26 = (bf16[128,512]{1,0:T(8,128)(2,1)S(1)}, bf16[128,512]{1,0:T(8,128)(2,1)S(1)}, u32[]{:S(2)}, u32[]{:S(2)}) collective-permute-start(bf16[128,512]{1,0:T(8,128)(2,1)S(1)} %fusion.5.own_ref), channel_id=1, source_target_pairs={{0,16},{8,24},{16,0},{24,8},{32,48},{40,56},{48,32},{56,40},{64,80... | collective-permute-start | bytes 393224 | tf_op jit(solution)/shard_map/grad_gather/ppermute | solution.py:409
  112.4 2.4 %collective-permute-start.27 = (bf16[128,512]{1,0:T(8,128)(2,1)S(1)}, bf16[128,512]{1,0:T(8,128)(2,1)S(1)}, u32[]{:S(2)}, u32[]{:S(2)}) collective-permute-start(bf16[128,512]{1,0:T(8,128)(2,1)S(1)} %fusion.5.own_ref), channel_id=1, source_target_pairs={{0,8},{8,16},{16,24},{24,0},{32,40},{40,48},{48,56},{56,32},{64,72... | collective-permute-start | bytes 393224 | tf_op jit(solution)/shard_map/grad_gather/ppermute | solution.py:409
  116.8 3.7 %collective-permute-done.25 = bf16[128,512]{1,0:T(8,128)(2,1)S(1)} collective-permute-done((bf16[128,512]{1,0:T(8,128)(2,1)S(1)}, bf16[128,512]{1,0:T(8,128)(2,1)S(1)}, u32[]{:S(2)}, u32[]{:S(2)}) %collective-permute-start.25) | collective-permute-done | bytes 131104 | tf_op jit(solution)/shard_map/grad_gather/ppermute | solution.py:409
  122.4 2.0 %collective-permute-start.31 = (bf16[384,512]{1,0:T(8,128)(2,1)S(1)}, bf16[384,512]{1,0:T(8,128)(2,1)S(1)}, u32[]{:S(2)}, u32[]{:S(2)}) collective-permute-start(bf16[384,512]{1,0:T(8,128)(2,1)S(1)} %constant_dynamic-update-slice_fusion.line_ref), channel_id=1, source_target_pairs={{0,32},{8,40},{16,48},{24,56},{32,64},{40,72},{48,80},{56,88},{64,... | collective-permute-start | bytes 1179656 | tf_op jit(solution)/shard_map/grad_gather/ppermute | solution.py:413
  124.4 7.2 %collective-permute-done.30.b1_ref = bf16[384,512]{1,0:T(8,128)(2,1)S(1)} collective-permute-done((bf16[384,512]{1,0:T(8,128)(2,1)S(1)}, bf16[384,512]{1,0:T(8,128)(2,1)S(1)}, u32[]{:S(2)}, u32[]{:S(2)}) %collective-permute-start.30) | collective-permute-done | bytes 393248 | tf_op jit(solution)/shard_map/grad_gather/ppermute | solution.py:414
  131.5 2.2 %collective-permute-start.34 = (bf16[256,512]{1,0:T(8,128)(2,1)S(1)}, bf16[256,512]{1,0:T(8,128)(2,1)S(1)}, u32[]{:S(2)}, u32[]{:S(2)}) collective-permute-start(bf16[256,512]{1,0:T(8,128)(2,1)S(1)} %slice.64), channel_id=1, source_target_pairs={{0,96},{8,104},{16,112},{24,120},{32,0},{40,8},{48,16},{56,24},{64... | collective-permute-start | bytes 786440 | tf_op jit(solution)/shard_map/grad_gather/ppermute | solution.py:416
  134.1 2.4 %columns.1.cols_ref = bf16[512,2048]{1,0:T(8,128)(2,1)S(1)} custom-call(s32[4]{0:T(128)S(1)} %pad_add_fusion.2.where_ref, bf16[2,16,32,256]{3,2,1,0:T(8,128)(2,1)S(1)} %slice.54.own_ref, bf16[2,16,32,256]{3,2,1,0:T(8,128)(2,1)S(1)} %collective-permute-done.13.after_ref, bf16[2,16,32,256]{3,2,1,0:T(8,128)(2,1)S(1)} %collective-permute-done.14.before_ref, ...), custom_call_target="tpu_custom_call" | custom-call | bytes 4194304 | tf_op jit(solution)/shard_map/columns_round_x/columns/pallas_call | solution.py:367
  137.4 2.5 %collective-permute-done.32.f0_ref = bf16[128,512]{1,0:T(8,128)(2,1)S(1)} collective-permute-done((bf16[128,512]{1,0:T(8,128)(2,1)S(1)}, bf16[128,512]{1,0:T(8,128)(2,1)S(1)}, u32[]{:S(2)}, u32[]{:S(2)}) %collective-permute-start.32) | collective-permute-done | bytes 131104 | tf_op jit(solution)/shard_map/grad_gather/ppermute | solution.py:412
  144.8 22.3 %all_to_all.24 = bf16[8,32,512]{2,1,0:T(8,128)(2,1)S(1)} all-to-all(bf16[8,32,512]{2,1,0:T(8,128)(2,1)S(1)} %bitcast.33), channel_id=1, replica_groups=mesh['grp'=2,'fsdp'=16,'tp'=8] {'tp'}, dimensions={0} | all-to-all | bytes 524288 | tf_op jit(solution)/shard_map/all_to_all | solution.py:447
  (123 shorter events, 27.6 us)
Async XLA Ops:
  0.6 10.9 %collective-permute-start = (bf16[256,512]{1,0:T(8,128)(2,1)}, bf16[256,512]{1,0:T(8,128)(2,1)S(1)}, u32[]{:S(2)}, u32[]{:S(2)}) collective-permute-start(bf16[256,512]{1,0:T(8,128)(2,1)} %refs_0_.1), channel_id=1, source_target_pairs={{0,24},{8,0},{16,8},{24,16},{32,56},{40,32},{48,40},{56,48},{64,88... | collective-permute-start | bytes 786440 | tf_op jit(solution)/shard_map/weight_gather/ppermute | solution.py:227
  2.6 14.8 %collective-permute-start.1 = (bf16[256,512]{1,0:T(8,128)(2,1)}, bf16[256,512]{1,0:T(8,128)(2,1)S(1)}, u32[]{:S(2)}, u32[]{:S(2)}) collective-permute-start(bf16[256,512]{1,0:T(8,128)(2,1)} %refs_0_.1), channel_id=1, source_target_pairs={{0,8},{8,16},{16,24},{24,0},{32,40},{40,48},{48,56},{56,32},{64,72... | collective-permute-start | bytes 786440 | tf_op jit(solution)/shard_map/weight_gather/ppermute | solution.py:228
  2.7 14.6 %collective-permute-start.2 = (bf16[256,512]{1,0:T(8,128)(2,1)}, bf16[256,512]{1,0:T(8,128)(2,1)S(1)}, u32[]{:S(2)}, u32[]{:S(2)}) collective-permute-start(bf16[256,512]{1,0:T(8,128)(2,1)} %refs_0_.1), channel_id=1, source_target_pairs={{0,96},{8,104},{16,112},{24,120},{32,0},{40,8},{48,16},{56,24},{64... | collective-permute-start | bytes 786440 | tf_op jit(solution)/shard_map/weight_gather/ppermute | solution.py:229
  5.8 11.6 %collective-permute-start.3 = (bf16[256,512]{1,0:T(8,128)(2,1)}, bf16[256,512]{1,0:T(8,128)(2,1)S(1)}, u32[]{:S(2)}, u32[]{:S(2)}) collective-permute-start(bf16[256,512]{1,0:T(8,128)(2,1)} %refs_0_.1), channel_id=1, source_target_pairs={{0,32},{8,40},{16,48},{24,56},{32,64},{40,72},{48,80},{56,88},{64,... | collective-permute-start | bytes 786440 | tf_op jit(solution)/shard_map/weight_gather/ppermute | solution.py:230
  17.4 25.3 %collective-permute-start.9 = (bf16[256,4096]{1,0:T(8,128)(2,1)}, bf16[256,4096]{1,0:T(8,128)(2,1)}, u32[]{:S(2)}, u32[]{:S(2)}) collective-permute-start(bf16[256,4096]{1,0:T(8,128)(2,1)} %get-tuple-element.30), channel_id=1, source_target_pairs={{0,128},{128,0},{1,129},{129,1},{2,130},{130,2},{3,131},{131,3},{4... | collective-permute-start | bytes 6291464 | tf_op jit(solution)/shard_map/weight_gather/ppermute | solution.py:234
  17.5 8.8 %collective-permute-start.4 = (bf16[256,512]{1,0:T(8,128)(2,1)S(1)}, bf16[256,512]{1,0:T(8,128)(2,1)}, u32[]{:S(2)}, u32[]{:S(2)}) collective-permute-start(bf16[256,512]{1,0:T(8,128)(2,1)S(1)} %collective-permute-done.refs_1_), channel_id=1, source_target_pairs={{0,24},{8,0},{16,8},{24,16},{32,56},{40,32},{48,40},{56,48},{64,88... | collective-permute-start | bytes 786440 | tf_op jit(solution)/shard_map/weight_gather/ppermute | solution.py:235
  17.8 10.1 %collective-permute-start.10 = (bf16[256,512]{1,0:T(8,128)(2,1)S(1)}, bf16[256,512]{1,0:T(8,128)(2,1)S(1)}, u32[]{:S(2)}, u32[]{:S(2)}) collective-permute-start(bf16[256,512]{1,0:T(8,128)(2,1)S(1)} %collective-permute-done.refs_1_), channel_id=1, source_target_pairs={{0,96},{8,104},{16,112},{24,120},{32,0},{40,8},{48,16},{56,24},{64... | collective-permute-start | bytes 786440 | tf_op jit(solution)/shard_map/weight_gather/ppermute | solution.py:238
  20.8 10.4 %collective-permute-start.11 = (bf16[256,512]{1,0:T(8,128)(2,1)S(1)}, bf16[256,512]{1,0:T(8,128)(2,1)S(1)}, u32[]{:S(2)}, u32[]{:S(2)}) collective-permute-start(bf16[256,512]{1,0:T(8,128)(2,1)S(1)} %collective-permute-done.refs_1_), channel_id=1, source_target_pairs={{0,32},{8,40},{16,48},{24,56},{32,64},{40,72},{48,80},{56,88},{64,... | collective-permute-start | bytes 786440 | tf_op jit(solution)/shard_map/weight_gather/ppermute | solution.py:238
  20.8 12.3 %collective-permute-start.7 = (bf16[256,512]{1,0:T(8,128)(2,1)S(1)}, bf16[256,512]{1,0:T(8,128)(2,1)}, u32[]{:S(2)}, u32[]{:S(2)}) collective-permute-start(bf16[256,512]{1,0:T(8,128)(2,1)S(1)} %collective-permute-done.1.refs_3_), channel_id=1, source_target_pairs={{0,96},{8,104},{16,112},{24,120},{32,0},{40,8},{48,16},{56,24},{64... | collective-permute-start | bytes 786440 | tf_op jit(solution)/shard_map/weight_gather/ppermute | solution.py:238
  26.3 10.5 %collective-permute-start.8 = (bf16[256,512]{1,0:T(8,128)(2,1)S(1)}, bf16[256,512]{1,0:T(8,128)(2,1)}, u32[]{:S(2)}, u32[]{:S(2)}) collective-permute-start(bf16[256,512]{1,0:T(8,128)(2,1)S(1)} %collective-permute-done.1.refs_3_), channel_id=1, source_target_pairs={{0,32},{8,40},{16,48},{24,56},{32,64},{40,72},{48,80},{56,88},{64,... | collective-permute-start | bytes 786440 | tf_op jit(solution)/shard_map/weight_gather/ppermute | solution.py:238
  27.9 10.2 %collective-permute-start.5 = (bf16[256,512]{1,0:T(8,128)(2,1)}, bf16[256,512]{1,0:T(8,128)(2,1)}, u32[]{:S(2)}, u32[]{:S(2)}) collective-permute-start(bf16[256,512]{1,0:T(8,128)(2,1)} %collective-permute-done.4.refs_2_), channel_id=1, source_target_pairs={{0,96},{8,104},{16,112},{24,120},{32,0},{40,8},{48,16},{56,24},{64... | collective-permute-start | bytes 786440 | tf_op jit(solution)/shard_map/weight_gather/ppermute | solution.py:238
  31.9 9.6 %collective-permute-start.6 = (bf16[256,512]{1,0:T(8,128)(2,1)}, bf16[256,512]{1,0:T(8,128)(2,1)}, u32[]{:S(2)}, u32[]{:S(2)}) collective-permute-start(bf16[256,512]{1,0:T(8,128)(2,1)} %collective-permute-done.4.refs_2_), channel_id=1, source_target_pairs={{0,32},{8,40},{16,48},{24,56},{32,64},{40,72},{48,80},{56,88},{64,... | collective-permute-start | bytes 786440 | tf_op jit(solution)/shard_map/weight_gather/ppermute | solution.py:238
  45.3 27.5 %all-to-all-start = ((bf16[32,48,256]{2,1,0:T(8,128)(2,1)}), bf16[32,48,256]{2,1,0:T(8,128)(2,1)S(1)}, u32[]{:S(2)}, u32[]{:S(2)}) async-start(bf16[32,48,256]{2,1,0:T(8,128)(2,1)} %bitcast.10), calls=%async_computation | async-start | bytes 1572864 | tf_op jit(solution)/shard_map/columns_exchange/all_to_all | solution.py:283
  53.3 19.6 %collective-permute-start.17 = (bf16[256,512]{1,0:T(8,128)(2,1)S(1)}, bf16[256,512]{1,0:T(8,128)(2,1)S(1)}, u32[]{:S(2)}, u32[]{:S(2)}) collective-permute-start(bf16[256,512]{1,0:T(8,128)(2,1)S(1)} %collective-permute-done.3.refs_8_), channel_id=1, source_target_pairs={{0,32},{8,40},{16,48},{24,56},{32,64},{40,72},{48,80},{56,88},{64,... | collective-permute-start | bytes 786440 | tf_op jit(solution)/shard_map/weight_gather/ppermute | solution.py:244
  54.8 18.1 %collective-permute-start.18 = (bf16[256,512]{1,0:T(8,128)(2,1)S(1)}, bf16[256,512]{1,0:T(8,128)(2,1)S(1)}, u32[]{:S(2)}, u32[]{:S(2)}) collective-permute-start(bf16[256,512]{1,0:T(8,128)(2,1)S(1)} %collective-permute-done.10.refs_5_), channel_id=1, source_target_pairs={{0,96},{8,104},{16,112},{24,120},{32,0},{40,8},{48,16},{56,24},{64... | collective-permute-start | bytes 786440 | tf_op jit(solution)/shard_map/weight_gather/ppermute | solution.py:244
  56.6 18.6 %collective-permute-start.19 = (bf16[256,512]{1,0:T(8,128)(2,1)}, bf16[256,512]{1,0:T(8,128)(2,1)S(1)}, u32[]{:S(2)}, u32[]{:S(2)}) collective-permute-start(bf16[256,512]{1,0:T(8,128)(2,1)} %collective-permute-done.6.refs_10_), channel_id=1, source_target_pairs={{0,32},{8,40},{16,48},{24,56},{32,64},{40,72},{48,80},{56,88},{64,... | collective-permute-start | bytes 786440 | tf_op jit(solution)/shard_map/weight_gather/ppermute | solution.py:244
  56.8 18.3 %collective-permute-start.20 = (bf16[256,512]{1,0:T(8,128)(2,1)}, bf16[256,512]{1,0:T(8,128)(2,1)S(1)}, u32[]{:S(2)}, u32[]{:S(2)}) collective-permute-start(bf16[256,512]{1,0:T(8,128)(2,1)} %collective-permute-done.7.refs_7_), channel_id=1, source_target_pairs={{0,96},{8,104},{16,112},{24,120},{32,0},{40,8},{48,16},{56,24},{64... | collective-permute-start | bytes 786440 | tf_op jit(solution)/shard_map/weight_gather/ppermute | solution.py:244
  78.5 14.7 %collective-permute-start.13 = (bf16[2,16,32,256]{3,2,1,0:T(8,128)(2,1)S(1)}, bf16[2,16,32,256]{3,2,1,0:T(8,128)(2,1)S(1)}, u32[]{:S(2)}, u32[]{:S(2)}) collective-permute-start(bf16[2,16,32,256]{3,2,1,0:T(8,128)(2,1)S(1)} %slice.54.own_ref), channel_id=1, source_target_pairs={{0,6},{1,7},{2,0},{3,1},{4,2},{5,3},{6,4},{7,5},{8,14},{9,15},{10,... | collective-permute-start | bytes 1572872 | tf_op jit(solution)/shard_map/columns_round_x/ppermute | solution.py:363
  81.3 15.6 %collective-permute-start.14 = (bf16[2,16,32,256]{3,2,1,0:T(8,128)(2,1)S(1)}, bf16[2,16,32,256]{3,2,1,0:T(8,128)(2,1)S(1)}, u32[]{:S(2)}, u32[]{:S(2)}) collective-permute-start(bf16[2,16,32,256]{3,2,1,0:T(8,128)(2,1)S(1)} %slice.54.own_ref), channel_id=1, source_target_pairs={{0,2},{1,3},{2,4},{3,5},{4,6},{5,7},{6,0},{7,1},{8,10},{9,11},{10,... | collective-permute-start | bytes 1572872 | tf_op jit(solution)/shard_map/columns_round_x/ppermute | solution.py:364
  82.1 14.9 %collective-permute-start.22 = (f32[32,256]{1,0:T(8,128)S(1)}, f32[32,256]{1,0:T(8,128)S(1)}, u32[]{:S(2)}, u32[]{:S(2)}) collective-permute-start(f32[32,256]{1,0:T(8,128)S(1)} %select_reduce_fusion), channel_id=1, source_target_pairs={{0,1},{1,0},{2,3},{3,2},{4,5},{5,4},{6,7},{7,6},{8,9},{9,8},{10,11... | collective-permute-start | bytes 98312 | tf_op jit(solution)/shard_map/quant_sum/ppermute | solution.py:382
  93.2 15.4 %collective-permute-start.15 = (bf16[16,32,256]{2,1,0:T(8,128)(2,1)S(1)}, bf16[16,32,256]{2,1,0:T(8,128)(2,1)S(1)}, u32[]{:S(2)}, u32[]{:S(2)}) collective-permute-start(bf16[16,32,256]{2,1,0:T(8,128)(2,1)S(1)} %slice_bitcast_fusion.1), channel_id=1, source_target_pairs={{0,6},{1,7},{2,0},{3,1},{4,2},{5,3},{6,4},{7,5},{8,14},{9,15},{10,... | collective-permute-start | bytes 786440 | tf_op jit(solution)/shard_map/columns_round_x/ppermute | solution.py:365
  97.0 11.6 %collective-permute-start.16 = (bf16[16,32,256]{2,1,0:T(8,128)(2,1)S(1)}, bf16[16,32,256]{2,1,0:T(8,128)(2,1)S(1)}, u32[]{:S(2)}, u32[]{:S(2)}) collective-permute-start(bf16[16,32,256]{2,1,0:T(8,128)(2,1)S(1)} %slice_bitcast_fusion), channel_id=1, source_target_pairs={{0,2},{1,3},{2,4},{3,5},{4,6},{5,7},{6,0},{7,1},{8,10},{9,11},{10,... | collective-permute-start | bytes 786440 | tf_op jit(solution)/shard_map/columns_round_x/ppermute | solution.py:366
  109.4 11.1 %collective-permute-start.25 = (bf16[128,512]{1,0:T(8,128)(2,1)S(1)}, bf16[128,512]{1,0:T(8,128)(2,1)S(1)}, u32[]{:S(2)}, u32[]{:S(2)}) collective-permute-start(bf16[128,512]{1,0:T(8,128)(2,1)S(1)} %fusion.5.own_ref), channel_id=1, source_target_pairs={{0,24},{8,0},{16,8},{24,16},{32,56},{40,32},{48,40},{56,48},{64,88... | collective-permute-start | bytes 393224 | tf_op jit(solution)/shard_map/grad_gather/ppermute | solution.py:409
  110.0 10.4 %collective-permute-start.26 = (bf16[128,512]{1,0:T(8,128)(2,1)S(1)}, bf16[128,512]{1,0:T(8,128)(2,1)S(1)}, u32[]{:S(2)}, u32[]{:S(2)}) collective-permute-start(bf16[128,512]{1,0:T(8,128)(2,1)S(1)} %fusion.5.own_ref), channel_id=1, source_target_pairs={{0,16},{8,24},{16,0},{24,8},{32,48},{40,56},{48,32},{56,40},{64,80... | collective-permute-start | bytes 393224 | tf_op jit(solution)/shard_map/grad_gather/ppermute | solution.py:409
  112.4 8.7 %collective-permute-start.27 = (bf16[128,512]{1,0:T(8,128)(2,1)S(1)}, bf16[128,512]{1,0:T(8,128)(2,1)S(1)}, u32[]{:S(2)}, u32[]{:S(2)}) collective-permute-start(bf16[128,512]{1,0:T(8,128)(2,1)S(1)} %fusion.5.own_ref), channel_id=1, source_target_pairs={{0,8},{8,16},{16,24},{24,0},{32,40},{40,48},{48,56},{56,32},{64,72... | collective-permute-start | bytes 393224 | tf_op jit(solution)/shard_map/grad_gather/ppermute | solution.py:409
  114.7 6.4 %collective-permute-start.28 = (bf16[128,512]{1,0:T(8,128)(2,1)S(1)}, bf16[128,512]{1,0:T(8,128)(2,1)S(1)}, u32[]{:S(2)}, u32[]{:S(2)}) collective-permute-start(bf16[128,512]{1,0:T(8,128)(2,1)S(1)} %fusion.5.own_ref), channel_id=1, source_target_pairs={{0,96},{8,104},{16,112},{24,120},{32,0},{40,8},{48,16},{56,24},{64... | collective-permute-start | bytes 393224 | tf_op jit(solution)/shard_map/grad_gather/ppermute | solution.py:407
  116.0 6.2 %collective-permute-start.29 = (bf16[128,512]{1,0:T(8,128)(2,1)S(1)}, bf16[128,512]{1,0:T(8,128)(2,1)S(1)}, u32[]{:S(2)}, u32[]{:S(2)}) collective-permute-start(bf16[128,512]{1,0:T(8,128)(2,1)S(1)} %fusion.5.own_ref), channel_id=1, source_target_pairs={{0,32},{8,40},{16,48},{24,56},{32,64},{40,72},{48,80},{56,88},{64,... | collective-permute-start | bytes 393224 | tf_op jit(solution)/shard_map/grad_gather/ppermute | solution.py:408
  122.3 9.3 %collective-permute-start.30 = (bf16[384,512]{1,0:T(8,128)(2,1)S(1)}, bf16[384,512]{1,0:T(8,128)(2,1)S(1)}, u32[]{:S(2)}, u32[]{:S(2)}) collective-permute-start(bf16[384,512]{1,0:T(8,128)(2,1)S(1)} %constant_dynamic-update-slice_fusion.line_ref), channel_id=1, source_target_pairs={{0,96},{8,104},{16,112},{24,120},{32,0},{40,8},{48,16},{56,24},{64... | collective-permute-start | bytes 1179656 | tf_op jit(solution)/shard_map/grad_gather/ppermute | solution.py:414
  122.4 11.4 %collective-permute-start.31 = (bf16[384,512]{1,0:T(8,128)(2,1)S(1)}, bf16[384,512]{1,0:T(8,128)(2,1)S(1)}, u32[]{:S(2)}, u32[]{:S(2)}) collective-permute-start(bf16[384,512]{1,0:T(8,128)(2,1)S(1)} %constant_dynamic-update-slice_fusion.line_ref), channel_id=1, source_target_pairs={{0,32},{8,40},{16,48},{24,56},{32,64},{40,72},{48,80},{56,88},{64,... | collective-permute-start | bytes 1179656 | tf_op jit(solution)/shard_map/grad_gather/ppermute | solution.py:413
  131.5 9.8 %collective-permute-start.34 = (bf16[256,512]{1,0:T(8,128)(2,1)S(1)}, bf16[256,512]{1,0:T(8,128)(2,1)S(1)}, u32[]{:S(2)}, u32[]{:S(2)}) collective-permute-start(bf16[256,512]{1,0:T(8,128)(2,1)S(1)} %slice.64), channel_id=1, source_target_pairs={{0,96},{8,104},{16,112},{24,120},{32,0},{40,8},{48,16},{56,24},{64... | collective-permute-start | bytes 786440 | tf_op jit(solution)/shard_map/grad_gather/ppermute | solution.py:416
  133.8 6.2 %collective-permute-start.32 = (bf16[128,512]{1,0:T(8,128)(2,1)S(1)}, bf16[128,512]{1,0:T(8,128)(2,1)S(1)}, u32[]{:S(2)}, u32[]{:S(2)}) collective-permute-start(bf16[128,512]{1,0:T(8,128)(2,1)S(1)} %collective-permute-done.29.a0_ref), channel_id=1, source_target_pairs={{0,32},{8,40},{16,48},{24,56},{32,64},{40,72},{48,80},{56,88},{64,... | collective-permute-start | bytes 393224 | tf_op jit(solution)/shard_map/grad_gather/ppermute | solution.py:412
  133.8 7.6 %collective-permute-start.33 = (bf16[128,512]{1,0:T(8,128)(2,1)S(1)}, bf16[128,512]{1,0:T(8,128)(2,1)S(1)}, u32[]{:S(2)}, u32[]{:S(2)}) collective-permute-start(bf16[128,512]{1,0:T(8,128)(2,1)S(1)} %slice.63), channel_id=1, source_target_pairs={{0,32},{8,40},{16,48},{24,56},{32,64},{40,72},{48,80},{56,88},{64,... | collective-permute-start | bytes 393224 | tf_op jit(solution)/shard_map/grad_gather/ppermute | solution.py:415
  (22 other events, 385.9 us)

commit v10 on v8

--- a/solution.py
+++ b/solution.py
@@ -399,7 +399,7 @@
         b0 = lax.ppermute(grad_preact, "fsdp", y_from(1))
         a0 = lax.ppermute(grad_preact, "fsdp", y_from(3))
         pieces_z = tuple(lax.ppermute(grad_preact, "fsdp", z_from(k)) for k in range(1, Z))
-        pieces_z, _ = lax.optimization_barrier((pieces_z, (b0, a0)))
+        pieces_z, _ = lax.optimization_barrier((pieces_z, b0))
         line = jnp.concatenate(pieces_z, 0)
         f0 = lax.ppermute(a0, "fsdp", y_from(3))
         a1 = lax.ppermute(line, "fsdp", y_from(3))

time: 149 us -> 150 us (level)
  starting transfers between devices: 58.1 us -> 56.4 us
    ppermute x1, waiting for transfers between devices: 3.37 us -> 5.44 us  [shards(): b0 = lax.ppermute(grad_preact, 'fsdp', y_from(1))]
    ppermute x1, starting transfers between devices: 1.86 us -> 0.01 us  [shards(): b0 = lax.ppermute(grad_preact, 'fsdp', y_from(1))]
    ppermute x1, starting transfers between devices: 2.45 us -> 4.24 us  [shards(): far_a = lax.ppermute(after[0], 'tp', x_from(1))]
  transfers between devices with their start and end apart: 37 -> 37, of which waited for: 17 -> 18; matrix products, arithmetic and copies ran while one was open for 3% -> 3% of each run, Pallas kernels for 13% -> 12%
where the time goes in v10:
time: 150 us; the launch traced here: 149 us
  starting transfers between devices  56.4 us (38%)
  waiting for transfers between devices  44.4 us (30%)
  blocking collectives  21.6 us (14%)
  Pallas kernels  18.9 us (13%)
  other arithmetic  3.26 us (2%)
  matrix products  1.84 us (1%)
  local copies, waits for them, and re-layouts  1.63 us (1%)
    all_to_all x1, blocking collectives, shards(): lax.all_to_all(updated, 'tp', split_axis=0, concat_axis=1, tiled=True)  21.6 us
    ppermute x4, starting transfers between devices, shards(): lax.ppermute(line, 'fsdp', y_from(1))  10.5 us
    ppermute x4, waiting for transfers between devices, shards(): lax.ppermute(line, 'fsdp', y_from(3))  10.5 us
    all_to_all x1, starting transfers between devices, shards(): lax.all_to_all(pieces.reshape(2 * shard_total, strip + 16, block), ('grp'...  6.8 us
    ppermute x3, waiting for transfers between devices, shards(): lax.ppermute(grad_preact, 'fsdp', z_from(k))  6.16 us
    pallas_call x1, Pallas kernels, shards(): pl.pallas_call(norm_kernel, grid=(rows_block // tile,), out_shape=(jax.Sh...  5.77 us
    ppermute x1, waiting for transfers between devices, shards(): b0 = lax.ppermute(grad_preact, 'fsdp', y_from(1))  5.44 us
    ppermute x3, starting transfers between devices, shards(): lax.ppermute(grad_preact, 'fsdp', z_from(k))  4.84 us
  transfers between devices with their start and end apart: 37, of which 18 were waited for; matrix products, arithmetic and copies ran while one was open for 3% of the time, Pallas kernels for 12%

profile of v10, /device:TPU:32, one launch (start us, length us, event | category | flops | bytes accessed | tf_op | source)
XLA Modules:
  0.0 149.2 jit_solution(1288544300498392634)
XLA Ops:
  0.6 1.9 %collective-permute-start.1 = (bf16[256,512]{1,0:T(8,128)(2,1)}, bf16[256,512]{1,0:T(8,128)(2,1)S(1)}, u32[]{:S(2)}, u32[]{:S(2)}) collective-permute-start(bf16[256,512]{1,0:T(8,128)(2,1)} %refs_0_.1), channel_id=1, source_target_pairs={{0,24},{8,0},{16,8},{24,16},{32,56},{40,32},{48,40},{56,48},{64,88... | collective-permute-start | bytes 786440 | tf_op jit(solution)/shard_map/weight_gather/ppermute | solution.py:226
  2.7 3.0 %collective-permute-start.2 = (bf16[256,512]{1,0:T(8,128)(2,1)}, bf16[256,512]{1,0:T(8,128)(2,1)S(1)}, u32[]{:S(2)}, u32[]{:S(2)}) collective-permute-start(bf16[256,512]{1,0:T(8,128)(2,1)} %refs_0_.1), channel_id=1, source_target_pairs={{0,96},{8,104},{16,112},{24,120},{32,0},{40,8},{48,16},{56,24},{64... | collective-permute-start | bytes 786440 | tf_op jit(solution)/shard_map/weight_gather/ppermute | solution.py:231
  5.9 5.8 %norm.1 = (bf16[256,4096]{1,0:T(8,128)(2,1)S(1)}, bf16[256,4096]{1,0:T(8,128)(2,1)}) custom-call(s32[4]{0:T(128)S(1)} %pad_add_fusion.1.where_ref, bf16[256,8192]{1,0:T(8,128)(2,1)} %bitcast.33, f32[1,8192]{1,0:T(1,128)} %bitcast.39), custom_call_target="tpu_custom_call" | custom-call | flops 12582912 | bytes 8388608 | tf_op jit(solution)/shard_map/rows_swap/norm/pallas_call | solution.py:207
  11.6 2.8 %collective-permute-start.6 = (bf16[256,512]{1,0:T(8,128)(2,1)S(1)}, bf16[256,512]{1,0:T(8,128)(2,1)S(1)}, u32[]{:S(2)}, u32[]{:S(2)}) collective-permute-start(bf16[256,512]{1,0:T(8,128)(2,1)S(1)} %collective-permute-done.1.refs_1_), channel_id=1, source_target_pairs={{0,24},{8,0},{16,8},{24,16},{32,56},{40,32},{48,40},{56,48},{64,88... | collective-permute-start | bytes 786440 | tf_op jit(solution)/shard_map/weight_gather/ppermute | solution.py:229
  14.4 3.2 %collective-permute-start.4 = (bf16[256,512]{1,0:T(8,128)(2,1)S(1)}, bf16[256,512]{1,0:T(8,128)(2,1)S(1)}, u32[]{:S(2)}, u32[]{:S(2)}) collective-permute-start(bf16[256,512]{1,0:T(8,128)(2,1)S(1)} %collective-permute-done.1.refs_1_), channel_id=1, source_target_pairs={{0,96},{8,104},{16,112},{24,120},{32,0},{40,8},{48,16},{56,24},{64... | collective-permute-start | bytes 786440 | tf_op jit(solution)/shard_map/weight_gather/ppermute | solution.py:231
  17.7 2.0 %collective-permute-start.5 = (bf16[256,512]{1,0:T(8,128)(2,1)S(1)}, bf16[256,512]{1,0:T(8,128)(2,1)}, u32[]{:S(2)}, u32[]{:S(2)}) collective-permute-start(bf16[256,512]{1,0:T(8,128)(2,1)S(1)} %collective-permute-done.1.refs_1_), channel_id=1, source_target_pairs={{0,32},{8,40},{16,48},{24,56},{32,64},{40,72},{48,80},{56,88},{64,... | collective-permute-start | bytes 786440 | tf_op jit(solution)/shard_map/weight_gather/ppermute | solution.py:231
  21.7 3.0 %collective-permute-start.7 = (bf16[256,512]{1,0:T(8,128)(2,1)S(1)}, bf16[256,512]{1,0:T(8,128)(2,1)}, u32[]{:S(2)}, u32[]{:S(2)}) collective-permute-start(bf16[256,512]{1,0:T(8,128)(2,1)S(1)} %collective-permute-done.6.refs_2_), channel_id=1, source_target_pairs={{0,96},{8,104},{16,112},{24,120},{32,0},{40,8},{48,16},{56,24},{64... | collective-permute-start | bytes 786440 | tf_op jit(solution)/shard_map/weight_gather/ppermute | solution.py:231
  24.8 3.5 %collective-permute-done.5.refs_9_ = bf16[256,512]{1,0:T(8,128)(2,1)} collective-permute-done((bf16[256,512]{1,0:T(8,128)(2,1)S(1)}, bf16[256,512]{1,0:T(8,128)(2,1)}, u32[]{:S(2)}, u32[]{:S(2)}) %collective-permute-start.5) | collective-permute-done | bytes 262176 | tf_op jit(solution)/shard_map/weight_gather/ppermute | solution.py:231
  28.2 1.8 %collective-permute-done.10.refs_7_ = bf16[256,512]{1,0:T(8,128)(2,1)} collective-permute-done((bf16[256,512]{1,0:T(8,128)(2,1)S(1)}, bf16[256,512]{1,0:T(8,128)(2,1)}, u32[]{:S(2)}, u32[]{:S(2)}) %collective-permute-start.10) | collective-permute-done | bytes 262176 | tf_op jit(solution)/shard_map/weight_gather/ppermute | solution.py:231
  30.0 3.7 %collective-permute-done.11.refs_11_ = bf16[256,512]{1,0:T(8,128)(2,1)S(1)} collective-permute-done((bf16[256,512]{1,0:T(8,128)(2,1)S(1)}, bf16[256,512]{1,0:T(8,128)(2,1)S(1)}, u32[]{:S(2)}, u32[]{:S(2)}) %collective-permute-start.11) | collective-permute-done | bytes 262176 | tf_op jit(solution)/shard_map/weight_gather/ppermute | solution.py:231
  33.7 3.3 %collective-permute-done.8.refs_10_ = bf16[256,512]{1,0:T(8,128)(2,1)S(1)} collective-permute-done((bf16[256,512]{1,0:T(8,128)(2,1)S(1)}, bf16[256,512]{1,0:T(8,128)(2,1)S(1)}, u32[]{:S(2)}, u32[]{:S(2)}) %collective-permute-start.8) | collective-permute-done | bytes 262176 | tf_op jit(solution)/shard_map/weight_gather/ppermute | solution.py:231
  40.8 1.7 %collective-permute-start.15 = (bf16[256,512]{1,0:T(8,128)(2,1)}, bf16[256,512]{1,0:T(8,128)(2,1)S(1)}, u32[]{:S(2)}, u32[]{:S(2)}) collective-permute-start(bf16[256,512]{1,0:T(8,128)(2,1)} %collective-permute-done.7.refs_6_), channel_id=1, source_target_pairs={{0,96},{8,104},{16,112},{24,120},{32,0},{40,8},{48,16},{56,24},{64... | collective-permute-start | bytes 786440 | tf_op jit(solution)/shard_map/weight_gather/ppermute | solution.py:236
  42.5 1.7 %collective-permute-start.16 = (bf16[256,512]{1,0:T(8,128)(2,1)}, bf16[256,512]{1,0:T(8,128)(2,1)S(1)}, u32[]{:S(2)}, u32[]{:S(2)}) collective-permute-start(bf16[256,512]{1,0:T(8,128)(2,1)} %collective-permute-done.10.refs_7_), channel_id=1, source_target_pairs={{0,96},{8,104},{16,112},{24,120},{32,0},{40,8},{48,16},{56,24},{64... | collective-permute-start | bytes 786440 | tf_op jit(solution)/shard_map/weight_gather/ppermute | solution.py:236
  44.3 2.6 %pieces.1 = bf16[2,16,48,256]{3,2,1,0:T(8,128)(2,1)} custom-call(s32[4]{0:T(128)S(1)} %pad_add_fusion.1.where_ref, bf16[256,4096]{1,0:T(8,128)(2,1)S(1)} %get-tuple-element.25.own_ref, bf16[256,4096]{1,0:T(8,128)(2,1)} %collective-permute-done.12.got_ref, bf16[16,256]{1,0:T(8,128)(2,1)S(1)} %pad.4.count_ref), custom_call_target="tpu_custom_call" | custom-call | bytes 1048576 | tf_op jit(solution)/shard_map/columns_exchange/pieces/pallas_call | solution.py:261
  46.9 6.8 %all-to-all-start = ((bf16[32,48,256]{2,1,0:T(8,128)(2,1)}), bf16[32,48,256]{2,1,0:T(8,128)(2,1)S(1)}, u32[]{:S(2)}, u32[]{:S(2)}) async-start(bf16[32,48,256]{2,1,0:T(8,128)(2,1)} %bitcast.11), calls=%async_computation | async-start | bytes 1572864 | tf_op jit(solution)/shard_map/columns_exchange/all_to_all | solution.py:276
  53.7 4.2 %early.1.early_ref = f32[512,512]{1,0:T(8,128)S(1)} custom-call(s32[4]{0:T(128)S(1)} %pad_add_fusion.1.where_ref, bf16[256,4096]{1,0:T(8,128)(2,1)} %copy-done.1, bf16[256,4096]{1,0:T(8,128)(2,1)} %collective-permute-done.12.got_ref, bf16[256,512]{1,0:T(8,128)(2,1)} %refs_0_.1, bf16[256,512]{1,0:T(8,128)(2,1)} %copy-done.3, bf16[256,512]{1,0:T(8,128)(2,1)} %copy-done.6, ...), custom_call_target="tpu_custom_call" | custom-call | flops 1610612736 | bytes 7340032 | tf_op jit(solution)/shard_map/early/pallas_call | solution.py:322
  58.0 2.6 %late.1 = (f32[256,512]{1,0:T(8,128)S(1)}, f32[256,512]{1,0:T(8,128)S(1)}) custom-call(s32[4]{0:T(128)S(1)} %pad_add_fusion.1.where_ref, bf16[256,4096]{1,0:T(8,128)(2,1)} %copy-done.1, bf16[256,4096]{1,0:T(8,128)(2,1)} %collective-permute-done.12.got_ref, f32[512,512]{1,0:T(8,128)S(1)} %early.1.early_ref, ...), custom_call_target="tpu_custom_call" | custom-call | flops 536870912 | bytes 3145728 | tf_op jit(solution)/shard_map/late/pallas_call | solution.py:332
  65.0 2.3 %collective-permute-done.18 = f32[32,256]{1,0:T(8,128)S(1)} collective-permute-done((f32[32,256]{1,0:T(8,128)S(1)}, f32[32,256]{1,0:T(8,128)S(1)}, u32[]{:S(2)}, u32[]{:S(2)}) %collective-permute-start.18) | collective-permute-done | bytes 32800 | tf_op jit(solution)/shard_map/quant_sum/ppermute | solution.py:356
  67.4 3.0 %collective-permute-start.19 = (f32[32,256]{1,0:T(8,128)S(1)}, f32[32,256]{1,0:T(8,128)S(1)}, u32[]{:S(2)}, u32[]{:S(2)}) collective-permute-start(f32[32,256]{1,0:T(8,128)S(1)} %add.54), channel_id=1, source_target_pairs={{0,4},{1,5},{2,6},{3,7},{4,0},{5,1},{6,2},{7,3},{8,12},{9,13},{10,... | collective-permute-start | bytes 98312 | tf_op jit(solution)/shard_map/quant_sum/ppermute | solution.py:356
  70.7 2.1 %collective-permute-done.19 = f32[32,256]{1,0:T(8,128)S(1)} collective-permute-done((f32[32,256]{1,0:T(8,128)S(1)}, f32[32,256]{1,0:T(8,128)S(1)}, u32[]{:S(2)}, u32[]{:S(2)}) %collective-permute-start.19) | collective-permute-done | bytes 32800 | tf_op jit(solution)/shard_map/quant_sum/ppermute | solution.py:356
  72.8 2.2 %all-to-all-done = bf16[32,48,256]{2,1,0:T(8,128)(2,1)S(1)} async-done(((bf16[32,48,256]{2,1,0:T(8,128)(2,1)}), bf16[32,48,256]{2,1,0:T(8,128)(2,1)S(1)}, u32[]{:S(2)}, u32[]{:S(2)}) %all-to-all-start) | async-done | bytes 786464 | tf_op jit(solution)/shard_map/columns_exchange/all_to_all | solution.py:276
  75.0 4.6 %collective-permute-start.24 = (f32[32,256]{1,0:T(8,128)S(1)}, f32[32,256]{1,0:T(8,128)S(1)}, u32[]{:S(2)}, u32[]{:S(2)}) collective-permute-start(f32[32,256]{1,0:T(8,128)S(1)} %add.55), channel_id=1, source_target_pairs={{0,1},{1,0},{2,3},{3,2},{4,5},{5,4},{6,7},{7,6},{8,9},{9,8},{10,11... | collective-permute-start | bytes 98312 | tf_op jit(solution)/shard_map/quant_sum/ppermute | solution.py:358
  79.8 2.8 %collective-permute-start.20 = (bf16[2,16,48,256]{3,2,1,0:T(8,128)(2,1)S(1)}, bf16[2,16,48,256]{3,2,1,0:T(8,128)(2,1)S(1)}, u32[]{:S(2)}, u32[]{:S(2)}) collective-permute-start(bf16[2,16,48,256]{3,2,1,0:T(8,128)(2,1)S(1)} %bitcast.30), channel_id=1, source_target_pairs={{0,6},{1,7},{2,0},{3,1},{4,2},{5,3},{6,4},{7,5},{8,14},{9,15},{10,... | collective-permute-start | bytes 2359304 | tf_op jit(solution)/shard_map/columns_round_x/ppermute | solution.py:360
  87.7 2.4 %collective-permute-start.27 = (bf16[128,512]{1,0:T(8,128)(2,1)S(1)}, bf16[128,512]{1,0:T(8,128)(2,1)S(1)}, u32[]{:S(2)}, u32[]{:S(2)}) collective-permute-start(bf16[128,512]{1,0:T(8,128)(2,1)S(1)} %fusion.5.own_ref), channel_id=1, source_target_pairs={{0,8},{8,16},{16,24},{24,0},{32,40},{40,48},{48,56},{56,32},{64,72... | collective-permute-start | bytes 393224 | tf_op jit(solution)/shard_map/grad_gather/ppermute | solution.py:401
  90.0 5.2 %collective-permute-done.25 = bf16[128,512]{1,0:T(8,128)(2,1)S(1)} collective-permute-done((bf16[128,512]{1,0:T(8,128)(2,1)S(1)}, bf16[128,512]{1,0:T(8,128)(2,1)S(1)}, u32[]{:S(2)}, u32[]{:S(2)}) %collective-permute-start.25) | collective-permute-done | bytes 131104 | tf_op jit(solution)/shard_map/grad_gather/ppermute | solution.py:401
  96.2 5.4 %collective-permute-done.28.b0_ref = bf16[128,512]{1,0:T(8,128)(2,1)S(1)} collective-permute-done((bf16[128,512]{1,0:T(8,128)(2,1)S(1)}, bf16[128,512]{1,0:T(8,128)(2,1)S(1)}, u32[]{:S(2)}, u32[]{:S(2)}) %collective-permute-start.28) | collective-permute-done | bytes 131104 | tf_op jit(solution)/shard_map/grad_gather/ppermute | solution.py:399
  104.0 4.2 %collective-permute-start.22 = (bf16[16,48,256]{2,1,0:T(8,128)(2,1)S(1)}, bf16[16,48,256]{2,1,0:T(8,128)(2,1)S(1)}, u32[]{:S(2)}, u32[]{:S(2)}) collective-permute-start(bf16[16,48,256]{2,1,0:T(8,128)(2,1)S(1)} %slice_bitcast_fusion.1), channel_id=1, source_target_pairs={{0,6},{1,7},{2,0},{3,1},{4,2},{5,3},{6,4},{7,5},{8,14},{9,15},{10,... | collective-permute-start | bytes 1179656 | tf_op jit(solution)/shard_map/columns_round_x/ppermute | solution.py:362
  108.5 4.1 %collective-permute-done.29.b1_ref = bf16[384,512]{1,0:T(8,128)(2,1)S(1)} collective-permute-done((bf16[384,512]{1,0:T(8,128)(2,1)S(1)}, bf16[384,512]{1,0:T(8,128)(2,1)S(1)}, u32[]{:S(2)}, u32[]{:S(2)}) %collective-permute-start.29) | collective-permute-done | bytes 393248 | tf_op jit(solution)/shard_map/grad_gather/ppermute | solution.py:406
  113.1 2.8 %collective-permute-done.30.a0_ref = bf16[128,512]{1,0:T(8,128)(2,1)S(1)} collective-permute-done((bf16[128,512]{1,0:T(8,128)(2,1)S(1)}, bf16[128,512]{1,0:T(8,128)(2,1)S(1)}, u32[]{:S(2)}, u32[]{:S(2)}) %collective-permute-start.30) | collective-permute-done | bytes 131104 | tf_op jit(solution)/shard_map/grad_gather/ppermute | solution.py:400
  117.4 2.4 %columns.1.cols_ref = bf16[512,2048]{1,0:T(8,128)(2,1)S(1)} custom-call(s32[4]{0:T(128)S(1)} %pad_add_fusion.1.where_ref, bf16[2,16,48,256]{3,2,1,0:T(8,128)(2,1)S(1)} %bitcast.32, bf16[2,16,48,256]{3,2,1,0:T(8,128)(2,1)S(1)} %collective-permute-done.20.after_ref, bf16[2,16,48,256]{3,2,1,0:T(8,128)(2,1)S(1)} %collective-permute-done.21.before_ref, ...), custom_call_target="tpu_custom_call" | custom-call | bytes 4194304 | tf_op jit(solution)/shard_map/columns_round_x/columns/pallas_call | solution.py:364
  124.0 1.9 %collective-permute-done.35 = f32[256,512]{1,0:T(8,128)S(1)} collective-permute-done((f32[256,512]{1,0:T(8,128)S(1)}, f32[256,512]{1,0:T(8,128)S(1)}, u32[]{:S(2)}, u32[]{:S(2)}) %collective-permute-start.35) | collective-permute-done | bytes 524320 | tf_op jit(solution)/shard_map/ppermute | solution.py:437
  126.8 21.6 %all_to_all.24 = bf16[8,32,512]{2,1,0:T(8,128)(2,1)S(1)} all-to-all(bf16[8,32,512]{2,1,0:T(8,128)(2,1)S(1)} %bitcast.35), channel_id=1, replica_groups=mesh['grp'=2,'fsdp'=16,'tp'=8] {'tp'}, dimensions={0} | all-to-all | bytes 524288 | tf_op jit(solution)/shard_map/all_to_all | solution.py:439
  (121 shorter events, 27.5 us)
Async XLA Ops:
  0.6 11.0 %collective-permute-start.1 = (bf16[256,512]{1,0:T(8,128)(2,1)}, bf16[256,512]{1,0:T(8,128)(2,1)S(1)}, u32[]{:S(2)}, u32[]{:S(2)}) collective-permute-start(bf16[256,512]{1,0:T(8,128)(2,1)} %refs_0_.1), channel_id=1, source_target_pairs={{0,24},{8,0},{16,8},{24,16},{32,56},{40,32},{48,40},{56,48},{64,88... | collective-permute-start | bytes 786440 | tf_op jit(solution)/shard_map/weight_gather/ppermute | solution.py:226
  2.6 15.1 %collective-permute-start.9 = (bf16[256,512]{1,0:T(8,128)(2,1)}, bf16[256,512]{1,0:T(8,128)(2,1)S(1)}, u32[]{:S(2)}, u32[]{:S(2)}) collective-permute-start(bf16[256,512]{1,0:T(8,128)(2,1)} %refs_0_.1), channel_id=1, source_target_pairs={{0,8},{8,16},{16,24},{24,0},{32,40},{40,48},{48,56},{56,32},{64,72... | collective-permute-start | bytes 786440 | tf_op jit(solution)/shard_map/weight_gather/ppermute | solution.py:227
  2.7 16.9 %collective-permute-start.2 = (bf16[256,512]{1,0:T(8,128)(2,1)}, bf16[256,512]{1,0:T(8,128)(2,1)S(1)}, u32[]{:S(2)}, u32[]{:S(2)}) collective-permute-start(bf16[256,512]{1,0:T(8,128)(2,1)} %refs_0_.1), channel_id=1, source_target_pairs={{0,96},{8,104},{16,112},{24,120},{32,0},{40,8},{48,16},{56,24},{64... | collective-permute-start | bytes 786440 | tf_op jit(solution)/shard_map/weight_gather/ppermute | solution.py:231
  5.8 15.1 %collective-permute-start.3 = (bf16[256,512]{1,0:T(8,128)(2,1)}, bf16[256,512]{1,0:T(8,128)(2,1)}, u32[]{:S(2)}, u32[]{:S(2)}) collective-permute-start(bf16[256,512]{1,0:T(8,128)(2,1)} %refs_0_.1), channel_id=1, source_target_pairs={{0,32},{8,40},{16,48},{24,56},{32,64},{40,72},{48,80},{56,88},{64,... | collective-permute-start | bytes 786440 | tf_op jit(solution)/shard_map/weight_gather/ppermute | solution.py:231
  11.6 10.1 %collective-permute-start.6 = (bf16[256,512]{1,0:T(8,128)(2,1)S(1)}, bf16[256,512]{1,0:T(8,128)(2,1)S(1)}, u32[]{:S(2)}, u32[]{:S(2)}) collective-permute-start(bf16[256,512]{1,0:T(8,128)(2,1)S(1)} %collective-permute-done.1.refs_1_), channel_id=1, source_target_pairs={{0,24},{8,0},{16,8},{24,16},{32,56},{40,32},{48,40},{56,48},{64,88... | collective-permute-start | bytes 786440 | tf_op jit(solution)/shard_map/weight_gather/ppermute | solution.py:229
  14.4 10.3 %collective-permute-start.4 = (bf16[256,512]{1,0:T(8,128)(2,1)S(1)}, bf16[256,512]{1,0:T(8,128)(2,1)S(1)}, u32[]{:S(2)}, u32[]{:S(2)}) collective-permute-start(bf16[256,512]{1,0:T(8,128)(2,1)S(1)} %collective-permute-done.1.refs_1_), channel_id=1, source_target_pairs={{0,96},{8,104},{16,112},{24,120},{32,0},{40,8},{48,16},{56,24},{64... | collective-permute-start | bytes 786440 | tf_op jit(solution)/shard_map/weight_gather/ppermute | solution.py:231
  17.7 10.6 %collective-permute-start.5 = (bf16[256,512]{1,0:T(8,128)(2,1)S(1)}, bf16[256,512]{1,0:T(8,128)(2,1)}, u32[]{:S(2)}, u32[]{:S(2)}) collective-permute-start(bf16[256,512]{1,0:T(8,128)(2,1)S(1)} %collective-permute-done.1.refs_1_), channel_id=1, source_target_pairs={{0,32},{8,40},{16,48},{24,56},{32,64},{40,72},{48,80},{56,88},{64,... | collective-permute-start | bytes 786440 | tf_op jit(solution)/shard_map/weight_gather/ppermute | solution.py:231
  19.7 10.4 %collective-permute-start.10 = (bf16[256,512]{1,0:T(8,128)(2,1)S(1)}, bf16[256,512]{1,0:T(8,128)(2,1)}, u32[]{:S(2)}, u32[]{:S(2)}) collective-permute-start(bf16[256,512]{1,0:T(8,128)(2,1)S(1)} %collective-permute-done.9.refs_3_), channel_id=1, source_target_pairs={{0,96},{8,104},{16,112},{24,120},{32,0},{40,8},{48,16},{56,24},{64... | collective-permute-start | bytes 786440 | tf_op jit(solution)/shard_map/weight_gather/ppermute | solution.py:231
  20.9 12.8 %collective-permute-start.11 = (bf16[256,512]{1,0:T(8,128)(2,1)S(1)}, bf16[256,512]{1,0:T(8,128)(2,1)S(1)}, u32[]{:S(2)}, u32[]{:S(2)}) collective-permute-start(bf16[256,512]{1,0:T(8,128)(2,1)S(1)} %collective-permute-done.9.refs_3_), channel_id=1, source_target_pairs={{0,32},{8,40},{16,48},{24,56},{32,64},{40,72},{48,80},{56,88},{64,... | collective-permute-start | bytes 786440 | tf_op jit(solution)/shard_map/weight_gather/ppermute | solution.py:231
  21.7 12.0 %collective-permute-start.7 = (bf16[256,512]{1,0:T(8,128)(2,1)S(1)}, bf16[256,512]{1,0:T(8,128)(2,1)}, u32[]{:S(2)}, u32[]{:S(2)}) collective-permute-start(bf16[256,512]{1,0:T(8,128)(2,1)S(1)} %collective-permute-done.6.refs_2_), channel_id=1, source_target_pairs={{0,96},{8,104},{16,112},{24,120},{32,0},{40,8},{48,16},{56,24},{64... | collective-permute-start | bytes 786440 | tf_op jit(solution)/shard_map/weight_gather/ppermute | solution.py:231
  24.8 12.3 %collective-permute-start.8 = (bf16[256,512]{1,0:T(8,128)(2,1)S(1)}, bf16[256,512]{1,0:T(8,128)(2,1)S(1)}, u32[]{:S(2)}, u32[]{:S(2)}) collective-permute-start(bf16[256,512]{1,0:T(8,128)(2,1)S(1)} %collective-permute-done.6.refs_2_), channel_id=1, source_target_pairs={{0,32},{8,40},{16,48},{24,56},{32,64},{40,72},{48,80},{56,88},{64,... | collective-permute-start | bytes 786440 | tf_op jit(solution)/shard_map/weight_gather/ppermute | solution.py:231
  37.8 6.4 %collective-permute-start.12 = (bf16[256,4096]{1,0:T(8,128)(2,1)}, bf16[256,4096]{1,0:T(8,128)(2,1)}, u32[]{:S(2)}, u32[]{:S(2)}) collective-permute-start(bf16[256,4096]{1,0:T(8,128)(2,1)} %get-tuple-element.31), channel_id=1, source_target_pairs={{0,128},{128,0},{1,129},{129,1},{2,130},{130,2},{3,131},{131,3},{4... | collective-permute-start | bytes 6291464 | tf_op jit(solution)/shard_map/rows_swap/ppermute | solution.py:242
  38.9 19.1 %collective-permute-start.13 = (bf16[256,512]{1,0:T(8,128)(2,1)}, bf16[256,512]{1,0:T(8,128)(2,1)S(1)}, u32[]{:S(2)}, u32[]{:S(2)}) collective-permute-start(bf16[256,512]{1,0:T(8,128)(2,1)} %collective-permute-done.3.refs_8_), channel_id=1, source_target_pairs={{0,32},{8,40},{16,48},{24,56},{32,64},{40,72},{48,80},{56,88},{64,... | collective-permute-start | bytes 786440 | tf_op jit(solution)/shard_map/weight_gather/ppermute | solution.py:236
  39.2 18.8 %collective-permute-start.14 = (bf16[256,512]{1,0:T(8,128)(2,1)}, bf16[256,512]{1,0:T(8,128)(2,1)S(1)}, u32[]{:S(2)}, u32[]{:S(2)}) collective-permute-start(bf16[256,512]{1,0:T(8,128)(2,1)} %collective-permute-done.5.refs_9_), channel_id=1, source_target_pairs={{0,32},{8,40},{16,48},{24,56},{32,64},{40,72},{48,80},{56,88},{64,... | collective-permute-start | bytes 786440 | tf_op jit(solution)/shard_map/weight_gather/ppermute | solution.py:236
  40.8 17.2 %collective-permute-start.15 = (bf16[256,512]{1,0:T(8,128)(2,1)}, bf16[256,512]{1,0:T(8,128)(2,1)S(1)}, u32[]{:S(2)}, u32[]{:S(2)}) collective-permute-start(bf16[256,512]{1,0:T(8,128)(2,1)} %collective-permute-done.7.refs_6_), channel_id=1, source_target_pairs={{0,96},{8,104},{16,112},{24,120},{32,0},{40,8},{48,16},{56,24},{64... | collective-permute-start | bytes 786440 | tf_op jit(solution)/shard_map/weight_gather/ppermute | solution.py:236
  42.5 15.6 %collective-permute-start.16 = (bf16[256,512]{1,0:T(8,128)(2,1)}, bf16[256,512]{1,0:T(8,128)(2,1)S(1)}, u32[]{:S(2)}, u32[]{:S(2)}) collective-permute-start(bf16[256,512]{1,0:T(8,128)(2,1)} %collective-permute-done.10.refs_7_), channel_id=1, source_target_pairs={{0,96},{8,104},{16,112},{24,120},{32,0},{40,8},{48,16},{56,24},{64... | collective-permute-start | bytes 786440 | tf_op jit(solution)/shard_map/weight_gather/ppermute | solution.py:236
  44.2 16.7 %collective-permute-start = (s32[33,128]{1,0:T(8,128)S(1)}, s32[33,128]{1,0:T(8,128)}, u32[]{:S(2)}, u32[]{:S(2)}) collective-permute-start(s32[33,128]{1,0:T(8,128)S(1)} %fusion.10), channel_id=1, source_target_pairs={{0,128},{128,0},{1,129},{129,1},{2,130},{130,2},{3,131},{131,3},{4... | collective-permute-start | bytes 50696 | tf_op jit(solution)/shard_map/rows_swap/ppermute | solution.py:245
  46.9 28.1 %all-to-all-start = ((bf16[32,48,256]{2,1,0:T(8,128)(2,1)}), bf16[32,48,256]{2,1,0:T(8,128)(2,1)S(1)}, u32[]{:S(2)}, u32[]{:S(2)}) async-start(bf16[32,48,256]{2,1,0:T(8,128)(2,1)} %bitcast.11), calls=%async_computation | async-start | bytes 1572864 | tf_op jit(solution)/shard_map/columns_exchange/all_to_all | solution.py:276
  75.0 7.9 %collective-permute-start.24 = (f32[32,256]{1,0:T(8,128)S(1)}, f32[32,256]{1,0:T(8,128)S(1)}, u32[]{:S(2)}, u32[]{:S(2)}) collective-permute-start(f32[32,256]{1,0:T(8,128)S(1)} %add.55), channel_id=1, source_target_pairs={{0,1},{1,0},{2,3},{3,2},{4,5},{5,4},{6,7},{7,6},{8,9},{9,8},{10,11... | collective-permute-start | bytes 98312 | tf_op jit(solution)/shard_map/quant_sum/ppermute | solution.py:358
  79.8 24.2 %collective-permute-start.20 = (bf16[2,16,48,256]{3,2,1,0:T(8,128)(2,1)S(1)}, bf16[2,16,48,256]{3,2,1,0:T(8,128)(2,1)S(1)}, u32[]{:S(2)}, u32[]{:S(2)}) collective-permute-start(bf16[2,16,48,256]{3,2,1,0:T(8,128)(2,1)S(1)} %bitcast.30), channel_id=1, source_target_pairs={{0,6},{1,7},{2,0},{3,1},{4,2},{5,3},{6,4},{7,5},{8,14},{9,15},{10,... | collective-permute-start | bytes 2359304 | tf_op jit(solution)/shard_map/columns_round_x/ppermute | solution.py:360
  83.7 11.6 %collective-permute-start.25 = (bf16[128,512]{1,0:T(8,128)(2,1)S(1)}, bf16[128,512]{1,0:T(8,128)(2,1)S(1)}, u32[]{:S(2)}, u32[]{:S(2)}) collective-permute-start(bf16[128,512]{1,0:T(8,128)(2,1)S(1)} %fusion.5.own_ref), channel_id=1, source_target_pairs={{0,24},{8,0},{16,8},{24,16},{32,56},{40,32},{48,40},{56,48},{64,88... | collective-permute-start | bytes 393224 | tf_op jit(solution)/shard_map/grad_gather/ppermute | solution.py:401
  85.2 23.1 %collective-permute-start.21 = (bf16[2,16,48,256]{3,2,1,0:T(8,128)(2,1)S(1)}, bf16[2,16,48,256]{3,2,1,0:T(8,128)(2,1)S(1)}, u32[]{:S(2)}, u32[]{:S(2)}) collective-permute-start(bf16[2,16,48,256]{3,2,1,0:T(8,128)(2,1)S(1)} %bitcast.31), channel_id=1, source_target_pairs={{0,2},{1,3},{2,4},{3,5},{4,6},{5,7},{6,0},{7,1},{8,10},{9,11},{10,... | collective-permute-start | bytes 2359304 | tf_op jit(solution)/shard_map/columns_round_x/ppermute | solution.py:361
  86.7 8.6 %collective-permute-start.26 = (bf16[128,512]{1,0:T(8,128)(2,1)S(1)}, bf16[128,512]{1,0:T(8,128)(2,1)S(1)}, u32[]{:S(2)}, u32[]{:S(2)}) collective-permute-start(bf16[128,512]{1,0:T(8,128)(2,1)S(1)} %fusion.5.own_ref), channel_id=1, source_target_pairs={{0,16},{8,24},{16,0},{24,8},{32,48},{40,56},{48,32},{56,40},{64,80... | collective-permute-start | bytes 393224 | tf_op jit(solution)/shard_map/grad_gather/ppermute | solution.py:401
  87.7 8.5 %collective-permute-start.27 = (bf16[128,512]{1,0:T(8,128)(2,1)S(1)}, bf16[128,512]{1,0:T(8,128)(2,1)S(1)}, u32[]{:S(2)}, u32[]{:S(2)}) collective-permute-start(bf16[128,512]{1,0:T(8,128)(2,1)S(1)} %fusion.5.own_ref), channel_id=1, source_target_pairs={{0,8},{8,16},{16,24},{24,0},{32,40},{40,48},{48,56},{56,32},{64,72... | collective-permute-start | bytes 393224 | tf_op jit(solution)/shard_map/grad_gather/ppermute | solution.py:401
  95.3 6.4 %collective-permute-start.28 = (bf16[128,512]{1,0:T(8,128)(2,1)S(1)}, bf16[128,512]{1,0:T(8,128)(2,1)S(1)}, u32[]{:S(2)}, u32[]{:S(2)}) collective-permute-start(bf16[128,512]{1,0:T(8,128)(2,1)S(1)} %fusion.5.own_ref), channel_id=1, source_target_pairs={{0,96},{8,104},{16,112},{24,120},{32,0},{40,8},{48,16},{56,24},{64... | collective-permute-start | bytes 393224 | tf_op jit(solution)/shard_map/grad_gather/ppermute | solution.py:399
  101.7 10.9 %collective-permute-start.29 = (bf16[384,512]{1,0:T(8,128)(2,1)S(1)}, bf16[384,512]{1,0:T(8,128)(2,1)S(1)}, u32[]{:S(2)}, u32[]{:S(2)}) collective-permute-start(bf16[384,512]{1,0:T(8,128)(2,1)S(1)} %constant_dynamic-update-slice_fusion.line_ref), channel_id=1, source_target_pairs={{0,96},{8,104},{16,112},{24,120},{32,0},{40,8},{48,16},{56,24},{64... | collective-permute-start | bytes 1179656 | tf_op jit(solution)/shard_map/grad_gather/ppermute | solution.py:406
  102.4 13.5 %collective-permute-start.31 = (bf16[384,512]{1,0:T(8,128)(2,1)S(1)}, bf16[384,512]{1,0:T(8,128)(2,1)S(1)}, u32[]{:S(2)}, u32[]{:S(2)}) collective-permute-start(bf16[384,512]{1,0:T(8,128)(2,1)S(1)} %constant_dynamic-update-slice_fusion.line_ref), channel_id=1, source_target_pairs={{0,32},{8,40},{16,48},{24,56},{32,64},{40,72},{48,80},{56,88},{64,... | collective-permute-start | bytes 1179656 | tf_op jit(solution)/shard_map/grad_gather/ppermute | solution.py:405
  104.0 12.1 %collective-permute-start.22 = (bf16[16,48,256]{2,1,0:T(8,128)(2,1)S(1)}, bf16[16,48,256]{2,1,0:T(8,128)(2,1)S(1)}, u32[]{:S(2)}, u32[]{:S(2)}) collective-permute-start(bf16[16,48,256]{2,1,0:T(8,128)(2,1)S(1)} %slice_bitcast_fusion.1), channel_id=1, source_target_pairs={{0,6},{1,7},{2,0},{3,1},{4,2},{5,3},{6,4},{7,5},{8,14},{9,15},{10,... | collective-permute-start | bytes 1179656 | tf_op jit(solution)/shard_map/columns_round_x/ppermute | solution.py:362
  108.3 9.1 %collective-permute-start.23 = (bf16[16,48,256]{2,1,0:T(8,128)(2,1)S(1)}, bf16[16,48,256]{2,1,0:T(8,128)(2,1)S(1)}, u32[]{:S(2)}, u32[]{:S(2)}) collective-permute-start(bf16[16,48,256]{2,1,0:T(8,128)(2,1)S(1)} %slice_bitcast_fusion), channel_id=1, source_target_pairs={{0,2},{1,3},{2,4},{3,5},{4,6},{5,7},{6,0},{7,1},{8,10},{9,11},{10,... | collective-permute-start | bytes 1179656 | tf_op jit(solution)/shard_map/columns_round_x/ppermute | solution.py:363
  108.4 7.5 %collective-permute-start.30 = (bf16[128,512]{1,0:T(8,128)(2,1)S(1)}, bf16[128,512]{1,0:T(8,128)(2,1)S(1)}, u32[]{:S(2)}, u32[]{:S(2)}) collective-permute-start(bf16[128,512]{1,0:T(8,128)(2,1)S(1)} %fusion.5.own_ref), channel_id=1, source_target_pairs={{0,32},{8,40},{16,48},{24,56},{32,64},{40,72},{48,80},{56,88},{64,... | collective-permute-start | bytes 393224 | tf_op jit(solution)/shard_map/grad_gather/ppermute | solution.py:400
  112.6 10.9 %collective-permute-start.34 = (bf16[256,512]{1,0:T(8,128)(2,1)S(1)}, bf16[256,512]{1,0:T(8,128)(2,1)S(1)}, u32[]{:S(2)}, u32[]{:S(2)}) collective-permute-start(bf16[256,512]{1,0:T(8,128)(2,1)S(1)} %slice.61), channel_id=1, source_target_pairs={{0,96},{8,104},{16,112},{24,120},{32,0},{40,8},{48,16},{56,24},{64... | collective-permute-start | bytes 786440 | tf_op jit(solution)/shard_map/grad_gather/ppermute | solution.py:408
  115.9 7.6 %collective-permute-start.33 = (bf16[128,512]{1,0:T(8,128)(2,1)S(1)}, bf16[128,512]{1,0:T(8,128)(2,1)S(1)}, u32[]{:S(2)}, u32[]{:S(2)}) collective-permute-start(bf16[128,512]{1,0:T(8,128)(2,1)S(1)} %slice.60), channel_id=1, source_target_pairs={{0,32},{8,40},{16,48},{24,56},{32,64},{40,72},{48,80},{56,88},{64,... | collective-permute-start | bytes 393224 | tf_op jit(solution)/shard_map/grad_gather/ppermute | solution.py:407
  (22 other events, 359.2 us)

commit v11 on v8

--- a/solution.py
+++ b/solution.py
@@ -398,7 +398,9 @@
     with jax.named_scope("grad_gather"):
         b0 = lax.ppermute(grad_preact, "fsdp", y_from(1))
         a0 = lax.ppermute(grad_preact, "fsdp", y_from(3))
-        pieces_z = tuple(lax.ppermute(grad_preact, "fsdp", z_from(k)) for k in range(1, Z))
+        after_g = lax.ppermute(grad_preact, "fsdp", z_from(1))
+        before_g = lax.ppermute(grad_preact, "fsdp", z_from(3))
+        pieces_z = (after_g, lax.ppermute(after_g, "fsdp", z_from(1)), before_g)
         pieces_z, _ = lax.optimization_barrier((pieces_z, (b0, a0)))
         line = jnp.concatenate(pieces_z, 0)
         f0 = lax.ppermute(a0, "fsdp", y_from(3))

time: 149 us -> 143 us (0.960)
  the two profiles are of different devices: /device:TPU:32 before, /device:TPU:1 now
where the time goes in v11:
time: 143 us
  starting transfers between devices  65.9 us (46%)
  waiting for transfers between devices  33.4 us (23%)
  Pallas kernels  18 us (13%)
  blocking collectives  17.9 us (13%)
  other arithmetic  3.25 us (2%)
  matrix products  1.84 us (1%)
  local copies, waits for them, and re-layouts  1.63 us (1%)
    all_to_all x1, blocking collectives, shards(): lax.all_to_all(updated, 'tp', split_axis=0, concat_axis=1, tiled=True)  17.9 us
    ppermute x4, starting transfers between devices, shards(): lax.ppermute(line, 'fsdp', y_from(1))  10.6 us
    ppermute x4, waiting for transfers between devices, shards(): lax.ppermute(line, 'fsdp', y_from(3))  6.87 us
    ppermute x1, starting transfers between devices, shards(): torso_grad = mine + lax.ppermute(theirs, 'grp', SWAP)  5.91 us
    pallas_call x1, Pallas kernels, shards(): pl.pallas_call(norm_kernel, grid=(rows_block // tile,), out_shape=(jax.Sh...  5.77 us
    ppermute x1, starting transfers between devices, shards(): after_z = lax.ppermute(torso_weight, 'fsdp', z_from(1))  5.25 us
    ppermute x1, waiting for transfers between devices, shards(): far_b = lax.ppermute(before[1], 'tp', x_from(3))  5.13 us
    ppermute x4, waiting for transfers between devices, shards(): lax.ppermute(line, 'fsdp', y_from(1))  4.97 us
  transfers between devices with their start and end apart: 37, of which 17 were waited for; matrix products, arithmetic and copies ran while one was open for 3% of the time, Pallas kernels for 12%

profile of v11, /device:TPU:1, one launch (start us, length us, event | category | flops | bytes accessed | tf_op | source)
XLA Modules:
  0.0 142.9 jit_solution(10510284512632672091)
XLA Ops:
  0.6 5.3 %collective-permute-start.1 = (bf16[256,512]{1,0:T(8,128)(2,1)}, bf16[256,512]{1,0:T(8,128)(2,1)S(1)}, u32[]{:S(2)}, u32[]{:S(2)}) collective-permute-start(bf16[256,512]{1,0:T(8,128)(2,1)} %refs_0_.1), channel_id=1, source_target_pairs={{0,24},{8,0},{16,8},{24,16},{32,56},{40,32},{48,40},{56,48},{64,88... | collective-permute-start | bytes 786440 | tf_op jit(solution)/shard_map/weight_gather/ppermute | solution.py:226
  5.9 2.7 %collective-permute-start.2 = (bf16[256,512]{1,0:T(8,128)(2,1)}, bf16[256,512]{1,0:T(8,128)(2,1)S(1)}, u32[]{:S(2)}, u32[]{:S(2)}) collective-permute-start(bf16[256,512]{1,0:T(8,128)(2,1)} %refs_0_.1), channel_id=1, source_target_pairs={{0,96},{8,104},{16,112},{24,120},{32,0},{40,8},{48,16},{56,24},{64... | collective-permute-start | bytes 786440 | tf_op jit(solution)/shard_map/weight_gather/ppermute | solution.py:231
  8.7 5.8 %norm.1 = (bf16[256,4096]{1,0:T(8,128)(2,1)S(1)}, bf16[256,4096]{1,0:T(8,128)(2,1)}) custom-call(s32[4]{0:T(128)S(1)} %pad_add_fusion.1.where_ref, bf16[256,8192]{1,0:T(8,128)(2,1)} %bitcast.33, f32[1,8192]{1,0:T(1,128)} %bitcast.39), custom_call_target="tpu_custom_call" | custom-call | flops 12582912 | bytes 8388608 | tf_op jit(solution)/shard_map/rows_swap/norm/pallas_call | solution.py:207
  14.5 3.3 %collective-permute-start.6 = (bf16[256,512]{1,0:T(8,128)(2,1)S(1)}, bf16[256,512]{1,0:T(8,128)(2,1)S(1)}, u32[]{:S(2)}, u32[]{:S(2)}) collective-permute-start(bf16[256,512]{1,0:T(8,128)(2,1)S(1)} %collective-permute-done.1.refs_1_), channel_id=1, source_target_pairs={{0,24},{8,0},{16,8},{24,16},{32,56},{40,32},{48,40},{56,48},{64,88... | collective-permute-start | bytes 786440 | tf_op jit(solution)/shard_map/weight_gather/ppermute | solution.py:229
  17.8 2.7 %collective-permute-start.4 = (bf16[256,512]{1,0:T(8,128)(2,1)S(1)}, bf16[256,512]{1,0:T(8,128)(2,1)S(1)}, u32[]{:S(2)}, u32[]{:S(2)}) collective-permute-start(bf16[256,512]{1,0:T(8,128)(2,1)S(1)} %collective-permute-done.1.refs_1_), channel_id=1, source_target_pairs={{0,96},{8,104},{16,112},{24,120},{32,0},{40,8},{48,16},{56,24},{64... | collective-permute-start | bytes 786440 | tf_op jit(solution)/shard_map/weight_gather/ppermute | solution.py:231
  20.6 2.7 %collective-permute-start.10 = (bf16[256,512]{1,0:T(8,128)(2,1)S(1)}, bf16[256,512]{1,0:T(8,128)(2,1)}, u32[]{:S(2)}, u32[]{:S(2)}) collective-permute-start(bf16[256,512]{1,0:T(8,128)(2,1)S(1)} %collective-permute-done.9.refs_3_), channel_id=1, source_target_pairs={{0,96},{8,104},{16,112},{24,120},{32,0},{40,8},{48,16},{56,24},{64... | collective-permute-start | bytes 786440 | tf_op jit(solution)/shard_map/weight_gather/ppermute | solution.py:231
  24.0 2.6 %collective-permute-start.7 = (bf16[256,512]{1,0:T(8,128)(2,1)S(1)}, bf16[256,512]{1,0:T(8,128)(2,1)}, u32[]{:S(2)}, u32[]{:S(2)}) collective-permute-start(bf16[256,512]{1,0:T(8,128)(2,1)S(1)} %collective-permute-done.6.refs_2_), channel_id=1, source_target_pairs={{0,96},{8,104},{16,112},{24,120},{32,0},{40,8},{48,16},{56,24},{64... | collective-permute-start | bytes 786440 | tf_op jit(solution)/shard_map/weight_gather/ppermute | solution.py:231
  27.1 2.6 %collective-permute-done.10.refs_7_ = bf16[256,512]{1,0:T(8,128)(2,1)} collective-permute-done((bf16[256,512]{1,0:T(8,128)(2,1)S(1)}, bf16[256,512]{1,0:T(8,128)(2,1)}, u32[]{:S(2)}, u32[]{:S(2)}) %collective-permute-start.10) | collective-permute-done | bytes 262176 | tf_op jit(solution)/shard_map/weight_gather/ppermute | solution.py:231
  29.7 3.2 %collective-permute-done.11.refs_11_ = bf16[256,512]{1,0:T(8,128)(2,1)S(1)} collective-permute-done((bf16[256,512]{1,0:T(8,128)(2,1)S(1)}, bf16[256,512]{1,0:T(8,128)(2,1)S(1)}, u32[]{:S(2)}, u32[]{:S(2)}) %collective-permute-start.11) | collective-permute-done | bytes 262176 | tf_op jit(solution)/shard_map/weight_gather/ppermute | solution.py:231
  32.9 2.4 %collective-permute-done.7.refs_6_ = bf16[256,512]{1,0:T(8,128)(2,1)} collective-permute-done((bf16[256,512]{1,0:T(8,128)(2,1)S(1)}, bf16[256,512]{1,0:T(8,128)(2,1)}, u32[]{:S(2)}, u32[]{:S(2)}) %collective-permute-start.7) | collective-permute-done | bytes 262176 | tf_op jit(solution)/shard_map/weight_gather/ppermute | solution.py:231
  35.3 3.1 %collective-permute-done.8.refs_10_ = bf16[256,512]{1,0:T(8,128)(2,1)S(1)} collective-permute-done((bf16[256,512]{1,0:T(8,128)(2,1)S(1)}, bf16[256,512]{1,0:T(8,128)(2,1)S(1)}, u32[]{:S(2)}, u32[]{:S(2)}) %collective-permute-start.8) | collective-permute-done | bytes 262176 | tf_op jit(solution)/shard_map/weight_gather/ppermute | solution.py:231
  39.1 3.3 %collective-permute-start.12 = (bf16[256,4096]{1,0:T(8,128)(2,1)}, bf16[256,4096]{1,0:T(8,128)(2,1)}, u32[]{:S(2)}, u32[]{:S(2)}) collective-permute-start(bf16[256,4096]{1,0:T(8,128)(2,1)} %get-tuple-element.31), channel_id=1, source_target_pairs={{0,128},{128,0},{1,129},{129,1},{2,130},{130,2},{3,131},{131,3},{4... | collective-permute-start | bytes 6291464 | tf_op jit(solution)/shard_map/rows_swap/ppermute | solution.py:242
  43.6 2.9 %collective-permute-start.15 = (bf16[256,512]{1,0:T(8,128)(2,1)}, bf16[256,512]{1,0:T(8,128)(2,1)S(1)}, u32[]{:S(2)}, u32[]{:S(2)}) collective-permute-start(bf16[256,512]{1,0:T(8,128)(2,1)} %collective-permute-done.7.refs_6_), channel_id=1, source_target_pairs={{0,96},{8,104},{16,112},{24,120},{32,0},{40,8},{48,16},{56,24},{64... | collective-permute-start | bytes 786440 | tf_op jit(solution)/shard_map/weight_gather/ppermute | solution.py:236
  50.5 4.7 %all-to-all-start = ((bf16[32,48,256]{2,1,0:T(8,128)(2,1)}), bf16[32,48,256]{2,1,0:T(8,128)(2,1)S(1)}, u32[]{:S(2)}, u32[]{:S(2)}) async-start(bf16[32,48,256]{2,1,0:T(8,128)(2,1)} %bitcast.11), calls=%async_computation | async-start | bytes 1572864 | tf_op jit(solution)/shard_map/columns_exchange/all_to_all | solution.py:276
  55.2 4.3 %early.1.early_ref = f32[512,512]{1,0:T(8,128)S(1)} custom-call(s32[4]{0:T(128)S(1)} %pad_add_fusion.1.where_ref, bf16[256,4096]{1,0:T(8,128)(2,1)} %copy-done.1, bf16[256,4096]{1,0:T(8,128)(2,1)} %collective-permute-done.12.got_ref, bf16[256,512]{1,0:T(8,128)(2,1)} %refs_0_.1, bf16[256,512]{1,0:T(8,128)(2,1)} %copy-done.3, bf16[256,512]{1,0:T(8,128)(2,1)} %copy-done.6, ...), custom_call_target="tpu_custom_call" | custom-call | flops 1610612736 | bytes 7340032 | tf_op jit(solution)/shard_map/early/pallas_call | solution.py:322
  59.5 2.6 %late.1 = (f32[256,512]{1,0:T(8,128)S(1)}, f32[256,512]{1,0:T(8,128)S(1)}) custom-call(s32[4]{0:T(128)S(1)} %pad_add_fusion.1.where_ref, bf16[256,4096]{1,0:T(8,128)(2,1)} %copy-done.1, bf16[256,4096]{1,0:T(8,128)(2,1)} %collective-permute-done.12.got_ref, f32[512,512]{1,0:T(8,128)S(1)} %early.1.early_ref, ...), custom_call_target="tpu_custom_call" | custom-call | flops 536870912 | bytes 3145728 | tf_op jit(solution)/shard_map/late/pallas_call | solution.py:332
  62.1 3.6 %collective-permute-start.17 = (f32[256,512]{1,0:T(8,128)S(1)}, f32[256,512]{1,0:T(8,128)S(1)}, u32[]{:S(2)}, u32[]{:S(2)}) collective-permute-start(f32[256,512]{1,0:T(8,128)S(1)} %get-tuple-element.39), channel_id=1, source_target_pairs={{0,128},{128,0},{1,129},{129,1},{2,130},{130,2},{3,131},{131,3},{4... | collective-permute-start | bytes 1572872 | tf_op jit(solution)/shard_map/ppermute | solution.py:342
  71.2 2.8 %collective-permute-start.19 = (f32[32,256]{1,0:T(8,128)S(1)}, f32[32,256]{1,0:T(8,128)S(1)}, u32[]{:S(2)}, u32[]{:S(2)}) collective-permute-start(f32[32,256]{1,0:T(8,128)S(1)} %add.54), channel_id=1, source_target_pairs={{0,4},{1,5},{2,6},{3,7},{4,0},{5,1},{6,2},{7,3},{8,12},{9,13},{10,... | collective-permute-start | bytes 98312 | tf_op jit(solution)/shard_map/quant_sum/ppermute | solution.py:356
  75.6 4.3 %collective-permute-start.24 = (f32[32,256]{1,0:T(8,128)S(1)}, f32[32,256]{1,0:T(8,128)S(1)}, u32[]{:S(2)}, u32[]{:S(2)}) collective-permute-start(f32[32,256]{1,0:T(8,128)S(1)} %add.55), channel_id=1, source_target_pairs={{0,1},{1,0},{2,3},{3,2},{4,5},{5,4},{6,7},{7,6},{8,9},{9,8},{10,11... | collective-permute-start | bytes 98312 | tf_op jit(solution)/shard_map/quant_sum/ppermute | solution.py:358
  80.1 2.5 %collective-permute-start.20 = (bf16[2,16,48,256]{3,2,1,0:T(8,128)(2,1)S(1)}, bf16[2,16,48,256]{3,2,1,0:T(8,128)(2,1)S(1)}, u32[]{:S(2)}, u32[]{:S(2)}) collective-permute-start(bf16[2,16,48,256]{3,2,1,0:T(8,128)(2,1)S(1)} %bitcast.30), channel_id=1, source_target_pairs={{0,6},{1,7},{2,0},{3,1},{4,2},{5,3},{6,4},{7,5},{8,14},{9,15},{10,... | collective-permute-start | bytes 2359304 | tf_op jit(solution)/shard_map/columns_round_x/ppermute | solution.py:360
  83.3 2.7 %collective-permute-start.25 = (bf16[128,512]{1,0:T(8,128)(2,1)S(1)}, bf16[128,512]{1,0:T(8,128)(2,1)S(1)}, u32[]{:S(2)}, u32[]{:S(2)}) collective-permute-start(bf16[128,512]{1,0:T(8,128)(2,1)S(1)} %fusion.5.own_ref), channel_id=1, source_target_pairs={{0,24},{8,0},{16,8},{24,16},{32,56},{40,32},{48,40},{56,48},{64,88... | collective-permute-start | bytes 393224 | tf_op jit(solution)/shard_map/grad_gather/ppermute | solution.py:401
  87.0 2.1 %collective-permute-start.28 = (bf16[128,512]{1,0:T(8,128)(2,1)S(1)}, bf16[128,512]{1,0:T(8,128)(2,1)S(1)}, u32[]{:S(2)}, u32[]{:S(2)}) collective-permute-start(bf16[128,512]{1,0:T(8,128)(2,1)S(1)} %fusion.5.own_ref), channel_id=1, source_target_pairs={{0,96},{8,104},{16,112},{24,120},{32,0},{40,8},{48,16},{56,24},{64... | collective-permute-start | bytes 393224 | tf_op jit(solution)/shard_map/grad_gather/ppermute | solution.py:399
  89.1 3.5 %collective-permute-done.27 = bf16[128,512]{1,0:T(8,128)(2,1)S(1)} collective-permute-done((bf16[128,512]{1,0:T(8,128)(2,1)S(1)}, bf16[128,512]{1,0:T(8,128)(2,1)S(1)}, u32[]{:S(2)}, u32[]{:S(2)}) %collective-permute-start.27) | collective-permute-done | bytes 131104 | tf_op jit(solution)/shard_map/grad_gather/ppermute | solution.py:402
  92.7 1.8 %collective-permute-done.29.a0_ref = bf16[128,512]{1,0:T(8,128)(2,1)S(1)} collective-permute-done((bf16[128,512]{1,0:T(8,128)(2,1)S(1)}, bf16[128,512]{1,0:T(8,128)(2,1)S(1)}, u32[]{:S(2)}, u32[]{:S(2)}) %collective-permute-start.29) | collective-permute-done | bytes 131104 | tf_op jit(solution)/shard_map/grad_gather/ppermute | solution.py:400
  94.5 2.3 %collective-permute-done.26 = bf16[128,512]{1,0:T(8,128)(2,1)S(1)} collective-permute-done((bf16[128,512]{1,0:T(8,128)(2,1)S(1)}, bf16[128,512]{1,0:T(8,128)(2,1)S(1)}, u32[]{:S(2)}, u32[]{:S(2)}) %collective-permute-start.26) | collective-permute-done | bytes 131104 | tf_op jit(solution)/shard_map/grad_gather/ppermute | solution.py:403
  98.6 2.6 %collective-permute-start.22 = (bf16[16,48,256]{2,1,0:T(8,128)(2,1)S(1)}, bf16[16,48,256]{2,1,0:T(8,128)(2,1)S(1)}, u32[]{:S(2)}, u32[]{:S(2)}) collective-permute-start(bf16[16,48,256]{2,1,0:T(8,128)(2,1)S(1)} %slice_bitcast_fusion.1), channel_id=1, source_target_pairs={{0,6},{1,7},{2,0},{3,1},{4,2},{5,3},{6,4},{7,5},{8,14},{9,15},{10,... | collective-permute-start | bytes 1179656 | tf_op jit(solution)/shard_map/columns_round_x/ppermute | solution.py:362
  101.2 2.4 %collective-permute-done.21.before_ref = bf16[2,16,48,256]{3,2,1,0:T(8,128)(2,1)S(1)} collective-permute-done((bf16[2,16,48,256]{3,2,1,0:T(8,128)(2,1)S(1)}, bf16[2,16,48,256]{3,2,1,0:T(8,128)(2,1)S(1)}, u32[]{:S(2)}, u32[]{:S(2)}) %collective-permute-start.21) | collective-permute-done | bytes 786464 | tf_op jit(solution)/shard_map/columns_round_x/ppermute | solution.py:361
  104.1 2.7 %collective-permute-start.34 = (bf16[256,512]{1,0:T(8,128)(2,1)S(1)}, bf16[256,512]{1,0:T(8,128)(2,1)S(1)}, u32[]{:S(2)}, u32[]{:S(2)}) collective-permute-start(bf16[256,512]{1,0:T(8,128)(2,1)S(1)} %slice.61), channel_id=1, source_target_pairs={{0,96},{8,104},{16,112},{24,120},{32,0},{40,8},{48,16},{56,24},{64... | collective-permute-start | bytes 786440 | tf_op jit(solution)/shard_map/grad_gather/ppermute | solution.py:410
  106.9 5.1 %collective-permute-done.23.far_b_ref = bf16[16,48,256]{2,1,0:T(8,128)(2,1)S(1)} collective-permute-done((bf16[16,48,256]{2,1,0:T(8,128)(2,1)S(1)}, bf16[16,48,256]{2,1,0:T(8,128)(2,1)S(1)}, u32[]{:S(2)}, u32[]{:S(2)}) %collective-permute-start.23) | collective-permute-done | bytes 393248 | tf_op jit(solution)/shard_map/columns_round_x/ppermute | solution.py:363
  112.1 2.4 %columns.1.cols_ref = bf16[512,2048]{1,0:T(8,128)(2,1)S(1)} custom-call(s32[4]{0:T(128)S(1)} %pad_add_fusion.1.where_ref, bf16[2,16,48,256]{3,2,1,0:T(8,128)(2,1)S(1)} %bitcast.32, bf16[2,16,48,256]{3,2,1,0:T(8,128)(2,1)S(1)} %collective-permute-done.20.after_ref, bf16[2,16,48,256]{3,2,1,0:T(8,128)(2,1)S(1)} %collective-permute-done.21.before_ref, ...), custom_call_target="tpu_custom_call" | custom-call | bytes 4194304 | tf_op jit(solution)/shard_map/columns_round_x/columns/pallas_call | solution.py:364
  115.9 5.9 %collective-permute-start.35 = (f32[256,512]{1,0:T(8,128)S(1)}, f32[256,512]{1,0:T(8,128)S(1)}, u32[]{:S(2)}, u32[]{:S(2)}) collective-permute-start(f32[256,512]{1,0:T(8,128)S(1)} %get-tuple-element.47), channel_id=1, source_target_pairs={{0,128},{128,0},{1,129},{129,1},{2,130},{130,2},{3,131},{131,3},{4... | collective-permute-start | bytes 1572872 | tf_op jit(solution)/shard_map/ppermute | solution.py:439
  124.3 17.9 %all_to_all.24 = bf16[8,32,512]{2,1,0:T(8,128)(2,1)S(1)} all-to-all(bf16[8,32,512]{2,1,0:T(8,128)(2,1)S(1)} %bitcast.35), channel_id=1, replica_groups=mesh['grp'=2,'fsdp'=16,'tp'=8] {'tp'}, dimensions={0} | all-to-all | bytes 524288 | tf_op jit(solution)/shard_map/all_to_all | solution.py:441
  (121 shorter events, 23.2 us)
Async XLA Ops:
  0.6 13.9 %collective-permute-start.1 = (bf16[256,512]{1,0:T(8,128)(2,1)}, bf16[256,512]{1,0:T(8,128)(2,1)S(1)}, u32[]{:S(2)}, u32[]{:S(2)}) collective-permute-start(bf16[256,512]{1,0:T(8,128)(2,1)} %refs_0_.1), channel_id=1, source_target_pairs={{0,24},{8,0},{16,8},{24,16},{32,56},{40,32},{48,40},{56,48},{64,88... | collective-permute-start | bytes 786440 | tf_op jit(solution)/shard_map/weight_gather/ppermute | solution.py:226
  5.9 14.6 %collective-permute-start.9 = (bf16[256,512]{1,0:T(8,128)(2,1)}, bf16[256,512]{1,0:T(8,128)(2,1)S(1)}, u32[]{:S(2)}, u32[]{:S(2)}) collective-permute-start(bf16[256,512]{1,0:T(8,128)(2,1)} %refs_0_.1), channel_id=1, source_target_pairs={{0,8},{8,16},{16,24},{24,0},{32,40},{40,48},{48,56},{56,32},{64,72... | collective-permute-start | bytes 786440 | tf_op jit(solution)/shard_map/weight_gather/ppermute | solution.py:227
  5.9 14.6 %collective-permute-start.2 = (bf16[256,512]{1,0:T(8,128)(2,1)}, bf16[256,512]{1,0:T(8,128)(2,1)S(1)}, u32[]{:S(2)}, u32[]{:S(2)}) collective-permute-start(bf16[256,512]{1,0:T(8,128)(2,1)} %refs_0_.1), channel_id=1, source_target_pairs={{0,96},{8,104},{16,112},{24,120},{32,0},{40,8},{48,16},{56,24},{64... | collective-permute-start | bytes 786440 | tf_op jit(solution)/shard_map/weight_gather/ppermute | solution.py:231
  8.6 14.6 %collective-permute-start.3 = (bf16[256,512]{1,0:T(8,128)(2,1)}, bf16[256,512]{1,0:T(8,128)(2,1)}, u32[]{:S(2)}, u32[]{:S(2)}) collective-permute-start(bf16[256,512]{1,0:T(8,128)(2,1)} %refs_0_.1), channel_id=1, source_target_pairs={{0,32},{8,40},{16,48},{24,56},{32,64},{40,72},{48,80},{56,88},{64,... | collective-permute-start | bytes 786440 | tf_op jit(solution)/shard_map/weight_gather/ppermute | solution.py:231
  14.5 9.5 %collective-permute-start.6 = (bf16[256,512]{1,0:T(8,128)(2,1)S(1)}, bf16[256,512]{1,0:T(8,128)(2,1)S(1)}, u32[]{:S(2)}, u32[]{:S(2)}) collective-permute-start(bf16[256,512]{1,0:T(8,128)(2,1)S(1)} %collective-permute-done.1.refs_1_), channel_id=1, source_target_pairs={{0,24},{8,0},{16,8},{24,16},{32,56},{40,32},{48,40},{56,48},{64,88... | collective-permute-start | bytes 786440 | tf_op jit(solution)/shard_map/weight_gather/ppermute | solution.py:229
  17.8 8.7 %collective-permute-start.4 = (bf16[256,512]{1,0:T(8,128)(2,1)S(1)}, bf16[256,512]{1,0:T(8,128)(2,1)S(1)}, u32[]{:S(2)}, u32[]{:S(2)}) collective-permute-start(bf16[256,512]{1,0:T(8,128)(2,1)S(1)} %collective-permute-done.1.refs_1_), channel_id=1, source_target_pairs={{0,96},{8,104},{16,112},{24,120},{32,0},{40,8},{48,16},{56,24},{64... | collective-permute-start | bytes 786440 | tf_op jit(solution)/shard_map/weight_gather/ppermute | solution.py:231
  20.5 6.5 %collective-permute-start.5 = (bf16[256,512]{1,0:T(8,128)(2,1)S(1)}, bf16[256,512]{1,0:T(8,128)(2,1)}, u32[]{:S(2)}, u32[]{:S(2)}) collective-permute-start(bf16[256,512]{1,0:T(8,128)(2,1)S(1)} %collective-permute-done.1.refs_1_), channel_id=1, source_target_pairs={{0,32},{8,40},{16,48},{24,56},{32,64},{40,72},{48,80},{56,88},{64,... | collective-permute-start | bytes 786440 | tf_op jit(solution)/shard_map/weight_gather/ppermute | solution.py:231
  20.6 9.1 %collective-permute-start.10 = (bf16[256,512]{1,0:T(8,128)(2,1)S(1)}, bf16[256,512]{1,0:T(8,128)(2,1)}, u32[]{:S(2)}, u32[]{:S(2)}) collective-permute-start(bf16[256,512]{1,0:T(8,128)(2,1)S(1)} %collective-permute-done.9.refs_3_), channel_id=1, source_target_pairs={{0,96},{8,104},{16,112},{24,120},{32,0},{40,8},{48,16},{56,24},{64... | collective-permute-start | bytes 786440 | tf_op jit(solution)/shard_map/weight_gather/ppermute | solution.py:231
  23.2 9.7 %collective-permute-start.11 = (bf16[256,512]{1,0:T(8,128)(2,1)S(1)}, bf16[256,512]{1,0:T(8,128)(2,1)S(1)}, u32[]{:S(2)}, u32[]{:S(2)}) collective-permute-start(bf16[256,512]{1,0:T(8,128)(2,1)S(1)} %collective-permute-done.9.refs_3_), channel_id=1, source_target_pairs={{0,32},{8,40},{16,48},{24,56},{32,64},{40,72},{48,80},{56,88},{64,... | collective-permute-start | bytes 786440 | tf_op jit(solution)/shard_map/weight_gather/ppermute | solution.py:231
  24.0 11.3 %collective-permute-start.7 = (bf16[256,512]{1,0:T(8,128)(2,1)S(1)}, bf16[256,512]{1,0:T(8,128)(2,1)}, u32[]{:S(2)}, u32[]{:S(2)}) collective-permute-start(bf16[256,512]{1,0:T(8,128)(2,1)S(1)} %collective-permute-done.6.refs_2_), channel_id=1, source_target_pairs={{0,96},{8,104},{16,112},{24,120},{32,0},{40,8},{48,16},{56,24},{64... | collective-permute-start | bytes 786440 | tf_op jit(solution)/shard_map/weight_gather/ppermute | solution.py:231
  26.6 11.8 %collective-permute-start.8 = (bf16[256,512]{1,0:T(8,128)(2,1)S(1)}, bf16[256,512]{1,0:T(8,128)(2,1)S(1)}, u32[]{:S(2)}, u32[]{:S(2)}) collective-permute-start(bf16[256,512]{1,0:T(8,128)(2,1)S(1)} %collective-permute-done.6.refs_2_), channel_id=1, source_target_pairs={{0,32},{8,40},{16,48},{24,56},{32,64},{40,72},{48,80},{56,88},{64,... | collective-permute-start | bytes 786440 | tf_op jit(solution)/shard_map/weight_gather/ppermute | solution.py:231
  39.1 8.6 %collective-permute-start.12 = (bf16[256,4096]{1,0:T(8,128)(2,1)}, bf16[256,4096]{1,0:T(8,128)(2,1)}, u32[]{:S(2)}, u32[]{:S(2)}) collective-permute-start(bf16[256,4096]{1,0:T(8,128)(2,1)} %get-tuple-element.31), channel_id=1, source_target_pairs={{0,128},{128,0},{1,129},{129,1},{2,130},{130,2},{3,131},{131,3},{4... | collective-permute-start | bytes 6291464 | tf_op jit(solution)/shard_map/rows_swap/ppermute | solution.py:242
  43.5 16.0 %collective-permute-start.13 = (bf16[256,512]{1,0:T(8,128)(2,1)}, bf16[256,512]{1,0:T(8,128)(2,1)S(1)}, u32[]{:S(2)}, u32[]{:S(2)}) collective-permute-start(bf16[256,512]{1,0:T(8,128)(2,1)} %collective-permute-done.3.refs_8_), channel_id=1, source_target_pairs={{0,32},{8,40},{16,48},{24,56},{32,64},{40,72},{48,80},{56,88},{64,... | collective-permute-start | bytes 786440 | tf_op jit(solution)/shard_map/weight_gather/ppermute | solution.py:236
  43.5 16.0 %collective-permute-start.14 = (bf16[256,512]{1,0:T(8,128)(2,1)}, bf16[256,512]{1,0:T(8,128)(2,1)S(1)}, u32[]{:S(2)}, u32[]{:S(2)}) collective-permute-start(bf16[256,512]{1,0:T(8,128)(2,1)} %collective-permute-done.5.refs_9_), channel_id=1, source_target_pairs={{0,32},{8,40},{16,48},{24,56},{32,64},{40,72},{48,80},{56,88},{64,... | collective-permute-start | bytes 786440 | tf_op jit(solution)/shard_map/weight_gather/ppermute | solution.py:236
  43.6 15.9 %collective-permute-start.15 = (bf16[256,512]{1,0:T(8,128)(2,1)}, bf16[256,512]{1,0:T(8,128)(2,1)S(1)}, u32[]{:S(2)}, u32[]{:S(2)}) collective-permute-start(bf16[256,512]{1,0:T(8,128)(2,1)} %collective-permute-done.7.refs_6_), channel_id=1, source_target_pairs={{0,96},{8,104},{16,112},{24,120},{32,0},{40,8},{48,16},{56,24},{64... | collective-permute-start | bytes 786440 | tf_op jit(solution)/shard_map/weight_gather/ppermute | solution.py:236
  46.5 13.0 %collective-permute-start.16 = (bf16[256,512]{1,0:T(8,128)(2,1)}, bf16[256,512]{1,0:T(8,128)(2,1)S(1)}, u32[]{:S(2)}, u32[]{:S(2)}) collective-permute-start(bf16[256,512]{1,0:T(8,128)(2,1)} %collective-permute-done.10.refs_7_), channel_id=1, source_target_pairs={{0,96},{8,104},{16,112},{24,120},{32,0},{40,8},{48,16},{56,24},{64... | collective-permute-start | bytes 786440 | tf_op jit(solution)/shard_map/weight_gather/ppermute | solution.py:236
  47.7 18.0 %collective-permute-start = (s32[33,128]{1,0:T(8,128)S(1)}, s32[33,128]{1,0:T(8,128)}, u32[]{:S(2)}, u32[]{:S(2)}) collective-permute-start(s32[33,128]{1,0:T(8,128)S(1)} %fusion.10), channel_id=1, source_target_pairs={{0,128},{128,0},{1,129},{129,1},{2,130},{130,2},{3,131},{131,3},{4... | collective-permute-start | bytes 50696 | tf_op jit(solution)/shard_map/rows_swap/ppermute | solution.py:245
  50.5 25.1 %all-to-all-start = ((bf16[32,48,256]{2,1,0:T(8,128)(2,1)}), bf16[32,48,256]{2,1,0:T(8,128)(2,1)S(1)}, u32[]{:S(2)}, u32[]{:S(2)}) async-start(bf16[32,48,256]{2,1,0:T(8,128)(2,1)} %bitcast.11), calls=%async_computation | async-start | bytes 1572864 | tf_op jit(solution)/shard_map/columns_exchange/all_to_all | solution.py:276
  75.6 7.0 %collective-permute-start.24 = (f32[32,256]{1,0:T(8,128)S(1)}, f32[32,256]{1,0:T(8,128)S(1)}, u32[]{:S(2)}, u32[]{:S(2)}) collective-permute-start(f32[32,256]{1,0:T(8,128)S(1)} %add.55), channel_id=1, source_target_pairs={{0,1},{1,0},{2,3},{3,2},{4,5},{5,4},{6,7},{7,6},{8,9},{9,8},{10,11... | collective-permute-start | bytes 98312 | tf_op jit(solution)/shard_map/quant_sum/ppermute | solution.py:358
  80.1 18.5 %collective-permute-start.20 = (bf16[2,16,48,256]{3,2,1,0:T(8,128)(2,1)S(1)}, bf16[2,16,48,256]{3,2,1,0:T(8,128)(2,1)S(1)}, u32[]{:S(2)}, u32[]{:S(2)}) collective-permute-start(bf16[2,16,48,256]{3,2,1,0:T(8,128)(2,1)S(1)} %bitcast.30), channel_id=1, source_target_pairs={{0,6},{1,7},{2,0},{3,1},{4,2},{5,3},{6,4},{7,5},{8,14},{9,15},{10,... | collective-permute-start | bytes 2359304 | tf_op jit(solution)/shard_map/columns_round_x/ppermute | solution.py:360
  83.3 5.8 %collective-permute-start.25 = (bf16[128,512]{1,0:T(8,128)(2,1)S(1)}, bf16[128,512]{1,0:T(8,128)(2,1)S(1)}, u32[]{:S(2)}, u32[]{:S(2)}) collective-permute-start(bf16[128,512]{1,0:T(8,128)(2,1)S(1)} %fusion.5.own_ref), channel_id=1, source_target_pairs={{0,24},{8,0},{16,8},{24,16},{32,56},{40,32},{48,40},{56,48},{64,88... | collective-permute-start | bytes 393224 | tf_op jit(solution)/shard_map/grad_gather/ppermute | solution.py:401
  86.0 6.7 %collective-permute-start.27 = (bf16[128,512]{1,0:T(8,128)(2,1)S(1)}, bf16[128,512]{1,0:T(8,128)(2,1)S(1)}, u32[]{:S(2)}, u32[]{:S(2)}) collective-permute-start(bf16[128,512]{1,0:T(8,128)(2,1)S(1)} %fusion.5.own_ref), channel_id=1, source_target_pairs={{0,8},{8,16},{16,24},{24,0},{32,40},{40,48},{48,56},{56,32},{64,72... | collective-permute-start | bytes 393224 | tf_op jit(solution)/shard_map/grad_gather/ppermute | solution.py:402
  86.0 17.6 %collective-permute-start.21 = (bf16[2,16,48,256]{3,2,1,0:T(8,128)(2,1)S(1)}, bf16[2,16,48,256]{3,2,1,0:T(8,128)(2,1)S(1)}, u32[]{:S(2)}, u32[]{:S(2)}) collective-permute-start(bf16[2,16,48,256]{3,2,1,0:T(8,128)(2,1)S(1)} %bitcast.31), channel_id=1, source_target_pairs={{0,2},{1,3},{2,4},{3,5},{4,6},{5,7},{6,0},{7,1},{8,10},{9,11},{10,... | collective-permute-start | bytes 2359304 | tf_op jit(solution)/shard_map/columns_round_x/ppermute | solution.py:361
  87.0 5.7 %collective-permute-start.28 = (bf16[128,512]{1,0:T(8,128)(2,1)S(1)}, bf16[128,512]{1,0:T(8,128)(2,1)S(1)}, u32[]{:S(2)}, u32[]{:S(2)}) collective-permute-start(bf16[128,512]{1,0:T(8,128)(2,1)S(1)} %fusion.5.own_ref), channel_id=1, source_target_pairs={{0,96},{8,104},{16,112},{24,120},{32,0},{40,8},{48,16},{56,24},{64... | collective-permute-start | bytes 393224 | tf_op jit(solution)/shard_map/grad_gather/ppermute | solution.py:399
  96.9 7.2 %collective-permute-start.30 = (bf16[384,512]{1,0:T(8,128)(2,1)S(1)}, bf16[384,512]{1,0:T(8,128)(2,1)S(1)}, u32[]{:S(2)}, u32[]{:S(2)}) collective-permute-start(bf16[384,512]{1,0:T(8,128)(2,1)S(1)} %constant_dynamic-update-slice_fusion.line_ref), channel_id=1, source_target_pairs={{0,96},{8,104},{16,112},{24,120},{32,0},{40,8},{48,16},{56,24},{64... | collective-permute-start | bytes 1179656 | tf_op jit(solution)/shard_map/grad_gather/ppermute | solution.py:408
  98.6 8.2 %collective-permute-start.31 = (bf16[384,512]{1,0:T(8,128)(2,1)S(1)}, bf16[384,512]{1,0:T(8,128)(2,1)S(1)}, u32[]{:S(2)}, u32[]{:S(2)}) collective-permute-start(bf16[384,512]{1,0:T(8,128)(2,1)S(1)} %constant_dynamic-update-slice_fusion.line_ref), channel_id=1, source_target_pairs={{0,32},{8,40},{16,48},{24,56},{32,64},{40,72},{48,80},{56,88},{64,... | collective-permute-start | bytes 1179656 | tf_op jit(solution)/shard_map/grad_gather/ppermute | solution.py:407
  98.6 8.3 %collective-permute-start.22 = (bf16[16,48,256]{2,1,0:T(8,128)(2,1)S(1)}, bf16[16,48,256]{2,1,0:T(8,128)(2,1)S(1)}, u32[]{:S(2)}, u32[]{:S(2)}) collective-permute-start(bf16[16,48,256]{2,1,0:T(8,128)(2,1)S(1)} %slice_bitcast_fusion.1), channel_id=1, source_target_pairs={{0,6},{1,7},{2,0},{3,1},{4,2},{5,3},{6,4},{7,5},{8,14},{9,15},{10,... | collective-permute-start | bytes 1179656 | tf_op jit(solution)/shard_map/columns_round_x/ppermute | solution.py:362
  103.7 8.4 %collective-permute-start.23 = (bf16[16,48,256]{2,1,0:T(8,128)(2,1)S(1)}, bf16[16,48,256]{2,1,0:T(8,128)(2,1)S(1)}, u32[]{:S(2)}, u32[]{:S(2)}) collective-permute-start(bf16[16,48,256]{2,1,0:T(8,128)(2,1)S(1)} %slice_bitcast_fusion), channel_id=1, source_target_pairs={{0,2},{1,3},{2,4},{3,5},{4,6},{5,7},{6,0},{7,1},{8,10},{9,11},{10,... | collective-permute-start | bytes 1179656 | tf_op jit(solution)/shard_map/columns_round_x/ppermute | solution.py:363
  104.1 11.4 %collective-permute-start.34 = (bf16[256,512]{1,0:T(8,128)(2,1)S(1)}, bf16[256,512]{1,0:T(8,128)(2,1)S(1)}, u32[]{:S(2)}, u32[]{:S(2)}) collective-permute-start(bf16[256,512]{1,0:T(8,128)(2,1)S(1)} %slice.61), channel_id=1, source_target_pairs={{0,96},{8,104},{16,112},{24,120},{32,0},{40,8},{48,16},{56,24},{64... | collective-permute-start | bytes 786440 | tf_op jit(solution)/shard_map/grad_gather/ppermute | solution.py:410
  106.8 8.6 %collective-permute-start.32 = (bf16[128,512]{1,0:T(8,128)(2,1)S(1)}, bf16[128,512]{1,0:T(8,128)(2,1)S(1)}, u32[]{:S(2)}, u32[]{:S(2)}) collective-permute-start(bf16[128,512]{1,0:T(8,128)(2,1)S(1)} %collective-permute-done.29.a0_ref), channel_id=1, source_target_pairs={{0,32},{8,40},{16,48},{24,56},{32,64},{40,72},{48,80},{56,88},{64,... | collective-permute-start | bytes 393224 | tf_op jit(solution)/shard_map/grad_gather/ppermute | solution.py:406
  106.8 8.6 %collective-permute-start.33 = (bf16[128,512]{1,0:T(8,128)(2,1)S(1)}, bf16[128,512]{1,0:T(8,128)(2,1)S(1)}, u32[]{:S(2)}, u32[]{:S(2)}) collective-permute-start(bf16[128,512]{1,0:T(8,128)(2,1)S(1)} %slice.60), channel_id=1, source_target_pairs={{0,32},{8,40},{16,48},{24,56},{32,64},{40,72},{48,80},{56,88},{64,... | collective-permute-start | bytes 393224 | tf_op jit(solution)/shard_map/grad_gather/ppermute | solution.py:409
  115.9 7.5 %collective-permute-start.35 = (f32[256,512]{1,0:T(8,128)S(1)}, f32[256,512]{1,0:T(8,128)S(1)}, u32[]{:S(2)}, u32[]{:S(2)}) collective-permute-start(f32[256,512]{1,0:T(8,128)S(1)} %get-tuple-element.47), channel_id=1, source_target_pairs={{0,128},{128,0},{1,129},{129,1},{2,130},{130,2},{3,131},{131,3},{4... | collective-permute-start | bytes 1572872 | tf_op jit(solution)/shard_map/ppermute | solution.py:439
  (22 other events, 392.1 us)
